TPU v7x, 32 devices: a whole 2x2x4 slice. The times are simulated.
32 devices in a mesh: groups: 2 (over x), node: 16 (over z, y, core).
Axes of the slice: x: 2, y: 2, z: 4, core: 2. Of those that a mesh axis runs over, the one named last changes fastest.
Arguments:
- unit_costs: bfloat16 [1024, 24, 2048], P(('groups', 'node')), parts along dimension 0, may hold values from -15 to 15
- hour_duals: bfloat16 [1024, 24, 2048], P(('groups', 'node')), parts along dimension 0, may hold values from -3 to 3
- inverse: bfloat16 [2048, 2048], replicated, may hold values from -0.5 to 1.5, as said below
- weights: int32 [1024], P(('groups', 'node')), parts along dimension 0, may hold values from 1 to 120
- section_three: int32 [1024], P(('groups', 'node')), parts along dimension 0, may hold values from 0 to 63, as said below
- prev_first: bfloat16 [16, 2048], P('groups'), parts along dimension 0, may hold values from -6 to 6
- prev_second: bfloat16 [32, 8, 512], P(('groups', 'node')), parts along dimension 0, may hold values from -6 to 6
- prev_third: bfloat16 [128, 8, 2048], P(('groups', 'node')), parts along dimension 0, may hold values from -6 to 6
- eta_mean: float32 [2], P('groups'), parts along dimension 0, may hold values from -2 to -1
- eta_duals: float32 [1024], P(('groups', 'node')), parts along dimension 0, may hold values from -1.2 to 1.2
Outputs:
- duals_new: bfloat16 [1024, 24, 2048], P(('groups', 'node')), parts along dimension 0
- first_avg: float32 [16, 2048], P('groups'), parts along dimension 0
- second_avg: float32 [32, 8, 512], P(('groups', 'node')), parts along dimension 0
- third_avg: float32 [128, 8, 2048], P(('groups', 'node')), parts along dimension 0
- eta_avg: float32 [2], P('groups'), parts along dimension 0
- eta_duals_new: float32 [1024], P(('groups', 'node')), parts along dimension 0
There are 2 independent parts, one for each index of `groups`. A program takes and returns all parts, laid end to end along the dimension named above; an argument that names none is the same for every part. Nothing has to cross between parts.
Inputs may be any that keep to these rules, and one draw needn't show every extreme that they name: `inverse`: A fixed matrix of order 2048. `section_three`: scenario s lies below section-2 node n = s // 128: its section-3 node is n * 16 + b with b from 0 to 15; every section-3 node holds exactly 8 scenarios.
All inputs are finite; a program needn't handle non-finite values.
Results may differ from a plain program's by a relative error of at most 0.0082.
Values may be sent and summed in bfloat16 or wider, within the bound.
No kernel may reach another device: no remote copies, remote signals or barrier semaphores. Data moves between devices by JAX's collectives and lax.ppermute only.
A program may use at most 128 MiB of HBM per device.

v0:
```python
import jax
import jax.numpy as jnp
from jax import lax
from jax.sharding import PartitionSpec as P

BRANCH = 16


PENALTY = 1.0
CVAR_WEIGHT = 0.25
CVAR_LEVEL = 0.75


def partner(value, axis, stride):
    mask = 2**stride
    pairs = [(source, source ^ mask) for source in range(lax.axis_size(axis))]
    return lax.ppermute(value, axis, pairs)


def joined(own_part, peer_part, is_upper, along):
    return jnp.where(
        is_upper,
        jnp.concatenate((peer_part, own_part), along),
        jnp.concatenate((own_part, peer_part), along),
    )


def body(
    unit_costs,
    hour_duals,
    inverse,
    weights,
    section_three,
    prev_first,
    prev_second,
    prev_third,
    eta_mean,
    eta_duals,
):
    scenarios, hour_count, columns = unit_costs.shape
    section_len = hour_count // 3
    shares = BRANCH // 4
    my_index = lax.axis_index("node")
    quarter = my_index % 4
    second_table = prev_second
    third_table = prev_third
    for bit_num in range(2):
        is_upper = my_index // 2**bit_num % 2 == 1
        received = partner((second_table, third_table), "node", bit_num)
        second_table = joined(second_table, received[0], is_upper, 2)
        third_table = joined(third_table, received[1], is_upper, 0)
    choose = (section_three % BRANCH)[:, None] == jnp.arange(BRANCH, dtype=jnp.int32)[None, :]
    picker = choose.astype(jnp.bfloat16)
    third_anchor = jnp.dot(
        picker,
        third_table.reshape(BRANCH, section_len * columns),
        preferred_element_type=jnp.float32,
    )
    anchor = jnp.concatenate(
        (
            jnp.broadcast_to(
                prev_first.astype(jnp.float32)[None], (scenarios, section_len, columns)
            ),
            jnp.broadcast_to(
                second_table[0].astype(jnp.float32)[None], (scenarios, section_len, columns)
            ),
            third_anchor.reshape(scenarios, section_len, columns),
        ),
        axis=1,
    )
    target = (
        PENALTY * anchor - unit_costs.astype(jnp.float32) - hour_duals.astype(jnp.float32)
    ).astype(jnp.bfloat16)
    mass_vec = weights.astype(jnp.float32)
    mass_local = jnp.sum(mass_vec)
    flat = target.reshape(-1, columns)
    solution = jnp.dot(flat, inverse, preferred_element_type=jnp.float32).reshape(
        scenarios, -1, columns
    )
    first_part = jnp.sum(mass_vec[:, None, None] * solution[:, :section_len], axis=0)
    scen_cost = jnp.sum(unit_costs.astype(jnp.float32) * solution, axis=(1, 2)) / (
        hour_count * columns
    )
    low_end = eta_mean[0] - (CVAR_WEIGHT + eta_duals) / PENALTY
    high_end = low_end + CVAR_WEIGHT / ((1.0 - CVAR_LEVEL) * PENALTY)
    eta_value = jnp.minimum(jnp.maximum(scen_cost, low_end), high_end)
    first_sum, eta_total, mass_sum = lax.psum(
        (first_part, jnp.sum(mass_vec * eta_value), mass_local), "node"
    )
    weighted = choose.astype(jnp.float32) * mass_vec[:, None]
    third_part = jnp.dot(
        weighted.T,
        solution[:, 2 * section_len :].reshape(scenarios, section_len * columns),
        precision=lax.Precision.HIGHEST,
        preferred_element_type=jnp.float32,
    )
    third_mass = jnp.sum(weighted, axis=0)
    second_part = jnp.sum(
        mass_vec[:, None, None] * solution[:, section_len : 2 * section_len], axis=0
    )
    for bit_num in (1, 0):
        is_upper = my_index // 2**bit_num % 2 == 1
        half_cols = second_part.shape[1] // 2
        half_rows = third_part.shape[0] // 2
        keep_second = jnp.where(is_upper, second_part[:, half_cols:], second_part[:, :half_cols])
        send_second = jnp.where(is_upper, second_part[:, :half_cols], second_part[:, half_cols:])
        keep_third = jnp.where(is_upper, third_part[half_rows:], third_part[:half_rows])
        send_third = jnp.where(is_upper, third_part[:half_rows], third_part[half_rows:])
        received = partner((send_second, send_third, third_mass), "node", bit_num)
        second_part = keep_second + received[0]
        third_part = keep_third + received[1]
        third_mass = third_mass + received[2]
    own_mass = lax.dynamic_slice_in_dim(third_mass, quarter * shares, shares, 0)
    third_share = third_part / own_mass[:, None]
    second_share = second_part / jnp.sum(third_mass)
    second_whole = second_share
    third_whole = third_share
    for bit_num in range(2):
        is_upper = my_index // 2**bit_num % 2 == 1
        received = partner((second_whole, third_whole), "node", bit_num)
        second_whole = joined(second_whole, received[0], is_upper, 1)
        third_whole = joined(third_whole, received[1], is_upper, 0)
    first_avg = first_sum / mass_sum
    new_third = jnp.dot(
        choose.astype(jnp.float32),
        third_whole,
        precision=lax.Precision.HIGHEST,
        preferred_element_type=jnp.float32,
    ).reshape(scenarios, section_len, columns)
    new_anchor = jnp.concatenate(
        (
            jnp.broadcast_to(first_avg[None], (scenarios, section_len, columns)),
            jnp.broadcast_to(second_whole[None], (scenarios, section_len, columns)),
            new_third,
        ),
        axis=1,
    )
    duals_new = (hour_duals.astype(jnp.float32) + PENALTY * (solution - new_anchor)).astype(
        jnp.bfloat16
    )
    eta_level = eta_total / mass_sum
    eta_duals_new = eta_duals + PENALTY * (eta_value - eta_level)
    return (
        duals_new,
        first_avg,
        second_share[None],
        third_share.reshape(shares, section_len, columns),
        jnp.reshape(eta_level, (1,)),
        eta_duals_new,
    )


def solution(mesh):
    in_specs = (
        P(("groups", "node"), None, None),
        P(("groups", "node"), None, None),
        P(),
        P(("groups", "node")),
        P(("groups", "node")),
        P("groups", None),
        P(("groups", "node"), None, None),
        P(("groups", "node"), None, None),
        P("groups"),
        P(("groups", "node")),
    )
    out_specs = (
        P(("groups", "node"), None, None),
        P("groups", None),
        P(("groups", "node"), None, None),
        P(("groups", "node"), None, None),
        P("groups"),
        P(("groups", "node")),
    )
    return jax.shard_map(body, mesh=mesh, in_specs=in_specs, out_specs=out_specs, check_vma=False)
```

profile of v0, /device:TPU:0, one launch (start us, length us, event | category | flops | bytes accessed | tf_op | source)
XLA Modules:
  0.0 154.4 jit_solution(12685654493900703658)
XLA Ops:
  7.2 0.6 collective-permute-start
  7.8 0.7 and_select_fusion
  8.4 0.7 convert_element_type.35
  9.2 2.6 %collective-permute-start.6 = (f32[16]{0:T(128)S(1)}, f32[16]{0:T(128)S(1)}, u32[]{:S(2)}, u32[]{:S(2)}) collective-permute-start(f32[16]{0:T(128)S(1)} %select_reduce_fusion), channel_id=1, source_target_pairs={{0,2},{1,3},{2,0},{3,1},{4,6},{5,7},{6,4},{7,5},{8,10},{9,11},{10,... | collective-permute-start | bytes 200 | tf_op jit(solution)/shard_map/ppermute | solution.py:17
  11.8 0.2 collective-permute-start.2
  12.7 1.0 copy.21
  13.7 0.4 collective-permute-start.7
  14.1 0.8 maximum_select_fusion.9
  14.8 1.3 collective-permute-start.1
  16.2 0.8 maximum_select_fusion.10
  16.9 1.6 %collective-permute-done.1 = bf16[1,8,1024]{2,1,0:T(8,128)(2,1)S(1)} collective-permute-done((bf16[1,8,1024]{2,1,0:T(8,128)(2,1)S(1)}, bf16[1,8,1024]{2,1,0:T(8,128)(2,1)S(1)}, u32[]{:S(2)}, u32[]{:S(2)}) %collective-permute-start.1) | collective-permute-done | bytes 16416 | tf_op jit(solution)/shard_map/ppermute | solution.py:17
  18.7 1.0 maximum_select_fusion.4
  19.7 1.4 collective-permute-start.3
  21.1 0.2 maximum_select_fusion.5
  21.4 5.7 %collective-permute-done.3 = bf16[8,8,2048]{2,1,0:T(8,128)(2,1)S(1)} collective-permute-done((bf16[8,8,2048]{2,1,0:T(8,128)(2,1)S(1)}, bf16[8,8,2048]{2,1,0:T(8,128)(2,1)S(1)}, u32[]{:S(2)}, u32[]{:S(2)}) %collective-permute-start.3) | collective-permute-done | bytes 262176 | tf_op jit(solution)/shard_map/ppermute | solution.py:17
  27.3 0.5 fusion.14
  27.8 1.2 copy.17
  29.1 0.2 broadcast_in_dim.11
  29.3 0.2 broadcast_in_dim.10
  29.7 1.4 copy-done.1
  31.1 9.9 %fusion.4 = (f32[32]{0:T(128)S(1)}, f32[32,24,2048]{2,1,0:T(8,128)S(1)}) fusion(bf16[32,24,2048]{2,1,0:T(8,128)(2,1)S(1)} %copy-done.8, bf16[2048,2048]{1,0:T(8,128)(2,1)} %param.12, bf16[32,24,2048]{2,1,0:T(8,128)(2,1)S(1)} %copy-done.1, f32[32,8,2048]{2,1,0:T(8,128)S(1)} %copy.17, f32[32,8,2048]{2,1,0:T(8,128)S(1)} %broadcast_in_dim.11, ...), kind=kOutput, calls=%fused_computation.8 | convolution fusion | flops 6458179584 | bytes 27263104 | tf_op jit(solution)/shard_map/dot_general | solution.py:77
  41.0 1.7 %fusion.7 = (f32[8,2048]{1,0:T(8,128)}, f32[8,2048]{1,0:T(8,128)S(1)}, f32[32,8,2048]{2,1,0:T(8,128)S(1)}) fusion(f32[32,24,2048]{2,1,0:T(8,128)S(1)} %get-tuple-element.17, f32[32]{0:T(128)S(1)} %convert_element_type.35), kind=kLoop, calls=%fused_computation.13 | loop fusion | flops 2064384 | bytes 8519808 | tf_op jit(solution)/shard_map/reduce_sum | solution.py:80
  42.7 0.9 copy-done
  43.7 1.2 copy.22
  44.9 1.1 fusion.19
  46.1 1.7 %collective-permute-start.4 = (f32[8,1024]{1,0:T(8,128)S(1)}, f32[8,1024]{1,0:T(8,128)S(1)}, u32[]{:S(2)}, u32[]{:S(2)}) collective-permute-start(f32[8,1024]{1,0:T(8,128)S(1)} %slice_select_fusion.2), channel_id=1, source_target_pairs={{0,2},{1,3},{2,0},{3,1},{4,6},{5,7},{6,4},{7,5},{8,10},{9,11},{10,... | collective-permute-start | bytes 98312 | tf_op jit(solution)/shard_map/ppermute | solution.py:17
  47.8 0.5 collective-permute-start.10
  48.3 0.6 fusion.32
  49.0 1.4 collective-permute-done.4
  50.5 9.8 %collective-permute-done.10 = f32[8,16384]{1,0:T(8,128)S(1)} collective-permute-done((f32[8,16384]{1,0:T(8,128)S(1)}, f32[8,16384]{1,0:T(8,128)S(1)}, u32[]{:S(2)}, u32[]{:S(2)}) %collective-permute-start.10) | collective-permute-done | bytes 524320 | tf_op jit(solution)/shard_map/ppermute | solution.py:17
  60.6 0.6 multiply_reduce_fusion
  61.2 33.9 %all-reduce = (f32[]{:T(128)}, f32[]{:T(128)}) all-reduce(f32[]{:T(128)} %get-tuple-element.9, f32[]{:T(128)} %get-tuple-element.8), channel_id=1, replica_groups=mesh['groups'=2,'node'=16] {'node'}, use_global_device_ids=true, to_apply=%region_3.4 | all-reduce | flops 2 | bytes 16 | tf_op jit(solution)/shard_map/psum | solution.py:87
  96.4 0.7 add_divide_fusion.1
  97.3 0.6 collective-permute-start.12
  97.9 0.5 subtract_add_fusion
  98.5 0.6 collective-permute-done.12
  99.1 0.2 maximum_select_fusion.3
  99.3 1.5 collective-permute-start.13
  100.8 36.0 %all-reduce.3.cloned.1.call-done = f32[8,2048]{1,0:T(8,128)} async-done(((f32[8,2048]{1,0:T(8,128)}), f32[8,2048]{1,0:T(8,128)}) %all-reduce.3.cloned.1.call-update) | async-done | bytes 65552 | tf_op jit(solution)/shard_map/psum | solution.py:87
  136.7 1.5 broadcast_divide_fusion
  138.3 0.9 copy.30
  139.1 1.0 fusion.8
  140.2 1.2 copy.23
  141.4 0.2 broadcast_in_dim.13
  141.7 0.2 broadcast_in_dim.12
  141.9 0.3 slice-done.1
  142.2 1.2 copy-done.2
  143.5 2.9 %fusion.3 = bf16[32,24,2048]{2,1,0:T(8,128)(2,1)} fusion(bf16[32,24,2048]{2,1,0:T(8,128)(2,1)S(1)} %copy-done.2, f32[32,24,2048]{2,1,0:T(8,128)S(1)} %bitcast.36, f32[32,8,2048]{2,1,0:T(8,128)S(1)} %bitcast.37, f32[32,8,2048]{2,1,0:T(8,128)S(1)} %broadcast_in_dim.13, f32[32,8,2048]{2,1,0:T(8,128)S(1)} %broadcast_in_dim.12), kind=kLoop, calls=%fused_computation.7 | loop fusion | flops 9437184 | bytes 18874368 | tf_op jit(solution)/shard_map/convert_element_type | solution.py:138
  (50 shorter events, 1.5 us)
Async XLA Ops:
  7.2 129.6 %all-reduce.3.cloned.1.call-start = ((), (), s32[]{:S(2)}) async-start(), calls=%async_computation | async-start | bytes 131072 | tf_op jit(solution)/shard_map/psum | solution.py:87
  7.2 6.8 %collective-permute-start = (bf16[1,8,512]{2,1,0:T(8,128)(2,1)}, bf16[1,8,512]{2,1,0:T(8,128)(2,1)S(1)}, u32[]{:S(2)}, u32[]{:S(2)}) collective-permute-start(bf16[1,8,512]{2,1,0:T(8,128)(2,1)} %param.16), channel_id=1, source_target_pairs={{0,1},{1,0},{2,3},{3,2},{4,5},{5,4},{6,7},{7,6},{8,9},{9,8},{10,11... | collective-permute-start | bytes 24584 | tf_op jit(solution)/shard_map/ppermute | solution.py:17
  9.2 4.5 %collective-permute-start.6 = (f32[16]{0:T(128)S(1)}, f32[16]{0:T(128)S(1)}, u32[]{:S(2)}, u32[]{:S(2)}) collective-permute-start(f32[16]{0:T(128)S(1)} %select_reduce_fusion), channel_id=1, source_target_pairs={{0,2},{1,3},{2,0},{3,1},{4,6},{5,7},{6,4},{7,5},{8,10},{9,11},{10,... | collective-permute-start | bytes 200 | tf_op jit(solution)/shard_map/ppermute | solution.py:17
  11.8 6.8 %collective-permute-start.2 = (bf16[4,8,2048]{2,1,0:T(8,128)(2,1)}, bf16[4,8,2048]{2,1,0:T(8,128)(2,1)S(1)}, u32[]{:S(2)}, u32[]{:S(2)}) collective-permute-start(bf16[4,8,2048]{2,1,0:T(8,128)(2,1)} %param.17), channel_id=1, source_target_pairs={{0,1},{1,0},{2,3},{3,2},{4,5},{5,4},{6,7},{7,6},{8,9},{9,8},{10,11... | collective-permute-start | bytes 393224 | tf_op jit(solution)/shard_map/ppermute | solution.py:17
  13.7 34.6 %collective-permute-start.7 = (f32[16]{0:T(128)S(1)}, f32[16]{0:T(128)S(1)}, u32[]{:S(2)}, u32[]{:S(2)}) collective-permute-start(f32[16]{0:T(128)S(1)} %add.69), channel_id=1, source_target_pairs={{0,1},{1,0},{2,3},{3,2},{4,5},{5,4},{6,7},{7,6},{8,9},{9,8},{10,11... | collective-permute-start | bytes 200 | tf_op jit(solution)/shard_map/ppermute | solution.py:17
  14.8 3.7 %collective-permute-start.1 = (bf16[1,8,1024]{2,1,0:T(8,128)(2,1)S(1)}, bf16[1,8,1024]{2,1,0:T(8,128)(2,1)S(1)}, u32[]{:S(2)}, u32[]{:S(2)}) collective-permute-start(bf16[1,8,1024]{2,1,0:T(8,128)(2,1)S(1)} %maximum_select_fusion.9), channel_id=1, source_target_pairs={{0,2},{1,3},{2,0},{3,1},{4,6},{5,7},{6,4},{7,5},{8,10},{9,11},{10,... | collective-permute-start | bytes 49160 | tf_op jit(solution)/shard_map/ppermute | solution.py:17
  19.7 7.3 %collective-permute-start.3 = (bf16[8,8,2048]{2,1,0:T(8,128)(2,1)S(1)}, bf16[8,8,2048]{2,1,0:T(8,128)(2,1)S(1)}, u32[]{:S(2)}, u32[]{:S(2)}) collective-permute-start(bf16[8,8,2048]{2,1,0:T(8,128)(2,1)S(1)} %maximum_select_fusion.4), channel_id=1, source_target_pairs={{0,2},{1,3},{2,0},{3,1},{4,6},{5,7},{6,4},{7,5},{8,10},{9,11},{10,... | collective-permute-start | bytes 786440 | tf_op jit(solution)/shard_map/ppermute | solution.py:17
  27.8 1.5 copy-start.5
  27.8 1.9 %copy-start.8 = (bf16[32,24,2048]{2,1,0:T(8,128)(2,1)S(1)}, bf16[32,24,2048]{2,1,0:T(8,128)(2,1)}, u32[]{:S(2)}) copy-start(bf16[32,24,2048]{2,1,0:T(8,128)(2,1)} %param.10) | copy-start | bytes 9437188
  29.1 2.1 %copy-start.1 = (bf16[32,24,2048]{2,1,0:T(8,128)(2,1)S(1)}, bf16[32,24,2048]{2,1,0:T(8,128)(2,1)}, u32[]{:S(2)}) copy-start(bf16[32,24,2048]{2,1,0:T(8,128)(2,1)} %param.11) | copy-start | bytes 9437188
  41.0 2.7 %copy-start = (f32[32,24,2048]{2,1,0:T(8,128)}, f32[32,24,2048]{2,1,0:T(8,128)S(1)}, u32[]{:S(2)}) copy-start(f32[32,24,2048]{2,1,0:T(8,128)S(1)} %get-tuple-element.17) | copy-start | bytes 18874372
  46.0 14.5 %copy-start.6 = (f32[32]{0:T(128)S(1)}, f32[32]{0:T(128)}, u32[]{:S(2)}) copy-start(f32[32]{0:T(128)} %param.19) | copy-start | bytes 388
  46.0 14.5 %copy-start.7 = (s32[32]{0:T(128)S(1)}, s32[32]{0:T(128)}, u32[]{:S(2)}) copy-start(s32[32]{0:T(128)} %param.13) | copy-start | bytes 388
  46.1 4.3 %collective-permute-start.4 = (f32[8,1024]{1,0:T(8,128)S(1)}, f32[8,1024]{1,0:T(8,128)S(1)}, u32[]{:S(2)}, u32[]{:S(2)}) collective-permute-start(f32[8,1024]{1,0:T(8,128)S(1)} %slice_select_fusion.2), channel_id=1, source_target_pairs={{0,2},{1,3},{2,0},{3,1},{4,6},{5,7},{6,4},{7,5},{8,10},{9,11},{10,... | collective-permute-start | bytes 98312 | tf_op jit(solution)/shard_map/ppermute | solution.py:17
  47.8 12.5 %collective-permute-start.10 = (f32[8,16384]{1,0:T(8,128)S(1)}, f32[8,16384]{1,0:T(8,128)S(1)}, u32[]{:S(2)}, u32[]{:S(2)}) collective-permute-start(f32[8,16384]{1,0:T(8,128)S(1)} %slice_select_fusion), channel_id=1, source_target_pairs={{0,2},{1,3},{2,0},{3,1},{4,6},{5,7},{6,4},{7,5},{8,10},{9,11},{10,... | collective-permute-start | bytes 1572872 | tf_op jit(solution)/shard_map/ppermute | solution.py:17
  50.4 46.0 %collective-permute-start.5 = (f32[8,512]{1,0:T(8,128)S(1)}, f32[8,512]{1,0:T(8,128)S(1)}, u32[]{:S(2)}, u32[]{:S(2)}) collective-permute-start(f32[8,512]{1,0:T(8,128)S(1)} %slice_select_fusion.3), channel_id=1, source_target_pairs={{0,1},{1,0},{2,3},{3,2},{4,5},{5,4},{6,7},{7,6},{8,9},{9,8},{10,11... | collective-permute-start | bytes 49160 | tf_op jit(solution)/shard_map/ppermute | solution.py:17
  60.5 36.7 %collective-permute-start.11 = (f32[4,16384]{1,0:T(4,128)S(1)}, f32[4,16384]{1,0:T(4,128)S(1)}, u32[]{:S(2)}, u32[]{:S(2)}) collective-permute-start(f32[4,16384]{1,0:T(4,128)S(1)} %slice_select_fusion.1), channel_id=1, source_target_pairs={{0,1},{1,0},{2,3},{3,2},{4,5},{5,4},{6,7},{7,6},{8,9},{9,8},{10,11... | collective-permute-start | bytes 786440 | tf_op jit(solution)/shard_map/ppermute | solution.py:17
  97.1 44.3 %copy-start.4 = (f32[8,512]{1,0:T(8,128)}, f32[8,512]{1,0:T(8,128)S(1)}, u32[]{:S(2)}) copy-start(f32[8,512]{1,0:T(8,128)S(1)} %add_divide_fusion.1) | copy-start | bytes 49156
  97.1 1.3 collective-permute-start.8
  97.3 1.7 %collective-permute-start.12 = (f32[4,16384]{1,0:T(4,128)S(1)}, f32[4,16384]{1,0:T(4,128)S(1)}, u32[]{:S(2)}, u32[]{:S(2)}) collective-permute-start(f32[4,16384]{1,0:T(4,128)S(1)} %add_divide_fusion), channel_id=1, source_target_pairs={{0,1},{1,0},{2,3},{3,2},{4,5},{5,4},{6,7},{7,6},{8,9},{9,8},{10,11... | collective-permute-start | bytes 786440 | tf_op jit(solution)/shard_map/ppermute | solution.py:17
  98.4 39.8 %collective-permute-start.9 = (f32[8,1024]{1,0:T(8,128)S(1)}, f32[8,1024]{1,0:T(8,128)S(1)}, u32[]{:S(2)}, u32[]{:S(2)}) collective-permute-start(f32[8,1024]{1,0:T(8,128)S(1)} %maximum_select_fusion.8), channel_id=1, source_target_pairs={{0,2},{1,3},{2,0},{3,1},{4,6},{5,7},{6,4},{7,5},{8,10},{9,11},{10,... | collective-permute-start | bytes 98312 | tf_op jit(solution)/shard_map/ppermute | solution.py:17
  99.3 39.9 %collective-permute-start.13 = (f32[8,16384]{1,0:T(8,128)S(1)}, f32[8,16384]{1,0:T(8,128)S(1)}, u32[]{:S(2)}, u32[]{:S(2)}) collective-permute-start(f32[8,16384]{1,0:T(8,128)S(1)} %maximum_select_fusion.3), channel_id=1, source_target_pairs={{0,2},{1,3},{2,0},{3,1},{4,6},{5,7},{6,4},{7,5},{8,10},{9,11},{10,... | collective-permute-start | bytes 1572872 | tf_op jit(solution)/shard_map/ppermute | solution.py:17
  138.2 3.5 %copy-start.3 = (f32[8,2048]{1,0:T(8,128)}, f32[8,2048]{1,0:T(8,128)S(1)}, u32[]{:S(2)}) copy-start(f32[8,2048]{1,0:T(8,128)S(1)} %broadcast_divide_fusion) | copy-start | bytes 196612
  139.1 2.8 %slice-start = ((s8[6291456]{0:T(1024)(128)(4,1)}), s8[4194304]{0:T(1024)(128)(4,1)S(1)}, s32[]{:S(2)}) async-start(s8[6291456]{0:T(1024)(128)(4,1)} %bitcast.35), calls=%async_computation.1 | async-start | bytes 8388608
  140.2 2.0 %slice-start.1 = ((s8[6291456]{0:T(1024)(128)(4,1)}), s8[2097152]{0:T(1024)(128)(4,1)S(1)}, s32[]{:S(2)}) async-start(s8[6291456]{0:T(1024)(128)(4,1)} %bitcast.35), calls=%async_computation.2 | async-start | bytes 4194304
  141.4 2.0 %copy-start.2 = (bf16[32,24,2048]{2,1,0:T(8,128)(2,1)S(1)}, bf16[32,24,2048]{2,1,0:T(8,128)(2,1)}, u32[]{:S(2)}) copy-start(bf16[32,24,2048]{2,1,0:T(8,128)(2,1)} %param.11) | copy-start | bytes 9437188
Sparse Core Ops, SparseCore 0:
  49.1 87.5 all-reduce.2
where the time goes:
time: 156 us; the launch traced here: 154 us
  waiting for transfers between devices  55.2 us (35%)
  blocking collectives  33.9 us (22%)
  between operations  17.5 us (11%)
  other arithmetic  13.4 us (9%)
  matrix products  12.5 us (8%)
  starting transfers between devices  11 us (7%)
  local copies, waits for them, and re-layouts  10.9 us (7%)
    psum x1, waiting for transfers between devices, body(): lax.psum((first_part, jnp.sum(mass_vec * eta_value), mass_local), 'node')  36 us
    psum x1, blocking collectives, body(): lax.psum((first_part, jnp.sum(mass_vec * eta_value), mass_local), 'node')  33.9 us
    ppermute x14, waiting for transfers between devices, partner(): return lax.ppermute(value, axis, pairs)  19.2 us
    ppermute x14, starting transfers between devices, partner(): return lax.ppermute(value, axis, pairs)  10.9 us
    dot_general x1, matrix products, body(): jnp.dot(flat, inverse, preferred_element_type=jnp.float32)  9.87 us
    unnamed x28, local copies, waits for them, and re-layouts  8.66 us
    select_n x8, other arithmetic, joined(): jnp.where(is_upper, jnp.concatenate((peer_part, own_part), along), jnp.co...  3.12 us
  transfers between devices with their start and end apart: 15, of which 6 were waited for; matrix products, arithmetic and copies ran while one was open for 18% of the time, Pallas kernels for 0%

commit v1 on v0

v1 whole, which is shorter than its diff:
```python
import functools

import jax
import jax.numpy as jnp
from jax import lax
from jax.experimental import pallas as pl
from jax.experimental.pallas import tpu as pltpu
from jax.sharding import PartitionSpec as P

BRANCH = 16
PENALTY = 1.0
CVAR_WEIGHT = 0.25
CVAR_LEVEL = 0.75
CHUNKS = 4
F32 = jnp.float32
BF16 = jnp.bfloat16

ANY = pl.BlockSpec(memory_space=pl.ANY)
HBM = pl.BlockSpec(memory_space=pltpu.HBM)
SMEM = pl.BlockSpec(memory_space=pltpu.SMEM)
VMEM = pl.BlockSpec(memory_space=pltpu.VMEM)


def partner(value, mask):
    pairs = [(source, source ^ mask) for source in range(lax.axis_size("node"))]
    return lax.ppermute(value, "node", pairs)


def in_hbm(value):
    return pltpu.with_memory_space_constraint(value, pltpu.HBM)


def params(mib):
    return pltpu.CompilerParams(vmem_limit_bytes=mib << 20)


def build_target(target, anchor_of, c_v, y_v, start, length):
    def step(i, carry):
        rows = []
        for k in range(2):
            s = 2 * i + k
            own = pl.ds(start, length)
            rows.append(
                PENALTY * anchor_of(s).astype(F32)
                - c_v[s, own, :].astype(F32)
                - y_v[s, own, :].astype(F32)
            )
        block = jnp.concatenate(rows, axis=0).astype(BF16)
        target[pl.ds(pl.multiple_of(i * 2 * length, 2 * length), 2 * length), :] = block
        return carry

    lax.fori_loop(0, c_v.shape[0] // 2, step, 0)


def multiply(target, inv_v, z, c_v, y_v, cost, start, length, before, fold):
    scenarios = c_v.shape[0]
    width = inv_v.shape[1] // CHUNKS
    for j in range(CHUNKS):
        before(j)
        cols = slice(j * width, (j + 1) * width)
        z[:, :, cols] = jnp.dot(
            target[...], inv_v[:, cols], preferred_element_type=F32
        ).reshape(scenarios, length, width)

        def step(s, carry):
            own = pl.ds(start, length)
            sol = z[s, :, cols]
            z[s, :, cols] = sol + y_v[s, own, cols].astype(F32)
            prod = c_v[s, own, cols].astype(F32) * sol
            part = prod[:, :128]
            for k in range(1, width // 128):
                part = part + prod[:, k * 128 : (k + 1) * 128]
            cost[s] = cost[s] + part
            return fold(s, cols, sol, carry)

        total = lax.fori_loop(0, scenarios, step, jnp.zeros((length, width), F32), unroll=4)
        fold(None, cols, None, total)


def first_kernel(w, sec, pf, c_hbm, y_hbm, inv_hbm, c_v, y_v, inv_v, z, a1, mass, cost, target, sems):
    scenarios, hours, columns = c_hbm.shape
    length = hours // 3
    width = columns // CHUNKS

    def rows(k):
        own = pl.ds(k * length, length)
        return (
            pltpu.make_async_copy(c_hbm.at[:, own, :], c_v.at[:, own, :], sems.at[2 * k]),
            pltpu.make_async_copy(y_hbm.at[:, own, :], y_v.at[:, own, :], sems.at[2 * k + 1]),
        )

    def chunk(j):
        own = pl.ds(j * width, width)
        return pltpu.make_async_copy(inv_hbm.at[:, own], inv_v.at[:, own], sems.at[6 + j])

    for copy in rows(0):
        copy.start()
    for j in range(CHUNKS):
        chunk(j).start()
    for k in (2, 1):
        for copy in rows(k):
            copy.start()

    mass[...] = jnp.zeros_like(mass)
    cost[...] = jnp.zeros_like(cost)

    def count(s, carry):
        node = pl.ds(sec[s] % BRANCH, 1)
        mass[node, :] = mass[node, :] + w[s].astype(F32)
        return carry

    lax.fori_loop(0, scenarios, count, 0)
    for copy in rows(0):
        copy.wait()
    build_target(target, lambda s: pf[...], c_v, y_v, 0, length)

    def fold(s, cols, sol, carry):
        if s is None:
            a1[:, cols] = carry
            return None
        return carry + w[s].astype(F32) * sol

    multiply(target, inv_v, z, c_v, y_v, cost, 0, length, lambda j: chunk(j).wait(), fold)
    for k in (2, 1):
        for copy in rows(k):
            copy.wait()


def third_kernel(w, sec, p0, p1, p2, p3, c_v, y_v, inv_v, cost_in, z, cost, keep, send, target, table, acc, sems):
    scenarios, hours, columns = c_v.shape
    length = hours // 3
    quarter = lax.axis_index("node") % 4
    shares = BRANCH // 4
    copies = [
        pltpu.make_async_copy(part, table.at[pl.ds(k * shares, shares)], sems.at[k])
        for k, part in enumerate((p0, p1, p2, p3))
    ]
    for copy in copies:
        copy.start()
    acc[...] = jnp.zeros_like(acc)
    cost[...] = cost_in[...]
    for copy in copies:
        copy.wait()

    def anchor_of(s):
        node = sec[s] % BRANCH
        return table[((node // shares) ^ quarter) * shares + node % shares]

    build_target(target, anchor_of, c_v, y_v, 2 * length, length)

    def fold(s, cols, sol, carry):
        if s is None:
            return None
        node = sec[s] % BRANCH
        half = (node // shares) % 2
        place = ((half ^ (quarter % 2)) * 2 + node // (2 * shares)) * shares + node % shares
        acc[place, :, cols] = acc[place, :, cols] + w[s].astype(F32) * sol
        return carry

    multiply(target, inv_v, z, c_v, y_v, cost, 2 * length, length, lambda j: None, fold)
    keep[...] = acc[: BRANCH // 2]
    send[...] = acc[BRANCH // 2 :].astype(BF16)


def second_kernel(
    w, mean, w_row, duals_row, p0, p1, p2, p3, c_v, y_v, inv_v, cost_in, z, a2, eta, scal, target, table, cost, sems
):
    scenarios, hours, columns = c_v.shape
    length = hours // 3
    quarter = lax.axis_index("node") % 4
    share = columns // 4
    copies = [
        pltpu.make_async_copy(
            part.at[0], table.at[:, pl.ds(pl.multiple_of((quarter ^ k) * share, share), share)], sems.at[k]
        )
        for k, part in enumerate((p0, p1, p2, p3))
    ]
    for copy in copies:
        copy.start()
    cost[...] = cost_in[...]
    for copy in copies:
        copy.wait()
    build_target(target, lambda s: table[...], c_v, y_v, length, length)

    def fold(s, cols, sol, carry):
        if s is None:
            a2[:, cols] = carry
            return None
        return carry + w[s].astype(F32) * sol

    multiply(target, inv_v, z, c_v, y_v, cost, length, length, lambda j: None, fold)
    lanes = jnp.sum(cost[...], axis=1)
    scen_cost = jnp.sum(lanes.T, axis=0, keepdims=True) / (hours * columns)
    p = w_row[...].astype(F32)
    low = mean[0] - (CVAR_WEIGHT + duals_row[...]) / PENALTY
    high = low + CVAR_WEIGHT / ((1.0 - CVAR_LEVEL) * PENALTY)
    level = jnp.minimum(jnp.maximum(scen_cost, low), high)
    eta[...] = level
    total = jnp.sum(p * level, axis=1, keepdims=True)
    mass = jnp.sum(p, axis=1, keepdims=True)
    row = lax.broadcasted_iota(jnp.int32, scal.shape, 0)
    scal[...] = jnp.where(row == 0, total, jnp.where(row == 1, mass, 0.0))


def chip_sum_kernel(keep, got, mass_own, mass_got, total, send, mass):
    value = keep[...] + got[...].astype(F32)
    total[...] = value
    send[...] = value.astype(BF16)
    mass[...] = mass_own[...] + mass_got[...]


def third_avg_kernel(total, got, mass_own, mass_got, avg, send, third_avg, mass):
    shares = BRANCH // 4
    quarter = lax.axis_index("node") % 4
    mass[...] = mass_own[...] + mass_got[...]
    for k in range(BRANCH // 2):
        node = ((k // shares) * 2 + quarter % 2) * shares + k % shares
        value = (total[k] + got[k].astype(F32)) / mass[pl.ds(node, 1), :][:, :1]
        avg[k] = value
        send[k] = value.astype(BF16)
    third_avg[...] = avg[pl.ds((quarter // 2) * shares, shares)]


def write_duals(z, avg_of, out, buf, sems, start, length):
    scenarios = z.shape[0]
    group = scenarios // 4

    def copy(g):
        own = pl.ds(g * group, group)
        return pltpu.make_async_copy(buf.at[own], out.at[own, pl.ds(start, length), :], sems.at[g])

    for g in range(4):

        def step(i, carry):
            s = g * group + i
            buf[s] = (z[s] - PENALTY * avg_of(s)).astype(BF16)
            return carry

        lax.fori_loop(0, group, step, 0)
        copy(g).start()
    return [copy(g) for g in range(4)]


def third_duals_kernel(sec, z, avg, got, out, buf, table, sems):
    length = z.shape[1]
    shares = BRANCH // 4
    quarter = lax.axis_index("node") % 4
    half_size = BRANCH // 2
    table[:half_size] = avg[...]
    table[half_size:] = got[...].astype(F32)

    def avg_of(s):
        node = sec[s] % BRANCH
        half = (node // shares) % 2
        return table[((half ^ (quarter % 2)) * 2 + node // (2 * shares)) * shares + node % shares]

    for copy in write_duals(z, avg_of, out, buf, sems, 2 * length, length):
        copy.wait()


def second_duals_kernel(z, a_own, a_got, mass, prior, out, second_avg, buf, full, sems):
    length, columns = full.shape
    quarter = lax.axis_index("node") % 4
    share = columns // 4
    whole = jnp.sum(mass[...], axis=0, keepdims=True)[:, :1]
    full[...] = (a_own[...] + a_got[...]) / whole
    second_avg[0] = full[:, pl.ds(pl.multiple_of(quarter * share, share), share)]
    for copy in write_duals(z, lambda s: full[...], out, buf, sems, length, length):
        copy.wait()


def first_duals_kernel(
    z, a_own, a_got, s_own, s_got, eta, duals_row, prior, out, first_avg, eta_avg, eta_duals, buf, sems
):
    scal = s_own[...] + s_got[...]
    total = jnp.sum(scal[0:1, 0:1])
    mass = jnp.sum(scal[1:2, 0:1])
    first_avg[...] = (a_own[...] + a_got[...]) / mass
    copies = write_duals(z, lambda s: first_avg[...], out, buf, sems, 0, first_avg.shape[0])
    level = scal[0:1, 0:1] / scal[1:2, 0:1]
    eta_avg[0] = jnp.sum(level)
    eta_duals[...] = duals_row[...] + PENALTY * (eta[...] - level)
    for copy in copies:
        copy.wait()


def body(
    unit_costs,
    hour_duals,
    inverse,
    weights,
    section_three,
    prev_first,
    prev_second,
    prev_third,
    eta_mean,
    eta_duals,
):
    scenarios, hours, columns = unit_costs.shape
    length = hours // 3
    half = BRANCH // 2
    nodes = lax.axis_size("node")
    dma = pltpu.SemaphoreType.DMA
    shape = jax.ShapeDtypeStruct
    w_row = weights.reshape(1, scenarios)
    duals_row = eta_duals.reshape(1, scenarios)

    y_third, y_second = partner((prev_third, prev_second), 2)

    c_v, y_v, inv_v, z1, a1, mass, cost = pl.pallas_call(
        first_kernel,
        name="first",
        in_specs=[SMEM, SMEM, VMEM, HBM, HBM, HBM],
        out_specs=[VMEM] * 7,
        out_shape=[
            pltpu.VMEM(unit_costs.shape, BF16),
            pltpu.VMEM(hour_duals.shape, BF16),
            pltpu.VMEM(inverse.shape, BF16),
            pltpu.VMEM((scenarios, length, columns), F32),
            shape((length, columns), F32),
            shape((BRANCH, 128), F32),
            pltpu.VMEM((scenarios, length, 128), F32),
        ],
        scratch_shapes=[pltpu.VMEM((scenarios * length, columns), BF16), dma((6 + CHUNKS,))],
        compiler_params=params(30),
    )(weights, section_three, prev_first, in_hbm(unit_costs), in_hbm(hour_duals), in_hbm(inverse))

    core_third, diag_third, core_second, diag_second, core_mass = partner(
        (prev_third, y_third, prev_second, y_second, mass), 1
    )

    z3, cost, keep, send = pl.pallas_call(
        third_kernel,
        name="third",
        in_specs=[SMEM, SMEM, ANY, ANY, ANY, ANY, VMEM, VMEM, VMEM, VMEM],
        out_specs=[VMEM] * 4,
        out_shape=[
            pltpu.VMEM((scenarios, length, columns), F32),
            pltpu.VMEM((scenarios, length, 128), F32),
            pltpu.VMEM((half, length, columns), F32),
            shape((half, length, columns), BF16),
        ],
        scratch_shapes=[
            pltpu.VMEM((scenarios * length, columns), BF16),
            pltpu.VMEM((BRANCH, length, columns), BF16),
            pltpu.VMEM((BRANCH, length, columns), F32),
            dma((4,)),
        ],
        compiler_params=params(30),
    )(weights, section_three, prev_third, core_third, y_third, diag_third, c_v, y_v, inv_v, cost)

    chip_got = partner(send, 1)
    chip_total, chip_send, chip_mass = pl.pallas_call(
        chip_sum_kernel,
        name="chip_sum",
        in_specs=[VMEM] * 4,
        out_specs=[VMEM] * 3,
        out_shape=[
            pltpu.VMEM((half, length, columns), F32),
            shape((half, length, columns), BF16),
            shape((BRANCH, 128), F32),
        ],
        compiler_params=params(8),
    )(keep, chip_got, mass, core_mass)
    node_got, mass_got = partner((chip_send, chip_mass), 2)

    z2, a2, eta, scal = pl.pallas_call(
        second_kernel,
        name="second",
        in_specs=[SMEM, SMEM, VMEM, VMEM, ANY, ANY, ANY, ANY, VMEM, VMEM, VMEM, VMEM],
        out_specs=[VMEM] * 4,
        out_shape=[
            pltpu.VMEM((scenarios, length, columns), F32),
            shape((length, columns), F32),
            shape((1, scenarios), F32),
            shape((8, 128), F32),
        ],
        scratch_shapes=[
            pltpu.VMEM((scenarios * length, columns), BF16),
            pltpu.VMEM((length, columns), BF16),
            pltpu.VMEM((scenarios, length, 128), F32),
            dma((4,)),
        ],
        compiler_params=params(30),
    )(
        weights, eta_mean, w_row, duals_row, prev_second, core_second, y_second, diag_second, c_v, y_v, inv_v, cost
    )

    got = partner((scal, a1, a2), 1)
    scal, a1, a2 = scal + got[0], a1 + got[1], a2 + got[2]
    mask = 4
    while mask < nodes:
        got = partner((scal, a1), mask)
        scal, a1 = scal + got[0], a1 + got[1]
        mask *= 2
    y_scal, y_a1, y_a2 = partner((scal, a1, a2), 2)

    avg, avg_send, third_avg, node_mass = pl.pallas_call(
        third_avg_kernel,
        name="third_avg",
        in_specs=[VMEM] * 4,
        out_specs=[VMEM] * 4,
        out_shape=[
            pltpu.VMEM((half, length, columns), F32),
            shape((half, length, columns), BF16),
            shape((BRANCH // 4, length, columns), F32),
            shape((BRANCH, 128), F32),
        ],
        compiler_params=params(8),
    )(chip_total, node_got, chip_mass, mass_got)
    avg_got = partner(avg_send, 1)

    buf = pltpu.VMEM((scenarios, length, columns), BF16)
    duals_shape = shape(hour_duals.shape, BF16)
    duals = pl.pallas_call(
        third_duals_kernel,
        name="third_duals",
        in_specs=[SMEM, VMEM, VMEM, VMEM],
        out_specs=ANY,
        out_shape=duals_shape,
        scratch_shapes=[buf, pltpu.VMEM((BRANCH, length, columns), F32), dma((4,))],
        compiler_params=params(8),
    )(section_three, z3, avg, avg_got)
    duals, second_avg = pl.pallas_call(
        second_duals_kernel,
        name="second_duals",
        in_specs=[VMEM, VMEM, VMEM, VMEM, ANY],
        out_specs=[ANY, VMEM],
        out_shape=[duals_shape, shape((1, length, columns // 4), F32)],
        scratch_shapes=[buf, pltpu.VMEM((length, columns), F32), dma((4,))],
        input_output_aliases={4: 0},
        compiler_params=params(8),
    )(z2, a2, y_a2, node_mass, duals)
    duals, first_avg, eta_avg, eta_duals_new = pl.pallas_call(
        first_duals_kernel,
        name="first_duals",
        in_specs=[VMEM] * 7 + [ANY],
        out_specs=[ANY, VMEM, SMEM, VMEM],
        out_shape=[
            duals_shape,
            shape((length, columns), F32),
            shape((1,), F32),
            shape((1, scenarios), F32),
        ],
        scratch_shapes=[buf, dma((4,))],
        input_output_aliases={7: 0},
        compiler_params=params(8),
    )(z1, a1, y_a1, scal, y_scal, eta, duals_row, duals)
    return duals, first_avg, second_avg, third_avg, eta_avg, eta_duals_new.reshape(scenarios)


def solution(mesh):
    row = P(("groups", "node"))
    in_specs = (row, row, P(), row, row, P("groups"), row, row, P("groups"), row)
    out_specs = (row, P("groups"), row, row, P("groups"), row)
    return jax.shard_map(body, mesh=mesh, in_specs=in_specs, out_specs=out_specs, check_vma=False)
```

time: 156 us -> 71.9 us (0.46)
  blocking collectives: 33.9 us -> 0 us
  waiting for transfers between devices: 55.2 us -> 25.5 us
  Pallas kernels: 0 us -> 25 us
  between operations: 17.5 us -> 1.45 us
  other arithmetic: 13.4 us -> 0.05 us
  matrix products: 12.5 us -> 0 us
  local copies, waits for them, and re-layouts: 10.9 us -> 2.09 us
  starting transfers between devices: 11 us -> 17.7 us
    psum x1 -> x0, waiting for transfers between devices: 36 us -> none  [body(): lax.psum((first_part, jnp.sum(mass_vec * eta_value), mass_local), 'node')]
    psum x1 -> x0, blocking collectives: 33.9 us -> none  [body(): lax.psum((first_part, jnp.sum(mass_vec * eta_value), mass_local), 'node')]
    pallas_call x0 -> x8, Pallas kernels: none -> 25 us  [the longest x1 7.06 us: body(): pl.pallas_call(third_kernel, name='third', in_specs=[SMEM, SMEM, ANY, ANY...]
    dot_general x4 -> x0, matrix products: 12.5 us -> none  [the longest x1 9.87 us: body(): jnp.dot(flat, inverse, preferred_element_type=jnp.float32)]
    ppermute x14 -> x21, starting transfers between devices: 10.9 us -> 17.7 us  [partner(): return lax.ppermute(value, 'node', pairs)]
    unnamed x28 -> x14, local copies, waits for them, and re-layouts: 8.66 us -> 2.09 us
    ppermute x14 -> x21, waiting for transfers between devices: 19.2 us -> 25.5 us  [partner(): return lax.ppermute(value, 'node', pairs)]
    select_n x13 -> x0, other arithmetic: 3.92 us -> none  [the longest x8 3.12 us: joined(): jnp.where(is_upper, jnp.concatenate((peer_part, own_part), along), jnp.co...]
  transfers between devices with their start and end apart: 15 -> 21, of which waited for: 6 -> 10; matrix products, arithmetic and copies ran while one was open for 18% -> 0% of each run, Pallas kernels for 0% -> 21%
where the time goes in v1:
time: 71.9 us; the launch traced here: 71.7 us
  waiting for transfers between devices  25.5 us (35%)
  Pallas kernels  25 us (35%)
  starting transfers between devices  17.7 us (25%)
  local copies, waits for them, and re-layouts  2.09 us (3%)
  between operations  1.45 us (2%)
    ppermute x21, waiting for transfers between devices, partner(): return lax.ppermute(value, 'node', pairs)  25.5 us
    ppermute x21, starting transfers between devices, partner(): return lax.ppermute(value, 'node', pairs)  17.7 us
    pallas_call x1, Pallas kernels, body(): pl.pallas_call(third_kernel, name='third', in_specs=[SMEM, SMEM, ANY, ANY...  7.06 us
    pallas_call x1, Pallas kernels, body(): pl.pallas_call(first_kernel, name='first', in_specs=[SMEM, SMEM, VMEM, HB...  6.43 us
    pallas_call x1, Pallas kernels, body(): pl.pallas_call(second_kernel, name='second', in_specs=[SMEM, SMEM, VMEM,...  4.8 us
    pallas_call x1, Pallas kernels, body(): pl.pallas_call(third_duals_kernel, name='third_duals', in_specs=[SMEM, VM...  2.24 us
    unnamed x14, local copies, waits for them, and re-layouts  2.09 us
    pallas_call x1, Pallas kernels, body(): pl.pallas_call(second_duals_kernel, name='second_duals', in_specs=[VMEM,...  1.77 us
  transfers between devices with their start and end apart: 21, of which 10 were waited for; matrix products, arithmetic and copies ran while one was open for 0% of the time, Pallas kernels for 21%

profile of v1, /device:TPU:0, one launch (start us, length us, event | category | flops | bytes accessed | tf_op | source)
XLA Modules:
  0.0 71.7 jit_solution(7947381507401144273)
XLA Ops:
  0.6 3.1 %collective-permute-start.8 = (bf16[4,8,2048]{2,1,0:T(8,128)(2,1)}, bf16[4,8,2048]{2,1,0:T(8,128)(2,1)S(1)}, u32[]{:S(2)}, u32[]{:S(2)}) collective-permute-start(bf16[4,8,2048]{2,1,0:T(8,128)(2,1)} %p0.2), channel_id=1, source_target_pairs={{0,2},{1,3},{2,0},{3,1},{4,6},{5,7},{6,4},{7,5},{8,10},{9,11},{10,... | collective-permute-start | bytes 393224 | tf_op jit(solution)/shard_map/ppermute | solution.py:26
  3.7 0.0 collective-permute-start.7
  3.7 3.7 %collective-permute-done.8.p2 = bf16[4,8,2048]{2,1,0:T(8,128)(2,1)S(1)} collective-permute-done((bf16[4,8,2048]{2,1,0:T(8,128)(2,1)}, bf16[4,8,2048]{2,1,0:T(8,128)(2,1)S(1)}, u32[]{:S(2)}, u32[]{:S(2)}) %collective-permute-start.8) | collective-permute-done | bytes 131104 | tf_op jit(solution)/shard_map/ppermute | solution.py:26
  7.4 0.0 collective-permute-start.9
  7.4 0.8 %copy-done.1 = bf16[8,2048]{1,0:T(8,128)(2,1)S(1)} copy-done((bf16[8,2048]{1,0:T(8,128)(2,1)S(1)}, bf16[8,2048]{1,0:T(8,128)(2,1)}, u32[]{:S(2)}) %copy-start.1) | copy-done | bytes 32792
  8.2 0.7 copy-done.3
  8.8 0.7 copy-done.4
  9.5 6.4 %first.1 = (bf16[32,24,2048]{2,1,0:T(8,128)(2,1)S(1)}, bf16[32,24,2048]{2,1,0:T(8,128)(2,1)S(1)}, bf16[2048,2048]{1,0:T(8,128)(2,1)S(1)}, f32[32,8,2048]{2,1,0:T...) custom-call(s32[32]{0:T(128)S(1)} %copy-done.3, s32[32]{0:T(128)S(1)} %copy-done.4, ...), custom_call_target="tpu_custom_call" | custom-call | tf_op jit(solution)/shard_map/first/pallas_call | solution.py:310
  15.9 0.0 collective-permute-done.7.p1
  15.9 0.0 collective-permute-done.9.p3
  15.9 0.0 copy-start.2
  16.0 0.0 copy-start.6
  16.0 7.1 %third.1 = (f32[32,8,2048]{2,1,0:T(8,128)S(1)}, f32[32,8,128]{2,1,0:T(8,128)S(1)}, f32[8,8,2048]{2,1,0:T(8,128)S(1)}, bf16[8,8,2048]{2,1,0:T(8,128)(2,1)S(1)}) custom-call(s32[32]{0:T(128)S(1)} %copy-done.3, s32[32]{0:T(128)S(1)} %copy-done.4, bf16[4,8,2048]{2,1,0:T(8,128)(2,1)S(1)} %copy-done, bf16[4,8,2048]{2,1,0:T(8,128)(2,1)S(1)} %collective-permute-done.7.p1, ...), custom_call_target="tpu_custom_call" | custom-call | tf_op jit(solution)/shard_map/third/pallas_call | solution.py:332
  23.0 0.6 collective-permute-start.16
  23.6 0.1 collective-permute-start.17
  23.7 1.1 %collective-permute-done.17.mass_got = f32[16,128]{1,0:T(8,128)S(1)} collective-permute-done((f32[16,128]{1,0:T(8,128)S(1)}, f32[16,128]{1,0:T(8,128)S(1)}, u32[]{:S(2)}, u32[]{:S(2)}) %collective-permute-start.17) | collective-permute-done | bytes 8224 | tf_op jit(solution)/shard_map/ppermute | solution.py:26
  24.8 0.0 collective-permute-done.16.got
  24.8 0.1 chip_sum.1
  24.9 1.8 %collective-permute-start.18 = (bf16[8,8,2048]{2,1,0:T(8,128)(2,1)S(1)}, bf16[8,8,2048]{2,1,0:T(8,128)(2,1)S(1)}, u32[]{:S(2)}, u32[]{:S(2)}) collective-permute-start(bf16[8,8,2048]{2,1,0:T(8,128)(2,1)S(1)} %get-tuple-element.49), channel_id=1, source_target_pairs={{0,2},{1,3},{2,0},{3,1},{4,6},{5,7},{6,4},{7,5},{8,10},{9,11},{10,... | collective-permute-start | bytes 786440 | tf_op jit(solution)/shard_map/ppermute | solution.py:26
  26.7 0.3 collective-permute-start.19
  27.0 6.7 %collective-permute-done.19.mass_got = f32[16,128]{1,0:T(8,128)S(1)} collective-permute-done((f32[16,128]{1,0:T(8,128)S(1)}, f32[16,128]{1,0:T(8,128)S(1)}, u32[]{:S(2)}, u32[]{:S(2)}) %collective-permute-start.19) | collective-permute-done | bytes 8224 | tf_op jit(solution)/shard_map/ppermute | solution.py:26
  33.7 0.0 collective-permute-done.18.got
  33.7 0.8 %third_avg.1 = (f32[8,8,2048]{2,1,0:T(8,128)S(1)}, bf16[8,8,2048]{2,1,0:T(8,128)(2,1)S(1)}, f32[4,8,2048]{2,1,0:T(8,128)}, f32[16,128]{1,0:T(8,128)S(1)}) custom-call(f32[8,8,2048]{2,1,0:T(8,128)S(1)} %get-tuple-element.48.total, bf16[8,8,2048]{2,1,0:T(8,128)(2,1)S(1)} %collective-permute-done.18.got, f32[16,128]{1,0:T(8,128)S(1)} %get-tuple-element.50.mass_own, ...), custom_call_target="tpu_custom_call" | custom-call | tf_op jit(solution)/shard_map/third_avg/pallas_call | solution.py:398
  34.5 0.0 collective-permute-start.20
  34.5 0.5 collective-permute-start
  35.0 1.1 %collective-permute-done = f32[8,2048]{1,0:T(8,128)S(1)} collective-permute-done((f32[8,2048]{1,0:T(8,128)S(1)}, f32[8,2048]{1,0:T(8,128)S(1)}, u32[]{:S(2)}, u32[]{:S(2)}) %collective-permute-start) | collective-permute-done | bytes 65568 | tf_op jit(solution)/shard_map/ppermute | solution.py:26
  36.2 1.9 %collective-permute-start.1 = (f32[8,2048]{1,0:T(8,128)S(1)}, f32[8,2048]{1,0:T(8,128)S(1)}, u32[]{:S(2)}, u32[]{:S(2)}) collective-permute-start(f32[8,2048]{1,0:T(8,128)S(1)} %add.21), channel_id=1, source_target_pairs={{0,4},{1,5},{2,6},{3,7},{4,0},{5,1},{6,2},{7,3},{8,12},{9,13},{10,... | collective-permute-start | bytes 196616 | tf_op jit(solution)/shard_map/ppermute | solution.py:26
  38.0 1.5 %collective-permute-start.5 = (bf16[1,8,512]{2,1,0:T(8,128)(2,1)S(1)}, bf16[1,8,512]{2,1,0:T(8,128)(2,1)S(1)}, u32[]{:S(2)}, u32[]{:S(2)}) collective-permute-start(bf16[1,8,512]{2,1,0:T(8,128)(2,1)S(1)} %copy-done.2), channel_id=1, source_target_pairs={{0,2},{1,3},{2,0},{3,1},{4,6},{5,7},{6,4},{7,5},{8,10},{9,11},{10,... | collective-permute-start | bytes 24584 | tf_op jit(solution)/shard_map/ppermute | solution.py:26
  39.6 2.1 %collective-permute-done.5.p2 = bf16[1,8,512]{2,1,0:T(8,128)(2,1)S(1)} collective-permute-done((bf16[1,8,512]{2,1,0:T(8,128)(2,1)S(1)}, bf16[1,8,512]{2,1,0:T(8,128)(2,1)S(1)}, u32[]{:S(2)}, u32[]{:S(2)}) %collective-permute-start.5) | collective-permute-done | bytes 8224 | tf_op jit(solution)/shard_map/ppermute | solution.py:26
  41.7 0.0 collective-permute-start.6
  42.4 0.5 collective-permute-done.6.p3
  42.9 4.8 %second.1 = (f32[32,8,2048]{2,1,0:T(8,128)S(1)}, f32[8,2048]{1,0:T(8,128)S(1)}, f32[1,32]{1,0:T(1,128)S(1)}, f32[8,128]{1,0:T(8,128)S(1)}) custom-call(s32[32]{0:T(128)S(1)} %copy-done.3, f32[1]{0:T(128)S(6)} %copy.20.mean, s32[1,32]{1,0:T(1,128)S(1)} %bitcast.3, f32[1,32]{1,0:T(1,128)S(1)} %bitcast.4, bf16[1,8,512]{2,1,0:T(8,128)(2,1)S(1)} %copy-done.2, ...), custom_call_target="tpu_custom_call" | custom-call | tf_op jit(solution)/shard_map/second/pallas_call | solution.py:367
  47.7 0.2 collective-permute-start.14
  47.9 2.6 %collective-permute-start.2 = (f32[8,2048]{1,0:T(8,128)S(1)}, f32[8,2048]{1,0:T(8,128)S(1)}, u32[]{:S(2)}, u32[]{:S(2)}) collective-permute-start(f32[8,2048]{1,0:T(8,128)S(1)} %add.22), channel_id=1, source_target_pairs={{0,8},{1,9},{2,10},{3,11},{4,12},{5,13},{6,14},{7,15},{8,0},{9,1},... | collective-permute-start | bytes 196616 | tf_op jit(solution)/shard_map/ppermute | solution.py:26
  50.6 1.6 %collective-permute-start.15 = (f32[8,2048]{1,0:T(8,128)S(1)}, f32[8,2048]{1,0:T(8,128)S(1)}, u32[]{:S(2)}, u32[]{:S(2)}) collective-permute-start(f32[8,2048]{1,0:T(8,128)S(1)} %add.27.a_own), channel_id=1, source_target_pairs={{0,2},{1,3},{2,0},{3,1},{4,6},{5,7},{6,4},{7,5},{8,10},{9,11},{10,... | collective-permute-start | bytes 196616 | tf_op jit(solution)/shard_map/ppermute | solution.py:26
  52.2 2.3 %collective-permute-done.2 = f32[8,2048]{1,0:T(8,128)S(1)} collective-permute-done((f32[8,2048]{1,0:T(8,128)S(1)}, f32[8,2048]{1,0:T(8,128)S(1)}, u32[]{:S(2)}, u32[]{:S(2)}) %collective-permute-start.2) | collective-permute-done | bytes 65568 | tf_op jit(solution)/shard_map/ppermute | solution.py:26
  54.5 1.6 %collective-permute-start.3 = (f32[8,2048]{1,0:T(8,128)S(1)}, f32[8,2048]{1,0:T(8,128)S(1)}, u32[]{:S(2)}, u32[]{:S(2)}) collective-permute-start(f32[8,2048]{1,0:T(8,128)S(1)} %add.23.a_own), channel_id=1, source_target_pairs={{0,2},{1,3},{2,0},{3,1},{4,6},{5,7},{6,4},{7,5},{8,10},{9,11},{10,... | collective-permute-start | bytes 196616 | tf_op jit(solution)/shard_map/ppermute | solution.py:26
  56.1 1.2 %collective-permute-done.10 = f32[8,128]{1,0:T(8,128)S(1)} collective-permute-done((f32[8,128]{1,0:T(8,128)S(1)}, f32[8,128]{1,0:T(8,128)S(1)}, u32[]{:S(2)}, u32[]{:S(2)}) %collective-permute-start.10) | collective-permute-done | bytes 4128 | tf_op jit(solution)/shard_map/ppermute | solution.py:26
  57.3 0.0 collective-permute-start.11
  57.3 3.6 %collective-permute-done.11 = f32[8,128]{1,0:T(8,128)S(1)} collective-permute-done((f32[8,128]{1,0:T(8,128)S(1)}, f32[8,128]{1,0:T(8,128)S(1)}, u32[]{:S(2)}, u32[]{:S(2)}) %collective-permute-start.11) | collective-permute-done | bytes 4128 | tf_op jit(solution)/shard_map/ppermute | solution.py:26
  60.9 1.4 %collective-permute-start.12 = (f32[8,128]{1,0:T(8,128)S(1)}, f32[8,128]{1,0:T(8,128)S(1)}, u32[]{:S(2)}, u32[]{:S(2)}) collective-permute-start(f32[8,128]{1,0:T(8,128)S(1)} %add.25), channel_id=1, source_target_pairs={{0,8},{1,9},{2,10},{3,11},{4,12},{5,13},{6,14},{7,15},{8,0},{9,1},... | collective-permute-start | bytes 12296 | tf_op jit(solution)/shard_map/ppermute | solution.py:26
  62.3 3.1 %collective-permute-done.12 = f32[8,128]{1,0:T(8,128)S(1)} collective-permute-done((f32[8,128]{1,0:T(8,128)S(1)}, f32[8,128]{1,0:T(8,128)S(1)}, u32[]{:S(2)}, u32[]{:S(2)}) %collective-permute-start.12) | collective-permute-done | bytes 4128 | tf_op jit(solution)/shard_map/ppermute | solution.py:26
  65.4 0.5 collective-permute-start.13
  65.9 2.2 %third_duals.1.prior = bf16[32,24,2048]{2,1,0:T(8,128)(2,1)} custom-call(s32[32]{0:T(128)S(1)} %copy-done.5, f32[32,8,2048]{2,1,0:T(8,128)S(1)} %get-tuple-element.52.z, f32[8,8,2048]{2,1,0:T(8,128)S(1)} %get-tuple-element.53.avg, bf16[8,8,2048]{2,1,0:T(8,128)(2,1)S(1)} %collective-permute-done.20.got), custom_call_target="tpu_custom_call" | custom-call | tf_op jit(solution)/shard_map/third_duals/pallas_call | solution.py:415
  68.1 0.0 collective-permute-done.15.a_got
  68.1 1.8 %second_duals.1 = (bf16[32,24,2048]{2,1,0:T(8,128)(2,1)}, f32[1,8,512]{2,1,0:T(8,128)}) custom-call(f32[32,8,2048]{2,1,0:T(8,128)S(1)} %get-tuple-element.43.z, f32[8,2048]{1,0:T(8,128)S(1)} %add.27.a_own, f32[8,2048]{1,0:T(8,128)S(1)} %collective-permute-done.15.a_got, f32[16,128]{1,0:T(8,128)S(1)} %get-tuple-element.51.mass, ...), custom_call_target="tpu_custom_call", output_to_operand_aliasing={{0}: (4, {})} | custom-call | tf_op jit(solution)/shard_map/second_duals/pallas_call | solution.py:424
  69.9 0.0 collective-permute-done.13.s_got
  69.9 1.8 %first_duals.1 = (bf16[32,24,2048]{2,1,0:T(8,128)(2,1)}, f32[8,2048]{1,0:T(8,128)}, f32[1]{0:T(128)}, f32[1,32]{1,0:T(1,128)}) custom-call(f32[32,8,2048]{2,1,0:T(8,128)S(1)} %get-tuple-element.34.z, f32[8,2048]{1,0:T(8,128)S(1)} %add.23.a_own, f32[8,2048]{1,0:T(8,128)S(1)} %collective-permute-done.3.a_got, ...), custom_call_target="tpu_custom_call", output_to_operand_aliasing={{0}: (7, {})} | custom-call | tf_op jit(solution)/shard_map/first_duals/pallas_call | solution.py:434
  (23 shorter events, 0.1 us)
Async XLA Ops:
  0.6 15.3 %copy-start = (bf16[4,8,2048]{2,1,0:T(8,128)(2,1)S(1)}, bf16[4,8,2048]{2,1,0:T(8,128)(2,1)}, u32[]{:S(2)}) copy-start(bf16[4,8,2048]{2,1,0:T(8,128)(2,1)} %p0.2) | copy-start | bytes 393220
  0.6 6.8 %collective-permute-start.8 = (bf16[4,8,2048]{2,1,0:T(8,128)(2,1)}, bf16[4,8,2048]{2,1,0:T(8,128)(2,1)S(1)}, u32[]{:S(2)}, u32[]{:S(2)}) collective-permute-start(bf16[4,8,2048]{2,1,0:T(8,128)(2,1)} %p0.2), channel_id=1, source_target_pairs={{0,2},{1,3},{2,0},{3,1},{4,6},{5,7},{6,4},{7,5},{8,10},{9,11},{10,... | collective-permute-start | bytes 393224 | tf_op jit(solution)/shard_map/ppermute | solution.py:26
  3.7 12.2 %collective-permute-start.7 = (bf16[4,8,2048]{2,1,0:T(8,128)(2,1)}, bf16[4,8,2048]{2,1,0:T(8,128)(2,1)S(1)}, u32[]{:S(2)}, u32[]{:S(2)}) collective-permute-start(bf16[4,8,2048]{2,1,0:T(8,128)(2,1)} %p0.2), channel_id=1, source_target_pairs={{0,1},{1,0},{2,3},{3,2},{4,5},{5,4},{6,7},{7,6},{8,9},{9,8},{10,11... | collective-permute-start | bytes 393224 | tf_op jit(solution)/shard_map/ppermute | solution.py:26
  7.4 8.5 %collective-permute-start.9 = (bf16[4,8,2048]{2,1,0:T(8,128)(2,1)S(1)}, bf16[4,8,2048]{2,1,0:T(8,128)(2,1)S(1)}, u32[]{:S(2)}, u32[]{:S(2)}) collective-permute-start(bf16[4,8,2048]{2,1,0:T(8,128)(2,1)S(1)} %collective-permute-done.8.p2), channel_id=1, source_target_pairs={{0,1},{1,0},{2,3},{3,2},{4,5},{5,4},{6,7},{7,6},{8,9},{9,8},{10,11... | collective-permute-start | bytes 393224 | tf_op jit(solution)/shard_map/ppermute | solution.py:26
  7.4 0.8 %copy-start.1 = (bf16[8,2048]{1,0:T(8,128)(2,1)S(1)}, bf16[8,2048]{1,0:T(8,128)(2,1)}, u32[]{:S(2)}) copy-start(bf16[8,2048]{1,0:T(8,128)(2,1)} %pf.1) | copy-start | bytes 98308
  8.2 0.7 copy-start.3
  8.8 0.7 copy-start.4
  15.9 22.1 %copy-start.2 = (bf16[1,8,512]{2,1,0:T(8,128)(2,1)S(1)}, bf16[1,8,512]{2,1,0:T(8,128)(2,1)}, u32[]{:S(2)}) copy-start(bf16[1,8,512]{2,1,0:T(8,128)(2,1)} %p0.3) | copy-start | bytes 24580
  16.0 26.9 %copy-start.6 = (f32[32]{0:T(128)S(1)}, f32[32]{0:T(128)}, u32[]{:S(2)}) copy-start(f32[32]{0:T(128)} %param.19) | copy-start | bytes 388
  23.0 1.8 %collective-permute-start.16 = (bf16[8,8,2048]{2,1,0:T(8,128)(2,1)S(1)}, bf16[8,8,2048]{2,1,0:T(8,128)(2,1)S(1)}, u32[]{:S(2)}, u32[]{:S(2)}) collective-permute-start(bf16[8,8,2048]{2,1,0:T(8,128)(2,1)S(1)} %get-tuple-element.46), channel_id=1, source_target_pairs={{0,1},{1,0},{2,3},{3,2},{4,5},{5,4},{6,7},{7,6},{8,9},{9,8},{10,11... | collective-permute-start | bytes 786440 | tf_op jit(solution)/shard_map/ppermute | solution.py:26
  23.6 1.2 %collective-permute-start.17 = (f32[16,128]{1,0:T(8,128)S(1)}, f32[16,128]{1,0:T(8,128)S(1)}, u32[]{:S(2)}, u32[]{:S(2)}) collective-permute-start(f32[16,128]{1,0:T(8,128)S(1)} %get-tuple-element.47.mass_own), channel_id=1, source_target_pairs={{0,1},{1,0},{2,3},{3,2},{4,5},{5,4},{6,7},{7,6},{8,9},{9,8},{10,11... | collective-permute-start | bytes 24584 | tf_op jit(solution)/shard_map/ppermute | solution.py:26
  24.9 8.8 %collective-permute-start.18 = (bf16[8,8,2048]{2,1,0:T(8,128)(2,1)S(1)}, bf16[8,8,2048]{2,1,0:T(8,128)(2,1)S(1)}, u32[]{:S(2)}, u32[]{:S(2)}) collective-permute-start(bf16[8,8,2048]{2,1,0:T(8,128)(2,1)S(1)} %get-tuple-element.49), channel_id=1, source_target_pairs={{0,2},{1,3},{2,0},{3,1},{4,6},{5,7},{6,4},{7,5},{8,10},{9,11},{10,... | collective-permute-start | bytes 786440 | tf_op jit(solution)/shard_map/ppermute | solution.py:26
  26.7 7.0 %collective-permute-start.19 = (f32[16,128]{1,0:T(8,128)S(1)}, f32[16,128]{1,0:T(8,128)S(1)}, u32[]{:S(2)}, u32[]{:S(2)}) collective-permute-start(f32[16,128]{1,0:T(8,128)S(1)} %get-tuple-element.50.mass_own), channel_id=1, source_target_pairs={{0,2},{1,3},{2,0},{3,1},{4,6},{5,7},{6,4},{7,5},{8,10},{9,11},{10,... | collective-permute-start | bytes 24584 | tf_op jit(solution)/shard_map/ppermute | solution.py:26
  34.5 31.3 %collective-permute-start.20 = (bf16[8,8,2048]{2,1,0:T(8,128)(2,1)S(1)}, bf16[8,8,2048]{2,1,0:T(8,128)(2,1)S(1)}, u32[]{:S(2)}, u32[]{:S(2)}) collective-permute-start(bf16[8,8,2048]{2,1,0:T(8,128)(2,1)S(1)} %get-tuple-element.54), channel_id=1, source_target_pairs={{0,1},{1,0},{2,3},{3,2},{4,5},{5,4},{6,7},{7,6},{8,9},{9,8},{10,11... | collective-permute-start | bytes 786440 | tf_op jit(solution)/shard_map/ppermute | solution.py:26
  34.5 1.6 %collective-permute-start = (f32[8,2048]{1,0:T(8,128)S(1)}, f32[8,2048]{1,0:T(8,128)S(1)}, u32[]{:S(2)}, u32[]{:S(2)}) collective-permute-start(f32[8,2048]{1,0:T(8,128)S(1)} %get-tuple-element.35), channel_id=1, source_target_pairs={{0,1},{1,0},{2,3},{3,2},{4,5},{5,4},{6,7},{7,6},{8,9},{9,8},{10,11... | collective-permute-start | bytes 196616 | tf_op jit(solution)/shard_map/ppermute | solution.py:26
  36.2 11.7 %collective-permute-start.1 = (f32[8,2048]{1,0:T(8,128)S(1)}, f32[8,2048]{1,0:T(8,128)S(1)}, u32[]{:S(2)}, u32[]{:S(2)}) collective-permute-start(f32[8,2048]{1,0:T(8,128)S(1)} %add.21), channel_id=1, source_target_pairs={{0,4},{1,5},{2,6},{3,7},{4,0},{5,1},{6,2},{7,3},{8,12},{9,13},{10,... | collective-permute-start | bytes 196616 | tf_op jit(solution)/shard_map/ppermute | solution.py:26
  38.0 3.7 %collective-permute-start.5 = (bf16[1,8,512]{2,1,0:T(8,128)(2,1)S(1)}, bf16[1,8,512]{2,1,0:T(8,128)(2,1)S(1)}, u32[]{:S(2)}, u32[]{:S(2)}) collective-permute-start(bf16[1,8,512]{2,1,0:T(8,128)(2,1)S(1)} %copy-done.2), channel_id=1, source_target_pairs={{0,2},{1,3},{2,0},{3,1},{4,6},{5,7},{6,4},{7,5},{8,10},{9,11},{10,... | collective-permute-start | bytes 24584 | tf_op jit(solution)/shard_map/ppermute | solution.py:26
  39.6 2.8 %collective-permute-start.4 = (bf16[1,8,512]{2,1,0:T(8,128)(2,1)S(1)}, bf16[1,8,512]{2,1,0:T(8,128)(2,1)S(1)}, u32[]{:S(2)}, u32[]{:S(2)}) collective-permute-start(bf16[1,8,512]{2,1,0:T(8,128)(2,1)S(1)} %copy-done.2), channel_id=1, source_target_pairs={{0,1},{1,0},{2,3},{3,2},{4,5},{5,4},{6,7},{7,6},{8,9},{9,8},{10,11... | collective-permute-start | bytes 24584 | tf_op jit(solution)/shard_map/ppermute | solution.py:26
  41.7 1.2 %collective-permute-start.6 = (bf16[1,8,512]{2,1,0:T(8,128)(2,1)S(1)}, bf16[1,8,512]{2,1,0:T(8,128)(2,1)S(1)}, u32[]{:S(2)}, u32[]{:S(2)}) collective-permute-start(bf16[1,8,512]{2,1,0:T(8,128)(2,1)S(1)} %collective-permute-done.5.p2), channel_id=1, source_target_pairs={{0,1},{1,0},{2,3},{3,2},{4,5},{5,4},{6,7},{7,6},{8,9},{9,8},{10,11... | collective-permute-start | bytes 24584 | tf_op jit(solution)/shard_map/ppermute | solution.py:26
  42.9 23.0 %copy-start.5 = (s32[32]{0:T(128)S(1)}, s32[32]{0:T(128)}, u32[]{:S(2)}) copy-start(s32[32]{0:T(128)} %sec.5) | copy-start | bytes 388
  47.7 2.9 %collective-permute-start.14 = (f32[8,2048]{1,0:T(8,128)S(1)}, f32[8,2048]{1,0:T(8,128)S(1)}, u32[]{:S(2)}, u32[]{:S(2)}) collective-permute-start(f32[8,2048]{1,0:T(8,128)S(1)} %get-tuple-element.44), channel_id=1, source_target_pairs={{0,1},{1,0},{2,3},{3,2},{4,5},{5,4},{6,7},{7,6},{8,9},{9,8},{10,11... | collective-permute-start | bytes 196616 | tf_op jit(solution)/shard_map/ppermute | solution.py:26
  47.9 6.5 %collective-permute-start.2 = (f32[8,2048]{1,0:T(8,128)S(1)}, f32[8,2048]{1,0:T(8,128)S(1)}, u32[]{:S(2)}, u32[]{:S(2)}) collective-permute-start(f32[8,2048]{1,0:T(8,128)S(1)} %add.22), channel_id=1, source_target_pairs={{0,8},{1,9},{2,10},{3,11},{4,12},{5,13},{6,14},{7,15},{8,0},{9,1},... | collective-permute-start | bytes 196616 | tf_op jit(solution)/shard_map/ppermute | solution.py:26
  50.6 17.5 %collective-permute-start.15 = (f32[8,2048]{1,0:T(8,128)S(1)}, f32[8,2048]{1,0:T(8,128)S(1)}, u32[]{:S(2)}, u32[]{:S(2)}) collective-permute-start(f32[8,2048]{1,0:T(8,128)S(1)} %add.27.a_own), channel_id=1, source_target_pairs={{0,2},{1,3},{2,0},{3,1},{4,6},{5,7},{6,4},{7,5},{8,10},{9,11},{10,... | collective-permute-start | bytes 196616 | tf_op jit(solution)/shard_map/ppermute | solution.py:26
  54.5 15.4 %collective-permute-start.3 = (f32[8,2048]{1,0:T(8,128)S(1)}, f32[8,2048]{1,0:T(8,128)S(1)}, u32[]{:S(2)}, u32[]{:S(2)}) collective-permute-start(f32[8,2048]{1,0:T(8,128)S(1)} %add.23.a_own), channel_id=1, source_target_pairs={{0,2},{1,3},{2,0},{3,1},{4,6},{5,7},{6,4},{7,5},{8,10},{9,11},{10,... | collective-permute-start | bytes 196616 | tf_op jit(solution)/shard_map/ppermute | solution.py:26
  56.1 1.2 %collective-permute-start.10 = (f32[8,128]{1,0:T(8,128)S(1)}, f32[8,128]{1,0:T(8,128)S(1)}, u32[]{:S(2)}, u32[]{:S(2)}) collective-permute-start(f32[8,128]{1,0:T(8,128)S(1)} %get-tuple-element.41), channel_id=1, source_target_pairs={{0,1},{1,0},{2,3},{3,2},{4,5},{5,4},{6,7},{7,6},{8,9},{9,8},{10,11... | collective-permute-start | bytes 12296 | tf_op jit(solution)/shard_map/ppermute | solution.py:26
  57.3 3.6 %collective-permute-start.11 = (f32[8,128]{1,0:T(8,128)S(1)}, f32[8,128]{1,0:T(8,128)S(1)}, u32[]{:S(2)}, u32[]{:S(2)}) collective-permute-start(f32[8,128]{1,0:T(8,128)S(1)} %add.24), channel_id=1, source_target_pairs={{0,4},{1,5},{2,6},{3,7},{4,0},{5,1},{6,2},{7,3},{8,12},{9,13},{10,... | collective-permute-start | bytes 12296 | tf_op jit(solution)/shard_map/ppermute | solution.py:26
  60.9 4.5 %collective-permute-start.12 = (f32[8,128]{1,0:T(8,128)S(1)}, f32[8,128]{1,0:T(8,128)S(1)}, u32[]{:S(2)}, u32[]{:S(2)}) collective-permute-start(f32[8,128]{1,0:T(8,128)S(1)} %add.25), channel_id=1, source_target_pairs={{0,8},{1,9},{2,10},{3,11},{4,12},{5,13},{6,14},{7,15},{8,0},{9,1},... | collective-permute-start | bytes 12296 | tf_op jit(solution)/shard_map/ppermute | solution.py:26
  65.4 4.5 %collective-permute-start.13 = (f32[8,128]{1,0:T(8,128)S(1)}, f32[8,128]{1,0:T(8,128)S(1)}, u32[]{:S(2)}, u32[]{:S(2)}) collective-permute-start(f32[8,128]{1,0:T(8,128)S(1)} %add.26.s_own), channel_id=1, source_target_pairs={{0,2},{1,3},{2,0},{3,1},{4,6},{5,7},{6,4},{7,5},{8,10},{9,11},{10,... | collective-permute-start | bytes 12296 | tf_op jit(solution)/shard_map/ppermute | solution.py:26

commit v2 on v1

v2 whole, which is shorter than its diff:
```python
import jax
import jax.numpy as jnp
from jax import lax
from jax.experimental import pallas as pl
from jax.experimental.pallas import tpu as pltpu
from jax.sharding import PartitionSpec as P

BRANCH = 16
SHARES = BRANCH // 4
HALF = BRANCH // 2
PENALTY = 1.0
CVAR_WEIGHT = 0.25
CVAR_LEVEL = 0.75
CHUNKS = 4
LANES = 128
F32 = jnp.float32
BF16 = jnp.bfloat16

ANY = pl.BlockSpec(memory_space=pl.ANY)
HBM = pl.BlockSpec(memory_space=pltpu.HBM)
SMEM = pl.BlockSpec(memory_space=pltpu.SMEM)
VMEM = pl.BlockSpec(memory_space=pltpu.VMEM)


def partner(value, mask):
    pairs = [(source, source ^ mask) for source in range(lax.axis_size("node"))]
    return lax.ppermute(value, "node", pairs)


def in_hbm(value):
    return pltpu.with_memory_space_constraint(value, pltpu.HBM)


def call(kernel, mib, **kwargs):
    return pl.pallas_call(kernel, compiler_params=pltpu.CompilerParams(vmem_limit_bytes=mib << 20), **kwargs)


def quarter_of():
    return lax.axis_index("node") % 4


def place_of(node, quarter):
    half = (node // SHARES) % 2
    return ((half ^ (quarter % 2)) * 2 + node // (2 * SHARES)) * SHARES + node % SHARES


def build_target(target, anchor_of, c_v, y_v):
    scenarios, length, _ = c_v.shape

    def step(i, carry):
        rows = []
        for k in range(2):
            s = 2 * i + k
            rows.append(PENALTY * anchor_of(s).astype(F32) - c_v[s].astype(F32) - y_v[s].astype(F32))
        block = jnp.concatenate(rows, axis=0).astype(BF16)
        target[pl.ds(pl.multiple_of(i * 2 * length, 2 * length), 2 * length), :] = block
        return carry

    lax.fori_loop(0, scenarios // 2, step, 0, unroll=2)


def multiply(target, inv_v, sol, c_v, cost, before, w, after):
    scenarios, length, columns = sol.shape
    width = columns // CHUNKS
    for j in range(CHUNKS):
        before(j)
        cols = slice(j * width, (j + 1) * width)
        sol[:, :, cols] = jnp.dot(target[...], inv_v[:, cols], preferred_element_type=F32).reshape(
            scenarios, length, width
        )

        def step(s, carry):
            own = sol[s, :, cols]
            prod = c_v[s, :, cols].astype(F32) * own
            part = prod[:, :LANES]
            for k in range(1, width // LANES):
                part = part + prod[:, k * LANES : (k + 1) * LANES]
            cost[s] = cost[s] + part
            return carry if w is None else carry + w[s].astype(F32) * own

        after(cols, lax.fori_loop(0, scenarios, step, jnp.zeros((length, width), F32), unroll=8))


def first_kernel(
    w_hbm, sec_hbm, pf_hbm, c_hbm, y_hbm, inv_hbm,
    w, sec, y_v, inv_v, sol, a1, mass, pick, cost, c_v, pf, target, sems,
):
    scenarios, length, columns = sol.shape
    width = columns // CHUNKS
    own = pl.ds(0, length)

    def chunk(j):
        part = pl.ds(j * width, width)
        return pltpu.make_async_copy(inv_hbm.at[:, part], inv_v.at[:, part], sems.at[5 + j])

    small = [
        pltpu.make_async_copy(w_hbm, w, sems.at[0]),
        pltpu.make_async_copy(sec_hbm, sec, sems.at[1]),
        pltpu.make_async_copy(pf_hbm, pf, sems.at[2]),
    ]
    rows = [
        pltpu.make_async_copy(c_hbm.at[:, own, :], c_v, sems.at[3]),
        pltpu.make_async_copy(y_hbm.at[:, own, :], y_v, sems.at[4]),
    ]
    for copy in small + rows + [chunk(j) for j in range(CHUNKS)]:
        copy.start()
    cost[...] = jnp.zeros_like(cost)
    mass[...] = jnp.zeros_like(mass)
    for copy in small:
        copy.wait()

    quarter = quarter_of()
    lane = lax.broadcasted_iota(jnp.int32, (1, scenarios * length), 1)

    def count(s, carry):
        total, place, weight = carry
        node = sec[s] % BRANCH
        p = w[s].astype(F32)
        mass[pl.ds(node, 1), :] = mass[pl.ds(node, 1), :] + p
        mine = lane // length == s
        return total + p, jnp.where(mine, place_of(node, quarter), place), jnp.where(mine, p, weight)

    total, place, weight = lax.fori_loop(
        0, scenarios, count, (jnp.float32(0), jnp.zeros(lane.shape, jnp.int32), jnp.zeros(lane.shape, F32))
    )
    a1[:, columns:] = jnp.full((length, LANES), total, F32)
    row = lax.broadcasted_iota(jnp.int32, pick.shape, 0)
    column = lax.broadcasted_iota(jnp.int32, pick.shape, 1)
    chosen = (row // length == place) & (row % length == column % length)
    pick[...] = jnp.where(chosen, weight, 0.0).astype(BF16)

    for copy in rows:
        copy.wait()
    build_target(target, lambda s: pf[...], c_v, y_v)

    def after(cols, total):
        a1[:, cols] = total

    multiply(target, inv_v, sol, c_v, cost, lambda j: chunk(j).wait(), w, after)


def section_copies(c_hbm, y_hbm, c_v, y_v, sems, section):
    length = c_v.shape[1]
    own = pl.ds(section * length, length)
    return [
        pltpu.make_async_copy(c_hbm.at[:, own, :], c_v, sems.at[0]),
        pltpu.make_async_copy(y_hbm.at[:, own, :], y_v, sems.at[1]),
    ]


def load_kernel(c_hbm, y_hbm, c_v, y_v, sems):
    copies = section_copies(c_hbm, y_hbm, c_v, y_v, sems, 2)
    for copy in copies:
        copy.start()
    for copy in copies:
        copy.wait()


def third_kernel(
    sec, p0, p1, p2, p3, c_hbm, y_hbm, c_v, y_v, inv_v, pick, cost_in,
    c2_v, y2_v, sol, cost, keep, send, target, table, acc, sems, sems2,
):
    scenarios, length, _ = sol.shape
    quarter = quarter_of()
    copies = [
        pltpu.make_async_copy(part, table.at[pl.ds(k * SHARES, SHARES)], sems.at[k])
        for k, part in enumerate((p0, p1, p2, p3))
    ]
    for copy in copies:
        copy.start()
    ahead = section_copies(c_hbm, y_hbm, c2_v, y2_v, sems2, 1)
    for copy in ahead:
        copy.start()
    cost[...] = cost_in[...]
    for copy in copies:
        copy.wait()

    def anchor_of(s):
        node = sec[s] % BRANCH
        return table[((node // SHARES) ^ quarter) * SHARES + node % SHARES]

    build_target(target, anchor_of, c_v, y_v)

    def after(cols, total):
        own = sol[:, :, cols]
        flat = own.reshape(scenarios * length, own.shape[2]).astype(BF16)
        sums = jnp.dot(pick[...], flat, preferred_element_type=F32).reshape(BRANCH, length, own.shape[2])
        keep[:, :, cols] = sums[:HALF]
        send[:, :, cols] = sums[HALF:].astype(BF16)

    multiply(target, inv_v, sol, c_v, cost, lambda j: None, None, after)
    for copy in ahead:
        copy.wait()


def second_kernel(
    w, w_row, low_row, p0, p1, p2, p3, c_v, y_v, inv_v, cost_in, sol, a2, eta, scal, target, table, cost, sems
):
    _, length, columns = sol.shape
    quarter = quarter_of()
    share = columns // 4
    copies = [
        pltpu.make_async_copy(
            part.at[0], table.at[:, pl.ds(pl.multiple_of((quarter ^ k) * share, share), share)], sems.at[k]
        )
        for k, part in enumerate((p0, p1, p2, p3))
    ]
    for copy in copies:
        copy.start()
    cost[...] = cost_in[...]
    for copy in copies:
        copy.wait()
    build_target(target, lambda s: table[...], c_v, y_v)

    def after(cols, total):
        a2[:, cols] = total

    multiply(target, inv_v, sol, c_v, cost, lambda j: None, w, after)
    lanes = jnp.sum(cost[...], axis=1)
    scen_cost = jnp.sum(lanes.T, axis=0, keepdims=True) / (3 * length * columns)
    p = w_row[...].astype(F32)
    low = low_row[...]
    high = low + CVAR_WEIGHT / ((1.0 - CVAR_LEVEL) * PENALTY)
    level = jnp.minimum(jnp.maximum(scen_cost, low), high)
    eta[...] = level
    total = jnp.sum(p * level, axis=1, keepdims=True)
    mass = jnp.sum(p, axis=1, keepdims=True)
    row = lax.broadcasted_iota(jnp.int32, scal.shape, 0)
    scal[...] = jnp.where(row == 0, total, jnp.where(row == 1, mass, 0.0))


def chip_sum_kernel(keep, got, mass_own, mass_got, total, send, mass):
    value = keep[...] + got[...].astype(F32)
    total[...] = value
    send[...] = value.astype(BF16)
    mass[...] = mass_own[...] + mass_got[...]


def third_avg_kernel(total, got, mass_own, mass_got, avg, send, third_avg, mass):
    quarter = quarter_of()
    mass[...] = mass_own[...] + mass_got[...]
    for k in range(HALF):
        node = ((k // SHARES) * 2 + quarter % 2) * SHARES + k % SHARES
        value = (total[k] + got[k].astype(F32)) / mass[pl.ds(node, 1), :][:, :1]
        avg[k] = value
        send[k] = value.astype(BF16)
    third_avg[...] = avg[pl.ds((quarter // 2) * SHARES, SHARES)]


def write_duals(sol, y_v, avg_of, out, buf, sems, section):
    scenarios, length, _ = sol.shape
    group = scenarios // 4

    def copy(g):
        own = pl.ds(g * group, group)
        return pltpu.make_async_copy(
            buf.at[own], out.at[own, pl.ds(section * length, length), :], sems.at[g]
        )

    for g in range(4):

        def step(i, carry):
            s = g * group + i
            buf[s] = (y_v[s].astype(F32) + PENALTY * (sol[s] - avg_of(s))).astype(BF16)
            return carry

        lax.fori_loop(0, group, step, 0, unroll=2)
        copy(g).start()
    return [copy(g) for g in range(4)]


def third_duals_kernel(sec, sol, y_v, avg, got, out, buf, table, sems):
    quarter = quarter_of()
    table[:HALF] = avg[...]
    table[HALF:] = got[...].astype(F32)
    for copy in write_duals(
        sol, y_v, lambda s: table[place_of(sec[s] % BRANCH, quarter)], out, buf, sems, 2
    ):
        copy.wait()


def second_duals_kernel(sol, y_v, a_own, a_got, mass, prior, out, second_avg, buf, full, sems):
    _, columns = full.shape
    quarter = quarter_of()
    share = columns // 4
    whole = jnp.sum(mass[...], axis=0, keepdims=True)[:, :1]
    full[...] = (a_own[...] + a_got[...]) / whole
    second_avg[0] = full[:, pl.ds(pl.multiple_of(quarter * share, share), share)]
    for copy in write_duals(sol, y_v, lambda s: full[...], out, buf, sems, 1):
        copy.wait()


def first_duals_kernel(sol, y_v, a_own, a_got, prior, out, first_avg, buf, sems):
    columns = first_avg.shape[1]
    whole = a_own[...] + a_got[...]
    first_avg[...] = whole[:, :columns] / whole[:, columns : columns + 1]
    for copy in write_duals(sol, y_v, lambda s: first_avg[...], out, buf, sems, 0):
        copy.wait()


def eta_kernel(s_own, s_got, eta, duals_row, eta_avg, eta_duals):
    scal = s_own[...] + s_got[...]
    level = scal[0:1, 0:1] / scal[1:2, 0:1]
    eta_avg[0] = jnp.sum(level)
    eta_duals[...] = duals_row[...] + PENALTY * (eta[...] - level)


def step(
    unit_costs,
    hour_duals,
    inverse,
    weights,
    section_three,
    prev_first,
    prev_second,
    prev_third,
    eta_mean,
    eta_duals,
):
    scenarios, hours, columns = unit_costs.shape
    length = hours // 3
    nodes = lax.axis_size("node")
    dma = pltpu.SemaphoreType.DMA
    shape = jax.ShapeDtypeStruct
    block = (scenarios, length, columns)
    rows = scenarios * length
    w_row = weights.reshape(1, scenarios)
    duals_row = eta_duals.reshape(1, scenarios)
    costs, duals, matrix = in_hbm(unit_costs), in_hbm(hour_duals), in_hbm(inverse)

    low_row = eta_mean[:, None] - (CVAR_WEIGHT + duals_row) / PENALTY
    y_third, y_second = partner((prev_third, prev_second), 2)

    w, sec, y1, inv_v, sol1, a1, mass, pick, cost = call(
        first_kernel,
        30,
        in_specs=[HBM] * 6,
        out_specs=[SMEM] * 2 + [VMEM] * 7,
        out_shape=[
            pltpu.SMEM((scenarios,), jnp.int32),
            pltpu.SMEM((scenarios,), jnp.int32),
            pltpu.VMEM(block, BF16),
            pltpu.VMEM(inverse.shape, BF16),
            pltpu.VMEM(block, F32),
            shape((length, columns + LANES), F32),
            shape((BRANCH, LANES), F32),
            pltpu.VMEM((BRANCH * length, rows), BF16),
            pltpu.VMEM((scenarios, length, LANES), F32),
        ],
        scratch_shapes=[
            pltpu.VMEM(block, BF16),
            pltpu.VMEM((length, columns), BF16),
            pltpu.VMEM((rows, columns), BF16),
            dma((5 + CHUNKS,)),
        ],
    )(in_hbm(weights), in_hbm(section_three), in_hbm(prev_first), costs, duals, matrix)

    core_third, diag_third, core_second, diag_second, core_mass, core_a1 = partner(
        (prev_third, y_third, prev_second, y_second, mass, a1), 1
    )
    c3, y3 = call(
        load_kernel,
        8,
        in_specs=[HBM] * 2,
        out_specs=[VMEM] * 2,
        out_shape=[pltpu.VMEM(block, BF16)] * 2,
        scratch_shapes=[dma((2,))],
    )(costs, duals)
    a1 = a1 + core_a1

    c2, y2, sol3, cost, keep, send = call(
        third_kernel,
        30,
        in_specs=[SMEM, ANY, ANY, ANY, ANY, HBM, HBM] + [VMEM] * 5,
        out_specs=[VMEM] * 6,
        out_shape=[
            pltpu.VMEM(block, BF16),
            pltpu.VMEM(block, BF16),
            pltpu.VMEM(block, F32),
            pltpu.VMEM((scenarios, length, LANES), F32),
            pltpu.VMEM((HALF, length, columns), F32),
            shape((HALF, length, columns), BF16),
        ],
        scratch_shapes=[
            pltpu.VMEM((rows, columns), BF16),
            pltpu.VMEM((BRANCH, length, columns), BF16),
            pltpu.VMEM((BRANCH, length, columns), F32),
            dma((4,)),
            dma((2,)),
        ],
    )(sec, prev_third, core_third, y_third, diag_third, costs, duals, c3, y3, inv_v, pick, cost)

    chip_got = partner(send, 1)
    a1 = a1 + partner(a1, 2)

    sol2, a2, eta, scal = call(
        second_kernel,
        30,
        in_specs=[SMEM, VMEM, VMEM, ANY, ANY, ANY, ANY, VMEM, VMEM, VMEM, VMEM],
        out_specs=[VMEM] * 4,
        out_shape=[
            pltpu.VMEM(block, F32),
            shape((length, columns), F32),
            shape((1, scenarios), F32),
            shape((8, LANES), F32),
        ],
        scratch_shapes=[
            pltpu.VMEM((rows, columns), BF16),
            pltpu.VMEM((length, columns), BF16),
            pltpu.VMEM((scenarios, length, LANES), F32),
            dma((4,)),
        ],
    )(w, w_row, low_row, prev_second, core_second, y_second, diag_second, c2, y2, inv_v, cost)

    core_scal, core_a2 = partner((scal, a2), 1)
    chip_total, chip_send, chip_mass = call(
        chip_sum_kernel,
        8,
        in_specs=[VMEM] * 4,
        out_specs=[VMEM] * 3,
        out_shape=[
            pltpu.VMEM((HALF, length, columns), F32),
            shape((HALF, length, columns), BF16),
            shape((BRANCH, LANES), F32),
        ],
    )(keep, chip_got, mass, core_mass)
    node_got, mass_got = partner((chip_send, chip_mass), 2)
    scal, a2 = scal + core_scal, a2 + core_a2

    masks = []
    while 4 << len(masks) < nodes:
        masks.append(4 << len(masks))
    y_a2 = partner(a2, 2)
    for mask in masks:
        a1_got = partner(a1, mask)
        scal = scal + partner(scal, mask)
        a1_own, a1 = a1, a1 + a1_got
    y_scal = partner(scal, 2)

    avg, avg_send, third_avg, node_mass = call(
        third_avg_kernel,
        8,
        in_specs=[VMEM] * 4,
        out_specs=[VMEM] * 4,
        out_shape=[
            pltpu.VMEM((HALF, length, columns), F32),
            shape((HALF, length, columns), BF16),
            shape((SHARES, length, columns), F32),
            shape((BRANCH, LANES), F32),
        ],
    )(chip_total, node_got, chip_mass, mass_got)
    avg_got = partner(avg_send, 1)

    buf = pltpu.VMEM(block, BF16)
    duals_shape = shape(hour_duals.shape, BF16)
    out, first_avg = call(
        first_duals_kernel,
        8,
        in_specs=[VMEM] * 4 + [SMEM],
        out_specs=[ANY, VMEM],
        out_shape=[duals_shape, shape((length, columns), F32)],
        scratch_shapes=[buf, dma((4,))],
    )(sol1, y1, a1_own, a1_got, sec)
    out, second_avg = call(
        second_duals_kernel,
        8,
        in_specs=[VMEM] * 5 + [ANY],
        out_specs=[ANY, VMEM],
        out_shape=[duals_shape, shape((1, length, columns // 4), F32)],
        scratch_shapes=[buf, pltpu.VMEM((length, columns), F32), dma((4,))],
        input_output_aliases={5: 0},
    )(sol2, y2, a2, y_a2, node_mass, out)
    out = call(
        lambda sec, sol, y_v, avg, got, prior, *rest: third_duals_kernel(sec, sol, y_v, avg, got, *rest),
        8,
        in_specs=[SMEM] + [VMEM] * 4 + [ANY],
        out_specs=ANY,
        out_shape=duals_shape,
        scratch_shapes=[buf, pltpu.VMEM((BRANCH, length, columns), F32), dma((4,))],
        input_output_aliases={5: 0},
    )(sec, sol3, y3, avg, avg_got, out)
    eta_avg, eta_duals_new = call(
        eta_kernel,
        8,
        in_specs=[VMEM] * 4,
        out_specs=[SMEM, VMEM],
        out_shape=[shape((1,), F32), shape((1, scenarios), F32)],
    )(scal, y_scal, eta, duals_row)
    return out, first_avg, second_avg, third_avg, eta_avg, eta_duals_new.reshape(scenarios)


def solution(mesh):
    row = P(("groups", "node"))
    in_specs = (row, row, P(), row, row, P("groups"), row, row, P("groups"), row)
    out_specs = (row, P("groups"), row, row, P("groups"), row)
    return jax.shard_map(step, mesh=mesh, in_specs=in_specs, out_specs=out_specs, check_vma=False)
```

time: 71.9 us -> 62.1 us (0.86)
  waiting for transfers between devices: 25.5 us -> 21.3 us
  Pallas kernels: 25 us -> 22.6 us
  local copies, waits for them, and re-layouts: 2.09 us -> 0.03 us
  starting transfers between devices: 17.7 us -> 16.5 us
    ppermute x21, waiting for transfers between devices: 25.5 us -> 21.3 us  [partner(): return lax.ppermute(value, 'node', pairs)]
    pallas_call x8 -> x10, Pallas kernels: 25 us -> 22.6 us  [the longest x1 5.63 us: step(): call(first_kernel, 30, in_specs=[HBM] * 6, out_specs=[SMEM] * 2 + [VMEM]...]
    unnamed x14 -> x8, local copies, waits for them, and re-layouts: 2.09 us -> 0.03 us
    ppermute x21, starting transfers between devices: 17.7 us -> 16.5 us  [partner(): return lax.ppermute(value, 'node', pairs)]
  transfers between devices with their start and end apart: 21 -> 21, of which waited for: 10 -> 8; matrix products, arithmetic and copies ran while one was open for 0% -> 0% of each run, Pallas kernels for 21% -> 26%
where the time goes in v2:
time: 62.1 us; the launch traced here: 62 us
  Pallas kernels  22.6 us (36%)
  waiting for transfers between devices  21.3 us (34%)
  starting transfers between devices  16.5 us (27%)
  between operations  1.48 us (2%)
    ppermute x21, waiting for transfers between devices, partner(): return lax.ppermute(value, 'node', pairs)  21.3 us
    ppermute x21, starting transfers between devices, partner(): return lax.ppermute(value, 'node', pairs)  16.5 us
    pallas_call x1, Pallas kernels, step(): call(first_kernel, 30, in_specs=[HBM] * 6, out_specs=[SMEM] * 2 + [VMEM]...  5.63 us
    pallas_call x1, Pallas kernels, step(): call(third_kernel, 30, in_specs=[SMEM, ANY, ANY, ANY, ANY, HBM, HBM] + [V...  4.76 us
    pallas_call x1, Pallas kernels, step(): call(second_kernel, 30, in_specs=[SMEM, VMEM, VMEM, ANY, ANY, ANY, ANY, V...  3.96 us
    pallas_call x1, Pallas kernels, step(): call(second_duals_kernel, 8, in_specs=[VMEM] * 5 + [ANY], out_specs=[ANY,...  1.82 us
    pallas_call x1, Pallas kernels, step(): call(first_duals_kernel, 8, in_specs=[VMEM] * 4 + [SMEM], out_specs=[ANY,...  1.78 us
    pallas_call x1, Pallas kernels, step(): call(load_kernel, 8, in_specs=[HBM] * 2, out_specs=[VMEM] * 2, out_shape=...  1.56 us
  transfers between devices with their start and end apart: 21, of which 8 were waited for; matrix products, arithmetic and copies ran while one was open for 0% of the time, Pallas kernels for 26%

profile of v2, /device:TPU:0, one launch (start us, length us, event | category | flops | bytes accessed | tf_op | source)
XLA Modules:
  0.0 62.0 jit_solution(13560138586475865407)
XLA Ops:
  0.6 3.1 %collective-permute-start.1 = (bf16[4,8,2048]{2,1,0:T(8,128)(2,1)}, bf16[4,8,2048]{2,1,0:T(8,128)(2,1)S(1)}, u32[]{:S(2)}, u32[]{:S(2)}) collective-permute-start(bf16[4,8,2048]{2,1,0:T(8,128)(2,1)} %p0.2), channel_id=1, source_target_pairs={{0,2},{1,3},{2,0},{3,1},{4,6},{5,7},{6,4},{7,5},{8,10},{9,11},{10,... | collective-permute-start | bytes 393224 | tf_op jit(solution)/shard_map/ppermute | solution.py:27
  3.7 0.0 collective-permute-start
  3.7 3.7 %collective-permute-done.1.p2 = bf16[4,8,2048]{2,1,0:T(8,128)(2,1)S(1)} collective-permute-done((bf16[4,8,2048]{2,1,0:T(8,128)(2,1)}, bf16[4,8,2048]{2,1,0:T(8,128)(2,1)S(1)}, u32[]{:S(2)}, u32[]{:S(2)}) %collective-permute-start.1) | collective-permute-done | bytes 131104 | tf_op jit(solution)/shard_map/ppermute | solution.py:27
  7.4 1.6 %shard_map.146 = (bf16[32,8,2048]{2,1,0:T(8,128)(2,1)S(1)}, bf16[32,8,2048]{2,1,0:T(8,128)(2,1)S(1)}) custom-call(bf16[32,24,2048]{2,1,0:T(8,128)(2,1)} %c_hbm.5, bf16[32,24,2048]{2,1,0:T(8,128)(2,1)} %y_hbm.5), custom_call_target="tpu_custom_call" | custom-call | tf_op jit(solution)/shard_map/pallas_call | solution.py:361
  9.0 0.0 copy-start
  9.0 5.6 %shard_map.145 = (s32[32]{0:T(128)S(4)}, s32[32]{0:T(128)S(4)}, bf16[32,8,2048]{2,1,0:T(8,128)(2,1)S(1)}, bf16[2048,2048]{1,0:T(8,128)(2,1)S(1)}, f32[32,8,2048]...) custom-call(s32[32]{0:T(128)} %w_hbm.1, ...), custom_call_target="tpu_custom_call" | custom-call | tf_op jit(solution)/shard_map/pallas_call | solution.py:334
  14.6 0.0 collective-permute-done.p1
  14.7 0.0 copy-start.1
  14.7 0.0 copy-start.3
  14.7 0.0 copy-start.2
  14.7 4.8 %shard_map.147 = (bf16[32,8,2048]{2,1,0:T(8,128)(2,1)S(1)}, bf16[32,8,2048]{2,1,0:T(8,128)(2,1)S(1)}, f32[32,8,2048]{2,1,0:T(8,128)S(1)}, f32[32,8,128]{2,1,0:T(...) custom-call(s32[32]{0:T(128)S(4)} %get-tuple-element.40.sec.prior, ...), custom_call_target="tpu_custom_call" | custom-call | tf_op jit(solution)/shard_map/pallas_call | solution.py:371
  19.5 0.6 collective-permute-start.3
  20.0 0.1 collective-permute-start.4
  20.1 1.1 %collective-permute-done.4.mass_got = f32[16,128]{1,0:T(8,128)S(1)} collective-permute-done((f32[16,128]{1,0:T(8,128)S(1)}, f32[16,128]{1,0:T(8,128)S(1)}, u32[]{:S(2)}, u32[]{:S(2)}) %collective-permute-start.4) | collective-permute-done | bytes 8224 | tf_op jit(solution)/shard_map/ppermute | solution.py:27
  21.2 0.1 shard_map.148
  21.3 1.8 %collective-permute-start.5 = (bf16[8,8,2048]{2,1,0:T(8,128)(2,1)S(1)}, bf16[8,8,2048]{2,1,0:T(8,128)(2,1)S(1)}, u32[]{:S(2)}, u32[]{:S(2)}) collective-permute-start(bf16[8,8,2048]{2,1,0:T(8,128)(2,1)S(1)} %get-tuple-element.51), channel_id=1, source_target_pairs={{0,2},{1,3},{2,0},{3,1},{4,6},{5,7},{6,4},{7,5},{8,10},{9,11},{10,... | collective-permute-start | bytes 786440 | tf_op jit(solution)/shard_map/ppermute | solution.py:27
  23.1 0.1 collective-permute-start.13
  23.2 1.2 %collective-permute-done.13 = f32[8,2176]{1,0:T(8,128)S(1)} collective-permute-done((f32[8,2176]{1,0:T(8,128)S(1)}, f32[8,2176]{1,0:T(8,128)S(1)}, u32[]{:S(2)}, u32[]{:S(2)}) %collective-permute-start.13) | collective-permute-done | bytes 69664 | tf_op jit(solution)/shard_map/ppermute | solution.py:27
  24.4 0.4 collective-permute-start.14
  24.7 1.7 %collective-permute-start.9 = (bf16[1,8,512]{2,1,0:T(8,128)(2,1)S(1)}, bf16[1,8,512]{2,1,0:T(8,128)(2,1)S(1)}, u32[]{:S(2)}, u32[]{:S(2)}) collective-permute-start(bf16[1,8,512]{2,1,0:T(8,128)(2,1)S(1)} %copy-done.1), channel_id=1, source_target_pairs={{0,2},{1,3},{2,0},{3,1},{4,6},{5,7},{6,4},{7,5},{8,10},{9,11},{10,... | collective-permute-start | bytes 24584 | tf_op jit(solution)/shard_map/ppermute | solution.py:27
  26.5 0.3 collective-permute-start.6
  27.4 4.3 %collective-permute-done.9.p2 = bf16[1,8,512]{2,1,0:T(8,128)(2,1)S(1)} collective-permute-done((bf16[1,8,512]{2,1,0:T(8,128)(2,1)S(1)}, bf16[1,8,512]{2,1,0:T(8,128)(2,1)S(1)}, u32[]{:S(2)}, u32[]{:S(2)}) %collective-permute-start.9) | collective-permute-done | bytes 8224 | tf_op jit(solution)/shard_map/ppermute | solution.py:27
  31.7 0.0 collective-permute-start.10
  31.7 0.0 collective-permute-done.14
  31.7 1.9 %collective-permute-start.15 = (f32[8,2176]{1,0:T(8,128)S(1)}, f32[8,2176]{1,0:T(8,128)S(1)}, u32[]{:S(2)}, u32[]{:S(2)}) collective-permute-start(f32[8,2176]{1,0:T(8,128)S(1)} %add.32), channel_id=1, source_target_pairs={{0,4},{1,5},{2,6},{3,7},{4,0},{5,1},{6,2},{7,3},{8,12},{9,13},{10,... | collective-permute-start | bytes 208904 | tf_op jit(solution)/shard_map/ppermute | solution.py:27
  33.6 0.8 %shard_map.149 = (f32[8,8,2048]{2,1,0:T(8,128)S(1)}, bf16[8,8,2048]{2,1,0:T(8,128)(2,1)S(1)}, f32[4,8,2048]{2,1,0:T(8,128)}, f32[16,128]{1,0:T(8,128)S(1)}) custom-call(f32[8,8,2048]{2,1,0:T(8,128)S(1)} %get-tuple-element.50.total, bf16[8,8,2048]{2,1,0:T(8,128)(2,1)S(1)} %collective-permute-done.5.got, f32[16,128]{1,0:T(8,128)S(1)} %get-tuple-element.52.mass_own, ...), custom_call_target="tpu_custom_call" | custom-call | tf_op jit(solution)/shard_map/pallas_call | solution.py:440
  34.4 0.2 collective-permute-start.7
  34.7 0.0 collective-permute-done.8.p1
  34.7 0.0 collective-permute-done.10.p3
  34.7 4.0 %shard_map.150 = (f32[32,8,2048]{2,1,0:T(8,128)S(1)}, f32[8,2048]{1,0:T(8,128)S(1)}, f32[1,32]{1,0:T(1,128)S(1)}, f32[8,128]{1,0:T(8,128)S(1)}) custom-call(s32[32]{0:T(128)S(4)} %get-tuple-element.55.w, s32[1,32]{1,0:T(1,128)S(1)} %bitcast.7, f32[1,32]{1,0:T(1,128)S(1)} %subtract_bitcast_fusion.low_row, bf16[1,8,512]{2,1,0:T(8,128)(2,1)S(1)} %copy-done.1, ...), custom_call_target="tpu_custom_call" | custom-call | tf_op jit(solution)/shard_map/pallas_call | solution.py:396
  38.6 0.3 collective-permute-start.11
  39.0 0.0 collective-permute-done.15
  39.0 2.6 %collective-permute-start.16 = (f32[8,2176]{1,0:T(8,128)S(1)}, f32[8,2176]{1,0:T(8,128)S(1)}, u32[]{:S(2)}, u32[]{:S(2)}) collective-permute-start(f32[8,2176]{1,0:T(8,128)S(1)} %add.33.a_own), channel_id=1, source_target_pairs={{0,8},{1,9},{2,10},{3,11},{4,12},{5,13},{6,14},{7,15},{8,0},{9,1},... | collective-permute-start | bytes 208904 | tf_op jit(solution)/shard_map/ppermute | solution.py:27
  41.7 0.0 collective-permute-done.11
  41.7 1.6 %collective-permute-start.12 = (f32[8,2048]{1,0:T(8,128)S(1)}, f32[8,2048]{1,0:T(8,128)S(1)}, u32[]{:S(2)}, u32[]{:S(2)}) collective-permute-start(f32[8,2048]{1,0:T(8,128)S(1)} %add.30.a_own), channel_id=1, source_target_pairs={{0,2},{1,3},{2,0},{3,1},{4,6},{5,7},{6,4},{7,5},{8,10},{9,11},{10,... | collective-permute-start | bytes 196616 | tf_op jit(solution)/shard_map/ppermute | solution.py:27
  43.3 0.0 collective-permute-start.17
  43.3 1.2 %collective-permute-done.17 = f32[8,128]{1,0:T(8,128)S(1)} collective-permute-done((f32[8,128]{1,0:T(8,128)S(1)}, f32[8,128]{1,0:T(8,128)S(1)}, u32[]{:S(2)}, u32[]{:S(2)}) %collective-permute-start.17) | collective-permute-done | bytes 4128 | tf_op jit(solution)/shard_map/ppermute | solution.py:27
  44.4 0.4 collective-permute-start.18
  44.9 3.2 %collective-permute-done.18 = f32[8,128]{1,0:T(8,128)S(1)} collective-permute-done((f32[8,128]{1,0:T(8,128)S(1)}, f32[8,128]{1,0:T(8,128)S(1)}, u32[]{:S(2)}, u32[]{:S(2)}) %collective-permute-start.18) | collective-permute-done | bytes 4128 | tf_op jit(solution)/shard_map/ppermute | solution.py:27
  48.1 0.9 %collective-permute-start.19 = (f32[8,128]{1,0:T(8,128)S(1)}, f32[8,128]{1,0:T(8,128)S(1)}, u32[]{:S(2)}, u32[]{:S(2)}) collective-permute-start(f32[8,128]{1,0:T(8,128)S(1)} %add.35), channel_id=1, source_target_pairs={{0,8},{1,9},{2,10},{3,11},{4,12},{5,13},{6,14},{7,15},{8,0},{9,1},... | collective-permute-start | bytes 12296 | tf_op jit(solution)/shard_map/ppermute | solution.py:27
  48.9 3.6 %collective-permute-done.19 = f32[8,128]{1,0:T(8,128)S(1)} collective-permute-done((f32[8,128]{1,0:T(8,128)S(1)}, f32[8,128]{1,0:T(8,128)S(1)}, u32[]{:S(2)}, u32[]{:S(2)}) %collective-permute-start.19) | collective-permute-done | bytes 4128 | tf_op jit(solution)/shard_map/ppermute | solution.py:27
  52.6 0.5 collective-permute-start.20
  53.1 3.1 %collective-permute-done.20.s_got = f32[8,128]{1,0:T(8,128)S(1)} collective-permute-done((f32[8,128]{1,0:T(8,128)S(1)}, f32[8,128]{1,0:T(8,128)S(1)}, u32[]{:S(2)}, u32[]{:S(2)}) %collective-permute-start.20) | collective-permute-done | bytes 4128 | tf_op jit(solution)/shard_map/ppermute | solution.py:27
  56.2 0.6 shard_map.154
  56.8 0.0 collective-permute-done.16.a_got
  56.8 1.8 %shard_map.151 = (bf16[32,24,2048]{2,1,0:T(8,128)(2,1)}, f32[8,2048]{1,0:T(8,128)}) custom-call(f32[32,8,2048]{2,1,0:T(8,128)S(1)} %get-tuple-element.62.sol, bf16[32,8,2048]{2,1,0:T(8,128)(2,1)S(1)} %get-tuple-element.63.y_v, f32[8,2176]{1,0:T(8,128)S(1)} %add.33.a_own, f32[8,2176]{1,0:T(8,128)S(1)} %collective-permute-done.16.a_got, ...), custom_call_target="tpu_custom_call" | custom-call | tf_op jit(solution)/shard_map/pallas_call | solution.py:456
  58.6 1.8 %shard_map.152 = (bf16[32,24,2048]{2,1,0:T(8,128)(2,1)}, f32[1,8,512]{2,1,0:T(8,128)}) custom-call(f32[32,8,2048]{2,1,0:T(8,128)S(1)} %get-tuple-element.59.sol, bf16[32,8,2048]{2,1,0:T(8,128)(2,1)S(1)} %get-tuple-element.57.y_v, f32[8,2048]{1,0:T(8,128)S(1)} %add.30.a_own, ...), custom_call_target="tpu_custom_call", output_to_operand_aliasing={{0}: (5, {})} | custom-call | tf_op jit(solution)/shard_map/pallas_call | solution.py:464
  60.4 1.5 %shard_map.153 = bf16[32,24,2048]{2,1,0:T(8,128)(2,1)} custom-call(s32[32]{0:T(128)S(4)} %get-tuple-element.40.sec.prior, f32[32,8,2048]{2,1,0:T(8,128)S(1)} %get-tuple-element.46.sol, bf16[32,8,2048]{2,1,0:T(8,128)(2,1)S(1)} %get-tuple-element.42.y_v, f32[8,8,2048]{2,1,0:T(8,128)S(1)} %get-tuple-element.53.avg, ...), custom_call_target="tpu_custom_call", output_to_operand_aliasing={{}: (5, {})} | custom-call | tf_op jit(solution)/shard_map/pallas_call | solution.py:473
  (20 shorter events, 0.1 us)
Async XLA Ops:
  0.6 6.8 %collective-permute-start.1 = (bf16[4,8,2048]{2,1,0:T(8,128)(2,1)}, bf16[4,8,2048]{2,1,0:T(8,128)(2,1)S(1)}, u32[]{:S(2)}, u32[]{:S(2)}) collective-permute-start(bf16[4,8,2048]{2,1,0:T(8,128)(2,1)} %p0.2), channel_id=1, source_target_pairs={{0,2},{1,3},{2,0},{3,1},{4,6},{5,7},{6,4},{7,5},{8,10},{9,11},{10,... | collective-permute-start | bytes 393224 | tf_op jit(solution)/shard_map/ppermute | solution.py:27
  3.7 10.9 %collective-permute-start = (bf16[4,8,2048]{2,1,0:T(8,128)(2,1)}, bf16[4,8,2048]{2,1,0:T(8,128)(2,1)S(1)}, u32[]{:S(2)}, u32[]{:S(2)}) collective-permute-start(bf16[4,8,2048]{2,1,0:T(8,128)(2,1)} %p0.2), channel_id=1, source_target_pairs={{0,1},{1,0},{2,3},{3,2},{4,5},{5,4},{6,7},{7,6},{8,9},{9,8},{10,11... | collective-permute-start | bytes 393224 | tf_op jit(solution)/shard_map/ppermute | solution.py:27
  7.4 7.2 %collective-permute-start.2 = (bf16[4,8,2048]{2,1,0:T(8,128)(2,1)S(1)}, bf16[4,8,2048]{2,1,0:T(8,128)(2,1)S(1)}, u32[]{:S(2)}, u32[]{:S(2)}) collective-permute-start(bf16[4,8,2048]{2,1,0:T(8,128)(2,1)S(1)} %collective-permute-done.1.p2), channel_id=1, source_target_pairs={{0,1},{1,0},{2,3},{3,2},{4,5},{5,4},{6,7},{7,6},{8,9},{9,8},{10,11... | collective-permute-start | bytes 393224 | tf_op jit(solution)/shard_map/ppermute | solution.py:27
  9.0 5.7 %copy-start = (bf16[4,8,2048]{2,1,0:T(8,128)(2,1)S(1)}, bf16[4,8,2048]{2,1,0:T(8,128)(2,1)}, u32[]{:S(2)}) copy-start(bf16[4,8,2048]{2,1,0:T(8,128)(2,1)} %p0.2) | copy-start | bytes 393220
  14.7 10.1 %copy-start.1 = (bf16[1,8,512]{2,1,0:T(8,128)(2,1)S(1)}, bf16[1,8,512]{2,1,0:T(8,128)(2,1)}, u32[]{:S(2)}) copy-start(bf16[1,8,512]{2,1,0:T(8,128)(2,1)} %p0.3) | copy-start | bytes 24580
  14.7 20.0 %copy-start.3 = (f32[32]{0:T(128)S(1)}, f32[32]{0:T(128)}, u32[]{:S(2)}) copy-start(f32[32]{0:T(128)} %param.19) | copy-start | bytes 388
  14.7 20.0 %copy-start.2 = (s32[32]{0:T(128)S(1)}, s32[32]{0:T(128)}, u32[]{:S(2)}) copy-start(s32[32]{0:T(128)} %w_hbm.1) | copy-start | bytes 388
  19.5 1.8 %collective-permute-start.3 = (bf16[8,8,2048]{2,1,0:T(8,128)(2,1)S(1)}, bf16[8,8,2048]{2,1,0:T(8,128)(2,1)S(1)}, u32[]{:S(2)}, u32[]{:S(2)}) collective-permute-start(bf16[8,8,2048]{2,1,0:T(8,128)(2,1)S(1)} %get-tuple-element.48), channel_id=1, source_target_pairs={{0,1},{1,0},{2,3},{3,2},{4,5},{5,4},{6,7},{7,6},{8,9},{9,8},{10,11... | collective-permute-start | bytes 786440 | tf_op jit(solution)/shard_map/ppermute | solution.py:27
  20.0 1.2 %collective-permute-start.4 = (f32[16,128]{1,0:T(8,128)S(1)}, f32[16,128]{1,0:T(8,128)S(1)}, u32[]{:S(2)}, u32[]{:S(2)}) collective-permute-start(f32[16,128]{1,0:T(8,128)S(1)} %get-tuple-element.49.mass_own), channel_id=1, source_target_pairs={{0,1},{1,0},{2,3},{3,2},{4,5},{5,4},{6,7},{7,6},{8,9},{9,8},{10,11... | collective-permute-start | bytes 24584 | tf_op jit(solution)/shard_map/ppermute | solution.py:27
  21.3 12.3 %collective-permute-start.5 = (bf16[8,8,2048]{2,1,0:T(8,128)(2,1)S(1)}, bf16[8,8,2048]{2,1,0:T(8,128)(2,1)S(1)}, u32[]{:S(2)}, u32[]{:S(2)}) collective-permute-start(bf16[8,8,2048]{2,1,0:T(8,128)(2,1)S(1)} %get-tuple-element.51), channel_id=1, source_target_pairs={{0,2},{1,3},{2,0},{3,1},{4,6},{5,7},{6,4},{7,5},{8,10},{9,11},{10,... | collective-permute-start | bytes 786440 | tf_op jit(solution)/shard_map/ppermute | solution.py:27
  23.1 1.3 %collective-permute-start.13 = (f32[8,2176]{1,0:T(8,128)S(1)}, f32[8,2176]{1,0:T(8,128)S(1)}, u32[]{:S(2)}, u32[]{:S(2)}) collective-permute-start(f32[8,2176]{1,0:T(8,128)S(1)} %get-tuple-element.64), channel_id=1, source_target_pairs={{0,1},{1,0},{2,3},{3,2},{4,5},{5,4},{6,7},{7,6},{8,9},{9,8},{10,11... | collective-permute-start | bytes 208904 | tf_op jit(solution)/shard_map/ppermute | solution.py:27
  24.4 7.3 %collective-permute-start.14 = (f32[8,2176]{1,0:T(8,128)S(1)}, f32[8,2176]{1,0:T(8,128)S(1)}, u32[]{:S(2)}, u32[]{:S(2)}) collective-permute-start(f32[8,2176]{1,0:T(8,128)S(1)} %add.31), channel_id=1, source_target_pairs={{0,2},{1,3},{2,0},{3,1},{4,6},{5,7},{6,4},{7,5},{8,10},{9,11},{10,... | collective-permute-start | bytes 208904 | tf_op jit(solution)/shard_map/ppermute | solution.py:27
  24.7 7.0 %collective-permute-start.9 = (bf16[1,8,512]{2,1,0:T(8,128)(2,1)S(1)}, bf16[1,8,512]{2,1,0:T(8,128)(2,1)S(1)}, u32[]{:S(2)}, u32[]{:S(2)}) collective-permute-start(bf16[1,8,512]{2,1,0:T(8,128)(2,1)S(1)} %copy-done.1), channel_id=1, source_target_pairs={{0,2},{1,3},{2,0},{3,1},{4,6},{5,7},{6,4},{7,5},{8,10},{9,11},{10,... | collective-permute-start | bytes 24584 | tf_op jit(solution)/shard_map/ppermute | solution.py:27
  26.5 7.1 %collective-permute-start.6 = (f32[16,128]{1,0:T(8,128)S(1)}, f32[16,128]{1,0:T(8,128)S(1)}, u32[]{:S(2)}, u32[]{:S(2)}) collective-permute-start(f32[16,128]{1,0:T(8,128)S(1)} %get-tuple-element.52.mass_own), channel_id=1, source_target_pairs={{0,2},{1,3},{2,0},{3,1},{4,6},{5,7},{6,4},{7,5},{8,10},{9,11},{10,... | collective-permute-start | bytes 24584 | tf_op jit(solution)/shard_map/ppermute | solution.py:27
  26.8 7.9 %collective-permute-start.8 = (bf16[1,8,512]{2,1,0:T(8,128)(2,1)S(1)}, bf16[1,8,512]{2,1,0:T(8,128)(2,1)S(1)}, u32[]{:S(2)}, u32[]{:S(2)}) collective-permute-start(bf16[1,8,512]{2,1,0:T(8,128)(2,1)S(1)} %copy-done.1), channel_id=1, source_target_pairs={{0,1},{1,0},{2,3},{3,2},{4,5},{5,4},{6,7},{7,6},{8,9},{9,8},{10,11... | collective-permute-start | bytes 24584 | tf_op jit(solution)/shard_map/ppermute | solution.py:27
  31.7 3.0 %collective-permute-start.10 = (bf16[1,8,512]{2,1,0:T(8,128)(2,1)S(1)}, bf16[1,8,512]{2,1,0:T(8,128)(2,1)S(1)}, u32[]{:S(2)}, u32[]{:S(2)}) collective-permute-start(bf16[1,8,512]{2,1,0:T(8,128)(2,1)S(1)} %collective-permute-done.9.p2), channel_id=1, source_target_pairs={{0,1},{1,0},{2,3},{3,2},{4,5},{5,4},{6,7},{7,6},{8,9},{9,8},{10,11... | collective-permute-start | bytes 24584 | tf_op jit(solution)/shard_map/ppermute | solution.py:27
  31.7 7.3 %collective-permute-start.15 = (f32[8,2176]{1,0:T(8,128)S(1)}, f32[8,2176]{1,0:T(8,128)S(1)}, u32[]{:S(2)}, u32[]{:S(2)}) collective-permute-start(f32[8,2176]{1,0:T(8,128)S(1)} %add.32), channel_id=1, source_target_pairs={{0,4},{1,5},{2,6},{3,7},{4,0},{5,1},{6,2},{7,3},{8,12},{9,13},{10,... | collective-permute-start | bytes 208904 | tf_op jit(solution)/shard_map/ppermute | solution.py:27
  34.4 26.0 %collective-permute-start.7 = (bf16[8,8,2048]{2,1,0:T(8,128)(2,1)S(1)}, bf16[8,8,2048]{2,1,0:T(8,128)(2,1)S(1)}, u32[]{:S(2)}, u32[]{:S(2)}) collective-permute-start(bf16[8,8,2048]{2,1,0:T(8,128)(2,1)S(1)} %get-tuple-element.54), channel_id=1, source_target_pairs={{0,1},{1,0},{2,3},{3,2},{4,5},{5,4},{6,7},{7,6},{8,9},{9,8},{10,11... | collective-permute-start | bytes 786440 | tf_op jit(solution)/shard_map/ppermute | solution.py:27
  38.6 3.0 %collective-permute-start.11 = (f32[8,2048]{1,0:T(8,128)S(1)}, f32[8,2048]{1,0:T(8,128)S(1)}, u32[]{:S(2)}, u32[]{:S(2)}) collective-permute-start(f32[8,2048]{1,0:T(8,128)S(1)} %get-tuple-element.60), channel_id=1, source_target_pairs={{0,1},{1,0},{2,3},{3,2},{4,5},{5,4},{6,7},{7,6},{8,9},{9,8},{10,11... | collective-permute-start | bytes 196616 | tf_op jit(solution)/shard_map/ppermute | solution.py:27
  39.0 17.8 %collective-permute-start.16 = (f32[8,2176]{1,0:T(8,128)S(1)}, f32[8,2176]{1,0:T(8,128)S(1)}, u32[]{:S(2)}, u32[]{:S(2)}) collective-permute-start(f32[8,2176]{1,0:T(8,128)S(1)} %add.33.a_own), channel_id=1, source_target_pairs={{0,8},{1,9},{2,10},{3,11},{4,12},{5,13},{6,14},{7,15},{8,0},{9,1},... | collective-permute-start | bytes 208904 | tf_op jit(solution)/shard_map/ppermute | solution.py:27
  41.7 16.9 %collective-permute-start.12 = (f32[8,2048]{1,0:T(8,128)S(1)}, f32[8,2048]{1,0:T(8,128)S(1)}, u32[]{:S(2)}, u32[]{:S(2)}) collective-permute-start(f32[8,2048]{1,0:T(8,128)S(1)} %add.30.a_own), channel_id=1, source_target_pairs={{0,2},{1,3},{2,0},{3,1},{4,6},{5,7},{6,4},{7,5},{8,10},{9,11},{10,... | collective-permute-start | bytes 196616 | tf_op jit(solution)/shard_map/ppermute | solution.py:27
  43.3 1.2 %collective-permute-start.17 = (f32[8,128]{1,0:T(8,128)S(1)}, f32[8,128]{1,0:T(8,128)S(1)}, u32[]{:S(2)}, u32[]{:S(2)}) collective-permute-start(f32[8,128]{1,0:T(8,128)S(1)} %get-tuple-element.70), channel_id=1, source_target_pairs={{0,1},{1,0},{2,3},{3,2},{4,5},{5,4},{6,7},{7,6},{8,9},{9,8},{10,11... | collective-permute-start | bytes 12296 | tf_op jit(solution)/shard_map/ppermute | solution.py:27
  44.4 3.6 %collective-permute-start.18 = (f32[8,128]{1,0:T(8,128)S(1)}, f32[8,128]{1,0:T(8,128)S(1)}, u32[]{:S(2)}, u32[]{:S(2)}) collective-permute-start(f32[8,128]{1,0:T(8,128)S(1)} %add.34), channel_id=1, source_target_pairs={{0,4},{1,5},{2,6},{3,7},{4,0},{5,1},{6,2},{7,3},{8,12},{9,13},{10,... | collective-permute-start | bytes 12296 | tf_op jit(solution)/shard_map/ppermute | solution.py:27
  48.1 4.5 %collective-permute-start.19 = (f32[8,128]{1,0:T(8,128)S(1)}, f32[8,128]{1,0:T(8,128)S(1)}, u32[]{:S(2)}, u32[]{:S(2)}) collective-permute-start(f32[8,128]{1,0:T(8,128)S(1)} %add.35), channel_id=1, source_target_pairs={{0,8},{1,9},{2,10},{3,11},{4,12},{5,13},{6,14},{7,15},{8,0},{9,1},... | collective-permute-start | bytes 12296 | tf_op jit(solution)/shard_map/ppermute | solution.py:27
  52.6 3.6 %collective-permute-start.20 = (f32[8,128]{1,0:T(8,128)S(1)}, f32[8,128]{1,0:T(8,128)S(1)}, u32[]{:S(2)}, u32[]{:S(2)}) collective-permute-start(f32[8,128]{1,0:T(8,128)S(1)} %add.36.s_own), channel_id=1, source_target_pairs={{0,2},{1,3},{2,0},{3,1},{4,6},{5,7},{6,4},{7,5},{8,10},{9,11},{10,... | collective-permute-start | bytes 12296 | tf_op jit(solution)/shard_map/ppermute | solution.py:27

commit v3 on v2

v3 whole, which is shorter than its diff:
```python
import jax
import jax.numpy as jnp
from jax import lax
from jax.experimental import pallas as pl
from jax.experimental.pallas import tpu as pltpu
from jax.sharding import PartitionSpec as P

BRANCH = 16
SHARES = BRANCH // 4
HALF = BRANCH // 2
PENALTY = 1.0
CVAR_WEIGHT = 0.25
CVAR_LEVEL = 0.75
CHUNKS = 4
LANES = 128
F32 = jnp.float32
BF16 = jnp.bfloat16

ANY = pl.BlockSpec(memory_space=pl.ANY)
HBM = pl.BlockSpec(memory_space=pltpu.HBM)
SMEM = pl.BlockSpec(memory_space=pltpu.SMEM)
VMEM = pl.BlockSpec(memory_space=pltpu.VMEM)


def partner(value, mask):
    pairs = [(source, source ^ mask) for source in range(lax.axis_size("node"))]
    return lax.ppermute(value, "node", pairs)


def in_hbm(value):
    return pltpu.with_memory_space_constraint(value, pltpu.HBM)


def call(kernel, mib, **kwargs):
    return pl.pallas_call(kernel, compiler_params=pltpu.CompilerParams(vmem_limit_bytes=mib << 20), **kwargs)


def quarter_of():
    return lax.axis_index("node") % 4


def place_of(node, quarter):
    half = (node // SHARES) % 2
    return ((half ^ (quarter % 2)) * 2 + node // (2 * SHARES)) * SHARES + node % SHARES


def build_target(target, anchor_of, c_v, y_v):
    scenarios, length, _ = c_v.shape

    def step(i, carry):
        rows = []
        for k in range(2):
            s = 2 * i + k
            rows.append(PENALTY * anchor_of(s).astype(F32) - c_v[s].astype(F32) - y_v[s].astype(F32))
        block = jnp.concatenate(rows, axis=0).astype(BF16)
        target[pl.ds(pl.multiple_of(i * 2 * length, 2 * length), 2 * length), :] = block
        return carry

    lax.fori_loop(0, scenarios // 2, step, 0, unroll=2)


def multiply(target, inv_v, sol, c_v, cost, before, w, after):
    scenarios, length, columns = sol.shape
    width = columns // CHUNKS

    def product(j):
        before(j)
        cols = slice(j * width, (j + 1) * width)
        sol[:, :, cols] = jnp.dot(target[...], inv_v[:, cols], preferred_element_type=F32).reshape(
            scenarios, length, width
        )

    def finish(j):
        cols = slice(j * width, (j + 1) * width)
        total = jnp.zeros((length, width), F32)
        for s in range(scenarios):
            own = sol[s, :, cols]
            prod = c_v[s, :, cols].astype(F32) * own
            part = prod[:, :LANES]
            for k in range(1, width // LANES):
                part = part + prod[:, k * LANES : (k + 1) * LANES]
            cost[s] = cost[s] + part
            if w is not None:
                total = total + w[s].astype(F32) * own
        after(cols, total)

    for j in range(CHUNKS):
        product(j)
        if j:
            finish(j - 1)
    finish(CHUNKS - 1)


def first_kernel(
    w_hbm, sec_hbm, pf_hbm, c_hbm, y_hbm, inv_hbm,
    w, sec, y1, c3, y3, inv_v, sol, a1, mass, pick, cost, c1, pf, target, sems,
):
    scenarios, length, columns = sol.shape
    width = columns // CHUNKS

    def chunk(j):
        part = pl.ds(j * width, width)
        return pltpu.make_async_copy(inv_hbm.at[:, part], inv_v.at[:, part], sems.at[9 + j])

    def rows(k, c_v, y_v):
        own = pl.ds(k * length, length)
        return [
            pltpu.make_async_copy(c_hbm.at[:, own, :], c_v, sems.at[3 + 2 * k]),
            pltpu.make_async_copy(y_hbm.at[:, own, :], y_v, sems.at[4 + 2 * k]),
        ]

    small = [
        pltpu.make_async_copy(w_hbm, w, sems.at[0]),
        pltpu.make_async_copy(sec_hbm, sec, sems.at[1]),
        pltpu.make_async_copy(pf_hbm, pf, sems.at[2]),
    ]
    first = rows(0, c1, y1)
    later = rows(2, c3, y3)
    for copy in small + first + [chunk(j) for j in range(CHUNKS)] + later:
        copy.start()
    cost[...] = jnp.zeros_like(cost)
    for copy in small:
        copy.wait()

    quarter = quarter_of()
    lane = lax.broadcasted_iota(jnp.int32, (1, scenarios * length), 1)
    slot = lax.broadcasted_iota(jnp.int32, mass.shape, 1)

    def count(s, carry):
        place, weight, masses = carry
        node = sec[s] % BRANCH
        p = w[s].astype(F32)
        mine = lane // length == s
        return (
            jnp.where(mine, place_of(node, quarter), place),
            jnp.where(mine, p, weight),
            masses + jnp.where(slot == node, p, 0.0),
        )

    place, weight, masses = lax.fori_loop(
        0, scenarios, count, (jnp.zeros(lane.shape, jnp.int32), jnp.zeros(lane.shape, F32), jnp.zeros(mass.shape, F32))
    )
    mass[...] = masses
    row = lax.broadcasted_iota(jnp.int32, pick.shape, 0)
    column = lax.broadcasted_iota(jnp.int32, pick.shape, 1)
    chosen = (row // length == place) & (row % length == column % length)
    pick[...] = jnp.where(chosen, weight, 0.0).astype(BF16)

    for copy in first:
        copy.wait()
    build_target(target, lambda s: pf[...], c1, y1)

    def after(cols, total):
        a1[:, cols] = total

    multiply(target, inv_v, sol, c1, cost, lambda j: chunk(j).wait(), w, after)
    for copy in later:
        copy.wait()


def packed(value):
    high = value.astype(BF16)
    rest = value - high.astype(F32)
    middle = rest.astype(BF16)
    return jnp.concatenate((high, middle, (rest - middle.astype(F32)).astype(BF16)), axis=1)


def unpacked(tiles):
    high, middle, low = (tiles[:, k * LANES : (k + 1) * LANES].astype(F32) for k in range(3))
    return high + middle + low


def node_mass(scal, node):
    row = scal[2:3, :]
    slot = lax.broadcasted_iota(jnp.int32, row.shape, 1)
    return jnp.sum(jnp.where(slot == node, row, 0.0), axis=1, keepdims=True)


def third_kernel(
    sec, p0, p1, p2, p3, c_hbm, y_hbm, c_v, y_v, inv_v, pick, cost_in,
    c2, y2, sol, cost, keep, send, target, table, sems,
):
    scenarios, length, _ = sol.shape
    quarter = quarter_of()
    copies = [
        pltpu.make_async_copy(part, table.at[pl.ds(k * SHARES, SHARES)], sems.at[k])
        for k, part in enumerate((p0, p1, p2, p3))
    ]
    own = pl.ds(length, length)
    ahead = [
        pltpu.make_async_copy(c_hbm.at[:, own, :], c2, sems.at[4]),
        pltpu.make_async_copy(y_hbm.at[:, own, :], y2, sems.at[5]),
    ]
    for copy in copies + ahead:
        copy.start()
    cost[...] = cost_in[...]
    for copy in copies:
        copy.wait()

    def anchor_of(s):
        node = sec[s] % BRANCH
        return table[((node // SHARES) ^ quarter) * SHARES + node % SHARES]

    build_target(target, anchor_of, c_v, y_v)

    def after(cols, total):
        own = sol[:, :, cols]
        flat = own.reshape(scenarios * length, own.shape[2]).astype(BF16)
        sums = jnp.dot(pick[...], flat, preferred_element_type=F32).reshape(BRANCH, length, own.shape[2])
        keep[:, :, cols] = sums[:HALF]
        send[:, :, cols] = sums[HALF:].astype(BF16)

    multiply(target, inv_v, sol, c_v, cost, lambda j: None, None, after)
    for copy in ahead:
        copy.wait()


def second_kernel(
    w, w_row, low_row, p0, p1, p2, p3, c_v, y_v, inv_v, cost_in, a1, mass,
    sol, eta, sums, target, table, cost, sems,
):
    _, length, columns = sol.shape
    share = columns // 4
    quarter = quarter_of()
    copies = [
        pltpu.make_async_copy(
            part.at[0], table.at[:, pl.ds(pl.multiple_of((quarter ^ k) * share, share), share)], sems.at[k]
        )
        for k, part in enumerate((p0, p1, p2, p3))
    ]
    for copy in copies:
        copy.start()
    cost[...] = cost_in[...]
    sums[:, :columns] = a1[...].astype(BF16)
    for copy in copies:
        copy.wait()
    build_target(target, lambda s: table[...], c_v, y_v)

    def after(cols, total):
        sums[:, columns + cols.start : columns + cols.stop] = total.astype(BF16)

    multiply(target, inv_v, sol, c_v, cost, lambda j: None, w, after)
    lanes = jnp.sum(cost[...], axis=1)
    scen_cost = jnp.sum(lanes.T, axis=0, keepdims=True) / (3 * length * columns)
    p = w_row[...].astype(F32)
    low = low_row[...]
    high = low + CVAR_WEIGHT / ((1.0 - CVAR_LEVEL) * PENALTY)
    level = jnp.minimum(jnp.maximum(scen_cost, low), high)
    eta[...] = level
    total = jnp.sum(p * level, axis=1, keepdims=True)
    whole = jnp.sum(p, axis=1, keepdims=True)
    row = lax.broadcasted_iota(jnp.int32, (length, LANES), 0)
    scal = jnp.where(row == 0, total, jnp.where(row == 1, whole, jnp.where(row == 2, mass[...], 0.0)))
    sums[:, 2 * columns :] = packed(scal)


def chip_sum_kernel(keep, got, s_own, s_got, total, send, sums):
    wide = sums.shape[1] - 3 * LANES
    value = keep[...] + got[...].astype(F32)
    total[...] = value
    send[...] = value.astype(BF16)
    sums[:, :wide] = (s_own[:, :wide].astype(F32) + s_got[:, :wide].astype(F32)).astype(BF16)
    sums[:, wide:] = packed(unpacked(s_own[:, wide:]) + unpacked(s_got[:, wide:]))


def node_sum_kernel(s_own, s_got, sums, a2, scal):
    columns = a2.shape[1]
    sums[:, :columns] = (s_own[:, :columns].astype(F32) + s_got[:, :columns].astype(F32)).astype(BF16)
    a2[...] = s_own[:, columns : 2 * columns].astype(F32) + s_got[:, columns : 2 * columns].astype(F32)
    value = unpacked(s_own[:, 2 * columns :]) + unpacked(s_got[:, 2 * columns :])
    scal[...] = value
    sums[:, columns:] = packed(value)


def far_sum_kernel(s_own, s_got, sums):
    columns = sums.shape[1] - 3 * LANES
    sums[:, :columns] = (s_own[:, :columns].astype(F32) + s_got[:, :columns].astype(F32)).astype(BF16)
    sums[:, columns:] = packed(unpacked(s_own[:, columns:]) + unpacked(s_got[:, columns:]))


def third_avg_kernel(total, got, scal, avg, send, third_avg, sem):
    quarter = quarter_of()
    for k in range(HALF):
        node = ((k // SHARES) * 2 + quarter % 2) * SHARES + k % SHARES
        value = (total[k] + got[k].astype(F32)) / node_mass(scal, node)
        avg[k] = value
        send[k] = value.astype(BF16)
    copy = pltpu.make_async_copy(avg.at[pl.ds((quarter // 2) * SHARES, SHARES)], third_avg, sem)
    copy.start()
    copy.wait()


def write_duals(sol, y_v, avg_of, out, buf, sems, section):
    scenarios, length, _ = sol.shape
    group = scenarios // 4

    def copy(g):
        own = pl.ds(g * group, group)
        return pltpu.make_async_copy(
            buf.at[own], out.at[own, pl.ds(section * length, length), :], sems.at[g]
        )

    for g in range(4):

        def step(i, carry):
            s = g * group + i
            buf[s] = (y_v[s].astype(F32) + PENALTY * (sol[s] - avg_of(s))).astype(BF16)
            return carry

        lax.fori_loop(0, group, step, 0, unroll=4)
        copy(g).start()
    return [copy(g) for g in range(4)]


def second_duals_kernel(sol, y_v, a2, scal, out, second_avg, buf, full, sems, sem):
    _, columns = full.shape
    quarter = quarter_of()
    share = columns // 4
    full[...] = a2[...] / jnp.sum(scal[2:3, :], axis=1, keepdims=True)
    own = pl.ds(pl.multiple_of(quarter * share, share), share)
    copy = pltpu.make_async_copy(full.at[:, own], second_avg.at[0], sem)
    copy.start()
    for other in write_duals(sol, y_v, lambda s: full[...], out, buf, sems, 1):
        other.wait()
    copy.wait()


def third_duals_kernel(sec, sol, y_v, avg, got, prior, out, buf, table, sems):
    quarter = quarter_of()
    table[:HALF] = avg[...]
    table[HALF:] = got[...].astype(F32)
    for copy in write_duals(
        sol, y_v, lambda s: table[place_of(sec[s] % BRANCH, quarter)], out, buf, sems, 2
    ):
        copy.wait()


def last_kernel(
    sol, y_v, s_own, s_got, eta, duals_row, prior, out, first_avg, eta_avg, eta_duals, buf, full, row, sems, sems2
):
    columns = full.shape[1]
    scal = unpacked(s_own[:, columns:]) + unpacked(s_got[:, columns:])
    total, mass = scal[0:1, 0:1], scal[1:2, 0:1]
    full[...] = (s_own[:, :columns].astype(F32) + s_got[:, :columns].astype(F32)) / mass
    level = total / mass
    row[...] = duals_row[...] + PENALTY * (eta[...] - level)
    copies = [
        pltpu.make_async_copy(full, first_avg, sems2.at[0]),
        pltpu.make_async_copy(row, eta_duals, sems2.at[1]),
    ]
    for copy in copies:
        copy.start()
    copies += write_duals(sol, y_v, lambda s: full[...], out, buf, sems, 0)
    eta_avg[0] = jnp.sum(level)
    for copy in copies:
        copy.wait()


def step(
    unit_costs,
    hour_duals,
    inverse,
    weights,
    section_three,
    prev_first,
    prev_second,
    prev_third,
    eta_mean,
    eta_duals,
):
    scenarios, hours, columns = unit_costs.shape
    length = hours // 3
    nodes = lax.axis_size("node")
    dma = pltpu.SemaphoreType.DMA
    shape = jax.ShapeDtypeStruct
    block = (scenarios, length, columns)
    rows = scenarios * length
    w_row = weights.reshape(1, scenarios)
    duals_row = eta_duals.reshape(1, scenarios)
    costs, duals, matrix = in_hbm(unit_costs), in_hbm(hour_duals), in_hbm(inverse)

    y_third, y_second = partner((prev_third, prev_second), 2)

    w, sec, y1, c3, y3, inv_v, sol1, a1, mass, pick, cost = call(
        first_kernel,
        32,
        in_specs=[HBM] * 6,
        out_specs=[SMEM, SMEM] + [VMEM] * 9,
        out_shape=[
            pltpu.SMEM((scenarios,), jnp.int32),
            pltpu.SMEM((scenarios,), jnp.int32),
            *[pltpu.VMEM(block, BF16)] * 3,
            pltpu.VMEM(inverse.shape, BF16),
            pltpu.VMEM(block, F32),
            pltpu.VMEM((length, columns), F32),
            pltpu.VMEM((1, LANES), F32),
            pltpu.VMEM((BRANCH * length, rows), BF16),
            pltpu.VMEM((scenarios, length, LANES), F32),
        ],
        scratch_shapes=[
            pltpu.VMEM(block, BF16),
            pltpu.VMEM((length, columns), BF16),
            pltpu.VMEM((rows, columns), BF16),
            dma((9 + CHUNKS,)),
        ],
    )(in_hbm(weights), in_hbm(section_three), in_hbm(prev_first), costs, duals, matrix)

    level_mean, y_third = lax.optimization_barrier((eta_mean, y_third))
    low_row = level_mean[:, None] - (CVAR_WEIGHT + duals_row) / PENALTY
    core_third, diag_third = partner((prev_third, y_third), 1)
    core_second, diag_second = partner((prev_second, y_second), 1)

    c2, y2, sol3, cost, keep, send = call(
        third_kernel,
        30,
        in_specs=[SMEM, ANY, ANY, ANY, ANY, HBM, HBM] + [VMEM] * 5,
        out_specs=[VMEM] * 6,
        out_shape=[
            pltpu.VMEM(block, BF16),
            pltpu.VMEM(block, BF16),
            pltpu.VMEM(block, F32),
            pltpu.VMEM((scenarios, length, LANES), F32),
            pltpu.VMEM((HALF, length, columns), F32),
            pltpu.VMEM((HALF, length, columns), BF16),
        ],
        scratch_shapes=[
            pltpu.VMEM((rows, columns), BF16),
            pltpu.VMEM((BRANCH, length, columns), BF16),
            dma((6,)),
        ],
    )(sec, prev_third, core_third, y_third, diag_third, costs, duals, c3, y3, inv_v, pick, cost)

    chip_got = partner(send, 1)

    sol2, eta, sums = call(
        second_kernel,
        30,
        in_specs=[SMEM, VMEM, VMEM, ANY, ANY, ANY, ANY] + [VMEM] * 6,
        out_specs=[VMEM] * 3,
        out_shape=[
            pltpu.VMEM(block, F32),
            pltpu.VMEM((1, scenarios), F32),
            pltpu.VMEM((length, 2 * columns + 3 * LANES), BF16),
        ],
        scratch_shapes=[
            pltpu.VMEM((rows, columns), BF16),
            pltpu.VMEM((length, columns), BF16),
            pltpu.VMEM((scenarios, length, LANES), F32),
            dma((4,)),
        ],
    )(
        w, w_row, low_row, prev_second, core_second, y_second, diag_second, c2, y2, inv_v, cost, a1, mass
    )

    core_sums = partner(sums, 1)
    chip_total, chip_send, sums = call(
        chip_sum_kernel,
        8,
        in_specs=[VMEM] * 4,
        out_specs=[VMEM] * 3,
        out_shape=[
            pltpu.VMEM((HALF, length, columns), F32),
            pltpu.VMEM((HALF, length, columns), BF16),
            pltpu.VMEM(sums.shape, BF16),
        ],
    )(keep, chip_got, sums, core_sums)
    y_sums = partner(sums, 2)
    node_got = partner(chip_send, 2)
    far_shape = pltpu.VMEM((length, columns + 3 * LANES), BF16)
    far, a2, scal = call(
        node_sum_kernel,
        8,
        in_specs=[VMEM] * 2,
        out_specs=[VMEM] * 3,
        out_shape=[far_shape, pltpu.VMEM((length, columns), F32), pltpu.VMEM((length, LANES), F32)],
    )(sums, y_sums)
    far_got = partner(far, 4)
    mask = 8
    while mask < nodes:
        far = call(far_sum_kernel, 8, in_specs=[VMEM] * 2, out_specs=VMEM, out_shape=far_shape)(far, far_got)
        far_got = partner(far, mask)
        mask *= 2

    buf = pltpu.VMEM(block, BF16)
    duals_shape = shape(hour_duals.shape, BF16)
    out, second_avg = call(
        second_duals_kernel,
        8,
        in_specs=[VMEM] * 4,
        out_specs=[HBM, HBM],
        out_shape=[duals_shape, shape((1, length, columns // 4), F32)],
        scratch_shapes=[buf, pltpu.VMEM((length, columns), F32), dma((4,)), dma],
    )(sol2, y2, a2, scal)

    avg, avg_send, third_avg = call(
        third_avg_kernel,
        8,
        in_specs=[VMEM] * 3,
        out_specs=[VMEM, VMEM, HBM],
        out_shape=[
            pltpu.VMEM((HALF, length, columns), F32),
            pltpu.VMEM((HALF, length, columns), BF16),
            shape((SHARES, length, columns), F32),
        ],
        scratch_shapes=[dma],
    )(chip_total, node_got, scal)
    avg_got = partner(avg_send, 1)
    out = call(
        third_duals_kernel,
        8,
        in_specs=[SMEM] + [VMEM] * 4 + [HBM],
        out_specs=HBM,
        out_shape=duals_shape,
        scratch_shapes=[buf, pltpu.VMEM((BRANCH, length, columns), F32), dma((4,))],
        input_output_aliases={5: 0},
    )(sec, sol3, y3, avg, avg_got, out)
    out, first_avg, eta_avg, eta_duals_new = call(
        last_kernel,
        8,
        in_specs=[VMEM] * 6 + [HBM],
        out_specs=[HBM, HBM, SMEM, HBM],
        out_shape=[
            duals_shape,
            shape((length, columns), F32),
            shape((1,), F32),
            shape((1, scenarios), F32),
        ],
        scratch_shapes=[
            buf,
            pltpu.VMEM((length, columns), F32),
            pltpu.VMEM((1, scenarios), F32),
            dma((4,)),
            dma((2,)),
        ],
        input_output_aliases={6: 0},
    )(sol1, y1, far, far_got, eta, duals_row, out)
    return out, first_avg, second_avg, third_avg, eta_avg, eta_duals_new.reshape(scenarios)


def solution(mesh):
    row = P(("groups", "node"))
    in_specs = (row, row, P(), row, row, P("groups"), row, row, P("groups"), row)
    out_specs = (row, P("groups"), row, row, P("groups"), row)
    return jax.shard_map(step, mesh=mesh, in_specs=in_specs, out_specs=out_specs, check_vma=False)
```

time: 62.1 us -> 47.1 us (0.76)
  waiting for transfers between devices: 21.3 us -> 15.1 us
  Pallas kernels: 22.6 us -> 17.8 us
  starting transfers between devices: 16.5 us -> 12.5 us
    ppermute x21 -> x13, waiting for transfers between devices: 21.3 us -> 15.1 us  [partner(): return lax.ppermute(value, 'node', pairs)]
    ppermute x21 -> x13, starting transfers between devices: 16.5 us -> 12.5 us  [partner(): return lax.ppermute(value, 'node', pairs)]
    pallas_call x8, Pallas kernels: 17.7 us -> 13.8 us  [the longest x1 5.5 us: step(): call(first_kernel, 32, in_specs=[HBM] * 6, out_specs=[SMEM, SMEM] + [VMEM...]
    pallas_call x1, Pallas kernels: 4.76 us -> 3.9 us  [step(): call(third_kernel, 30, in_specs=[SMEM, ANY, ANY, ANY, ANY, HBM, HBM] + [V...]
  transfers between devices with their start and end apart: 21 -> 13, of which waited for: 8 -> 4; matrix products, arithmetic and copies ran while one was open for 0% -> 0% of each run, Pallas kernels for 26% -> 32%
where the time goes in v3:
time: 47.1 us; the launch traced here: 46.9 us
  Pallas kernels  17.8 us (38%)
  waiting for transfers between devices  15.1 us (32%)
  starting transfers between devices  12.5 us (27%)
  between operations  1.44 us (3%)
    ppermute x13, waiting for transfers between devices, partner(): return lax.ppermute(value, 'node', pairs)  15.1 us
    ppermute x13, starting transfers between devices, partner(): return lax.ppermute(value, 'node', pairs)  12.5 us
    pallas_call x1, Pallas kernels, step(): call(first_kernel, 32, in_specs=[HBM] * 6, out_specs=[SMEM, SMEM] + [VMEM...  5.5 us
    pallas_call x1, Pallas kernels, step(): call(third_kernel, 30, in_specs=[SMEM, ANY, ANY, ANY, ANY, HBM, HBM] + [V...  3.9 us
    pallas_call x1, Pallas kernels, step(): call(second_kernel, 30, in_specs=[SMEM, VMEM, VMEM, ANY, ANY, ANY, ANY] +...  3.16 us
    pallas_call x1, Pallas kernels, step(): call(last_kernel, 8, in_specs=[VMEM] * 6 + [HBM], out_specs=[HBM, HBM, SM...  1.7 us
    pallas_call x1, Pallas kernels, step(): call(third_duals_kernel, 8, in_specs=[SMEM] + [VMEM] * 4 + [HBM], out_spe...  1.4 us
    pallas_call x1, Pallas kernels, step(): call(second_duals_kernel, 8, in_specs=[VMEM] * 4, out_specs=[HBM, HBM], o...  1.17 us
  transfers between devices with their start and end apart: 13, of which 4 were waited for; matrix products, arithmetic and copies ran while one was open for 0% of the time, Pallas kernels for 32%

profile of v3, /device:TPU:0, one launch (start us, length us, event | category | flops | bytes accessed | tf_op | source)
XLA Modules:
  0.0 46.9 jit_solution(2448842608770429702)
XLA Ops:
  0.6 3.1 %collective-permute-start.1 = (bf16[4,8,2048]{2,1,0:T(8,128)(2,1)}, bf16[4,8,2048]{2,1,0:T(8,128)(2,1)S(1)}, u32[]{:S(2)}, u32[]{:S(2)}) collective-permute-start(bf16[4,8,2048]{2,1,0:T(8,128)(2,1)} %p0.2), channel_id=1, source_target_pairs={{0,2},{1,3},{2,0},{3,1},{4,6},{5,7},{6,4},{7,5},{8,10},{9,11},{10,... | collective-permute-start | bytes 393224 | tf_op jit(solution)/shard_map/ppermute | solution.py:27
  3.7 0.0 collective-permute-start
  3.7 3.7 %collective-permute-done.1.p2 = bf16[4,8,2048]{2,1,0:T(8,128)(2,1)S(1)} collective-permute-done((bf16[4,8,2048]{2,1,0:T(8,128)(2,1)}, bf16[4,8,2048]{2,1,0:T(8,128)(2,1)S(1)}, u32[]{:S(2)}, u32[]{:S(2)}) %collective-permute-start.1) | collective-permute-done | bytes 131104 | tf_op jit(solution)/shard_map/ppermute | solution.py:27
  7.4 0.0 collective-permute-start.2
  7.4 1.7 %collective-permute-start.5 = (bf16[1,8,512]{2,1,0:T(8,128)(2,1)}, bf16[1,8,512]{2,1,0:T(8,128)(2,1)S(1)}, u32[]{:S(2)}, u32[]{:S(2)}) collective-permute-start(bf16[1,8,512]{2,1,0:T(8,128)(2,1)} %p0.3), channel_id=1, source_target_pairs={{0,2},{1,3},{2,0},{3,1},{4,6},{5,7},{6,4},{7,5},{8,10},{9,11},{10,... | collective-permute-start | bytes 24584 | tf_op jit(solution)/shard_map/ppermute | solution.py:27
  9.1 0.2 collective-permute-start.4
  10.0 0.0 copy-start
  10.0 5.5 %shard_map.145 = (s32[32]{0:T(128)S(4)}, s32[32]{0:T(128)S(4)}, bf16[32,8,2048]{2,1,0:T(8,128)(2,1)S(1)}, bf16[32,8,2048]{2,1,0:T(8,128)(2,1)S(1)}, bf16[32,8,20...) custom-call(s32[32]{0:T(128)} %w_hbm.1, ...), custom_call_target="tpu_custom_call" | custom-call | tf_op jit(solution)/shard_map/pallas_call | solution.py:384
  15.5 0.0 collective-permute-done.5.p2
  15.6 0.3 collective-permute-start.6
  15.9 0.0 collective-permute-done.p1
  15.9 0.0 collective-permute-done.2.p3
  15.9 0.0 copy-done
  15.9 0.0 copy-start.3
  15.9 0.0 copy-start.1
  15.9 0.0 copy-start.2
  16.0 3.9 %shard_map.146 = (bf16[32,8,2048]{2,1,0:T(8,128)(2,1)S(1)}, bf16[32,8,2048]{2,1,0:T(8,128)(2,1)S(1)}, f32[32,8,2048]{2,1,0:T(8,128)S(1)}, f32[32,8,128]{2,1,0:T(...) custom-call(s32[32]{0:T(128)S(4)} %get-tuple-element.45.sec, bf16[4,8,2048]{2,1,0:T(8,128)(2,1)S(1)} %copy-done, ...), custom_call_target="tpu_custom_call" | custom-call | tf_op jit(solution)/shard_map/pallas_call | solution.py:413
  19.9 0.3 collective-permute-start.3
  20.2 0.0 copy-done.3
  20.2 0.0 collective-permute-done.4.p1
  20.2 0.0 collective-permute-done.6.p3
  20.2 0.0 copy-done.1
  20.2 0.0 copy-done.2
  20.2 3.2 %shard_map.147 = (f32[32,8,2048]{2,1,0:T(8,128)S(1)}, f32[1,32]{1,0:T(1,128)S(1)}, bf16[8,4480]{1,0:T(8,128)(2,1)S(1)}) custom-call(s32[32]{0:T(128)S(4)} %get-tuple-element.54.w, s32[1,32]{1,0:T(1,128)S(1)} %bitcast.7, f32[1,32]{1,0:T(1,128)S(1)} %subtract_bitcast_fusion.low_row, bf16[1,8,512]{2,1,0:T(8,128)(2,1)S(1)} %copy-done.1, ...), custom_call_target="tpu_custom_call" | custom-call | tf_op jit(solution)/shard_map/pallas_call | solution.py:435
  23.4 0.3 collective-permute-start.7
  23.7 1.0 %collective-permute-done.7.s_got = bf16[8,4480]{1,0:T(8,128)(2,1)S(1)} collective-permute-done((bf16[8,4480]{1,0:T(8,128)(2,1)S(1)}, bf16[8,4480]{1,0:T(8,128)(2,1)S(1)}, u32[]{:S(2)}, u32[]{:S(2)}) %collective-permute-start.7) | collective-permute-done | bytes 71712 | tf_op jit(solution)/shard_map/ppermute | solution.py:27
  24.7 0.0 collective-permute-done.3.got
  24.7 0.1 shard_map.148
  24.8 0.3 collective-permute-start.11
  25.1 1.7 %collective-permute-start.8 = (bf16[8,4480]{1,0:T(8,128)(2,1)S(1)}, bf16[8,4480]{1,0:T(8,128)(2,1)S(1)}, u32[]{:S(2)}, u32[]{:S(2)}) collective-permute-start(bf16[8,4480]{1,0:T(8,128)(2,1)S(1)} %get-tuple-element.62.s_own), channel_id=1, source_target_pairs={{0,2},{1,3},{2,0},{3,1},{4,6},{5,7},{6,4},{7,5},{8,10},{9,11},{10,... | collective-permute-start | bytes 215048 | tf_op jit(solution)/shard_map/ppermute | solution.py:27
  26.9 8.0 %collective-permute-done.8.s_got = bf16[8,4480]{1,0:T(8,128)(2,1)S(1)} collective-permute-done((bf16[8,4480]{1,0:T(8,128)(2,1)S(1)}, bf16[8,4480]{1,0:T(8,128)(2,1)S(1)}, u32[]{:S(2)}, u32[]{:S(2)}) %collective-permute-start.8) | collective-permute-done | bytes 71712 | tf_op jit(solution)/shard_map/ppermute | solution.py:27
  34.9 0.0 collective-permute-done.11.got
  34.9 0.9 %shard_map.151 = (f32[8,8,2048]{2,1,0:T(8,128)S(1)}, bf16[8,8,2048]{2,1,0:T(8,128)(2,1)S(1)}, f32[4,8,2048]{2,1,0:T(8,128)}) custom-call(f32[8,8,2048]{2,1,0:T(8,128)S(1)} %get-tuple-element.66.total, bf16[8,8,2048]{2,1,0:T(8,128)(2,1)S(1)} %collective-permute-done.11.got, f32[8,128]{1,0:T(8,128)S(1)} %get-tuple-element.68.scal), custom_call_target="tpu_custom_call" | custom-call | tf_op jit(solution)/shard_map/pallas_call | solution.py:495
  35.8 0.1 collective-permute-start.12
  35.9 1.6 %collective-permute-start.9 = (bf16[8,2432]{1,0:T(8,128)(2,1)S(1)}, bf16[8,2432]{1,0:T(8,128)(2,1)S(1)}, u32[]{:S(2)}, u32[]{:S(2)}) collective-permute-start(bf16[8,2432]{1,0:T(8,128)(2,1)S(1)} %get-tuple-element.63.s_own), channel_id=1, source_target_pairs={{0,4},{1,5},{2,6},{3,7},{4,0},{5,1},{6,2},{7,3},{8,12},{9,13},{10,... | collective-permute-start | bytes 116744 | tf_op jit(solution)/shard_map/ppermute | solution.py:27
  37.5 2.4 %collective-permute-done.9.s_got = bf16[8,2432]{1,0:T(8,128)(2,1)S(1)} collective-permute-done((bf16[8,2432]{1,0:T(8,128)(2,1)S(1)}, bf16[8,2432]{1,0:T(8,128)(2,1)S(1)}, u32[]{:S(2)}, u32[]{:S(2)}) %collective-permute-start.9) | collective-permute-done | bytes 38944 | tf_op jit(solution)/shard_map/ppermute | solution.py:27
  39.9 2.6 %collective-permute-start.10 = (bf16[8,2432]{1,0:T(8,128)(2,1)S(1)}, bf16[8,2432]{1,0:T(8,128)(2,1)S(1)}, u32[]{:S(2)}, u32[]{:S(2)}) collective-permute-start(bf16[8,2432]{1,0:T(8,128)(2,1)S(1)} %shard_map.150.s_own), channel_id=1, source_target_pairs={{0,8},{1,9},{2,10},{3,11},{4,12},{5,13},{6,14},{7,15},{8,0},{9,1},... | collective-permute-start | bytes 116744 | tf_op jit(solution)/shard_map/ppermute | solution.py:27
  42.6 1.2 %shard_map.152 = (bf16[32,24,2048]{2,1,0:T(8,128)(2,1)}, f32[1,8,512]{2,1,0:T(8,128)}) custom-call(f32[32,8,2048]{2,1,0:T(8,128)S(1)} %get-tuple-element.71.sol, bf16[32,8,2048]{2,1,0:T(8,128)(2,1)S(1)} %get-tuple-element.57.y_v, f32[8,2048]{1,0:T(8,128)S(1)} %get-tuple-element.72.a2, f32[8,128]{1,0:T(8,128)S(1)} %get-tuple-element.68.scal), custom_call_target="tpu_custom_call" | custom-call | tf_op jit(solution)/shard_map/pallas_call | solution.py:486
  43.8 0.0 collective-permute-done.12.got
  43.8 1.4 %shard_map.153.prior = bf16[32,24,2048]{2,1,0:T(8,128)(2,1)} custom-call(s32[32]{0:T(128)S(4)} %get-tuple-element.45.sec, f32[32,8,2048]{2,1,0:T(8,128)S(1)} %get-tuple-element.65.sol, bf16[32,8,2048]{2,1,0:T(8,128)(2,1)S(1)} %get-tuple-element.48.y_v, f32[8,8,2048]{2,1,0:T(8,128)S(1)} %get-tuple-element.69.avg, ...), custom_call_target="tpu_custom_call", output_to_operand_aliasing={{}: (5, {})} | custom-call | tf_op jit(solution)/shard_map/pallas_call | solution.py:508
  45.2 0.0 collective-permute-done.10.s_got
  45.2 1.7 %shard_map.154 = (bf16[32,24,2048]{2,1,0:T(8,128)(2,1)}, f32[8,2048]{1,0:T(8,128)}, f32[1]{0:T(128)}, f32[1,32]{1,0:T(1,128)}) custom-call(f32[32,8,2048]{2,1,0:T(8,128)S(1)} %get-tuple-element.43.sol, bf16[32,8,2048]{2,1,0:T(8,128)(2,1)S(1)} %get-tuple-element.44.y_v, bf16[8,2432]{1,0:T(8,128)(2,1)S(1)} %shard_map.150.s_own, ...), custom_call_target="tpu_custom_call", output_to_operand_aliasing={{0}: (6, {})} | custom-call | tf_op jit(solution)/shard_map/pallas_call | solution.py:517
  (3 shorter events, 0.1 us)
Async XLA Ops:
  0.6 6.8 %collective-permute-start.1 = (bf16[4,8,2048]{2,1,0:T(8,128)(2,1)}, bf16[4,8,2048]{2,1,0:T(8,128)(2,1)S(1)}, u32[]{:S(2)}, u32[]{:S(2)}) collective-permute-start(bf16[4,8,2048]{2,1,0:T(8,128)(2,1)} %p0.2), channel_id=1, source_target_pairs={{0,2},{1,3},{2,0},{3,1},{4,6},{5,7},{6,4},{7,5},{8,10},{9,11},{10,... | collective-permute-start | bytes 393224 | tf_op jit(solution)/shard_map/ppermute | solution.py:27
  3.7 12.2 %collective-permute-start = (bf16[4,8,2048]{2,1,0:T(8,128)(2,1)}, bf16[4,8,2048]{2,1,0:T(8,128)(2,1)S(1)}, u32[]{:S(2)}, u32[]{:S(2)}) collective-permute-start(bf16[4,8,2048]{2,1,0:T(8,128)(2,1)} %p0.2), channel_id=1, source_target_pairs={{0,1},{1,0},{2,3},{3,2},{4,5},{5,4},{6,7},{7,6},{8,9},{9,8},{10,11... | collective-permute-start | bytes 393224 | tf_op jit(solution)/shard_map/ppermute | solution.py:27
  7.4 8.5 %collective-permute-start.2 = (bf16[4,8,2048]{2,1,0:T(8,128)(2,1)S(1)}, bf16[4,8,2048]{2,1,0:T(8,128)(2,1)S(1)}, u32[]{:S(2)}, u32[]{:S(2)}) collective-permute-start(bf16[4,8,2048]{2,1,0:T(8,128)(2,1)S(1)} %collective-permute-done.1.p2), channel_id=1, source_target_pairs={{0,1},{1,0},{2,3},{3,2},{4,5},{5,4},{6,7},{7,6},{8,9},{9,8},{10,11... | collective-permute-start | bytes 393224 | tf_op jit(solution)/shard_map/ppermute | solution.py:27
  7.4 8.1 %collective-permute-start.5 = (bf16[1,8,512]{2,1,0:T(8,128)(2,1)}, bf16[1,8,512]{2,1,0:T(8,128)(2,1)S(1)}, u32[]{:S(2)}, u32[]{:S(2)}) collective-permute-start(bf16[1,8,512]{2,1,0:T(8,128)(2,1)} %p0.3), channel_id=1, source_target_pairs={{0,2},{1,3},{2,0},{3,1},{4,6},{5,7},{6,4},{7,5},{8,10},{9,11},{10,... | collective-permute-start | bytes 24584 | tf_op jit(solution)/shard_map/ppermute | solution.py:27
  9.1 11.0 %collective-permute-start.4 = (bf16[1,8,512]{2,1,0:T(8,128)(2,1)}, bf16[1,8,512]{2,1,0:T(8,128)(2,1)S(1)}, u32[]{:S(2)}, u32[]{:S(2)}) collective-permute-start(bf16[1,8,512]{2,1,0:T(8,128)(2,1)} %p0.3), channel_id=1, source_target_pairs={{0,1},{1,0},{2,3},{3,2},{4,5},{5,4},{6,7},{7,6},{8,9},{9,8},{10,11... | collective-permute-start | bytes 24584 | tf_op jit(solution)/shard_map/ppermute | solution.py:27
  10.0 5.9 %copy-start = (bf16[4,8,2048]{2,1,0:T(8,128)(2,1)S(1)}, bf16[4,8,2048]{2,1,0:T(8,128)(2,1)}, u32[]{:S(2)}) copy-start(bf16[4,8,2048]{2,1,0:T(8,128)(2,1)} %p0.2) | copy-start | bytes 393220
  15.6 4.6 %collective-permute-start.6 = (bf16[1,8,512]{2,1,0:T(8,128)(2,1)S(1)}, bf16[1,8,512]{2,1,0:T(8,128)(2,1)S(1)}, u32[]{:S(2)}, u32[]{:S(2)}) collective-permute-start(bf16[1,8,512]{2,1,0:T(8,128)(2,1)S(1)} %collective-permute-done.5.p2), channel_id=1, source_target_pairs={{0,1},{1,0},{2,3},{3,2},{4,5},{5,4},{6,7},{7,6},{8,9},{9,8},{10,11... | collective-permute-start | bytes 24584 | tf_op jit(solution)/shard_map/ppermute | solution.py:27
  15.9 4.2 %copy-start.3 = (f32[32]{0:T(128)S(1)}, f32[32]{0:T(128)}, u32[]{:S(2)}) copy-start(f32[32]{0:T(128)} %param.19) | copy-start | bytes 388
  15.9 4.3 %copy-start.1 = (bf16[1,8,512]{2,1,0:T(8,128)(2,1)S(1)}, bf16[1,8,512]{2,1,0:T(8,128)(2,1)}, u32[]{:S(2)}) copy-start(bf16[1,8,512]{2,1,0:T(8,128)(2,1)} %p0.3) | copy-start | bytes 24580
  15.9 4.3 %copy-start.2 = (s32[32]{0:T(128)S(1)}, s32[32]{0:T(128)}, u32[]{:S(2)}) copy-start(s32[32]{0:T(128)} %w_hbm.1) | copy-start | bytes 388
  19.9 4.8 %collective-permute-start.3 = (bf16[8,8,2048]{2,1,0:T(8,128)(2,1)S(1)}, bf16[8,8,2048]{2,1,0:T(8,128)(2,1)S(1)}, u32[]{:S(2)}, u32[]{:S(2)}) collective-permute-start(bf16[8,8,2048]{2,1,0:T(8,128)(2,1)S(1)} %get-tuple-element.53), channel_id=1, source_target_pairs={{0,1},{1,0},{2,3},{3,2},{4,5},{5,4},{6,7},{7,6},{8,9},{9,8},{10,11... | collective-permute-start | bytes 786440 | tf_op jit(solution)/shard_map/ppermute | solution.py:27
  23.4 1.3 %collective-permute-start.7 = (bf16[8,4480]{1,0:T(8,128)(2,1)S(1)}, bf16[8,4480]{1,0:T(8,128)(2,1)S(1)}, u32[]{:S(2)}, u32[]{:S(2)}) collective-permute-start(bf16[8,4480]{1,0:T(8,128)(2,1)S(1)} %get-tuple-element.61.s_own), channel_id=1, source_target_pairs={{0,1},{1,0},{2,3},{3,2},{4,5},{5,4},{6,7},{7,6},{8,9},{9,8},{10,11... | collective-permute-start | bytes 215048 | tf_op jit(solution)/shard_map/ppermute | solution.py:27
  24.8 10.1 %collective-permute-start.11 = (bf16[8,8,2048]{2,1,0:T(8,128)(2,1)S(1)}, bf16[8,8,2048]{2,1,0:T(8,128)(2,1)S(1)}, u32[]{:S(2)}, u32[]{:S(2)}) collective-permute-start(bf16[8,8,2048]{2,1,0:T(8,128)(2,1)S(1)} %get-tuple-element.67), channel_id=1, source_target_pairs={{0,2},{1,3},{2,0},{3,1},{4,6},{5,7},{6,4},{7,5},{8,10},{9,11},{10,... | collective-permute-start | bytes 786440 | tf_op jit(solution)/shard_map/ppermute | solution.py:27
  25.1 9.7 %collective-permute-start.8 = (bf16[8,4480]{1,0:T(8,128)(2,1)S(1)}, bf16[8,4480]{1,0:T(8,128)(2,1)S(1)}, u32[]{:S(2)}, u32[]{:S(2)}) collective-permute-start(bf16[8,4480]{1,0:T(8,128)(2,1)S(1)} %get-tuple-element.62.s_own), channel_id=1, source_target_pairs={{0,2},{1,3},{2,0},{3,1},{4,6},{5,7},{6,4},{7,5},{8,10},{9,11},{10,... | collective-permute-start | bytes 215048 | tf_op jit(solution)/shard_map/ppermute | solution.py:27
  35.8 8.0 %collective-permute-start.12 = (bf16[8,8,2048]{2,1,0:T(8,128)(2,1)S(1)}, bf16[8,8,2048]{2,1,0:T(8,128)(2,1)S(1)}, u32[]{:S(2)}, u32[]{:S(2)}) collective-permute-start(bf16[8,8,2048]{2,1,0:T(8,128)(2,1)S(1)} %get-tuple-element.70), channel_id=1, source_target_pairs={{0,1},{1,0},{2,3},{3,2},{4,5},{5,4},{6,7},{7,6},{8,9},{9,8},{10,11... | collective-permute-start | bytes 786440 | tf_op jit(solution)/shard_map/ppermute | solution.py:27
  35.9 4.0 %collective-permute-start.9 = (bf16[8,2432]{1,0:T(8,128)(2,1)S(1)}, bf16[8,2432]{1,0:T(8,128)(2,1)S(1)}, u32[]{:S(2)}, u32[]{:S(2)}) collective-permute-start(bf16[8,2432]{1,0:T(8,128)(2,1)S(1)} %get-tuple-element.63.s_own), channel_id=1, source_target_pairs={{0,4},{1,5},{2,6},{3,7},{4,0},{5,1},{6,2},{7,3},{8,12},{9,13},{10,... | collective-permute-start | bytes 116744 | tf_op jit(solution)/shard_map/ppermute | solution.py:27
  39.9 5.3 %collective-permute-start.10 = (bf16[8,2432]{1,0:T(8,128)(2,1)S(1)}, bf16[8,2432]{1,0:T(8,128)(2,1)S(1)}, u32[]{:S(2)}, u32[]{:S(2)}) collective-permute-start(bf16[8,2432]{1,0:T(8,128)(2,1)S(1)} %shard_map.150.s_own), channel_id=1, source_target_pairs={{0,8},{1,9},{2,10},{3,11},{4,12},{5,13},{6,14},{7,15},{8,0},{9,1},... | collective-permute-start | bytes 116744 | tf_op jit(solution)/shard_map/ppermute | solution.py:27

commit v4 on v3

v4 whole, which is shorter than its diff:
```python
import jax
import jax.numpy as jnp
from jax import lax
from jax.experimental import pallas as pl
from jax.experimental.pallas import tpu as pltpu
from jax.sharding import PartitionSpec as P

BRANCH = 16
SHARES = BRANCH // 4
HALF = BRANCH // 2
PENALTY = 1.0
CVAR_WEIGHT = 0.25
CVAR_LEVEL = 0.75
CHUNKS = 4
LANES = 128
F32 = jnp.float32
BF16 = jnp.bfloat16

ANY = pl.BlockSpec(memory_space=pl.ANY)
HBM = pl.BlockSpec(memory_space=pltpu.HBM)
SMEM = pl.BlockSpec(memory_space=pltpu.SMEM)
VMEM = pl.BlockSpec(memory_space=pltpu.VMEM)


def partner(value, mask):
    pairs = [(source, source ^ mask) for source in range(lax.axis_size("node"))]
    return lax.ppermute(value, "node", pairs)


def in_hbm(value):
    return pltpu.with_memory_space_constraint(value, pltpu.HBM)


def call(kernel, mib, **kwargs):
    return pl.pallas_call(kernel, compiler_params=pltpu.CompilerParams(vmem_limit_bytes=mib << 20), **kwargs)


def quarter_of():
    return lax.axis_index("node") % 4


def place_of(node, quarter):
    half = (node // SHARES) % 2
    return ((half ^ (quarter % 2)) * 2 + node // (2 * SHARES)) * SHARES + node % SHARES


def build_target(target, anchor_of, c_v, y_v):
    scenarios, length, _ = c_v.shape

    def step(i, carry):
        rows = []
        for k in range(2):
            s = 2 * i + k
            rows.append(PENALTY * anchor_of(s).astype(F32) - c_v[s].astype(F32) - y_v[s].astype(F32))
        block = jnp.concatenate(rows, axis=0).astype(BF16)
        target[pl.ds(pl.multiple_of(i * 2 * length, 2 * length), 2 * length), :] = block
        return carry

    lax.fori_loop(0, scenarios // 2, step, 0, unroll=2)


def multiply(target, inv_v, sol, c_v, cost, before, w, after, start=0):
    scenarios, length, columns = sol.shape
    width = inv_v.shape[1] // CHUNKS

    def product(j):
        before(j)
        sol[:, :, j * width : (j + 1) * width] = jnp.dot(
            target[...], inv_v[:, start + j * width : start + (j + 1) * width], preferred_element_type=F32
        ).reshape(scenarios, length, width)

    def finish(j):
        cols = slice(j * width, (j + 1) * width)
        total = jnp.zeros((length, width), F32)
        for s in range(scenarios):
            own = sol[s, :, cols]
            prod = c_v[s, :, start + cols.start : start + cols.stop].astype(F32) * own
            part = prod[:, :LANES]
            for k in range(1, width // LANES):
                part = part + prod[:, k * LANES : (k + 1) * LANES]
            cost[s] = cost[s] + part
            if w is not None:
                total = total + w[s].astype(F32) * own
        after(cols, total)

    count = columns // width
    for j in range(count):
        product(j)
        if j:
            finish(j - 1)
    finish(count - 1)


def first_kernel(
    w_hbm, sec_hbm, w_row_hbm, sec_row_hbm, pf_hbm, c_hbm, y_hbm, inv_hbm,
    w, sec, y1, c2, y2, c3, y3, inv_v, sol, a1, mass, pick, cost, c1, pf, w_row, sec_row, target, sems,
):
    scenarios, length, columns = sol.shape
    width = columns // CHUNKS

    def chunk(j):
        part = pl.ds(j * width, width)
        return pltpu.make_async_copy(inv_hbm.at[:, part], inv_v.at[:, part], sems.at[11 + j])

    def rows(k, c_v, y_v):
        own = pl.ds(k * length, length)
        return [
            pltpu.make_async_copy(c_hbm.at[:, own, :], c_v, sems.at[5 + 2 * k]),
            pltpu.make_async_copy(y_hbm.at[:, own, :], y_v, sems.at[6 + 2 * k]),
        ]

    small = [
        pltpu.make_async_copy(source, into, sems.at[k])
        for k, (source, into) in enumerate(
            ((w_row_hbm, w_row), (sec_row_hbm, sec_row), (w_hbm, w), (sec_hbm, sec), (pf_hbm, pf))
        )
    ]
    first = rows(0, c1, y1)
    later = rows(2, c3, y3) + rows(1, c2, y2)
    for copy in small + first + [chunk(j) for j in range(CHUNKS)] + later:
        copy.start()
    cost[...] = jnp.zeros_like(cost)
    for copy in small:
        copy.wait()

    node = sec_row[...] % BRANCH
    place = place_of(node, quarter_of())
    p = w_row[...].astype(F32)
    into_node = lax.broadcasted_iota(jnp.int32, (LANES, scenarios), 0) == node
    mass[...] = jnp.sum(jnp.where(into_node, p, 0.0).T, axis=0, keepdims=True)
    into_place = lax.broadcasted_iota(jnp.int32, (BRANCH * length, scenarios), 0) // length == place
    shape = (scenarios, scenarios * length)
    spread = lax.broadcasted_iota(jnp.int32, shape, 1) // length == lax.broadcasted_iota(jnp.int32, shape, 0)
    weight = jnp.dot(
        jnp.where(into_place, p, 0.0).astype(BF16),
        jnp.where(spread, 1.0, 0.0).astype(BF16),
        preferred_element_type=F32,
    )
    row = lax.broadcasted_iota(jnp.int32, pick.shape, 0)
    column = lax.broadcasted_iota(jnp.int32, pick.shape, 1)
    pick[...] = jnp.where(row % length == column % length, weight, 0.0).astype(BF16)

    for copy in first:
        copy.wait()
    build_target(target, lambda s: pf[...], c1, y1)

    def after(cols, total):
        a1[:, cols] = total

    multiply(target, inv_v, sol, c1, cost, lambda j: chunk(j).wait(), w, after)
    for copy in later:
        copy.wait()


def packed(value):
    high = value.astype(BF16)
    rest = value - high.astype(F32)
    middle = rest.astype(BF16)
    return jnp.concatenate((high, middle, (rest - middle.astype(F32)).astype(BF16)), axis=1)


def unpacked(tiles):
    high, middle, low = (tiles[:, k * LANES : (k + 1) * LANES].astype(F32) for k in range(3))
    return high + middle + low


def node_mass(scal, node):
    row = scal[2:3, :]
    slot = lax.broadcasted_iota(jnp.int32, row.shape, 1)
    return jnp.sum(jnp.where(slot == node, row, 0.0), axis=1, keepdims=True)


def third_kernel(
    sec, p0, p1, p2, p3, c_v, y_v, inv_v, pick, cost_in, sol, cost, keep, send, target, table
):
    scenarios, length, _ = sol.shape
    quarter = quarter_of()
    cost[...] = cost_in[...]
    for k, part in enumerate((p0, p1, p2, p3)):
        table[k * SHARES : (k + 1) * SHARES] = part[:SHARES]

    def anchor_of(s):
        node = sec[s] % BRANCH
        return table[((node // SHARES) ^ quarter) * SHARES + node % SHARES]

    build_target(target, anchor_of, c_v, y_v)

    def after(cols, total):
        own = sol[:, :, cols]
        flat = own.reshape(scenarios * length, own.shape[2]).astype(BF16)
        sums = jnp.dot(pick[...], flat, preferred_element_type=F32).reshape(BRANCH, length, own.shape[2])
        keep[:, :, cols] = sums[:HALF]
        send[:, :, cols] = sums[HALF:].astype(BF16)

    multiply(target, inv_v, sol, c_v, cost, lambda j: None, None, after)


def left_kernel(w, p0, p1, p2, p3, c_v, y_v, inv_v, cost_in, target, sol, a2, cost, table):
    share = table.shape[1] // 4
    quarter = quarter_of()
    cost[...] = cost_in[...]
    for k, part in enumerate((p0, p1, p2, p3)):
        table[:, pl.ds(pl.multiple_of((quarter ^ k) * share, share), share)] = part[SHARES, :, :share]
    build_target(target, lambda s: table[...], c_v, y_v)

    def after(cols, total):
        a2[:, cols] = total

    multiply(target, inv_v, sol, c_v, cost, lambda j: None, w, after)


def right_kernel(w, w_row, level_row, target, c_v, inv_v, cost_in, a1, a2, mass, sol, eta, sums, cost):
    scenarios, length, half = sol.shape
    columns = 2 * half
    cost[...] = cost_in[...]
    sums[:, :columns] = a1[...].astype(BF16)
    sums[:, columns : columns + half] = a2[...].astype(BF16)

    def after(cols, total):
        first = columns + half + cols.start
        sums[:, first : first + cols.stop - cols.start] = total.astype(BF16)

    multiply(target, inv_v, sol, c_v, cost, lambda j: None, w, after, half)
    lanes = jnp.sum(cost[...], axis=1)
    scen_cost = jnp.sum(lanes.T, axis=0, keepdims=True) / (3 * length * columns)
    p = w_row[...].astype(F32)
    low = level_row[:, scenarios:] - (CVAR_WEIGHT + level_row[:, :scenarios]) / PENALTY
    high = low + CVAR_WEIGHT / ((1.0 - CVAR_LEVEL) * PENALTY)
    level = jnp.minimum(jnp.maximum(scen_cost, low), high)
    eta[...] = level
    total = jnp.sum(p * level, axis=1, keepdims=True)
    whole = jnp.sum(p, axis=1, keepdims=True)
    row = lax.broadcasted_iota(jnp.int32, (length, LANES), 0)
    scal = jnp.where(row == 0, total, jnp.where(row == 1, whole, jnp.where(row == 2, mass[...], 0.0)))
    sums[:, 2 * columns :] = packed(scal)


def chip_sum_kernel(keep, got, total, send1, send2):
    cut = send1.shape[0]
    value = keep[...] + got[...].astype(F32)
    total[...] = value
    send1[...] = value[:cut].astype(BF16)
    send2[...] = value[cut:].astype(BF16)


def node_sum_kernel(s_own, s_got, sums, a2, scal):
    columns = a2.shape[1]
    sums[:, :columns] = (s_own[:, :columns].astype(F32) + s_got[:, :columns].astype(F32)).astype(BF16)
    a2[...] = s_own[:, columns : 2 * columns].astype(F32) + s_got[:, columns : 2 * columns].astype(F32)
    value = unpacked(s_own[:, 2 * columns :]) + unpacked(s_got[:, 2 * columns :])
    scal[...] = value
    sums[:, columns:] = packed(value)


def far_sum_kernel(s_own, s_got, sums):
    columns = sums.shape[1] - 3 * LANES
    sums[:, :columns] = (s_own[:, :columns].astype(F32) + s_got[:, :columns].astype(F32)).astype(BF16)
    sums[:, columns:] = packed(unpacked(s_own[:, columns:]) + unpacked(s_got[:, columns:]))


def third_avg_kernel(total, got1, got2, scal, avg, send):
    quarter = quarter_of()
    cut = got1.shape[0]
    for k in range(HALF):
        node = ((k // SHARES) * 2 + quarter % 2) * SHARES + k % SHARES
        got = got1[k] if k < cut else got2[k - cut]
        value = (total[k] + got.astype(F32)) / node_mass(scal, node)
        avg[k] = value
        send[k] = value.astype(BF16)


def write_duals(sols, y_v, avg_of, out, buf, sems, section):
    scenarios, length, _ = y_v.shape
    group = scenarios // 4

    def copy(g):
        own = pl.ds(g * group, group)
        return pltpu.make_async_copy(
            buf.at[own], out.at[own, pl.ds(section * length, length), :], sems.at[g]
        )

    for g in range(4):

        def step(i, carry):
            s = g * group + i
            avg = avg_of(s)
            start = 0
            for sol in sols:
                cols = slice(start, start + sol.shape[2])
                fresh = y_v[s, :, cols].astype(F32) + PENALTY * (sol[s] - avg[:, cols])
                buf[s, :, cols] = fresh.astype(BF16)
                start = cols.stop
            return carry

        lax.fori_loop(0, group, step, 0, unroll=4)
        copy(g).start()
    return [copy(g) for g in range(4)]


def second_duals_kernel(left, right, y_v, a2, scal, out, second_avg, buf, full, sems, sem):
    _, columns = full.shape
    quarter = quarter_of()
    share = columns // 4
    full[...] = a2[...] / jnp.sum(scal[2:3, :], axis=1, keepdims=True)
    own = pl.ds(pl.multiple_of(quarter * share, share), share)
    copy = pltpu.make_async_copy(full.at[:, own], second_avg.at[0], sem)
    copy.start()
    for other in write_duals((left, right), y_v, lambda s: full[...], out, buf, sems, 1):
        other.wait()
    copy.wait()


def third_duals_kernel(sec, sol, y_v, avg, got, prior, out, third_avg, buf, table, sems, sem):
    quarter = quarter_of()
    copy = pltpu.make_async_copy(avg.at[pl.ds((quarter // 2) * SHARES, SHARES)], third_avg, sem)
    copy.start()
    table[:HALF] = avg[...]
    table[HALF:] = got[...].astype(F32)
    for other in write_duals(
        (sol,), y_v, lambda s: table[place_of(sec[s] % BRANCH, quarter)], out, buf, sems, 2
    ):
        other.wait()
    copy.wait()


def last_kernel(
    sol, y_v, s_own, s_got, eta, duals_row, prior,
    out, first_avg, eta_avg, eta_duals, buf, full, row, one, sems, sems2,
):
    columns = full.shape[1]
    scal = unpacked(s_own[:, columns:]) + unpacked(s_got[:, columns:])
    total, mass = scal[0:1, 0:1], scal[1:2, 0:1]
    full[...] = (s_own[:, :columns].astype(F32) + s_got[:, :columns].astype(F32)) / mass
    level = total / mass
    row[...] = duals_row[...] + PENALTY * (eta[...] - level)
    one[0] = jnp.sum(level)
    copies = [
        pltpu.make_async_copy(full, first_avg, sems2.at[0]),
        pltpu.make_async_copy(row, eta_duals, sems2.at[1]),
        pltpu.make_async_copy(one, eta_avg, sems2.at[2]),
    ]
    for copy in copies:
        copy.start()
    copies += write_duals((sol,), y_v, lambda s: full[...], out, buf, sems, 0)
    for copy in copies:
        copy.wait()


def step(
    unit_costs,
    hour_duals,
    inverse,
    weights,
    section_three,
    prev_first,
    prev_second,
    prev_third,
    eta_mean,
    eta_duals,
):
    scenarios, hours, columns = unit_costs.shape
    length = hours // 3
    nodes = lax.axis_size("node")
    dma = pltpu.SemaphoreType.DMA
    shape = jax.ShapeDtypeStruct
    block = (scenarios, length, columns)
    rows = scenarios * length
    w_row = weights.reshape(1, scenarios)
    duals_row = eta_duals.reshape(1, scenarios)
    costs, duals, matrix = in_hbm(unit_costs), in_hbm(hour_duals), in_hbm(inverse)

    tail = jnp.pad(prev_second, ((0, 0), (0, 0), (0, columns - columns // 4)))
    prev = jnp.concatenate((prev_third, tail))
    y_prev = partner(prev, 2)

    w, sec, y1, c2, y2, c3, y3, inv_v, sol1, a1, mass, pick, cost = call(
        first_kernel,
        32,
        in_specs=[HBM] * 8,
        out_specs=[SMEM, SMEM] + [VMEM] * 11,
        out_shape=[
            pltpu.SMEM((scenarios,), jnp.int32),
            pltpu.SMEM((scenarios,), jnp.int32),
            *[pltpu.VMEM(block, BF16)] * 5,
            pltpu.VMEM(inverse.shape, BF16),
            pltpu.VMEM(block, F32),
            pltpu.VMEM((length, columns), F32),
            pltpu.VMEM((1, LANES), F32),
            pltpu.VMEM((BRANCH * length, rows), BF16),
            pltpu.VMEM((scenarios, length, LANES), F32),
        ],
        scratch_shapes=[
            pltpu.VMEM(block, BF16),
            pltpu.VMEM((length, columns), BF16),
            pltpu.VMEM((1, scenarios), jnp.int32),
            pltpu.VMEM((1, scenarios), jnp.int32),
            pltpu.VMEM((rows, columns), BF16),
            dma((11 + CHUNKS,)),
        ],
    )(
        in_hbm(weights),
        in_hbm(section_three),
        in_hbm(w_row),
        in_hbm(section_three.reshape(1, scenarios)),
        in_hbm(prev_first),
        costs,
        duals,
        matrix,
    )

    y_prev, joined = lax.optimization_barrier((y_prev, (eta_mean, eta_duals)))
    level_row = jnp.concatenate((joined[1], joined[0])).reshape(1, scenarios + 1)
    core_prev, diag_prev = partner((prev, y_prev), 1)
    pieces = (prev, core_prev, y_prev, diag_prev)

    sol3, cost, keep, send = call(
        third_kernel,
        30,
        in_specs=[SMEM] + [VMEM] * 9,
        out_specs=[VMEM] * 4,
        out_shape=[
            pltpu.VMEM(block, F32),
            pltpu.VMEM((scenarios, length, LANES), F32),
            pltpu.VMEM((HALF, length, columns), F32),
            pltpu.VMEM((HALF, length, columns), BF16),
        ],
        scratch_shapes=[pltpu.VMEM((rows, columns), BF16), pltpu.VMEM((BRANCH, length, columns), BF16)],
    )(sec, *pieces, c3, y3, inv_v, pick, cost)

    chip_got = partner(send, 1)
    half_block = (scenarios, length, columns // 2)
    target2, left, a2, cost = call(
        left_kernel,
        30,
        in_specs=[SMEM] + [VMEM] * 8,
        out_specs=[VMEM] * 4,
        out_shape=[
            pltpu.VMEM((rows, columns), BF16),
            pltpu.VMEM(half_block, F32),
            pltpu.VMEM((length, columns // 2), F32),
            pltpu.VMEM((scenarios, length, LANES), F32),
        ],
        scratch_shapes=[pltpu.VMEM((length, columns), BF16)],
    )(w, *pieces, c2, y2, inv_v, cost)
    cut = HALF // 2
    chip_total, chip_send1, chip_send2 = call(
        chip_sum_kernel,
        8,
        in_specs=[VMEM] * 2,
        out_specs=[VMEM] * 3,
        out_shape=[
            pltpu.VMEM((HALF, length, columns), F32),
            pltpu.VMEM((cut, length, columns), BF16),
            pltpu.VMEM((HALF - cut, length, columns), BF16),
        ],
    )(keep, chip_got)
    node_got1 = partner(chip_send1, 2)

    right, eta, sums = call(
        right_kernel,
        30,
        in_specs=[SMEM] + [VMEM] * 9,
        out_specs=[VMEM] * 3,
        out_shape=[
            pltpu.VMEM(half_block, F32),
            pltpu.VMEM((1, scenarios), F32),
            pltpu.VMEM((length, 2 * columns + 3 * LANES), BF16),
        ],
        scratch_shapes=[pltpu.VMEM((scenarios, length, LANES), F32)],
    )(w, w_row, level_row, target2, c2, inv_v, cost, a1, a2, mass)

    core_sums = partner(sums, 1)
    sums = call(
        far_sum_kernel, 8, in_specs=[VMEM] * 2, out_specs=VMEM, out_shape=pltpu.VMEM(sums.shape, BF16)
    )(sums, core_sums)
    y_sums = partner(sums, 2)
    node_got2 = partner(chip_send2, 2)
    far_shape = pltpu.VMEM((length, columns + 3 * LANES), BF16)
    far, a2, scal = call(
        node_sum_kernel,
        8,
        in_specs=[VMEM] * 2,
        out_specs=[VMEM] * 3,
        out_shape=[far_shape, pltpu.VMEM((length, columns), F32), pltpu.VMEM((length, LANES), F32)],
    )(sums, y_sums)
    far_got = partner(far, 4)
    mask = 8
    while mask < nodes:
        far = call(far_sum_kernel, 8, in_specs=[VMEM] * 2, out_specs=VMEM, out_shape=far_shape)(far, far_got)
        far_got = partner(far, mask)
        mask *= 2

    buf = pltpu.VMEM(block, BF16)
    duals_shape = shape(hour_duals.shape, BF16)
    out, second_avg = call(
        second_duals_kernel,
        8,
        in_specs=[VMEM] * 5,
        out_specs=[HBM, HBM],
        out_shape=[duals_shape, shape((1, length, columns // 4), F32)],
        scratch_shapes=[buf, pltpu.VMEM((length, columns), F32), dma((4,)), dma],
    )(left, right, y2, a2, scal)

    avg, avg_send = call(
        third_avg_kernel,
        8,
        in_specs=[VMEM] * 4,
        out_specs=[VMEM] * 2,
        out_shape=[
            pltpu.VMEM((HALF, length, columns), F32),
            pltpu.VMEM((HALF, length, columns), BF16),
        ],
    )(chip_total, node_got1, node_got2, scal)
    avg_got = partner(avg_send, 1)
    out, third_avg = call(
        third_duals_kernel,
        8,
        in_specs=[SMEM] + [VMEM] * 4 + [HBM],
        out_specs=[HBM, HBM],
        out_shape=[duals_shape, shape((SHARES, length, columns), F32)],
        scratch_shapes=[buf, pltpu.VMEM((BRANCH, length, columns), F32), dma((4,)), dma],
        input_output_aliases={5: 0},
    )(sec, sol3, y3, avg, avg_got, out)
    out, first_avg, eta_avg, eta_duals_new = call(
        last_kernel,
        8,
        in_specs=[VMEM] * 6 + [HBM],
        out_specs=[HBM] * 4,
        out_shape=[
            duals_shape,
            shape((length, columns), F32),
            shape((1,), F32),
            shape((1, scenarios), F32),
        ],
        scratch_shapes=[
            buf,
            pltpu.VMEM((length, columns), F32),
            pltpu.VMEM((1, scenarios), F32),
            pltpu.SMEM((1,), F32),
            dma((4,)),
            dma((3,)),
        ],
        input_output_aliases={6: 0},
    )(sol1, y1, far, far_got, eta, duals_row, out)
    return out, first_avg, second_avg, third_avg, eta_avg, eta_duals_new.reshape(scenarios)


def solution(mesh):
    row = P(("groups", "node"))
    in_specs = (row, row, P(), row, row, P("groups"), row, row, P("groups"), row)
    out_specs = (row, P("groups"), row, row, P("groups"), row)
    return jax.shard_map(step, mesh=mesh, in_specs=in_specs, out_specs=out_specs, check_vma=False)
```

time: 47.1 us -> 43.9 us (0.932)
  waiting for transfers between devices: 15.1 us -> 12.8 us
  Pallas kernels: 17.8 us -> 16.1 us
  other arithmetic: 0.01 us -> 1.01 us
    ppermute x13 -> x11, waiting for transfers between devices: 15.1 us -> 12.8 us  [partner(): return lax.ppermute(value, 'node', pairs)]
    pallas_call x7 -> x9, Pallas kernels: 16.4 us -> 14.7 us  [the longest x1 5.55 us: step(): call(first_kernel, 32, in_specs=[HBM] * 8, out_specs=[SMEM, SMEM] + [VMEM...]
    concatenate x0 -> x1, other arithmetic: none -> 0.93 us  [step(): prev = jnp.concatenate((prev_third, tail))]
    ppermute x13 -> x11, starting transfers between devices: 12.5 us -> 12.3 us  [partner(): return lax.ppermute(value, 'node', pairs)]
  transfers between devices with their start and end apart: 13 -> 11, of which waited for: 4 -> 3; matrix products, arithmetic and copies ran while one was open for 0% -> 0% of each run, Pallas kernels for 32% -> 27%
where the time goes in v4:
time: 43.9 us; the launch traced here: 43.7 us
  Pallas kernels  16.1 us (37%)
  waiting for transfers between devices  12.8 us (29%)
  starting transfers between devices  12.3 us (28%)
  between operations  1.42 us (3%)
  other arithmetic  1.01 us (2%)
    ppermute x11, waiting for transfers between devices, partner(): return lax.ppermute(value, 'node', pairs)  12.8 us
    ppermute x11, starting transfers between devices, partner(): return lax.ppermute(value, 'node', pairs)  12.3 us
    pallas_call x1, Pallas kernels, step(): call(first_kernel, 32, in_specs=[HBM] * 8, out_specs=[SMEM, SMEM] + [VMEM...  5.55 us
    pallas_call x1, Pallas kernels, step(): call(third_kernel, 30, in_specs=[SMEM] + [VMEM] * 9, out_specs=[VMEM] * 4...  3.2 us
    pallas_call x1, Pallas kernels, step(): call(left_kernel, 30, in_specs=[SMEM] + [VMEM] * 8, out_specs=[VMEM] * 4,...  1.71 us
    pallas_call x1, Pallas kernels, step(): call(right_kernel, 30, in_specs=[SMEM] + [VMEM] * 9, out_specs=[VMEM] * 3...  1.62 us
    pallas_call x1, Pallas kernels, step(): call(third_duals_kernel, 8, in_specs=[SMEM] + [VMEM] * 4 + [HBM], out_spe...  1.41 us
    pallas_call x1, Pallas kernels, step(): call(last_kernel, 8, in_specs=[VMEM] * 6 + [HBM], out_specs=[HBM] * 4, ou...  1.18 us
  transfers between devices with their start and end apart: 11, of which 3 were waited for; matrix products, arithmetic and copies ran while one was open for 0% of the time, Pallas kernels for 27%

profile of v4, /device:TPU:0, one launch (start us, length us, event | category | flops | bytes accessed | tf_op | source)
XLA Modules:
  0.0 43.7 jit_solution(8654934387729461798)
XLA Ops:
  0.6 0.9 %fusion.1.p0 = bf16[5,8,2048]{2,1,0:T(8,128)(2,1)S(1)} fusion(bf16[1,8,512]{2,1,0:T(8,128)(2,1)} %param.16, bf16[4,8,2048]{2,1,0:T(8,128)(2,1)} %param.17), kind=kLoop, calls=%fused_computation.2 | loop fusion | flops 491520 | bytes 303104 | tf_op jit(solution)/shard_map/concatenate | solution.py:373
  1.6 3.1 %collective-permute-start = (bf16[5,8,2048]{2,1,0:T(8,128)(2,1)S(1)}, bf16[5,8,2048]{2,1,0:T(8,128)(2,1)S(1)}, u32[]{:S(2)}, u32[]{:S(2)}) collective-permute-start(bf16[5,8,2048]{2,1,0:T(8,128)(2,1)S(1)} %fusion.1.p0), channel_id=1, source_target_pairs={{0,2},{1,3},{2,0},{3,1},{4,6},{5,7},{6,4},{7,5},{8,10},{9,11},{10,... | collective-permute-start | bytes 491528 | tf_op jit(solution)/shard_map/ppermute | solution.py:27
  4.6 0.0 collective-permute-start.1
  4.6 4.2 %collective-permute-done.p2 = bf16[5,8,2048]{2,1,0:T(8,128)(2,1)S(1)} collective-permute-done((bf16[5,8,2048]{2,1,0:T(8,128)(2,1)S(1)}, bf16[5,8,2048]{2,1,0:T(8,128)(2,1)S(1)}, u32[]{:S(2)}, u32[]{:S(2)}) %collective-permute-start) | collective-permute-done | bytes 163872 | tf_op jit(solution)/shard_map/ppermute | solution.py:27
  8.8 0.0 collective-permute-start.2
  8.8 5.6 %shard_map.145 = (s32[32]{0:T(128)S(4)}, s32[32]{0:T(128)S(4)}, bf16[32,8,2048]{2,1,0:T(8,128)(2,1)S(1)}, bf16[32,8,2048]{2,1,0:T(8,128)(2,1)S(1)}, bf16[32,8,20...) custom-call(s32[32]{0:T(128)} %w_hbm.1, ...), custom_call_target="tpu_custom_call" | custom-call | tf_op jit(solution)/shard_map/pallas_call | solution.py:376
  14.4 0.0 collective-permute-done.1.p1
  14.4 0.0 collective-permute-done.2.p3
  14.4 0.0 copy-start.1
  14.4 3.2 %shard_map.146 = (f32[32,8,2048]{2,1,0:T(8,128)S(1)}, f32[32,8,128]{2,1,0:T(8,128)S(1)}, f32[8,8,2048]{2,1,0:T(8,128)S(1)}, bf16[8,8,2048]{2,1,0:T(8,128)(2,1)S(1)}) custom-call(s32[32]{0:T(128)S(4)} %get-tuple-element.58.sec, bf16[5,8,2048]{2,1,0:T(8,128)(2,1)S(1)} %fusion.1.p0, bf16[5,8,2048]{2,1,0:T(8,128)(2,1)S(1)} %collective-permute-done.1.p1, ...), custom_call_target="tpu_custom_call" | custom-call | tf_op jit(solution)/shard_map/pallas_call | solution.py:416
  17.6 0.6 %collective-permute-start.7 = (bf16[8,8,2048]{2,1,0:T(8,128)(2,1)S(1)}, bf16[8,8,2048]{2,1,0:T(8,128)(2,1)S(1)}, u32[]{:S(2)}, u32[]{:S(2)}) collective-permute-start(bf16[8,8,2048]{2,1,0:T(8,128)(2,1)S(1)} %get-tuple-element.74), channel_id=1, source_target_pairs={{0,1},{1,0},{2,3},{3,2},{4,5},{5,4},{6,7},{7,6},{8,9},{9,8},{10,11... | collective-permute-start | bytes 786440 | tf_op jit(solution)/shard_map/ppermute | solution.py:27
  18.8 0.0 copy-done.1
  18.8 0.1 maximum_bitcast_fusion.level_row
  18.9 0.0 copy-start
  18.9 1.7 %shard_map.147 = (bf16[256,2048]{1,0:T(8,128)(2,1)S(1)}, f32[32,8,1024]{2,1,0:T(8,128)S(1)}, f32[8,1024]{1,0:T(8,128)S(1)}, f32[32,8,128]{2,1,0:T(8,128)S(1)}) custom-call(s32[32]{0:T(128)S(4)} %get-tuple-element.51.w, bf16[5,8,2048]{2,1,0:T(8,128)(2,1)S(1)} %fusion.1.p0, bf16[5,8,2048]{2,1,0:T(8,128)(2,1)S(1)} %collective-permute-done.1.p1, ...), custom_call_target="tpu_custom_call" | custom-call | tf_op jit(solution)/shard_map/pallas_call | solution.py:432
  20.6 0.0 copy-done
  20.7 1.6 %shard_map.148 = (f32[32,8,1024]{2,1,0:T(8,128)S(1)}, f32[1,32]{1,0:T(1,128)S(1)}, bf16[8,4480]{1,0:T(8,128)(2,1)S(1)}) custom-call(s32[32]{0:T(128)S(4)} %get-tuple-element.51.w, s32[1,32]{1,0:T(1,128)S(1)} %bitcast.7, f32[1,33]{1,0:T(1,128)S(1)} %maximum_bitcast_fusion.level_row, bf16[256,2048]{1,0:T(8,128)(2,1)S(1)} %get-tuple-element.64.target, ...), custom_call_target="tpu_custom_call" | custom-call | tf_op jit(solution)/shard_map/pallas_call | solution.py:459
  22.3 0.0 collective-permute-start.3
  22.3 0.0 collective-permute-done.7.got
  22.3 0.1 shard_map.152
  22.4 1.8 %collective-permute-start.8 = (bf16[4,8,2048]{2,1,0:T(8,128)(2,1)S(1)}, bf16[4,8,2048]{2,1,0:T(8,128)(2,1)S(1)}, u32[]{:S(2)}, u32[]{:S(2)}) collective-permute-start(bf16[4,8,2048]{2,1,0:T(8,128)(2,1)S(1)} %get-tuple-element.76), channel_id=1, source_target_pairs={{0,2},{1,3},{2,0},{3,1},{4,6},{5,7},{6,4},{7,5},{8,10},{9,11},{10,... | collective-permute-start | bytes 393224 | tf_op jit(solution)/shard_map/ppermute | solution.py:27
  24.2 0.3 collective-permute-start.9
  24.5 0.0 collective-permute-done.3.s_got
  24.5 1.8 %collective-permute-start.4 = (bf16[8,4480]{1,0:T(8,128)(2,1)S(1)}, bf16[8,4480]{1,0:T(8,128)(2,1)S(1)}, u32[]{:S(2)}, u32[]{:S(2)}) collective-permute-start(bf16[8,4480]{1,0:T(8,128)(2,1)S(1)} %shard_map.149.s_own), channel_id=1, source_target_pairs={{0,2},{1,3},{2,0},{3,1},{4,6},{5,7},{6,4},{7,5},{8,10},{9,11},{10,... | collective-permute-start | bytes 215048 | tf_op jit(solution)/shard_map/ppermute | solution.py:27
  26.3 6.4 %collective-permute-done.4.s_got = bf16[8,4480]{1,0:T(8,128)(2,1)S(1)} collective-permute-done((bf16[8,4480]{1,0:T(8,128)(2,1)S(1)}, bf16[8,4480]{1,0:T(8,128)(2,1)S(1)}, u32[]{:S(2)}, u32[]{:S(2)}) %collective-permute-start.4) | collective-permute-done | bytes 71712 | tf_op jit(solution)/shard_map/ppermute | solution.py:27
  32.7 0.0 collective-permute-done.8.got1
  32.7 0.0 collective-permute-done.9.got2
  32.8 0.2 shard_map.153
  32.9 0.1 collective-permute-start.10
  33.0 1.8 %collective-permute-start.5 = (bf16[8,2432]{1,0:T(8,128)(2,1)S(1)}, bf16[8,2432]{1,0:T(8,128)(2,1)S(1)}, u32[]{:S(2)}, u32[]{:S(2)}) collective-permute-start(bf16[8,2432]{1,0:T(8,128)(2,1)S(1)} %get-tuple-element.70.s_own), channel_id=1, source_target_pairs={{0,4},{1,5},{2,6},{3,7},{4,0},{5,1},{6,2},{7,3},{8,12},{9,13},{10,... | collective-permute-start | bytes 116744 | tf_op jit(solution)/shard_map/ppermute | solution.py:27
  34.8 2.2 %collective-permute-done.5.s_got = bf16[8,2432]{1,0:T(8,128)(2,1)S(1)} collective-permute-done((bf16[8,2432]{1,0:T(8,128)(2,1)S(1)}, bf16[8,2432]{1,0:T(8,128)(2,1)S(1)}, u32[]{:S(2)}, u32[]{:S(2)}) %collective-permute-start.5) | collective-permute-done | bytes 38944 | tf_op jit(solution)/shard_map/ppermute | solution.py:27
  37.1 2.9 %collective-permute-start.6 = (bf16[8,2432]{1,0:T(8,128)(2,1)S(1)}, bf16[8,2432]{1,0:T(8,128)(2,1)S(1)}, u32[]{:S(2)}, u32[]{:S(2)}) collective-permute-start(bf16[8,2432]{1,0:T(8,128)(2,1)S(1)} %shard_map.151.s_own), channel_id=1, source_target_pairs={{0,8},{1,9},{2,10},{3,11},{4,12},{5,13},{6,14},{7,15},{8,0},{9,1},... | collective-permute-start | bytes 116744 | tf_op jit(solution)/shard_map/ppermute | solution.py:27
  39.9 1.2 %shard_map.154 = (bf16[32,24,2048]{2,1,0:T(8,128)(2,1)}, f32[1,8,512]{2,1,0:T(8,128)}) custom-call(f32[32,8,1024]{2,1,0:T(8,128)S(1)} %get-tuple-element.81.left, f32[32,8,1024]{2,1,0:T(8,128)S(1)} %get-tuple-element.82.right, bf16[32,8,2048]{2,1,0:T(8,128)(2,1)S(1)} %get-tuple-element.56.y_v, f32[8,2048]{1,0:T(8,128)S(1)} %get-tuple-element.83.a2, ...), custom_call_target="tpu_custom_call" | custom-call | tf_op jit(solution)/shard_map/pallas_call | solution.py:495
  41.1 0.0 collective-permute-done.10.got
  41.1 1.4 %shard_map.155 = (bf16[32,24,2048]{2,1,0:T(8,128)(2,1)}, f32[4,8,2048]{2,1,0:T(8,128)}) custom-call(s32[32]{0:T(128)S(4)} %get-tuple-element.58.sec, f32[32,8,2048]{2,1,0:T(8,128)S(1)} %get-tuple-element.72.sol, bf16[32,8,2048]{2,1,0:T(8,128)(2,1)S(1)} %get-tuple-element.60.y_v, ...), custom_call_target="tpu_custom_call", output_to_operand_aliasing={{0}: (5, {})} | custom-call | tf_op jit(solution)/shard_map/pallas_call | solution.py:515
  42.5 0.0 collective-permute-done.6.s_got
  42.5 1.2 %shard_map.156 = (bf16[32,24,2048]{2,1,0:T(8,128)(2,1)}, f32[8,2048]{1,0:T(8,128)}, f32[1]{0:T(128)}, f32[1,32]{1,0:T(1,128)}) custom-call(f32[32,8,2048]{2,1,0:T(8,128)S(1)} %get-tuple-element.49.sol, bf16[32,8,2048]{2,1,0:T(8,128)(2,1)S(1)} %get-tuple-element.50.y_v, bf16[8,2432]{1,0:T(8,128)(2,1)S(1)} %shard_map.151.s_own, ...), custom_call_target="tpu_custom_call", output_to_operand_aliasing={{0}: (6, {})} | custom-call | tf_op jit(solution)/shard_map/pallas_call | solution.py:524
  (3 shorter events, 0.1 us)
Async XLA Ops:
  1.6 7.3 %collective-permute-start = (bf16[5,8,2048]{2,1,0:T(8,128)(2,1)S(1)}, bf16[5,8,2048]{2,1,0:T(8,128)(2,1)S(1)}, u32[]{:S(2)}, u32[]{:S(2)}) collective-permute-start(bf16[5,8,2048]{2,1,0:T(8,128)(2,1)S(1)} %fusion.1.p0), channel_id=1, source_target_pairs={{0,2},{1,3},{2,0},{3,1},{4,6},{5,7},{6,4},{7,5},{8,10},{9,11},{10,... | collective-permute-start | bytes 491528 | tf_op jit(solution)/shard_map/ppermute | solution.py:27
  4.6 9.8 %collective-permute-start.1 = (bf16[5,8,2048]{2,1,0:T(8,128)(2,1)S(1)}, bf16[5,8,2048]{2,1,0:T(8,128)(2,1)S(1)}, u32[]{:S(2)}, u32[]{:S(2)}) collective-permute-start(bf16[5,8,2048]{2,1,0:T(8,128)(2,1)S(1)} %fusion.1.p0), channel_id=1, source_target_pairs={{0,1},{1,0},{2,3},{3,2},{4,5},{5,4},{6,7},{7,6},{8,9},{9,8},{10,11... | collective-permute-start | bytes 491528 | tf_op jit(solution)/shard_map/ppermute | solution.py:27
  8.8 5.6 %collective-permute-start.2 = (bf16[5,8,2048]{2,1,0:T(8,128)(2,1)S(1)}, bf16[5,8,2048]{2,1,0:T(8,128)(2,1)S(1)}, u32[]{:S(2)}, u32[]{:S(2)}) collective-permute-start(bf16[5,8,2048]{2,1,0:T(8,128)(2,1)S(1)} %collective-permute-done.p2), channel_id=1, source_target_pairs={{0,1},{1,0},{2,3},{3,2},{4,5},{5,4},{6,7},{7,6},{8,9},{9,8},{10,11... | collective-permute-start | bytes 491528 | tf_op jit(solution)/shard_map/ppermute | solution.py:27
  14.4 4.4 %copy-start.1 = (f32[32]{0:T(128)S(1)}, f32[32]{0:T(128)}, u32[]{:S(2)}) copy-start(f32[32]{0:T(128)} %param.19) | copy-start | bytes 388
  17.6 4.7 %collective-permute-start.7 = (bf16[8,8,2048]{2,1,0:T(8,128)(2,1)S(1)}, bf16[8,8,2048]{2,1,0:T(8,128)(2,1)S(1)}, u32[]{:S(2)}, u32[]{:S(2)}) collective-permute-start(bf16[8,8,2048]{2,1,0:T(8,128)(2,1)S(1)} %get-tuple-element.74), channel_id=1, source_target_pairs={{0,1},{1,0},{2,3},{3,2},{4,5},{5,4},{6,7},{7,6},{8,9},{9,8},{10,11... | collective-permute-start | bytes 786440 | tf_op jit(solution)/shard_map/ppermute | solution.py:27
  18.9 1.7 %copy-start = (s32[32]{0:T(128)S(1)}, s32[32]{0:T(128)}, u32[]{:S(2)}) copy-start(s32[32]{0:T(128)} %w_hbm.1) | copy-start | bytes 388
  22.3 2.2 %collective-permute-start.3 = (bf16[8,4480]{1,0:T(8,128)(2,1)S(1)}, bf16[8,4480]{1,0:T(8,128)(2,1)S(1)}, u32[]{:S(2)}, u32[]{:S(2)}) collective-permute-start(bf16[8,4480]{1,0:T(8,128)(2,1)S(1)} %get-tuple-element.69.s_own), channel_id=1, source_target_pairs={{0,1},{1,0},{2,3},{3,2},{4,5},{5,4},{6,7},{7,6},{8,9},{9,8},{10,11... | collective-permute-start | bytes 215048 | tf_op jit(solution)/shard_map/ppermute | solution.py:27
  22.4 10.4 %collective-permute-start.8 = (bf16[4,8,2048]{2,1,0:T(8,128)(2,1)S(1)}, bf16[4,8,2048]{2,1,0:T(8,128)(2,1)S(1)}, u32[]{:S(2)}, u32[]{:S(2)}) collective-permute-start(bf16[4,8,2048]{2,1,0:T(8,128)(2,1)S(1)} %get-tuple-element.76), channel_id=1, source_target_pairs={{0,2},{1,3},{2,0},{3,1},{4,6},{5,7},{6,4},{7,5},{8,10},{9,11},{10,... | collective-permute-start | bytes 393224 | tf_op jit(solution)/shard_map/ppermute | solution.py:27
  24.2 8.5 %collective-permute-start.9 = (bf16[4,8,2048]{2,1,0:T(8,128)(2,1)S(1)}, bf16[4,8,2048]{2,1,0:T(8,128)(2,1)S(1)}, u32[]{:S(2)}, u32[]{:S(2)}) collective-permute-start(bf16[4,8,2048]{2,1,0:T(8,128)(2,1)S(1)} %get-tuple-element.77), channel_id=1, source_target_pairs={{0,2},{1,3},{2,0},{3,1},{4,6},{5,7},{6,4},{7,5},{8,10},{9,11},{10,... | collective-permute-start | bytes 393224 | tf_op jit(solution)/shard_map/ppermute | solution.py:27
  24.5 8.2 %collective-permute-start.4 = (bf16[8,4480]{1,0:T(8,128)(2,1)S(1)}, bf16[8,4480]{1,0:T(8,128)(2,1)S(1)}, u32[]{:S(2)}, u32[]{:S(2)}) collective-permute-start(bf16[8,4480]{1,0:T(8,128)(2,1)S(1)} %shard_map.149.s_own), channel_id=1, source_target_pairs={{0,2},{1,3},{2,0},{3,1},{4,6},{5,7},{6,4},{7,5},{8,10},{9,11},{10,... | collective-permute-start | bytes 215048 | tf_op jit(solution)/shard_map/ppermute | solution.py:27
  32.9 8.2 %collective-permute-start.10 = (bf16[8,8,2048]{2,1,0:T(8,128)(2,1)S(1)}, bf16[8,8,2048]{2,1,0:T(8,128)(2,1)S(1)}, u32[]{:S(2)}, u32[]{:S(2)}) collective-permute-start(bf16[8,8,2048]{2,1,0:T(8,128)(2,1)S(1)} %get-tuple-element.80), channel_id=1, source_target_pairs={{0,1},{1,0},{2,3},{3,2},{4,5},{5,4},{6,7},{7,6},{8,9},{9,8},{10,11... | collective-permute-start | bytes 786440 | tf_op jit(solution)/shard_map/ppermute | solution.py:27
  33.0 4.0 %collective-permute-start.5 = (bf16[8,2432]{1,0:T(8,128)(2,1)S(1)}, bf16[8,2432]{1,0:T(8,128)(2,1)S(1)}, u32[]{:S(2)}, u32[]{:S(2)}) collective-permute-start(bf16[8,2432]{1,0:T(8,128)(2,1)S(1)} %get-tuple-element.70.s_own), channel_id=1, source_target_pairs={{0,4},{1,5},{2,6},{3,7},{4,0},{5,1},{6,2},{7,3},{8,12},{9,13},{10,... | collective-permute-start | bytes 116744 | tf_op jit(solution)/shard_map/ppermute | solution.py:27
  37.1 5.5 %collective-permute-start.6 = (bf16[8,2432]{1,0:T(8,128)(2,1)S(1)}, bf16[8,2432]{1,0:T(8,128)(2,1)S(1)}, u32[]{:S(2)}, u32[]{:S(2)}) collective-permute-start(bf16[8,2432]{1,0:T(8,128)(2,1)S(1)} %shard_map.151.s_own), channel_id=1, source_target_pairs={{0,8},{1,9},{2,10},{3,11},{4,12},{5,13},{6,14},{7,15},{8,0},{9,1},... | collective-permute-start | bytes 116744 | tf_op jit(solution)/shard_map/ppermute | solution.py:27

commit v5 on v4

--- a/solution.py
+++ b/solution.py
@@ -91,23 +91,37 @@
     finish(count - 1)
 
 
+def join_kernel(third, second, joined, sems):
+    shares, share = third.shape[0], second.shape[2]
+    copies = [
+        pltpu.make_async_copy(third, joined.at[pl.ds(0, shares)], sems.at[0]),
+        pltpu.make_async_copy(second.at[0], joined.at[shares, :, pl.ds(0, share)], sems.at[1]),
+    ]
+    for copy in copies:
+        copy.start()
+    for copy in copies:
+        copy.wait()
+
+
+def section_rows(c_hbm, y_hbm, c_v, y_v, sems, section):
+    length = c_v.shape[1]
+    own = pl.ds(section * length, length)
+    return [
+        pltpu.make_async_copy(c_hbm.at[:, own, :], c_v, sems.at[0]),
+        pltpu.make_async_copy(y_hbm.at[:, own, :], y_v, sems.at[1]),
+    ]
+
+
 def first_kernel(
     w_hbm, sec_hbm, w_row_hbm, sec_row_hbm, pf_hbm, c_hbm, y_hbm, inv_hbm,
-    w, sec, y1, c2, y2, c3, y3, inv_v, sol, a1, mass, pick, cost, c1, pf, w_row, sec_row, target, sems,
+    w, sec, c1, y1, inv_v, sol, a1, mass, pick, cost, target, pf, w_row, sec_row, sems, row_sems,
 ):
-    scenarios, length, columns = sol.shape
+    scenarios, length, columns = c1.shape
     width = columns // CHUNKS
 
     def chunk(j):
         part = pl.ds(j * width, width)
-        return pltpu.make_async_copy(inv_hbm.at[:, part], inv_v.at[:, part], sems.at[11 + j])
-
-    def rows(k, c_v, y_v):
-        own = pl.ds(k * length, length)
-        return [
-            pltpu.make_async_copy(c_hbm.at[:, own, :], c_v, sems.at[5 + 2 * k]),
-            pltpu.make_async_copy(y_hbm.at[:, own, :], y_v, sems.at[6 + 2 * k]),
-        ]
+        return pltpu.make_async_copy(inv_hbm.at[:, part], inv_v.at[:, part], sems.at[5 + j])
 
     small = [
         pltpu.make_async_copy(source, into, sems.at[k])
@@ -115,9 +129,8 @@
             ((w_row_hbm, w_row), (sec_row_hbm, sec_row), (w_hbm, w), (sec_hbm, sec), (pf_hbm, pf))
         )
     ]
-    first = rows(0, c1, y1)
-    later = rows(2, c3, y3) + rows(1, c2, y2)
-    for copy in small + first + [chunk(j) for j in range(CHUNKS)] + later:
+    first = section_rows(c_hbm, y_hbm, c1, y1, row_sems, 0)
+    for copy in small + first + [chunk(j) for j in range(CHUNKS)]:
         copy.start()
     cost[...] = jnp.zeros_like(cost)
     for copy in small:
@@ -148,7 +161,20 @@
         a1[:, cols] = total
 
     multiply(target, inv_v, sol, c1, cost, lambda j: chunk(j).wait(), w, after)
-    for copy in later:
+    chunk(CHUNKS - 1).wait()
+
+
+def rest_kernel(w, target, c1, inv_v, cost_in, c_hbm, y_hbm, c3, y3, sol, a1, cost, sems):
+    ahead = section_rows(c_hbm, y_hbm, c3, y3, sems, 2)
+    for copy in ahead:
+        copy.start()
+    cost[...] = cost_in[...]
+
+    def after(cols, total):
+        a1[:, cols] = total
+
+    multiply(target, inv_v, sol, c1, cost, lambda j: None, w, after, c1.shape[2] - sol.shape[2])
+    for copy in ahead:
         copy.wait()
 
 
@@ -171,10 +197,17 @@
 
 
 def third_kernel(
-    sec, p0, p1, p2, p3, c_v, y_v, inv_v, pick, cost_in, sol, cost, keep, send, target, table
+    sec, p0, p1, p2, p3, c_v, y_v, inv_v, pick, cost_in, a_left, a_right, c_hbm, y_hbm,
+    c2, y2, sol, cost, keep, send, target, table, sems,
 ):
     scenarios, length, _ = sol.shape
     quarter = quarter_of()
+    ahead = section_rows(c_hbm, y_hbm, c2, y2, sems, 1)
+    for copy in ahead:
+        copy.start()
+    cut = a_left.shape[1]
+    send[HALF, :, :cut] = a_left[...].astype(BF16)
+    send[HALF, :, cut:] = a_right[...].astype(BF16)
     cost[...] = cost_in[...]
     for k, part in enumerate((p0, p1, p2, p3)):
         table[k * SHARES : (k + 1) * SHARES] = part[:SHARES]
@@ -190,9 +223,11 @@
         flat = own.reshape(scenarios * length, own.shape[2]).astype(BF16)
         sums = jnp.dot(pick[...], flat, preferred_element_type=F32).reshape(BRANCH, length, own.shape[2])
         keep[:, :, cols] = sums[:HALF]
-        send[:, :, cols] = sums[HALF:].astype(BF16)
+        send[:HALF, :, cols] = sums[HALF:].astype(BF16)
 
     multiply(target, inv_v, sol, c_v, cost, lambda j: None, None, after)
+    for copy in ahead:
+        copy.wait()
 
 
 def left_kernel(w, p0, p1, p2, p3, c_v, y_v, inv_v, cost_in, target, sol, a2, cost, table):
@@ -209,22 +244,20 @@
     multiply(target, inv_v, sol, c_v, cost, lambda j: None, w, after)
 
 
-def right_kernel(w, w_row, level_row, target, c_v, inv_v, cost_in, a1, a2, mass, sol, eta, sums, cost):
-    scenarios, length, half = sol.shape
+def right_kernel(w, w_row, mean, duals_row, target, c_v, inv_v, cost_in, a2, mass, sol, eta, sums, cost):
+    _, length, half = sol.shape
     columns = 2 * half
     cost[...] = cost_in[...]
-    sums[:, :columns] = a1[...].astype(BF16)
-    sums[:, columns : columns + half] = a2[...].astype(BF16)
+    sums[:, :half] = a2[...].astype(BF16)
 
     def after(cols, total):
-        first = columns + half + cols.start
-        sums[:, first : first + cols.stop - cols.start] = total.astype(BF16)
+        sums[:, half + cols.start : half + cols.stop] = total.astype(BF16)
 
     multiply(target, inv_v, sol, c_v, cost, lambda j: None, w, after, half)
     lanes = jnp.sum(cost[...], axis=1)
     scen_cost = jnp.sum(lanes.T, axis=0, keepdims=True) / (3 * length * columns)
     p = w_row[...].astype(F32)
-    low = level_row[:, scenarios:] - (CVAR_WEIGHT + level_row[:, :scenarios]) / PENALTY
+    low = mean[...] - (CVAR_WEIGHT + duals_row[...]) / PENALTY
     high = low + CVAR_WEIGHT / ((1.0 - CVAR_LEVEL) * PENALTY)
     level = jnp.minimum(jnp.maximum(scen_cost, low), high)
     eta[...] = level
@@ -232,22 +265,25 @@
     whole = jnp.sum(p, axis=1, keepdims=True)
     row = lax.broadcasted_iota(jnp.int32, (length, LANES), 0)
     scal = jnp.where(row == 0, total, jnp.where(row == 1, whole, jnp.where(row == 2, mass[...], 0.0)))
-    sums[:, 2 * columns :] = packed(scal)
-
-
-def chip_sum_kernel(keep, got, total, send1, send2):
-    cut = send1.shape[0]
-    value = keep[...] + got[...].astype(F32)
+    sums[:, columns:] = packed(scal)
+
+
+def chip_sum_kernel(keep, sent, got, total, send1, send2):
+    half = keep.shape[0]
+    cut = half - send2.shape[0]
+    value = keep[...] + got[:half].astype(F32)
     total[...] = value
-    send1[...] = value[:cut].astype(BF16)
+    send1[:cut] = value[:cut].astype(BF16)
+    send1[cut] = (sent[half].astype(F32) + got[half].astype(F32)).astype(BF16)
     send2[...] = value[cut:].astype(BF16)
 
 
-def node_sum_kernel(s_own, s_got, sums, a2, scal):
+def node_sum_kernel(s_own, s_got, sent, got, sums, a2, scal):
     columns = a2.shape[1]
-    sums[:, :columns] = (s_own[:, :columns].astype(F32) + s_got[:, :columns].astype(F32)).astype(BF16)
-    a2[...] = s_own[:, columns : 2 * columns].astype(F32) + s_got[:, columns : 2 * columns].astype(F32)
-    value = unpacked(s_own[:, 2 * columns :]) + unpacked(s_got[:, 2 * columns :])
+    last = sent.shape[0] - 1
+    sums[:, :columns] = (sent[last].astype(F32) + got[last].astype(F32)).astype(BF16)
+    a2[...] = s_own[:, :columns].astype(F32) + s_got[:, :columns].astype(F32)
+    value = unpacked(s_own[:, columns:]) + unpacked(s_got[:, columns:])
     scal[...] = value
     sums[:, columns:] = packed(value)
 
@@ -260,7 +296,7 @@
 
 def third_avg_kernel(total, got1, got2, scal, avg, send):
     quarter = quarter_of()
-    cut = got1.shape[0]
+    cut = total.shape[0] - got2.shape[0]
     for k in range(HALF):
         node = ((k // SHARES) * 2 + quarter % 2) * SHARES + k % SHARES
         got = got1[k] if k < cut else got2[k - cut]
@@ -324,7 +360,7 @@
 
 
 def last_kernel(
-    sol, y_v, s_own, s_got, eta, duals_row, prior,
+    left, right, y_v, s_own, s_got, eta, duals_row, prior,
     out, first_avg, eta_avg, eta_duals, buf, full, row, one, sems, sems2,
 ):
     columns = full.shape[1]
@@ -341,7 +377,7 @@
     ]
     for copy in copies:
         copy.start()
-    copies += write_duals((sol,), y_v, lambda s: full[...], out, buf, sems, 0)
+    copies += write_duals((left, right), y_v, lambda s: full[...], out, buf, sems, 0)
     for copy in copies:
         copy.wait()
 
@@ -369,33 +405,42 @@
     duals_row = eta_duals.reshape(1, scenarios)
     costs, duals, matrix = in_hbm(unit_costs), in_hbm(hour_duals), in_hbm(inverse)
 
-    tail = jnp.pad(prev_second, ((0, 0), (0, 0), (0, columns - columns // 4)))
-    prev = jnp.concatenate((prev_third, tail))
+    prev = call(
+        join_kernel,
+        8,
+        in_specs=[HBM, HBM],
+        out_specs=VMEM,
+        out_shape=pltpu.VMEM((SHARES + 1, length, columns), BF16),
+        scratch_shapes=[dma((2,))],
+    )(in_hbm(prev_third), in_hbm(prev_second))
     y_prev = partner(prev, 2)
-
-    w, sec, y1, c2, y2, c3, y3, inv_v, sol1, a1, mass, pick, cost = call(
+    mean = partner(eta_mean, 0)
+
+    most = columns - columns // CHUNKS
+    w, sec, c1, y1, inv_v, sol1, a_left, mass, pick, cost, target1 = call(
         first_kernel,
         32,
         in_specs=[HBM] * 8,
-        out_specs=[SMEM, SMEM] + [VMEM] * 11,
+        out_specs=[SMEM, SMEM] + [VMEM] * 9,
         out_shape=[
             pltpu.SMEM((scenarios,), jnp.int32),
             pltpu.SMEM((scenarios,), jnp.int32),
-            *[pltpu.VMEM(block, BF16)] * 5,
+            pltpu.VMEM(block, BF16),
+            pltpu.VMEM(block, BF16),
             pltpu.VMEM(inverse.shape, BF16),
-            pltpu.VMEM(block, F32),
-            pltpu.VMEM((length, columns), F32),
+            pltpu.VMEM((scenarios, length, most), F32),
+            pltpu.VMEM((length, most), F32),
             pltpu.VMEM((1, LANES), F32),
             pltpu.VMEM((BRANCH * length, rows), BF16),
             pltpu.VMEM((scenarios, length, LANES), F32),
+            pltpu.VMEM((rows, columns), BF16),
         ],
         scratch_shapes=[
-            pltpu.VMEM(block, BF16),
             pltpu.VMEM((length, columns), BF16),
             pltpu.VMEM((1, scenarios), jnp.int32),
             pltpu.VMEM((1, scenarios), jnp.int32),
-            pltpu.VMEM((rows, columns), BF16),
-            dma((11 + CHUNKS,)),
+            dma((5 + CHUNKS,)),
+            dma((2,)),
         ],
     )(
         in_hbm(weights),
@@ -408,24 +453,42 @@
         matrix,
     )
 
-    y_prev, joined = lax.optimization_barrier((y_prev, (eta_mean, eta_duals)))
-    level_row = jnp.concatenate((joined[1], joined[0])).reshape(1, scenarios + 1)
     core_prev, diag_prev = partner((prev, y_prev), 1)
     pieces = (prev, core_prev, y_prev, diag_prev)
-
-    sol3, cost, keep, send = call(
+    c3, y3, sol1_rest, a_right, cost = call(
+        rest_kernel,
+        30,
+        in_specs=[SMEM] + [VMEM] * 4 + [HBM] * 2,
+        out_specs=[VMEM] * 5,
+        out_shape=[
+            pltpu.VMEM(block, BF16),
+            pltpu.VMEM(block, BF16),
+            pltpu.VMEM((scenarios, length, columns - most), F32),
+            pltpu.VMEM((length, columns - most), F32),
+            pltpu.VMEM((scenarios, length, LANES), F32),
+        ],
+        scratch_shapes=[dma((2,))],
+    )(w, target1, c1, inv_v, cost, costs, duals)
+
+    c2, y2, sol3, cost, keep, send = call(
         third_kernel,
         30,
-        in_specs=[SMEM] + [VMEM] * 9,
-        out_specs=[VMEM] * 4,
-        out_shape=[
+        in_specs=[SMEM] + [VMEM] * 11 + [HBM] * 2,
+        out_specs=[VMEM] * 6,
+        out_shape=[
+            pltpu.VMEM(block, BF16),
+            pltpu.VMEM(block, BF16),
             pltpu.VMEM(block, F32),
             pltpu.VMEM((scenarios, length, LANES), F32),
             pltpu.VMEM((HALF, length, columns), F32),
-            pltpu.VMEM((HALF, length, columns), BF16),
-        ],
-        scratch_shapes=[pltpu.VMEM((rows, columns), BF16), pltpu.VMEM((BRANCH, length, columns), BF16)],
-    )(sec, *pieces, c3, y3, inv_v, pick, cost)
+            pltpu.VMEM((HALF + 1, length, columns), BF16),
+        ],
+        scratch_shapes=[
+            pltpu.VMEM((rows, columns), BF16),
+            pltpu.VMEM((BRANCH, length, columns), BF16),
+            dma((2,)),
+        ],
+    )(sec, *pieces, c3, y3, inv_v, pick, cost, a_left, a_right, costs, duals)
 
     chip_got = partner(send, 1)
     half_block = (scenarios, length, columns // 2)
@@ -446,14 +509,14 @@
     chip_total, chip_send1, chip_send2 = call(
         chip_sum_kernel,
         8,
-        in_specs=[VMEM] * 2,
+        in_specs=[VMEM] * 3,
         out_specs=[VMEM] * 3,
         out_shape=[
             pltpu.VMEM((HALF, length, columns), F32),
-            pltpu.VMEM((cut, length, columns), BF16),
+            pltpu.VMEM((cut + 1, length, columns), BF16),
             pltpu.VMEM((HALF - cut, length, columns), BF16),
         ],
-    )(keep, chip_got)
+    )(keep, send, chip_got)
     node_got1 = partner(chip_send1, 2)
 
     right, eta, sums = call(
@@ -464,10 +527,10 @@
         out_shape=[
             pltpu.VMEM(half_block, F32),
             pltpu.VMEM((1, scenarios), F32),
-            pltpu.VMEM((length, 2 * columns + 3 * LANES), BF16),
+            pltpu.VMEM((length, columns + 3 * LANES), BF16),
         ],
         scratch_shapes=[pltpu.VMEM((scenarios, length, LANES), F32)],
-    )(w, w_row, level_row, target2, c2, inv_v, cost, a1, a2, mass)
+    )(w, w_row, mean.reshape(1, 1), duals_row, target2, c2, inv_v, cost, a2, mass)
 
     core_sums = partner(sums, 1)
     sums = call(
@@ -479,10 +542,10 @@
     far, a2, scal = call(
         node_sum_kernel,
         8,
-        in_specs=[VMEM] * 2,
+        in_specs=[VMEM] * 4,
         out_specs=[VMEM] * 3,
         out_shape=[far_shape, pltpu.VMEM((length, columns), F32), pltpu.VMEM((length, LANES), F32)],
-    )(sums, y_sums)
+    )(sums, y_sums, chip_send1, node_got1)
     far_got = partner(far, 4)
     mask = 8
     while mask < nodes:
@@ -524,7 +587,7 @@
     out, first_avg, eta_avg, eta_duals_new = call(
         last_kernel,
         8,
-        in_specs=[VMEM] * 6 + [HBM],
+        in_specs=[VMEM] * 7 + [HBM],
         out_specs=[HBM] * 4,
         out_shape=[
             duals_shape,
@@ -540,8 +603,8 @@
             dma((4,)),
             dma((3,)),
         ],
-        input_output_aliases={6: 0},
-    )(sol1, y1, far, far_got, eta, duals_row, out)
+        input_output_aliases={7: 0},
+    )(sol1, sol1_rest, y1, far, far_got, eta, duals_row, out)
     return out, first_avg, second_avg, third_avg, eta_avg, eta_duals_new.reshape(scenarios)
 
 

time: 43.9 us -> 46 us (1.048)
  Pallas kernels: 16.1 us -> 20.5 us
  waiting for transfers between devices: 12.8 us -> 11.1 us
  starting transfers between devices: 12.3 us -> 13.5 us
  other arithmetic: 1.01 us -> 0 us
  between operations: 1.42 us -> 0.78 us
    pallas_call x4 -> x6, Pallas kernels: 4.48 us -> 7.61 us  [the longest x1 3.18 us: step(): call(third_kernel, 30, in_specs=[SMEM] + [VMEM] * 11 + [HBM] * 2, out_spe...]
    ppermute x11 -> x12, waiting for transfers between devices: 12.8 us -> 11.1 us  [partner(): return lax.ppermute(value, 'node', pairs)]
    ppermute x11 -> x12, starting transfers between devices: 12.3 us -> 13.5 us  [partner(): return lax.ppermute(value, 'node', pairs)]
    concatenate x1 -> x0, other arithmetic: 0.93 us -> none  [step(): prev = jnp.concatenate((prev_third, tail))]
    pallas_call x1, Pallas kernels: 5.55 us -> 6.26 us  [step(): call(first_kernel, 32, in_specs=[HBM] * 8, out_specs=[SMEM, SMEM] + [VMEM...]
    pallas_call x1, Pallas kernels: 1.62 us -> 2.18 us  [step(): call(right_kernel, 30, in_specs=[SMEM] + [VMEM] * 9, out_specs=[VMEM] * 3...]
  transfers between devices with their start and end apart: 11 -> 12, of which waited for: 3 -> 5; matrix products, arithmetic and copies ran while one was open for 0% -> 0% of each run, Pallas kernels for 27% -> 33%
where the time goes in v5:
time: 46 us; the launch traced here: 45.9 us
  Pallas kernels  20.5 us (45%)
  starting transfers between devices  13.5 us (29%)
  waiting for transfers between devices  11.1 us (24%)
  between operations  0.78 us (2%)
    ppermute x12, starting transfers between devices, partner(): return lax.ppermute(value, 'node', pairs)  13.5 us
    ppermute x12, waiting for transfers between devices, partner(): return lax.ppermute(value, 'node', pairs)  11.1 us
    pallas_call x1, Pallas kernels, step(): call(first_kernel, 32, in_specs=[HBM] * 8, out_specs=[SMEM, SMEM] + [VMEM...  6.26 us
    pallas_call x1, Pallas kernels, step(): call(third_kernel, 30, in_specs=[SMEM] + [VMEM] * 11 + [HBM] * 2, out_spe...  3.18 us
    pallas_call x1, Pallas kernels, step(): call(rest_kernel, 30, in_specs=[SMEM] + [VMEM] * 4 + [HBM] * 2, out_specs...  2.21 us
    pallas_call x1, Pallas kernels, step(): call(right_kernel, 30, in_specs=[SMEM] + [VMEM] * 9, out_specs=[VMEM] * 3...  2.18 us
    pallas_call x1, Pallas kernels, step(): call(left_kernel, 30, in_specs=[SMEM] + [VMEM] * 8, out_specs=[VMEM] * 4,...  1.66 us
    pallas_call x1, Pallas kernels, step(): call(third_duals_kernel, 8, in_specs=[SMEM] + [VMEM] * 4 + [HBM], out_spe...  1.41 us
  transfers between devices with their start and end apart: 12, of which 5 were waited for; matrix products, arithmetic and copies ran while one was open for 0% of the time, Pallas kernels for 33%

profile of v5, /device:TPU:0, one launch (start us, length us, event | category | flops | bytes accessed | tf_op | source)
XLA Modules:
  0.0 45.9 jit_solution(12844298200906416783)
XLA Ops:
  0.6 0.9 %shard_map.147.p0 = bf16[5,8,2048]{2,1,0:T(8,128)(2,1)S(1)} custom-call(bf16[4,8,2048]{2,1,0:T(8,128)(2,1)} %third.1, bf16[1,8,512]{2,1,0:T(8,128)(2,1)} %second.1), custom_call_target="tpu_custom_call" | custom-call | tf_op jit(solution)/shard_map/pallas_call | solution.py:408
  1.6 3.1 %collective-permute-start.2 = (bf16[5,8,2048]{2,1,0:T(8,128)(2,1)S(1)}, bf16[5,8,2048]{2,1,0:T(8,128)(2,1)S(1)}, u32[]{:S(2)}, u32[]{:S(2)}) collective-permute-start(bf16[5,8,2048]{2,1,0:T(8,128)(2,1)S(1)} %shard_map.147.p0), channel_id=1, source_target_pairs={{0,2},{1,3},{2,0},{3,1},{4,6},{5,7},{6,4},{7,5},{8,10},{9,11},{10,... | collective-permute-start | bytes 491528 | tf_op jit(solution)/shard_map/ppermute | solution.py:27
  4.6 0.0 collective-permute-start.1
  4.6 4.2 %collective-permute-done.2.p2 = bf16[5,8,2048]{2,1,0:T(8,128)(2,1)S(1)} collective-permute-done((bf16[5,8,2048]{2,1,0:T(8,128)(2,1)S(1)}, bf16[5,8,2048]{2,1,0:T(8,128)(2,1)S(1)}, u32[]{:S(2)}, u32[]{:S(2)}) %collective-permute-start.2) | collective-permute-done | bytes 163872 | tf_op jit(solution)/shard_map/ppermute | solution.py:27
  8.8 0.0 collective-permute-start.3
  8.8 6.3 %shard_map.145 = (s32[32]{0:T(128)S(4)}, s32[32]{0:T(128)S(4)}, bf16[32,8,2048]{2,1,0:T(8,128)(2,1)S(1)}, bf16[32,8,2048]{2,1,0:T(8,128)(2,1)S(1)}, bf16[2048,20...) custom-call(s32[32]{0:T(128)} %w_hbm.1, ...), custom_call_target="tpu_custom_call" | custom-call | tf_op jit(solution)/shard_map/pallas_call | solution.py:420
  15.1 2.2 %shard_map.146 = (bf16[32,8,2048]{2,1,0:T(8,128)(2,1)S(1)}, bf16[32,8,2048]{2,1,0:T(8,128)(2,1)S(1)}, f32[32,8,512]{2,1,0:T(8,128)S(1)}, f32[8,512]{1,0:T(8,128)S(1)}, f32[32,8,128]{2,1,0:T(8,128)S(1)}) custom-call(s32[32]{0:T(128)S(4)} %get-tuple-element.52.w, bf16[256,2048]{1,0:T(8,128)(2,1)S(1)} %get-tuple-element.53.target, ...), custom_call_target="tpu_custom_call" | custom-call | tf_op jit(solution)/shard_map/pallas_call | solution.py:458
  17.3 0.0 collective-permute-done.1.p1
  17.3 0.0 collective-permute-done.3.p3
  17.3 3.2 %shard_map.148 = (bf16[32,8,2048]{2,1,0:T(8,128)(2,1)S(1)}, bf16[32,8,2048]{2,1,0:T(8,128)(2,1)S(1)}, f32[32,8,2048]{2,1,0:T(8,128)S(1)}, f32[32,8,128]{2,1,0:T(...) custom-call(s32[32]{0:T(128)S(4)} %get-tuple-element.59.sec, ...), custom_call_target="tpu_custom_call" | custom-call | tf_op jit(solution)/shard_map/pallas_call | solution.py:473
  20.5 0.6 %collective-permute-start.6 = (bf16[9,8,2048]{2,1,0:T(8,128)(2,1)S(1)}, bf16[9,8,2048]{2,1,0:T(8,128)(2,1)S(1)}, u32[]{:S(2)}, u32[]{:S(2)}) collective-permute-start(bf16[9,8,2048]{2,1,0:T(8,128)(2,1)S(1)} %get-tuple-element.75.sent), channel_id=1, source_target_pairs={{0,1},{1,0},{2,3},{3,2},{4,5},{5,4},{6,7},{7,6},{8,9},{9,8},{10,11... | collective-permute-start | bytes 884744 | tf_op jit(solution)/shard_map/ppermute | solution.py:27
  21.1 1.2 %collective-permute-done.6.got = bf16[9,8,2048]{2,1,0:T(8,128)(2,1)S(1)} collective-permute-done((bf16[9,8,2048]{2,1,0:T(8,128)(2,1)S(1)}, bf16[9,8,2048]{2,1,0:T(8,128)(2,1)S(1)}, u32[]{:S(2)}, u32[]{:S(2)}) %collective-permute-start.6) | collective-permute-done | bytes 294944 | tf_op jit(solution)/shard_map/ppermute | solution.py:27
  22.3 0.1 shard_map.152
  22.4 1.8 %collective-permute-start.7 = (bf16[5,8,2048]{2,1,0:T(8,128)(2,1)S(1)}, bf16[5,8,2048]{2,1,0:T(8,128)(2,1)S(1)}, u32[]{:S(2)}, u32[]{:S(2)}) collective-permute-start(bf16[5,8,2048]{2,1,0:T(8,128)(2,1)S(1)} %get-tuple-element.76.sent), channel_id=1, source_target_pairs={{0,2},{1,3},{2,0},{3,1},{4,6},{5,7},{6,4},{7,5},{8,10},{9,11},{10,... | collective-permute-start | bytes 491528 | tf_op jit(solution)/shard_map/ppermute | solution.py:27
  24.2 0.3 collective-permute-start.10
  24.5 1.2 %collective-permute-start = (f32[1]{0:T(128)}, f32[1]{0:T(128)}, u32[]{:S(2)}, u32[]{:S(2)}) collective-permute-start(f32[1]{0:T(128)} %param.18), channel_id=1, source_target_pairs={{0,0},{1,1},{2,2},{3,3},{4,4},{5,5},{6,6},{7,7},{8,8},{9,9},{10,10... | collective-permute-start | bytes 20 | tf_op jit(solution)/shard_map/ppermute | solution.py:27
  25.6 0.0 copy-start
  25.7 0.0 copy-start.1
  25.7 1.7 %shard_map.149 = (bf16[256,2048]{1,0:T(8,128)(2,1)S(1)}, f32[32,8,1024]{2,1,0:T(8,128)S(1)}, f32[8,1024]{1,0:T(8,128)S(1)}, f32[32,8,128]{2,1,0:T(8,128)S(1)}) custom-call(s32[32]{0:T(128)S(4)} %get-tuple-element.52.w, bf16[5,8,2048]{2,1,0:T(8,128)(2,1)S(1)} %shard_map.147.p0, bf16[5,8,2048]{2,1,0:T(8,128)(2,1)S(1)} %collective-permute-done.1.p1, ...), custom_call_target="tpu_custom_call" | custom-call | tf_op jit(solution)/shard_map/pallas_call | solution.py:495
  27.3 0.0 collective-permute-done
  27.3 0.0 copy-done
  27.3 0.0 copy-done.1
  27.4 2.2 %shard_map.150 = (f32[32,8,1024]{2,1,0:T(8,128)S(1)}, f32[1,32]{1,0:T(1,128)S(1)}, bf16[8,2432]{1,0:T(8,128)(2,1)S(1)}) custom-call(s32[32]{0:T(128)S(4)} %get-tuple-element.52.w, s32[1,32]{1,0:T(1,128)S(1)} %bitcast.6, f32[1,1]{1,0:T(1,128)} %bitcast.2.mean, f32[1,32]{1,0:T(1,128)S(1)} %bitcast.7, bf16[256,2048]{1,0:T(8,128)(2,1)S(1)} %get-tuple-element.69.target, ...), custom_call_target="tpu_custom_call" | custom-call | tf_op jit(solution)/shard_map/pallas_call | solution.py:522
  29.5 0.0 collective-permute-start.4
  29.5 1.2 %collective-permute-done.4.s_got = bf16[8,2432]{1,0:T(8,128)(2,1)S(1)} collective-permute-done((bf16[8,2432]{1,0:T(8,128)(2,1)S(1)}, bf16[8,2432]{1,0:T(8,128)(2,1)S(1)}, u32[]{:S(2)}, u32[]{:S(2)}) %collective-permute-start.4) | collective-permute-done | bytes 38944 | tf_op jit(solution)/shard_map/ppermute | solution.py:27
  30.8 1.8 %collective-permute-start.5 = (bf16[8,2432]{1,0:T(8,128)(2,1)S(1)}, bf16[8,2432]{1,0:T(8,128)(2,1)S(1)}, u32[]{:S(2)}, u32[]{:S(2)}) collective-permute-start(bf16[8,2432]{1,0:T(8,128)(2,1)S(1)} %shard_map.151.s_own), channel_id=1, source_target_pairs={{0,2},{1,3},{2,0},{3,1},{4,6},{5,7},{6,4},{7,5},{8,10},{9,11},{10,... | collective-permute-start | bytes 116744 | tf_op jit(solution)/shard_map/ppermute | solution.py:27
  32.6 2.2 %collective-permute-done.5.s_got = bf16[8,2432]{1,0:T(8,128)(2,1)S(1)} collective-permute-done((bf16[8,2432]{1,0:T(8,128)(2,1)S(1)}, bf16[8,2432]{1,0:T(8,128)(2,1)S(1)}, u32[]{:S(2)}, u32[]{:S(2)}) %collective-permute-start.5) | collective-permute-done | bytes 38944 | tf_op jit(solution)/shard_map/ppermute | solution.py:27
  34.8 0.0 collective-permute-done.7.got.got1
  34.9 0.0 collective-permute-done.10.got2
  34.9 0.2 shard_map.155
  35.0 0.1 collective-permute-start.11
  35.1 1.9 %collective-permute-start.8 = (bf16[8,2432]{1,0:T(8,128)(2,1)S(1)}, bf16[8,2432]{1,0:T(8,128)(2,1)S(1)}, u32[]{:S(2)}, u32[]{:S(2)}) collective-permute-start(bf16[8,2432]{1,0:T(8,128)(2,1)S(1)} %get-tuple-element.77.s_own), channel_id=1, source_target_pairs={{0,4},{1,5},{2,6},{3,7},{4,0},{5,1},{6,2},{7,3},{8,12},{9,13},{10,... | collective-permute-start | bytes 116744 | tf_op jit(solution)/shard_map/ppermute | solution.py:27
  37.0 2.2 %collective-permute-done.8.s_got = bf16[8,2432]{1,0:T(8,128)(2,1)S(1)} collective-permute-done((bf16[8,2432]{1,0:T(8,128)(2,1)S(1)}, bf16[8,2432]{1,0:T(8,128)(2,1)S(1)}, u32[]{:S(2)}, u32[]{:S(2)}) %collective-permute-start.8) | collective-permute-done | bytes 38944 | tf_op jit(solution)/shard_map/ppermute | solution.py:27
  39.2 2.9 %collective-permute-start.9 = (bf16[8,2432]{1,0:T(8,128)(2,1)S(1)}, bf16[8,2432]{1,0:T(8,128)(2,1)S(1)}, u32[]{:S(2)}, u32[]{:S(2)}) collective-permute-start(bf16[8,2432]{1,0:T(8,128)(2,1)S(1)} %shard_map.154.s_own), channel_id=1, source_target_pairs={{0,8},{1,9},{2,10},{3,11},{4,12},{5,13},{6,14},{7,15},{8,0},{9,1},... | collective-permute-start | bytes 116744 | tf_op jit(solution)/shard_map/ppermute | solution.py:27
  42.0 1.2 %shard_map.156 = (bf16[32,24,2048]{2,1,0:T(8,128)(2,1)}, f32[1,8,512]{2,1,0:T(8,128)}) custom-call(f32[32,8,1024]{2,1,0:T(8,128)S(1)} %get-tuple-element.85.left, f32[32,8,1024]{2,1,0:T(8,128)S(1)} %get-tuple-element.86.right, bf16[32,8,2048]{2,1,0:T(8,128)(2,1)S(1)} %get-tuple-element.67.y_v, f32[8,2048]{1,0:T(8,128)S(1)} %get-tuple-element.87.a2, ...), custom_call_target="tpu_custom_call" | custom-call | tf_op jit(solution)/shard_map/pallas_call | solution.py:558
  43.2 0.0 collective-permute-done.11.got
  43.2 1.4 %shard_map.157 = (bf16[32,24,2048]{2,1,0:T(8,128)(2,1)}, f32[4,8,2048]{2,1,0:T(8,128)}) custom-call(s32[32]{0:T(128)S(4)} %get-tuple-element.59.sec, f32[32,8,2048]{2,1,0:T(8,128)S(1)} %get-tuple-element.79.sol, bf16[32,8,2048]{2,1,0:T(8,128)(2,1)S(1)} %get-tuple-element.61.y_v, ...), custom_call_target="tpu_custom_call", output_to_operand_aliasing={{0}: (5, {})} | custom-call | tf_op jit(solution)/shard_map/pallas_call | solution.py:578
  44.7 0.0 collective-permute-done.9.s_got
  44.7 1.2 %shard_map.158 = (bf16[32,24,2048]{2,1,0:T(8,128)(2,1)}, f32[8,2048]{1,0:T(8,128)}, f32[1]{0:T(128)}, f32[1,32]{1,0:T(1,128)}) custom-call(f32[32,8,1536]{2,1,0:T(8,128)S(1)} %get-tuple-element.51.left, f32[32,8,512]{2,1,0:T(8,128)S(1)} %get-tuple-element.57.right, bf16[32,8,2048]{2,1,0:T(8,128)(2,1)S(1)} %get-tuple-element.58.y_v, ...), custom_call_target="tpu_custom_call", output_to_operand_aliasing={{0}: (7, {})} | custom-call | tf_op jit(solution)/shard_map/pallas_call | solution.py:587
  (3 shorter events, 0.1 us)
Async XLA Ops:
  1.6 7.3 %collective-permute-start.2 = (bf16[5,8,2048]{2,1,0:T(8,128)(2,1)S(1)}, bf16[5,8,2048]{2,1,0:T(8,128)(2,1)S(1)}, u32[]{:S(2)}, u32[]{:S(2)}) collective-permute-start(bf16[5,8,2048]{2,1,0:T(8,128)(2,1)S(1)} %shard_map.147.p0), channel_id=1, source_target_pairs={{0,2},{1,3},{2,0},{3,1},{4,6},{5,7},{6,4},{7,5},{8,10},{9,11},{10,... | collective-permute-start | bytes 491528 | tf_op jit(solution)/shard_map/ppermute | solution.py:27
  4.6 12.7 %collective-permute-start.1 = (bf16[5,8,2048]{2,1,0:T(8,128)(2,1)S(1)}, bf16[5,8,2048]{2,1,0:T(8,128)(2,1)S(1)}, u32[]{:S(2)}, u32[]{:S(2)}) collective-permute-start(bf16[5,8,2048]{2,1,0:T(8,128)(2,1)S(1)} %shard_map.147.p0), channel_id=1, source_target_pairs={{0,1},{1,0},{2,3},{3,2},{4,5},{5,4},{6,7},{7,6},{8,9},{9,8},{10,11... | collective-permute-start | bytes 491528 | tf_op jit(solution)/shard_map/ppermute | solution.py:27
  8.8 8.5 %collective-permute-start.3 = (bf16[5,8,2048]{2,1,0:T(8,128)(2,1)S(1)}, bf16[5,8,2048]{2,1,0:T(8,128)(2,1)S(1)}, u32[]{:S(2)}, u32[]{:S(2)}) collective-permute-start(bf16[5,8,2048]{2,1,0:T(8,128)(2,1)S(1)} %collective-permute-done.2.p2), channel_id=1, source_target_pairs={{0,1},{1,0},{2,3},{3,2},{4,5},{5,4},{6,7},{7,6},{8,9},{9,8},{10,11... | collective-permute-start | bytes 491528 | tf_op jit(solution)/shard_map/ppermute | solution.py:27
  20.5 1.8 %collective-permute-start.6 = (bf16[9,8,2048]{2,1,0:T(8,128)(2,1)S(1)}, bf16[9,8,2048]{2,1,0:T(8,128)(2,1)S(1)}, u32[]{:S(2)}, u32[]{:S(2)}) collective-permute-start(bf16[9,8,2048]{2,1,0:T(8,128)(2,1)S(1)} %get-tuple-element.75.sent), channel_id=1, source_target_pairs={{0,1},{1,0},{2,3},{3,2},{4,5},{5,4},{6,7},{7,6},{8,9},{9,8},{10,11... | collective-permute-start | bytes 884744 | tf_op jit(solution)/shard_map/ppermute | solution.py:27
  22.4 12.4 %collective-permute-start.7 = (bf16[5,8,2048]{2,1,0:T(8,128)(2,1)S(1)}, bf16[5,8,2048]{2,1,0:T(8,128)(2,1)S(1)}, u32[]{:S(2)}, u32[]{:S(2)}) collective-permute-start(bf16[5,8,2048]{2,1,0:T(8,128)(2,1)S(1)} %get-tuple-element.76.sent), channel_id=1, source_target_pairs={{0,2},{1,3},{2,0},{3,1},{4,6},{5,7},{6,4},{7,5},{8,10},{9,11},{10,... | collective-permute-start | bytes 491528 | tf_op jit(solution)/shard_map/ppermute | solution.py:27
  24.2 10.7 %collective-permute-start.10 = (bf16[4,8,2048]{2,1,0:T(8,128)(2,1)S(1)}, bf16[4,8,2048]{2,1,0:T(8,128)(2,1)S(1)}, u32[]{:S(2)}, u32[]{:S(2)}) collective-permute-start(bf16[4,8,2048]{2,1,0:T(8,128)(2,1)S(1)} %get-tuple-element.81), channel_id=1, source_target_pairs={{0,2},{1,3},{2,0},{3,1},{4,6},{5,7},{6,4},{7,5},{8,10},{9,11},{10,... | collective-permute-start | bytes 393224 | tf_op jit(solution)/shard_map/ppermute | solution.py:27
  24.5 2.9 %collective-permute-start = (f32[1]{0:T(128)}, f32[1]{0:T(128)}, u32[]{:S(2)}, u32[]{:S(2)}) collective-permute-start(f32[1]{0:T(128)} %param.18), channel_id=1, source_target_pairs={{0,0},{1,1},{2,2},{3,3},{4,4},{5,5},{6,6},{7,7},{8,8},{9,9},{10,10... | collective-permute-start | bytes 20 | tf_op jit(solution)/shard_map/ppermute | solution.py:27
  25.6 1.7 %copy-start = (s32[32]{0:T(128)S(1)}, s32[32]{0:T(128)}, u32[]{:S(2)}) copy-start(s32[32]{0:T(128)} %w_hbm.1) | copy-start | bytes 388
  25.7 1.7 %copy-start.1 = (f32[32]{0:T(128)S(1)}, f32[32]{0:T(128)}, u32[]{:S(2)}) copy-start(f32[32]{0:T(128)} %param.19) | copy-start | bytes 388
  29.5 1.2 %collective-permute-start.4 = (bf16[8,2432]{1,0:T(8,128)(2,1)S(1)}, bf16[8,2432]{1,0:T(8,128)(2,1)S(1)}, u32[]{:S(2)}, u32[]{:S(2)}) collective-permute-start(bf16[8,2432]{1,0:T(8,128)(2,1)S(1)} %get-tuple-element.73.s_own), channel_id=1, source_target_pairs={{0,1},{1,0},{2,3},{3,2},{4,5},{5,4},{6,7},{7,6},{8,9},{9,8},{10,11... | collective-permute-start | bytes 116744 | tf_op jit(solution)/shard_map/ppermute | solution.py:27
  30.8 4.0 %collective-permute-start.5 = (bf16[8,2432]{1,0:T(8,128)(2,1)S(1)}, bf16[8,2432]{1,0:T(8,128)(2,1)S(1)}, u32[]{:S(2)}, u32[]{:S(2)}) collective-permute-start(bf16[8,2432]{1,0:T(8,128)(2,1)S(1)} %shard_map.151.s_own), channel_id=1, source_target_pairs={{0,2},{1,3},{2,0},{3,1},{4,6},{5,7},{6,4},{7,5},{8,10},{9,11},{10,... | collective-permute-start | bytes 116744 | tf_op jit(solution)/shard_map/ppermute | solution.py:27
  35.0 8.2 %collective-permute-start.11 = (bf16[8,8,2048]{2,1,0:T(8,128)(2,1)S(1)}, bf16[8,8,2048]{2,1,0:T(8,128)(2,1)S(1)}, u32[]{:S(2)}, u32[]{:S(2)}) collective-permute-start(bf16[8,8,2048]{2,1,0:T(8,128)(2,1)S(1)} %get-tuple-element.84), channel_id=1, source_target_pairs={{0,1},{1,0},{2,3},{3,2},{4,5},{5,4},{6,7},{7,6},{8,9},{9,8},{10,11... | collective-permute-start | bytes 786440 | tf_op jit(solution)/shard_map/ppermute | solution.py:27
  35.1 4.0 %collective-permute-start.8 = (bf16[8,2432]{1,0:T(8,128)(2,1)S(1)}, bf16[8,2432]{1,0:T(8,128)(2,1)S(1)}, u32[]{:S(2)}, u32[]{:S(2)}) collective-permute-start(bf16[8,2432]{1,0:T(8,128)(2,1)S(1)} %get-tuple-element.77.s_own), channel_id=1, source_target_pairs={{0,4},{1,5},{2,6},{3,7},{4,0},{5,1},{6,2},{7,3},{8,12},{9,13},{10,... | collective-permute-start | bytes 116744 | tf_op jit(solution)/shard_map/ppermute | solution.py:27
  39.2 5.5 %collective-permute-start.9 = (bf16[8,2432]{1,0:T(8,128)(2,1)S(1)}, bf16[8,2432]{1,0:T(8,128)(2,1)S(1)}, u32[]{:S(2)}, u32[]{:S(2)}) collective-permute-start(bf16[8,2432]{1,0:T(8,128)(2,1)S(1)} %shard_map.154.s_own), channel_id=1, source_target_pairs={{0,8},{1,9},{2,10},{3,11},{4,12},{5,13},{6,14},{7,15},{8,0},{9,1},... | collective-permute-start | bytes 116744 | tf_op jit(solution)/shard_map/ppermute | solution.py:27

commit v6 on v4

--- a/solution.py
+++ b/solution.py
@@ -45,18 +45,16 @@
 
 
 def build_target(target, anchor_of, c_v, y_v):
-    scenarios, length, _ = c_v.shape
-
-    def step(i, carry):
-        rows = []
-        for k in range(2):
-            s = 2 * i + k
-            rows.append(PENALTY * anchor_of(s).astype(F32) - c_v[s].astype(F32) - y_v[s].astype(F32))
-        block = jnp.concatenate(rows, axis=0).astype(BF16)
-        target[pl.ds(pl.multiple_of(i * 2 * length, 2 * length), 2 * length), :] = block
-        return carry
-
-    lax.fori_loop(0, scenarios // 2, step, 0, unroll=2)
+    scenarios, length, columns = c_v.shape
+    width = columns // 1
+    for j in range(1):
+        cols = slice(j * width, (j + 1) * width)
+        for i in range(scenarios // 2):
+            rows = [
+                PENALTY * anchor_of(s, cols).astype(F32) - c_v[s, :, cols].astype(F32) - y_v[s, :, cols].astype(F32)
+                for s in (2 * i, 2 * i + 1)
+            ]
+            target[i * 2 * length : (i + 1) * 2 * length, cols] = jnp.concatenate(rows, axis=0).astype(BF16)
 
 
 def multiply(target, inv_v, sol, c_v, cost, before, w, after, start=0):
@@ -142,7 +140,7 @@
 
     for copy in first:
         copy.wait()
-    build_target(target, lambda s: pf[...], c1, y1)
+    build_target(target, lambda s, cols: pf[:, cols], c1, y1)
 
     def after(cols, total):
         a1[:, cols] = total
@@ -171,17 +169,18 @@
 
 
 def third_kernel(
-    sec, p0, p1, p2, p3, c_v, y_v, inv_v, pick, cost_in, sol, cost, keep, send, target, table
+    sec, p0, p1, p2, p3, c_v, y_v, inv_v, pick, cost_in, a1, sol, cost, keep, send, target, table
 ):
     scenarios, length, _ = sol.shape
     quarter = quarter_of()
+    send[HALF] = a1[...].astype(BF16)
     cost[...] = cost_in[...]
     for k, part in enumerate((p0, p1, p2, p3)):
         table[k * SHARES : (k + 1) * SHARES] = part[:SHARES]
 
-    def anchor_of(s):
+    def anchor_of(s, cols):
         node = sec[s] % BRANCH
-        return table[((node // SHARES) ^ quarter) * SHARES + node % SHARES]
+        return table[((node // SHARES) ^ quarter) * SHARES + node % SHARES, :, cols]
 
     build_target(target, anchor_of, c_v, y_v)
 
@@ -190,7 +189,7 @@
         flat = own.reshape(scenarios * length, own.shape[2]).astype(BF16)
         sums = jnp.dot(pick[...], flat, preferred_element_type=F32).reshape(BRANCH, length, own.shape[2])
         keep[:, :, cols] = sums[:HALF]
-        send[:, :, cols] = sums[HALF:].astype(BF16)
+        send[:HALF, :, cols] = sums[HALF:].astype(BF16)
 
     multiply(target, inv_v, sol, c_v, cost, lambda j: None, None, after)
 
@@ -201,7 +200,7 @@
     cost[...] = cost_in[...]
     for k, part in enumerate((p0, p1, p2, p3)):
         table[:, pl.ds(pl.multiple_of((quarter ^ k) * share, share), share)] = part[SHARES, :, :share]
-    build_target(target, lambda s: table[...], c_v, y_v)
+    build_target(target, lambda s, cols: table[:, cols], c_v, y_v)
 
     def after(cols, total):
         a2[:, cols] = total
@@ -209,16 +208,14 @@
     multiply(target, inv_v, sol, c_v, cost, lambda j: None, w, after)
 
 
-def right_kernel(w, w_row, level_row, target, c_v, inv_v, cost_in, a1, a2, mass, sol, eta, sums, cost):
+def right_kernel(w, w_row, level_row, target, c_v, inv_v, cost_in, a2, mass, sol, eta, sums, cost):
     scenarios, length, half = sol.shape
     columns = 2 * half
     cost[...] = cost_in[...]
-    sums[:, :columns] = a1[...].astype(BF16)
-    sums[:, columns : columns + half] = a2[...].astype(BF16)
+    sums[:, :half] = a2[...].astype(BF16)
 
     def after(cols, total):
-        first = columns + half + cols.start
-        sums[:, first : first + cols.stop - cols.start] = total.astype(BF16)
+        sums[:, half + cols.start : half + cols.stop] = total.astype(BF16)
 
     multiply(target, inv_v, sol, c_v, cost, lambda j: None, w, after, half)
     lanes = jnp.sum(cost[...], axis=1)
@@ -232,22 +229,25 @@
     whole = jnp.sum(p, axis=1, keepdims=True)
     row = lax.broadcasted_iota(jnp.int32, (length, LANES), 0)
     scal = jnp.where(row == 0, total, jnp.where(row == 1, whole, jnp.where(row == 2, mass[...], 0.0)))
-    sums[:, 2 * columns :] = packed(scal)
-
-
-def chip_sum_kernel(keep, got, total, send1, send2):
-    cut = send1.shape[0]
-    value = keep[...] + got[...].astype(F32)
+    sums[:, columns:] = packed(scal)
+
+
+def chip_sum_kernel(keep, sent, got, total, send1, send2):
+    half = keep.shape[0]
+    cut = half - send2.shape[0]
+    value = keep[...] + got[:half].astype(F32)
     total[...] = value
-    send1[...] = value[:cut].astype(BF16)
+    send1[:cut] = value[:cut].astype(BF16)
+    send1[cut] = (sent[half].astype(F32) + got[half].astype(F32)).astype(BF16)
     send2[...] = value[cut:].astype(BF16)
 
 
-def node_sum_kernel(s_own, s_got, sums, a2, scal):
+def node_sum_kernel(s_own, s_got, sent, got, sums, a2, scal):
     columns = a2.shape[1]
-    sums[:, :columns] = (s_own[:, :columns].astype(F32) + s_got[:, :columns].astype(F32)).astype(BF16)
-    a2[...] = s_own[:, columns : 2 * columns].astype(F32) + s_got[:, columns : 2 * columns].astype(F32)
-    value = unpacked(s_own[:, 2 * columns :]) + unpacked(s_got[:, 2 * columns :])
+    last = sent.shape[0] - 1
+    sums[:, :columns] = (sent[last].astype(F32) + got[last].astype(F32)).astype(BF16)
+    a2[...] = s_own[:, :columns].astype(F32) + s_got[:, :columns].astype(F32)
+    value = unpacked(s_own[:, columns:]) + unpacked(s_got[:, columns:])
     scal[...] = value
     sums[:, columns:] = packed(value)
 
@@ -260,7 +260,7 @@
 
 def third_avg_kernel(total, got1, got2, scal, avg, send):
     quarter = quarter_of()
-    cut = got1.shape[0]
+    cut = total.shape[0] - got2.shape[0]
     for k in range(HALF):
         node = ((k // SHARES) * 2 + quarter % 2) * SHARES + k % SHARES
         got = got1[k] if k < cut else got2[k - cut]
@@ -416,16 +416,16 @@
     sol3, cost, keep, send = call(
         third_kernel,
         30,
-        in_specs=[SMEM] + [VMEM] * 9,
+        in_specs=[SMEM] + [VMEM] * 10,
         out_specs=[VMEM] * 4,
         out_shape=[
             pltpu.VMEM(block, F32),
             pltpu.VMEM((scenarios, length, LANES), F32),
             pltpu.VMEM((HALF, length, columns), F32),
-            pltpu.VMEM((HALF, length, columns), BF16),
+            pltpu.VMEM((HALF + 1, length, columns), BF16),
         ],
         scratch_shapes=[pltpu.VMEM((rows, columns), BF16), pltpu.VMEM((BRANCH, length, columns), BF16)],
-    )(sec, *pieces, c3, y3, inv_v, pick, cost)
+    )(sec, *pieces, c3, y3, inv_v, pick, cost, a1)
 
     chip_got = partner(send, 1)
     half_block = (scenarios, length, columns // 2)
@@ -446,28 +446,28 @@
     chip_total, chip_send1, chip_send2 = call(
         chip_sum_kernel,
         8,
-        in_specs=[VMEM] * 2,
+        in_specs=[VMEM] * 3,
         out_specs=[VMEM] * 3,
         out_shape=[
             pltpu.VMEM((HALF, length, columns), F32),
-            pltpu.VMEM((cut, length, columns), BF16),
+            pltpu.VMEM((cut + 1, length, columns), BF16),
             pltpu.VMEM((HALF - cut, length, columns), BF16),
         ],
-    )(keep, chip_got)
+    )(keep, send, chip_got)
     node_got1 = partner(chip_send1, 2)
 
     right, eta, sums = call(
         right_kernel,
         30,
-        in_specs=[SMEM] + [VMEM] * 9,
+        in_specs=[SMEM] + [VMEM] * 8,
         out_specs=[VMEM] * 3,
         out_shape=[
             pltpu.VMEM(half_block, F32),
             pltpu.VMEM((1, scenarios), F32),
-            pltpu.VMEM((length, 2 * columns + 3 * LANES), BF16),
+            pltpu.VMEM((length, columns + 3 * LANES), BF16),
         ],
         scratch_shapes=[pltpu.VMEM((scenarios, length, LANES), F32)],
-    )(w, w_row, level_row, target2, c2, inv_v, cost, a1, a2, mass)
+    )(w, w_row, level_row, target2, c2, inv_v, cost, a2, mass)
 
     core_sums = partner(sums, 1)
     sums = call(
@@ -479,10 +479,10 @@
     far, a2, scal = call(
         node_sum_kernel,
         8,
-        in_specs=[VMEM] * 2,
+        in_specs=[VMEM] * 4,
         out_specs=[VMEM] * 3,
         out_shape=[far_shape, pltpu.VMEM((length, columns), F32), pltpu.VMEM((length, LANES), F32)],
-    )(sums, y_sums)
+    )(sums, y_sums, chip_send1, node_got1)
     far_got = partner(far, 4)
     mask = 8
     while mask < nodes:

time: 43.9 us -> 40.9 us (0.932)
  waiting for transfers between devices: 12.8 us -> 10.4 us
  Pallas kernels: 16.1 us -> 15.5 us
    ppermute x11, waiting for transfers between devices: 12.8 us -> 10.4 us  [partner(): return lax.ppermute(value, 'node', pairs)]
  transfers between devices with their start and end apart: 11 -> 11, of which waited for: 3 -> 5; matrix products, arithmetic and copies ran while one was open for 0% -> 0% of each run, Pallas kernels for 27% -> 27%
where the time goes in v6:
time: 40.9 us; the launch traced here: 40.7 us
  Pallas kernels  15.5 us (38%)
  starting transfers between devices  12.3 us (30%)
  waiting for transfers between devices  10.4 us (25%)
  between operations  1.41 us (3%)
  other arithmetic  1.01 us (2%)
    ppermute x11, starting transfers between devices, partner(): return lax.ppermute(value, 'node', pairs)  12.3 us
    ppermute x11, waiting for transfers between devices, partner(): return lax.ppermute(value, 'node', pairs)  10.4 us
    pallas_call x1, Pallas kernels, step(): call(first_kernel, 32, in_specs=[HBM] * 8, out_specs=[SMEM, SMEM] + [VMEM...  5.53 us
    pallas_call x1, Pallas kernels, step(): call(third_kernel, 30, in_specs=[SMEM] + [VMEM] * 10, out_specs=[VMEM] *...  2.92 us
    pallas_call x1, Pallas kernels, step(): call(right_kernel, 30, in_specs=[SMEM] + [VMEM] * 8, out_specs=[VMEM] * 3...  1.59 us
    pallas_call x1, Pallas kernels, step(): call(third_duals_kernel, 8, in_specs=[SMEM] + [VMEM] * 4 + [HBM], out_spe...  1.41 us
    pallas_call x1, Pallas kernels, step(): call(left_kernel, 30, in_specs=[SMEM] + [VMEM] * 8, out_specs=[VMEM] * 4,...  1.38 us
    pallas_call x1, Pallas kernels, step(): call(last_kernel, 8, in_specs=[VMEM] * 6 + [HBM], out_specs=[HBM] * 4, ou...  1.18 us
  transfers between devices with their start and end apart: 11, of which 5 were waited for; matrix products, arithmetic and copies ran while one was open for 0% of the time, Pallas kernels for 27%

profile of v6, /device:TPU:0, one launch (start us, length us, event | category | flops | bytes accessed | tf_op | source)
XLA Modules:
  0.0 40.7 jit_solution(5262932461470123676)
XLA Ops:
  0.6 0.9 %fusion.1.p0 = bf16[5,8,2048]{2,1,0:T(8,128)(2,1)S(1)} fusion(bf16[1,8,512]{2,1,0:T(8,128)(2,1)} %param.16, bf16[4,8,2048]{2,1,0:T(8,128)(2,1)} %param.17), kind=kLoop, calls=%fused_computation.2 | loop fusion | flops 491520 | bytes 303104 | tf_op jit(solution)/shard_map/concatenate | solution.py:373
  1.6 3.1 %collective-permute-start = (bf16[5,8,2048]{2,1,0:T(8,128)(2,1)S(1)}, bf16[5,8,2048]{2,1,0:T(8,128)(2,1)S(1)}, u32[]{:S(2)}, u32[]{:S(2)}) collective-permute-start(bf16[5,8,2048]{2,1,0:T(8,128)(2,1)S(1)} %fusion.1.p0), channel_id=1, source_target_pairs={{0,2},{1,3},{2,0},{3,1},{4,6},{5,7},{6,4},{7,5},{8,10},{9,11},{10,... | collective-permute-start | bytes 491528 | tf_op jit(solution)/shard_map/ppermute | solution.py:27
  4.6 0.0 collective-permute-start.1
  4.6 4.2 %collective-permute-done.p2 = bf16[5,8,2048]{2,1,0:T(8,128)(2,1)S(1)} collective-permute-done((bf16[5,8,2048]{2,1,0:T(8,128)(2,1)S(1)}, bf16[5,8,2048]{2,1,0:T(8,128)(2,1)S(1)}, u32[]{:S(2)}, u32[]{:S(2)}) %collective-permute-start) | collective-permute-done | bytes 163872 | tf_op jit(solution)/shard_map/ppermute | solution.py:27
  8.8 0.0 collective-permute-start.2
  8.8 5.5 %shard_map.145 = (s32[32]{0:T(128)S(4)}, s32[32]{0:T(128)S(4)}, bf16[32,8,2048]{2,1,0:T(8,128)(2,1)S(1)}, bf16[32,8,2048]{2,1,0:T(8,128)(2,1)S(1)}, bf16[32,8,20...) custom-call(s32[32]{0:T(128)} %w_hbm.1, ...), custom_call_target="tpu_custom_call" | custom-call | tf_op jit(solution)/shard_map/pallas_call | solution.py:376
  14.4 0.0 collective-permute-done.1.p1
  14.4 0.0 collective-permute-done.2.p3
  14.4 0.0 copy-start.1
  14.4 2.9 %shard_map.146 = (f32[32,8,2048]{2,1,0:T(8,128)S(1)}, f32[32,8,128]{2,1,0:T(8,128)S(1)}, f32[8,8,2048]{2,1,0:T(8,128)S(1)}, bf16[9,8,2048]{2,1,0:T(8,128)(2,1)S(1)}) custom-call(s32[32]{0:T(128)S(4)} %get-tuple-element.58.sec, bf16[5,8,2048]{2,1,0:T(8,128)(2,1)S(1)} %fusion.1.p0, bf16[5,8,2048]{2,1,0:T(8,128)(2,1)S(1)} %collective-permute-done.1.p1, ...), custom_call_target="tpu_custom_call" | custom-call | tf_op jit(solution)/shard_map/pallas_call | solution.py:416
  17.3 0.6 %collective-permute-start.5 = (bf16[9,8,2048]{2,1,0:T(8,128)(2,1)S(1)}, bf16[9,8,2048]{2,1,0:T(8,128)(2,1)S(1)}, u32[]{:S(2)}, u32[]{:S(2)}) collective-permute-start(bf16[9,8,2048]{2,1,0:T(8,128)(2,1)S(1)} %get-tuple-element.71.sent), channel_id=1, source_target_pairs={{0,1},{1,0},{2,3},{3,2},{4,5},{5,4},{6,7},{7,6},{8,9},{9,8},{10,11... | collective-permute-start | bytes 884744 | tf_op jit(solution)/shard_map/ppermute | solution.py:27
  18.6 0.6 %collective-permute-done.5.got = bf16[9,8,2048]{2,1,0:T(8,128)(2,1)S(1)} collective-permute-done((bf16[9,8,2048]{2,1,0:T(8,128)(2,1)S(1)}, bf16[9,8,2048]{2,1,0:T(8,128)(2,1)S(1)}, u32[]{:S(2)}, u32[]{:S(2)}) %collective-permute-start.5) | collective-permute-done | bytes 294944 | tf_op jit(solution)/shard_map/ppermute | solution.py:27
  19.1 0.1 shard_map.150
  19.2 1.8 %collective-permute-start.6 = (bf16[5,8,2048]{2,1,0:T(8,128)(2,1)S(1)}, bf16[5,8,2048]{2,1,0:T(8,128)(2,1)S(1)}, u32[]{:S(2)}, u32[]{:S(2)}) collective-permute-start(bf16[5,8,2048]{2,1,0:T(8,128)(2,1)S(1)} %get-tuple-element.72.sent), channel_id=1, source_target_pairs={{0,2},{1,3},{2,0},{3,1},{4,6},{5,7},{6,4},{7,5},{8,10},{9,11},{10,... | collective-permute-start | bytes 491528 | tf_op jit(solution)/shard_map/ppermute | solution.py:27
  21.0 0.3 collective-permute-start.9
  21.3 0.0 copy-done.1
  21.3 0.1 maximum_bitcast_fusion.level_row
  21.4 0.0 copy-start
  21.4 1.4 %shard_map.147 = (bf16[256,2048]{1,0:T(8,128)(2,1)S(1)}, f32[32,8,1024]{2,1,0:T(8,128)S(1)}, f32[8,1024]{1,0:T(8,128)S(1)}, f32[32,8,128]{2,1,0:T(8,128)S(1)}) custom-call(s32[32]{0:T(128)S(4)} %get-tuple-element.51.w, bf16[5,8,2048]{2,1,0:T(8,128)(2,1)S(1)} %fusion.1.p0, bf16[5,8,2048]{2,1,0:T(8,128)(2,1)S(1)} %collective-permute-done.1.p1, ...), custom_call_target="tpu_custom_call" | custom-call | tf_op jit(solution)/shard_map/pallas_call | solution.py:432
  22.8 0.0 copy-done
  22.8 1.6 %shard_map.148 = (f32[32,8,1024]{2,1,0:T(8,128)S(1)}, f32[1,32]{1,0:T(1,128)S(1)}, bf16[8,2432]{1,0:T(8,128)(2,1)S(1)}) custom-call(s32[32]{0:T(128)S(4)} %get-tuple-element.51.w, s32[1,32]{1,0:T(1,128)S(1)} %bitcast.7, f32[1,33]{1,0:T(1,128)S(1)} %maximum_bitcast_fusion.level_row, bf16[256,2048]{1,0:T(8,128)(2,1)S(1)} %get-tuple-element.65.target, ...), custom_call_target="tpu_custom_call" | custom-call | tf_op jit(solution)/shard_map/pallas_call | solution.py:459
  24.4 0.0 collective-permute-start.3
  24.4 1.2 %collective-permute-done.3.s_got = bf16[8,2432]{1,0:T(8,128)(2,1)S(1)} collective-permute-done((bf16[8,2432]{1,0:T(8,128)(2,1)S(1)}, bf16[8,2432]{1,0:T(8,128)(2,1)S(1)}, u32[]{:S(2)}, u32[]{:S(2)}) %collective-permute-start.3) | collective-permute-done | bytes 38944 | tf_op jit(solution)/shard_map/ppermute | solution.py:27
  25.6 1.8 %collective-permute-start.4 = (bf16[8,2432]{1,0:T(8,128)(2,1)S(1)}, bf16[8,2432]{1,0:T(8,128)(2,1)S(1)}, u32[]{:S(2)}, u32[]{:S(2)}) collective-permute-start(bf16[8,2432]{1,0:T(8,128)(2,1)S(1)} %shard_map.149.s_own), channel_id=1, source_target_pairs={{0,2},{1,3},{2,0},{3,1},{4,6},{5,7},{6,4},{7,5},{8,10},{9,11},{10,... | collective-permute-start | bytes 116744 | tf_op jit(solution)/shard_map/ppermute | solution.py:27
  27.4 2.2 %collective-permute-done.4.s_got = bf16[8,2432]{1,0:T(8,128)(2,1)S(1)} collective-permute-done((bf16[8,2432]{1,0:T(8,128)(2,1)S(1)}, bf16[8,2432]{1,0:T(8,128)(2,1)S(1)}, u32[]{:S(2)}, u32[]{:S(2)}) %collective-permute-start.4) | collective-permute-done | bytes 38944 | tf_op jit(solution)/shard_map/ppermute | solution.py:27
  29.6 0.0 collective-permute-done.6.got.got1
  29.7 0.0 collective-permute-done.9.got2
  29.7 0.2 shard_map.153
  29.8 0.1 collective-permute-start.10
  29.9 1.9 %collective-permute-start.7 = (bf16[8,2432]{1,0:T(8,128)(2,1)S(1)}, bf16[8,2432]{1,0:T(8,128)(2,1)S(1)}, u32[]{:S(2)}, u32[]{:S(2)}) collective-permute-start(bf16[8,2432]{1,0:T(8,128)(2,1)S(1)} %get-tuple-element.73.s_own), channel_id=1, source_target_pairs={{0,4},{1,5},{2,6},{3,7},{4,0},{5,1},{6,2},{7,3},{8,12},{9,13},{10,... | collective-permute-start | bytes 116744 | tf_op jit(solution)/shard_map/ppermute | solution.py:27
  31.8 2.2 %collective-permute-done.7.s_got = bf16[8,2432]{1,0:T(8,128)(2,1)S(1)} collective-permute-done((bf16[8,2432]{1,0:T(8,128)(2,1)S(1)}, bf16[8,2432]{1,0:T(8,128)(2,1)S(1)}, u32[]{:S(2)}, u32[]{:S(2)}) %collective-permute-start.7) | collective-permute-done | bytes 38944 | tf_op jit(solution)/shard_map/ppermute | solution.py:27
  34.0 2.9 %collective-permute-start.8 = (bf16[8,2432]{1,0:T(8,128)(2,1)S(1)}, bf16[8,2432]{1,0:T(8,128)(2,1)S(1)}, u32[]{:S(2)}, u32[]{:S(2)}) collective-permute-start(bf16[8,2432]{1,0:T(8,128)(2,1)S(1)} %shard_map.152.s_own), channel_id=1, source_target_pairs={{0,8},{1,9},{2,10},{3,11},{4,12},{5,13},{6,14},{7,15},{8,0},{9,1},... | collective-permute-start | bytes 116744 | tf_op jit(solution)/shard_map/ppermute | solution.py:27
  36.9 1.2 %shard_map.154 = (bf16[32,24,2048]{2,1,0:T(8,128)(2,1)}, f32[1,8,512]{2,1,0:T(8,128)}) custom-call(f32[32,8,1024]{2,1,0:T(8,128)S(1)} %get-tuple-element.81.left, f32[32,8,1024]{2,1,0:T(8,128)S(1)} %get-tuple-element.82.right, bf16[32,8,2048]{2,1,0:T(8,128)(2,1)S(1)} %get-tuple-element.56.y_v, f32[8,2048]{1,0:T(8,128)S(1)} %get-tuple-element.83.a2, ...), custom_call_target="tpu_custom_call" | custom-call | tf_op jit(solution)/shard_map/pallas_call | solution.py:495
  38.0 0.0 collective-permute-done.10.got
  38.1 1.4 %shard_map.155 = (bf16[32,24,2048]{2,1,0:T(8,128)(2,1)}, f32[4,8,2048]{2,1,0:T(8,128)}) custom-call(s32[32]{0:T(128)S(4)} %get-tuple-element.58.sec, f32[32,8,2048]{2,1,0:T(8,128)S(1)} %get-tuple-element.75.sol, bf16[32,8,2048]{2,1,0:T(8,128)(2,1)S(1)} %get-tuple-element.60.y_v, ...), custom_call_target="tpu_custom_call", output_to_operand_aliasing={{0}: (5, {})} | custom-call | tf_op jit(solution)/shard_map/pallas_call | solution.py:515
  39.5 0.0 collective-permute-done.8.s_got
  39.5 1.2 %shard_map.156 = (bf16[32,24,2048]{2,1,0:T(8,128)(2,1)}, f32[8,2048]{1,0:T(8,128)}, f32[1]{0:T(128)}, f32[1,32]{1,0:T(1,128)}) custom-call(f32[32,8,2048]{2,1,0:T(8,128)S(1)} %get-tuple-element.49.sol, bf16[32,8,2048]{2,1,0:T(8,128)(2,1)S(1)} %get-tuple-element.50.y_v, bf16[8,2432]{1,0:T(8,128)(2,1)S(1)} %shard_map.152.s_own, ...), custom_call_target="tpu_custom_call", output_to_operand_aliasing={{0}: (6, {})} | custom-call | tf_op jit(solution)/shard_map/pallas_call | solution.py:524
  (3 shorter events, 0.1 us)
Async XLA Ops:
  1.6 7.3 %collective-permute-start = (bf16[5,8,2048]{2,1,0:T(8,128)(2,1)S(1)}, bf16[5,8,2048]{2,1,0:T(8,128)(2,1)S(1)}, u32[]{:S(2)}, u32[]{:S(2)}) collective-permute-start(bf16[5,8,2048]{2,1,0:T(8,128)(2,1)S(1)} %fusion.1.p0), channel_id=1, source_target_pairs={{0,2},{1,3},{2,0},{3,1},{4,6},{5,7},{6,4},{7,5},{8,10},{9,11},{10,... | collective-permute-start | bytes 491528 | tf_op jit(solution)/shard_map/ppermute | solution.py:27
  4.6 9.7 %collective-permute-start.1 = (bf16[5,8,2048]{2,1,0:T(8,128)(2,1)S(1)}, bf16[5,8,2048]{2,1,0:T(8,128)(2,1)S(1)}, u32[]{:S(2)}, u32[]{:S(2)}) collective-permute-start(bf16[5,8,2048]{2,1,0:T(8,128)(2,1)S(1)} %fusion.1.p0), channel_id=1, source_target_pairs={{0,1},{1,0},{2,3},{3,2},{4,5},{5,4},{6,7},{7,6},{8,9},{9,8},{10,11... | collective-permute-start | bytes 491528 | tf_op jit(solution)/shard_map/ppermute | solution.py:27
  8.8 5.6 %collective-permute-start.2 = (bf16[5,8,2048]{2,1,0:T(8,128)(2,1)S(1)}, bf16[5,8,2048]{2,1,0:T(8,128)(2,1)S(1)}, u32[]{:S(2)}, u32[]{:S(2)}) collective-permute-start(bf16[5,8,2048]{2,1,0:T(8,128)(2,1)S(1)} %collective-permute-done.p2), channel_id=1, source_target_pairs={{0,1},{1,0},{2,3},{3,2},{4,5},{5,4},{6,7},{7,6},{8,9},{9,8},{10,11... | collective-permute-start | bytes 491528 | tf_op jit(solution)/shard_map/ppermute | solution.py:27
  14.4 6.9 %copy-start.1 = (f32[32]{0:T(128)S(1)}, f32[32]{0:T(128)}, u32[]{:S(2)}) copy-start(f32[32]{0:T(128)} %param.19) | copy-start | bytes 388
  17.3 1.8 %collective-permute-start.5 = (bf16[9,8,2048]{2,1,0:T(8,128)(2,1)S(1)}, bf16[9,8,2048]{2,1,0:T(8,128)(2,1)S(1)}, u32[]{:S(2)}, u32[]{:S(2)}) collective-permute-start(bf16[9,8,2048]{2,1,0:T(8,128)(2,1)S(1)} %get-tuple-element.71.sent), channel_id=1, source_target_pairs={{0,1},{1,0},{2,3},{3,2},{4,5},{5,4},{6,7},{7,6},{8,9},{9,8},{10,11... | collective-permute-start | bytes 884744 | tf_op jit(solution)/shard_map/ppermute | solution.py:27
  19.2 10.5 %collective-permute-start.6 = (bf16[5,8,2048]{2,1,0:T(8,128)(2,1)S(1)}, bf16[5,8,2048]{2,1,0:T(8,128)(2,1)S(1)}, u32[]{:S(2)}, u32[]{:S(2)}) collective-permute-start(bf16[5,8,2048]{2,1,0:T(8,128)(2,1)S(1)} %get-tuple-element.72.sent), channel_id=1, source_target_pairs={{0,2},{1,3},{2,0},{3,1},{4,6},{5,7},{6,4},{7,5},{8,10},{9,11},{10,... | collective-permute-start | bytes 491528 | tf_op jit(solution)/shard_map/ppermute | solution.py:27
  21.0 8.7 %collective-permute-start.9 = (bf16[4,8,2048]{2,1,0:T(8,128)(2,1)S(1)}, bf16[4,8,2048]{2,1,0:T(8,128)(2,1)S(1)}, u32[]{:S(2)}, u32[]{:S(2)}) collective-permute-start(bf16[4,8,2048]{2,1,0:T(8,128)(2,1)S(1)} %get-tuple-element.77), channel_id=1, source_target_pairs={{0,2},{1,3},{2,0},{3,1},{4,6},{5,7},{6,4},{7,5},{8,10},{9,11},{10,... | collective-permute-start | bytes 393224 | tf_op jit(solution)/shard_map/ppermute | solution.py:27
  21.4 1.4 %copy-start = (s32[32]{0:T(128)S(1)}, s32[32]{0:T(128)}, u32[]{:S(2)}) copy-start(s32[32]{0:T(128)} %w_hbm.1) | copy-start | bytes 388
  24.4 1.2 %collective-permute-start.3 = (bf16[8,2432]{1,0:T(8,128)(2,1)S(1)}, bf16[8,2432]{1,0:T(8,128)(2,1)S(1)}, u32[]{:S(2)}, u32[]{:S(2)}) collective-permute-start(bf16[8,2432]{1,0:T(8,128)(2,1)S(1)} %get-tuple-element.69.s_own), channel_id=1, source_target_pairs={{0,1},{1,0},{2,3},{3,2},{4,5},{5,4},{6,7},{7,6},{8,9},{9,8},{10,11... | collective-permute-start | bytes 116744 | tf_op jit(solution)/shard_map/ppermute | solution.py:27
  25.6 4.0 %collective-permute-start.4 = (bf16[8,2432]{1,0:T(8,128)(2,1)S(1)}, bf16[8,2432]{1,0:T(8,128)(2,1)S(1)}, u32[]{:S(2)}, u32[]{:S(2)}) collective-permute-start(bf16[8,2432]{1,0:T(8,128)(2,1)S(1)} %shard_map.149.s_own), channel_id=1, source_target_pairs={{0,2},{1,3},{2,0},{3,1},{4,6},{5,7},{6,4},{7,5},{8,10},{9,11},{10,... | collective-permute-start | bytes 116744 | tf_op jit(solution)/shard_map/ppermute | solution.py:27
  29.8 8.2 %collective-permute-start.10 = (bf16[8,8,2048]{2,1,0:T(8,128)(2,1)S(1)}, bf16[8,8,2048]{2,1,0:T(8,128)(2,1)S(1)}, u32[]{:S(2)}, u32[]{:S(2)}) collective-permute-start(bf16[8,8,2048]{2,1,0:T(8,128)(2,1)S(1)} %get-tuple-element.80), channel_id=1, source_target_pairs={{0,1},{1,0},{2,3},{3,2},{4,5},{5,4},{6,7},{7,6},{8,9},{9,8},{10,11... | collective-permute-start | bytes 786440 | tf_op jit(solution)/shard_map/ppermute | solution.py:27
  29.9 4.0 %collective-permute-start.7 = (bf16[8,2432]{1,0:T(8,128)(2,1)S(1)}, bf16[8,2432]{1,0:T(8,128)(2,1)S(1)}, u32[]{:S(2)}, u32[]{:S(2)}) collective-permute-start(bf16[8,2432]{1,0:T(8,128)(2,1)S(1)} %get-tuple-element.73.s_own), channel_id=1, source_target_pairs={{0,4},{1,5},{2,6},{3,7},{4,0},{5,1},{6,2},{7,3},{8,12},{9,13},{10,... | collective-permute-start | bytes 116744 | tf_op jit(solution)/shard_map/ppermute | solution.py:27
  34.0 5.5 %collective-permute-start.8 = (bf16[8,2432]{1,0:T(8,128)(2,1)S(1)}, bf16[8,2432]{1,0:T(8,128)(2,1)S(1)}, u32[]{:S(2)}, u32[]{:S(2)}) collective-permute-start(bf16[8,2432]{1,0:T(8,128)(2,1)S(1)} %shard_map.152.s_own), channel_id=1, source_target_pairs={{0,8},{1,9},{2,10},{3,11},{4,12},{5,13},{6,14},{7,15},{8,0},{9,1},... | collective-permute-start | bytes 116744 | tf_op jit(solution)/shard_map/ppermute | solution.py:27

commit v7 on v6

--- a/solution.py
+++ b/solution.py
@@ -45,16 +45,13 @@
 
 
 def build_target(target, anchor_of, c_v, y_v):
-    scenarios, length, columns = c_v.shape
-    width = columns // 1
-    for j in range(1):
-        cols = slice(j * width, (j + 1) * width)
-        for i in range(scenarios // 2):
-            rows = [
-                PENALTY * anchor_of(s, cols).astype(F32) - c_v[s, :, cols].astype(F32) - y_v[s, :, cols].astype(F32)
-                for s in (2 * i, 2 * i + 1)
-            ]
-            target[i * 2 * length : (i + 1) * 2 * length, cols] = jnp.concatenate(rows, axis=0).astype(BF16)
+    scenarios, length, _ = c_v.shape
+    for i in range(scenarios // 2):
+        rows = [
+            PENALTY * anchor_of(s).astype(F32) - c_v[s].astype(F32) - y_v[s].astype(F32)
+            for s in (2 * i, 2 * i + 1)
+        ]
+        target[i * 2 * length : (i + 1) * 2 * length, :] = jnp.concatenate(rows, axis=0).astype(BF16)
 
 
 def multiply(target, inv_v, sol, c_v, cost, before, w, after, start=0):
@@ -140,7 +137,7 @@
 
     for copy in first:
         copy.wait()
-    build_target(target, lambda s, cols: pf[:, cols], c1, y1)
+    build_target(target, lambda s: pf[...], c1, y1)
 
     def after(cols, total):
         a1[:, cols] = total
@@ -178,9 +175,9 @@
     for k, part in enumerate((p0, p1, p2, p3)):
         table[k * SHARES : (k + 1) * SHARES] = part[:SHARES]
 
-    def anchor_of(s, cols):
+    def anchor_of(s):
         node = sec[s] % BRANCH
-        return table[((node // SHARES) ^ quarter) * SHARES + node % SHARES, :, cols]
+        return table[((node // SHARES) ^ quarter) * SHARES + node % SHARES]
 
     build_target(target, anchor_of, c_v, y_v)
 
@@ -200,7 +197,7 @@
     cost[...] = cost_in[...]
     for k, part in enumerate((p0, p1, p2, p3)):
         table[:, pl.ds(pl.multiple_of((quarter ^ k) * share, share), share)] = part[SHARES, :, :share]
-    build_target(target, lambda s, cols: table[:, cols], c_v, y_v)
+    build_target(target, lambda s: table[...], c_v, y_v)
 
     def after(cols, total):
         a2[:, cols] = total
@@ -242,12 +239,17 @@
     send2[...] = value[cut:].astype(BF16)
 
 
-def node_sum_kernel(s_own, s_got, sent, got, sums, a2, scal):
+def core_sum_kernel(s_own, s_got, scal, a2):
     columns = a2.shape[1]
+    scal[...] = packed(unpacked(s_own[:, columns:]) + unpacked(s_got[:, columns:]))
+    a2[...] = (s_own[:, :columns].astype(F32) + s_got[:, :columns].astype(F32)).astype(BF16)
+
+
+def node_sum_kernel(s_own, s_got, sent, got, sums, scal):
+    columns = sent.shape[2]
     last = sent.shape[0] - 1
     sums[:, :columns] = (sent[last].astype(F32) + got[last].astype(F32)).astype(BF16)
-    a2[...] = s_own[:, :columns].astype(F32) + s_got[:, :columns].astype(F32)
-    value = unpacked(s_own[:, columns:]) + unpacked(s_got[:, columns:])
+    value = unpacked(s_own[...]) + unpacked(s_got[...])
     scal[...] = value
     sums[:, columns:] = packed(value)
 
@@ -280,9 +282,7 @@
         )
 
     for g in range(4):
-
-        def step(i, carry):
-            s = g * group + i
+        for s in range(g * group, (g + 1) * group):
             avg = avg_of(s)
             start = 0
             for sol in sols:
@@ -290,37 +290,34 @@
                 fresh = y_v[s, :, cols].astype(F32) + PENALTY * (sol[s] - avg[:, cols])
                 buf[s, :, cols] = fresh.astype(BF16)
                 start = cols.stop
-            return carry
-
-        lax.fori_loop(0, group, step, 0, unroll=4)
         copy(g).start()
     return [copy(g) for g in range(4)]
 
 
-def second_duals_kernel(left, right, y_v, a2, scal, out, second_avg, buf, full, sems, sem):
+def later_duals_kernel(
+    sec, left, right, y2, a_own, a_got, scal, sol3, y3, avg, got,
+    out, second_avg, third_avg, buf2, buf3, full, table, sems2, sems3, sems,
+):
     _, columns = full.shape
     quarter = quarter_of()
     share = columns // 4
-    full[...] = a2[...] / jnp.sum(scal[2:3, :], axis=1, keepdims=True)
+    whole = jnp.sum(scal[2:3, :], axis=1, keepdims=True)
+    full[...] = (a_own[...].astype(F32) + a_got[...].astype(F32)) / whole
     own = pl.ds(pl.multiple_of(quarter * share, share), share)
-    copy = pltpu.make_async_copy(full.at[:, own], second_avg.at[0], sem)
-    copy.start()
-    for other in write_duals((left, right), y_v, lambda s: full[...], out, buf, sems, 1):
-        other.wait()
-    copy.wait()
-
-
-def third_duals_kernel(sec, sol, y_v, avg, got, prior, out, third_avg, buf, table, sems, sem):
-    quarter = quarter_of()
-    copy = pltpu.make_async_copy(avg.at[pl.ds((quarter // 2) * SHARES, SHARES)], third_avg, sem)
-    copy.start()
+    copies = [
+        pltpu.make_async_copy(full.at[:, own], second_avg.at[0], sems.at[0]),
+        pltpu.make_async_copy(avg.at[pl.ds((quarter // 2) * SHARES, SHARES)], third_avg, sems.at[1]),
+    ]
+    for copy in copies:
+        copy.start()
+    copies += write_duals((left, right), y2, lambda s: full[...], out, buf2, sems2, 1)
     table[:HALF] = avg[...]
     table[HALF:] = got[...].astype(F32)
-    for other in write_duals(
-        (sol,), y_v, lambda s: table[place_of(sec[s] % BRANCH, quarter)], out, buf, sems, 2
-    ):
-        other.wait()
-    copy.wait()
+    copies += write_duals(
+        (sol3,), y3, lambda s: table[place_of(sec[s] % BRANCH, quarter)], out, buf3, sems3, 2
+    )
+    for copy in copies:
+        copy.wait()
 
 
 def last_kernel(
@@ -470,19 +467,24 @@
     )(w, w_row, level_row, target2, c2, inv_v, cost, a2, mass)
 
     core_sums = partner(sums, 1)
-    sums = call(
-        far_sum_kernel, 8, in_specs=[VMEM] * 2, out_specs=VMEM, out_shape=pltpu.VMEM(sums.shape, BF16)
+    scal_chip, a2 = call(
+        core_sum_kernel,
+        8,
+        in_specs=[VMEM] * 2,
+        out_specs=[VMEM] * 2,
+        out_shape=[pltpu.VMEM((length, 3 * LANES), BF16), pltpu.VMEM((length, columns), BF16)],
     )(sums, core_sums)
-    y_sums = partner(sums, 2)
+    y_scal = partner(scal_chip, 2)
     node_got2 = partner(chip_send2, 2)
+    a2_got = partner(a2, 2)
     far_shape = pltpu.VMEM((length, columns + 3 * LANES), BF16)
-    far, a2, scal = call(
+    far, scal = call(
         node_sum_kernel,
         8,
         in_specs=[VMEM] * 4,
-        out_specs=[VMEM] * 3,
-        out_shape=[far_shape, pltpu.VMEM((length, columns), F32), pltpu.VMEM((length, LANES), F32)],
-    )(sums, y_sums, chip_send1, node_got1)
+        out_specs=[VMEM] * 2,
+        out_shape=[far_shape, pltpu.VMEM((length, LANES), F32)],
+    )(scal_chip, y_scal, chip_send1, node_got1)
     far_got = partner(far, 4)
     mask = 8
     while mask < nodes:
@@ -492,15 +494,6 @@
 
     buf = pltpu.VMEM(block, BF16)
     duals_shape = shape(hour_duals.shape, BF16)
-    out, second_avg = call(
-        second_duals_kernel,
-        8,
-        in_specs=[VMEM] * 5,
-        out_specs=[HBM, HBM],
-        out_shape=[duals_shape, shape((1, length, columns // 4), F32)],
-        scratch_shapes=[buf, pltpu.VMEM((length, columns), F32), dma((4,)), dma],
-    )(left, right, y2, a2, scal)
-
     avg, avg_send = call(
         third_avg_kernel,
         8,
@@ -512,15 +505,26 @@
         ],
     )(chip_total, node_got1, node_got2, scal)
     avg_got = partner(avg_send, 1)
-    out, third_avg = call(
-        third_duals_kernel,
-        8,
-        in_specs=[SMEM] + [VMEM] * 4 + [HBM],
-        out_specs=[HBM, HBM],
-        out_shape=[duals_shape, shape((SHARES, length, columns), F32)],
-        scratch_shapes=[buf, pltpu.VMEM((BRANCH, length, columns), F32), dma((4,)), dma],
-        input_output_aliases={5: 0},
-    )(sec, sol3, y3, avg, avg_got, out)
+    out, second_avg, third_avg = call(
+        later_duals_kernel,
+        12,
+        in_specs=[SMEM] + [VMEM] * 10,
+        out_specs=[HBM] * 3,
+        out_shape=[
+            duals_shape,
+            shape((1, length, columns // 4), F32),
+            shape((SHARES, length, columns), F32),
+        ],
+        scratch_shapes=[
+            buf,
+            buf,
+            pltpu.VMEM((length, columns), F32),
+            pltpu.VMEM((BRANCH, length, columns), F32),
+            dma((4,)),
+            dma((4,)),
+            dma((2,)),
+        ],
+    )(sec, left, right, y2, a2, a2_got, scal, sol3, y3, avg, avg_got)
     out, first_avg, eta_avg, eta_duals_new = call(
         last_kernel,
         8,

time: 40.9 us -> 44.2 us (1.081)
  waiting for transfers between devices: 10.4 us -> 13.1 us
  starting transfers between devices: 12.3 us -> 13.9 us
  Pallas kernels: 15.5 us -> 14.5 us
    ppermute x11 -> x12, waiting for transfers between devices: 10.4 us -> 13.1 us  [partner(): return lax.ppermute(value, 'node', pairs)]
    ppermute x11 -> x12, starting transfers between devices: 12.3 us -> 13.9 us  [partner(): return lax.ppermute(value, 'node', pairs)]
    pallas_call x4 -> x3, Pallas kernels: 2.63 us -> 1.7 us  [the longest x1 1.67 us: step(): call(later_duals_kernel, 12, in_specs=[SMEM] + [VMEM] * 10, out_specs=[HB...]
  transfers between devices with their start and end apart: 11 -> 12, of which waited for: 5 -> 6; matrix products, arithmetic and copies ran while one was open for 0% -> 0% of each run, Pallas kernels for 27% -> 23%
where the time goes in v7:
time: 44.2 us; the launch traced here: 44 us
  Pallas kernels  14.5 us (33%)
  starting transfers between devices  13.9 us (31%)
  waiting for transfers between devices  13.1 us (30%)
  between operations  1.4 us (3%)
  other arithmetic  1.01 us (2%)
    ppermute x12, starting transfers between devices, partner(): return lax.ppermute(value, 'node', pairs)  13.9 us
    ppermute x12, waiting for transfers between devices, partner(): return lax.ppermute(value, 'node', pairs)  13.1 us
    pallas_call x1, Pallas kernels, step(): call(first_kernel, 32, in_specs=[HBM] * 8, out_specs=[SMEM, SMEM] + [VMEM...  5.53 us
    pallas_call x1, Pallas kernels, step(): call(third_kernel, 30, in_specs=[SMEM] + [VMEM] * 10, out_specs=[VMEM] *...  2.92 us
    pallas_call x1, Pallas kernels, step(): call(later_duals_kernel, 12, in_specs=[SMEM] + [VMEM] * 10, out_specs=[HB...  1.67 us
    pallas_call x1, Pallas kernels, step(): call(right_kernel, 30, in_specs=[SMEM] + [VMEM] * 8, out_specs=[VMEM] * 3...  1.59 us
    pallas_call x1, Pallas kernels, step(): call(left_kernel, 30, in_specs=[SMEM] + [VMEM] * 8, out_specs=[VMEM] * 4,...  1.37 us
    pallas_call x1, Pallas kernels, step(): call(last_kernel, 8, in_specs=[VMEM] * 6 + [HBM], out_specs=[HBM] * 4, ou...  1.14 us
  transfers between devices with their start and end apart: 12, of which 6 were waited for; matrix products, arithmetic and copies ran while one was open for 0% of the time, Pallas kernels for 23%

profile of v7, /device:TPU:0, one launch (start us, length us, event | category | flops | bytes accessed | tf_op | source)
XLA Modules:
  0.0 44.0 jit_solution(10249240742194100792)
XLA Ops:
  0.6 0.9 %fusion.1.p0 = bf16[5,8,2048]{2,1,0:T(8,128)(2,1)S(1)} fusion(bf16[1,8,512]{2,1,0:T(8,128)(2,1)} %param.16, bf16[4,8,2048]{2,1,0:T(8,128)(2,1)} %param.17), kind=kLoop, calls=%fused_computation.2 | loop fusion | flops 491520 | bytes 303104 | tf_op jit(solution)/shard_map/concatenate | solution.py:370
  1.6 3.1 %collective-permute-start = (bf16[5,8,2048]{2,1,0:T(8,128)(2,1)S(1)}, bf16[5,8,2048]{2,1,0:T(8,128)(2,1)S(1)}, u32[]{:S(2)}, u32[]{:S(2)}) collective-permute-start(bf16[5,8,2048]{2,1,0:T(8,128)(2,1)S(1)} %fusion.1.p0), channel_id=1, source_target_pairs={{0,2},{1,3},{2,0},{3,1},{4,6},{5,7},{6,4},{7,5},{8,10},{9,11},{10,... | collective-permute-start | bytes 491528 | tf_op jit(solution)/shard_map/ppermute | solution.py:27
  4.6 0.0 collective-permute-start.1
  4.6 4.2 %collective-permute-done.p2 = bf16[5,8,2048]{2,1,0:T(8,128)(2,1)S(1)} collective-permute-done((bf16[5,8,2048]{2,1,0:T(8,128)(2,1)S(1)}, bf16[5,8,2048]{2,1,0:T(8,128)(2,1)S(1)}, u32[]{:S(2)}, u32[]{:S(2)}) %collective-permute-start) | collective-permute-done | bytes 163872 | tf_op jit(solution)/shard_map/ppermute | solution.py:27
  8.8 0.0 collective-permute-start.2
  8.8 5.5 %shard_map.145 = (s32[32]{0:T(128)S(4)}, s32[32]{0:T(128)S(4)}, bf16[32,8,2048]{2,1,0:T(8,128)(2,1)S(1)}, bf16[32,8,2048]{2,1,0:T(8,128)(2,1)S(1)}, bf16[32,8,20...) custom-call(s32[32]{0:T(128)} %w_hbm.1, ...), custom_call_target="tpu_custom_call" | custom-call | tf_op jit(solution)/shard_map/pallas_call | solution.py:373
  14.4 0.0 collective-permute-done.1.p1
  14.4 0.0 collective-permute-done.2.p3
  14.4 0.0 copy-start.1
  14.4 2.9 %shard_map.146 = (f32[32,8,2048]{2,1,0:T(8,128)S(1)}, f32[32,8,128]{2,1,0:T(8,128)S(1)}, f32[8,8,2048]{2,1,0:T(8,128)S(1)}, bf16[9,8,2048]{2,1,0:T(8,128)(2,1)S(1)}) custom-call(s32[32]{0:T(128)S(4)} %get-tuple-element.58.sec, bf16[5,8,2048]{2,1,0:T(8,128)(2,1)S(1)} %fusion.1.p0, bf16[5,8,2048]{2,1,0:T(8,128)(2,1)S(1)} %collective-permute-done.1.p1, ...), custom_call_target="tpu_custom_call" | custom-call | tf_op jit(solution)/shard_map/pallas_call | solution.py:413
  17.3 0.6 %collective-permute-start.5 = (bf16[9,8,2048]{2,1,0:T(8,128)(2,1)S(1)}, bf16[9,8,2048]{2,1,0:T(8,128)(2,1)S(1)}, u32[]{:S(2)}, u32[]{:S(2)}) collective-permute-start(bf16[9,8,2048]{2,1,0:T(8,128)(2,1)S(1)} %get-tuple-element.72.sent), channel_id=1, source_target_pairs={{0,1},{1,0},{2,3},{3,2},{4,5},{5,4},{6,7},{7,6},{8,9},{9,8},{10,11... | collective-permute-start | bytes 884744 | tf_op jit(solution)/shard_map/ppermute | solution.py:27
  17.9 1.2 %collective-permute-done.5.got = bf16[9,8,2048]{2,1,0:T(8,128)(2,1)S(1)} collective-permute-done((bf16[9,8,2048]{2,1,0:T(8,128)(2,1)S(1)}, bf16[9,8,2048]{2,1,0:T(8,128)(2,1)S(1)}, u32[]{:S(2)}, u32[]{:S(2)}) %collective-permute-start.5) | collective-permute-done | bytes 294944 | tf_op jit(solution)/shard_map/ppermute | solution.py:27
  19.1 0.1 shard_map.150
  19.2 1.8 %collective-permute-start.6 = (bf16[5,8,2048]{2,1,0:T(8,128)(2,1)S(1)}, bf16[5,8,2048]{2,1,0:T(8,128)(2,1)S(1)}, u32[]{:S(2)}, u32[]{:S(2)}) collective-permute-start(bf16[5,8,2048]{2,1,0:T(8,128)(2,1)S(1)} %get-tuple-element.73.sent), channel_id=1, source_target_pairs={{0,2},{1,3},{2,0},{3,1},{4,6},{5,7},{6,4},{7,5},{8,10},{9,11},{10,... | collective-permute-start | bytes 491528 | tf_op jit(solution)/shard_map/ppermute | solution.py:27
  21.7 0.4 collective-permute-start.10
  22.0 0.0 copy-done.1
  22.0 0.1 maximum_bitcast_fusion.level_row
  22.1 0.0 copy-start
  22.1 1.4 %shard_map.147 = (bf16[256,2048]{1,0:T(8,128)(2,1)S(1)}, f32[32,8,1024]{2,1,0:T(8,128)S(1)}, f32[8,1024]{1,0:T(8,128)S(1)}, f32[32,8,128]{2,1,0:T(8,128)S(1)}) custom-call(s32[32]{0:T(128)S(4)} %get-tuple-element.51.w, bf16[5,8,2048]{2,1,0:T(8,128)(2,1)S(1)} %fusion.1.p0, bf16[5,8,2048]{2,1,0:T(8,128)(2,1)S(1)} %collective-permute-done.1.p1, ...), custom_call_target="tpu_custom_call" | custom-call | tf_op jit(solution)/shard_map/pallas_call | solution.py:429
  23.5 0.0 copy-done
  23.5 1.6 %shard_map.148 = (f32[32,8,1024]{2,1,0:T(8,128)S(1)}, f32[1,32]{1,0:T(1,128)S(1)}, bf16[8,2432]{1,0:T(8,128)(2,1)S(1)}) custom-call(s32[32]{0:T(128)S(4)} %get-tuple-element.51.w, s32[1,32]{1,0:T(1,128)S(1)} %bitcast.7, f32[1,33]{1,0:T(1,128)S(1)} %maximum_bitcast_fusion.level_row, bf16[256,2048]{1,0:T(8,128)(2,1)S(1)} %get-tuple-element.65.target, ...), custom_call_target="tpu_custom_call" | custom-call | tf_op jit(solution)/shard_map/pallas_call | solution.py:456
  25.1 0.0 collective-permute-start.3
  25.1 1.2 %collective-permute-done.3.s_got = bf16[8,2432]{1,0:T(8,128)(2,1)S(1)} collective-permute-done((bf16[8,2432]{1,0:T(8,128)(2,1)S(1)}, bf16[8,2432]{1,0:T(8,128)(2,1)S(1)}, u32[]{:S(2)}, u32[]{:S(2)}) %collective-permute-start.3) | collective-permute-done | bytes 38944 | tf_op jit(solution)/shard_map/ppermute | solution.py:27
  26.3 1.8 %collective-permute-start.4 = (bf16[8,384]{1,0:T(8,128)(2,1)S(1)}, bf16[8,384]{1,0:T(8,128)(2,1)S(1)}, u32[]{:S(2)}, u32[]{:S(2)}) collective-permute-start(bf16[8,384]{1,0:T(8,128)(2,1)S(1)} %get-tuple-element.70.s_own), channel_id=1, source_target_pairs={{0,2},{1,3},{2,0},{3,1},{4,6},{5,7},{6,4},{7,5},{8,10},{9,11},{10,... | collective-permute-start | bytes 18440 | tf_op jit(solution)/shard_map/ppermute | solution.py:27
  28.1 1.9 %collective-permute-done.4.s_got = bf16[8,384]{1,0:T(8,128)(2,1)S(1)} collective-permute-done((bf16[8,384]{1,0:T(8,128)(2,1)S(1)}, bf16[8,384]{1,0:T(8,128)(2,1)S(1)}, u32[]{:S(2)}, u32[]{:S(2)}) %collective-permute-start.4) | collective-permute-done | bytes 6176 | tf_op jit(solution)/shard_map/ppermute | solution.py:27
  30.0 0.0 collective-permute-done.6.got.got1
  30.0 0.0 collective-permute-done.10.got2
  30.0 0.2 shard_map.153
  30.2 0.1 collective-permute-start.11
  30.3 1.9 %collective-permute-start.7 = (bf16[8,2432]{1,0:T(8,128)(2,1)S(1)}, bf16[8,2432]{1,0:T(8,128)(2,1)S(1)}, u32[]{:S(2)}, u32[]{:S(2)}) collective-permute-start(bf16[8,2432]{1,0:T(8,128)(2,1)S(1)} %get-tuple-element.74.s_own), channel_id=1, source_target_pairs={{0,4},{1,5},{2,6},{3,7},{4,0},{5,1},{6,2},{7,3},{8,12},{9,13},{10,... | collective-permute-start | bytes 116744 | tf_op jit(solution)/shard_map/ppermute | solution.py:27
  32.2 2.2 %collective-permute-done.7.s_got = bf16[8,2432]{1,0:T(8,128)(2,1)S(1)} collective-permute-done((bf16[8,2432]{1,0:T(8,128)(2,1)S(1)}, bf16[8,2432]{1,0:T(8,128)(2,1)S(1)}, u32[]{:S(2)}, u32[]{:S(2)}) %collective-permute-start.7) | collective-permute-done | bytes 38944 | tf_op jit(solution)/shard_map/ppermute | solution.py:27
  34.3 2.9 %collective-permute-start.8 = (bf16[8,2432]{1,0:T(8,128)(2,1)S(1)}, bf16[8,2432]{1,0:T(8,128)(2,1)S(1)}, u32[]{:S(2)}, u32[]{:S(2)}) collective-permute-start(bf16[8,2432]{1,0:T(8,128)(2,1)S(1)} %shard_map.152.s_own), channel_id=1, source_target_pairs={{0,8},{1,9},{2,10},{3,11},{4,12},{5,13},{6,14},{7,15},{8,0},{9,1},... | collective-permute-start | bytes 116744 | tf_op jit(solution)/shard_map/ppermute | solution.py:27
  37.2 1.5 %collective-permute-start.9 = (bf16[8,2048]{1,0:T(8,128)(2,1)S(1)}, bf16[8,2048]{1,0:T(8,128)(2,1)S(1)}, u32[]{:S(2)}, u32[]{:S(2)}) collective-permute-start(bf16[8,2048]{1,0:T(8,128)(2,1)S(1)} %get-tuple-element.78.a_own), channel_id=1, source_target_pairs={{0,2},{1,3},{2,0},{3,1},{4,6},{5,7},{6,4},{7,5},{8,10},{9,11},{10,... | collective-permute-start | bytes 98312 | tf_op jit(solution)/shard_map/ppermute | solution.py:27
  38.7 2.4 %collective-permute-done.9.a_got = bf16[8,2048]{1,0:T(8,128)(2,1)S(1)} collective-permute-done((bf16[8,2048]{1,0:T(8,128)(2,1)S(1)}, bf16[8,2048]{1,0:T(8,128)(2,1)S(1)}, u32[]{:S(2)}, u32[]{:S(2)}) %collective-permute-start.9) | collective-permute-done | bytes 32800 | tf_op jit(solution)/shard_map/ppermute | solution.py:27
  41.1 0.0 collective-permute-done.11.got
  41.2 1.7 %shard_map.154 = (bf16[32,24,2048]{2,1,0:T(8,128)(2,1)}, f32[1,8,512]{2,1,0:T(8,128)}, f32[4,8,2048]{2,1,0:T(8,128)}) custom-call(s32[32]{0:T(128)S(4)} %get-tuple-element.58.sec, f32[32,8,1024]{2,1,0:T(8,128)S(1)} %get-tuple-element.76.left, f32[32,8,1024]{2,1,0:T(8,128)S(1)} %get-tuple-element.77.right, bf16[32,8,2048]{2,1,0:T(8,128)(2,1)S(1)} %get-tuple-element.56.y_v.y2, ...), custom_call_target="tpu_custom_call" | custom-call | tf_op jit(solution)/shard_map/pallas_call | solution.py:508
  42.8 0.0 collective-permute-done.8.s_got
  42.8 1.1 %shard_map.155 = (bf16[32,24,2048]{2,1,0:T(8,128)(2,1)}, f32[8,2048]{1,0:T(8,128)}, f32[1]{0:T(128)}, f32[1,32]{1,0:T(1,128)}) custom-call(f32[32,8,2048]{2,1,0:T(8,128)S(1)} %get-tuple-element.49.sol, bf16[32,8,2048]{2,1,0:T(8,128)(2,1)S(1)} %get-tuple-element.50.y_v, bf16[8,2432]{1,0:T(8,128)(2,1)S(1)} %shard_map.152.s_own, ...), custom_call_target="tpu_custom_call", output_to_operand_aliasing={{0}: (6, {})} | custom-call | tf_op jit(solution)/shard_map/pallas_call | solution.py:528
  (3 shorter events, 0.1 us)
Async XLA Ops:
  1.6 7.3 %collective-permute-start = (bf16[5,8,2048]{2,1,0:T(8,128)(2,1)S(1)}, bf16[5,8,2048]{2,1,0:T(8,128)(2,1)S(1)}, u32[]{:S(2)}, u32[]{:S(2)}) collective-permute-start(bf16[5,8,2048]{2,1,0:T(8,128)(2,1)S(1)} %fusion.1.p0), channel_id=1, source_target_pairs={{0,2},{1,3},{2,0},{3,1},{4,6},{5,7},{6,4},{7,5},{8,10},{9,11},{10,... | collective-permute-start | bytes 491528 | tf_op jit(solution)/shard_map/ppermute | solution.py:27
  4.6 9.7 %collective-permute-start.1 = (bf16[5,8,2048]{2,1,0:T(8,128)(2,1)S(1)}, bf16[5,8,2048]{2,1,0:T(8,128)(2,1)S(1)}, u32[]{:S(2)}, u32[]{:S(2)}) collective-permute-start(bf16[5,8,2048]{2,1,0:T(8,128)(2,1)S(1)} %fusion.1.p0), channel_id=1, source_target_pairs={{0,1},{1,0},{2,3},{3,2},{4,5},{5,4},{6,7},{7,6},{8,9},{9,8},{10,11... | collective-permute-start | bytes 491528 | tf_op jit(solution)/shard_map/ppermute | solution.py:27
  8.8 5.6 %collective-permute-start.2 = (bf16[5,8,2048]{2,1,0:T(8,128)(2,1)S(1)}, bf16[5,8,2048]{2,1,0:T(8,128)(2,1)S(1)}, u32[]{:S(2)}, u32[]{:S(2)}) collective-permute-start(bf16[5,8,2048]{2,1,0:T(8,128)(2,1)S(1)} %collective-permute-done.p2), channel_id=1, source_target_pairs={{0,1},{1,0},{2,3},{3,2},{4,5},{5,4},{6,7},{7,6},{8,9},{9,8},{10,11... | collective-permute-start | bytes 491528 | tf_op jit(solution)/shard_map/ppermute | solution.py:27
  14.4 7.6 %copy-start.1 = (f32[32]{0:T(128)S(1)}, f32[32]{0:T(128)}, u32[]{:S(2)}) copy-start(f32[32]{0:T(128)} %param.19) | copy-start | bytes 388
  17.3 1.8 %collective-permute-start.5 = (bf16[9,8,2048]{2,1,0:T(8,128)(2,1)S(1)}, bf16[9,8,2048]{2,1,0:T(8,128)(2,1)S(1)}, u32[]{:S(2)}, u32[]{:S(2)}) collective-permute-start(bf16[9,8,2048]{2,1,0:T(8,128)(2,1)S(1)} %get-tuple-element.72.sent), channel_id=1, source_target_pairs={{0,1},{1,0},{2,3},{3,2},{4,5},{5,4},{6,7},{7,6},{8,9},{9,8},{10,11... | collective-permute-start | bytes 884744 | tf_op jit(solution)/shard_map/ppermute | solution.py:27
  19.2 10.8 %collective-permute-start.6 = (bf16[5,8,2048]{2,1,0:T(8,128)(2,1)S(1)}, bf16[5,8,2048]{2,1,0:T(8,128)(2,1)S(1)}, u32[]{:S(2)}, u32[]{:S(2)}) collective-permute-start(bf16[5,8,2048]{2,1,0:T(8,128)(2,1)S(1)} %get-tuple-element.73.sent), channel_id=1, source_target_pairs={{0,2},{1,3},{2,0},{3,1},{4,6},{5,7},{6,4},{7,5},{8,10},{9,11},{10,... | collective-permute-start | bytes 491528 | tf_op jit(solution)/shard_map/ppermute | solution.py:27
  21.7 8.4 %collective-permute-start.10 = (bf16[4,8,2048]{2,1,0:T(8,128)(2,1)S(1)}, bf16[4,8,2048]{2,1,0:T(8,128)(2,1)S(1)}, u32[]{:S(2)}, u32[]{:S(2)}) collective-permute-start(bf16[4,8,2048]{2,1,0:T(8,128)(2,1)S(1)} %get-tuple-element.82), channel_id=1, source_target_pairs={{0,2},{1,3},{2,0},{3,1},{4,6},{5,7},{6,4},{7,5},{8,10},{9,11},{10,... | collective-permute-start | bytes 393224 | tf_op jit(solution)/shard_map/ppermute | solution.py:27
  22.1 1.4 %copy-start = (s32[32]{0:T(128)S(1)}, s32[32]{0:T(128)}, u32[]{:S(2)}) copy-start(s32[32]{0:T(128)} %w_hbm.1) | copy-start | bytes 388
  25.1 1.2 %collective-permute-start.3 = (bf16[8,2432]{1,0:T(8,128)(2,1)S(1)}, bf16[8,2432]{1,0:T(8,128)(2,1)S(1)}, u32[]{:S(2)}, u32[]{:S(2)}) collective-permute-start(bf16[8,2432]{1,0:T(8,128)(2,1)S(1)} %get-tuple-element.69.s_own), channel_id=1, source_target_pairs={{0,1},{1,0},{2,3},{3,2},{4,5},{5,4},{6,7},{7,6},{8,9},{9,8},{10,11... | collective-permute-start | bytes 116744 | tf_op jit(solution)/shard_map/ppermute | solution.py:27
  26.3 3.7 %collective-permute-start.4 = (bf16[8,384]{1,0:T(8,128)(2,1)S(1)}, bf16[8,384]{1,0:T(8,128)(2,1)S(1)}, u32[]{:S(2)}, u32[]{:S(2)}) collective-permute-start(bf16[8,384]{1,0:T(8,128)(2,1)S(1)} %get-tuple-element.70.s_own), channel_id=1, source_target_pairs={{0,2},{1,3},{2,0},{3,1},{4,6},{5,7},{6,4},{7,5},{8,10},{9,11},{10,... | collective-permute-start | bytes 18440 | tf_op jit(solution)/shard_map/ppermute | solution.py:27
  30.2 11.0 %collective-permute-start.11 = (bf16[8,8,2048]{2,1,0:T(8,128)(2,1)S(1)}, bf16[8,8,2048]{2,1,0:T(8,128)(2,1)S(1)}, u32[]{:S(2)}, u32[]{:S(2)}) collective-permute-start(bf16[8,8,2048]{2,1,0:T(8,128)(2,1)S(1)} %get-tuple-element.84), channel_id=1, source_target_pairs={{0,1},{1,0},{2,3},{3,2},{4,5},{5,4},{6,7},{7,6},{8,9},{9,8},{10,11... | collective-permute-start | bytes 786440 | tf_op jit(solution)/shard_map/ppermute | solution.py:27
  30.3 4.0 %collective-permute-start.7 = (bf16[8,2432]{1,0:T(8,128)(2,1)S(1)}, bf16[8,2432]{1,0:T(8,128)(2,1)S(1)}, u32[]{:S(2)}, u32[]{:S(2)}) collective-permute-start(bf16[8,2432]{1,0:T(8,128)(2,1)S(1)} %get-tuple-element.74.s_own), channel_id=1, source_target_pairs={{0,4},{1,5},{2,6},{3,7},{4,0},{5,1},{6,2},{7,3},{8,12},{9,13},{10,... | collective-permute-start | bytes 116744 | tf_op jit(solution)/shard_map/ppermute | solution.py:27
  34.3 8.5 %collective-permute-start.8 = (bf16[8,2432]{1,0:T(8,128)(2,1)S(1)}, bf16[8,2432]{1,0:T(8,128)(2,1)S(1)}, u32[]{:S(2)}, u32[]{:S(2)}) collective-permute-start(bf16[8,2432]{1,0:T(8,128)(2,1)S(1)} %shard_map.152.s_own), channel_id=1, source_target_pairs={{0,8},{1,9},{2,10},{3,11},{4,12},{5,13},{6,14},{7,15},{8,0},{9,1},... | collective-permute-start | bytes 116744 | tf_op jit(solution)/shard_map/ppermute | solution.py:27
  37.2 3.9 %collective-permute-start.9 = (bf16[8,2048]{1,0:T(8,128)(2,1)S(1)}, bf16[8,2048]{1,0:T(8,128)(2,1)S(1)}, u32[]{:S(2)}, u32[]{:S(2)}) collective-permute-start(bf16[8,2048]{1,0:T(8,128)(2,1)S(1)} %get-tuple-element.78.a_own), channel_id=1, source_target_pairs={{0,2},{1,3},{2,0},{3,1},{4,6},{5,7},{6,4},{7,5},{8,10},{9,11},{10,... | collective-permute-start | bytes 98312 | tf_op jit(solution)/shard_map/ppermute | solution.py:27

commit v8 on v7

--- a/solution.py
+++ b/solution.py
@@ -209,10 +209,17 @@
     scenarios, length, half = sol.shape
     columns = 2 * half
     cost[...] = cost_in[...]
-    sums[:, :half] = a2[...].astype(BF16)
+
+    def keep(first, value):
+        high = value.astype(BF16)
+        own = slice(first, first + value.shape[1])
+        sums[:, own] = high
+        sums[:, columns + own.start : columns + own.stop] = (value - high.astype(F32)).astype(BF16)
+
+    keep(0, a2[...])
 
     def after(cols, total):
-        sums[:, half + cols.start : half + cols.stop] = total.astype(BF16)
+        keep(half + cols.start, total)
 
     multiply(target, inv_v, sol, c_v, cost, lambda j: None, w, after, half)
     lanes = jnp.sum(cost[...], axis=1)
@@ -226,7 +233,7 @@
     whole = jnp.sum(p, axis=1, keepdims=True)
     row = lax.broadcasted_iota(jnp.int32, (length, LANES), 0)
     scal = jnp.where(row == 0, total, jnp.where(row == 1, whole, jnp.where(row == 2, mass[...], 0.0)))
-    sums[:, columns:] = packed(scal)
+    sums[:, 2 * columns :] = packed(scal)
 
 
 def chip_sum_kernel(keep, sent, got, total, send1, send2):
@@ -241,8 +248,9 @@
 
 def core_sum_kernel(s_own, s_got, scal, a2):
     columns = a2.shape[1]
-    scal[...] = packed(unpacked(s_own[:, columns:]) + unpacked(s_got[:, columns:]))
-    a2[...] = (s_own[:, :columns].astype(F32) + s_got[:, :columns].astype(F32)).astype(BF16)
+    scal[...] = packed(unpacked(s_own[:, 2 * columns :]) + unpacked(s_got[:, 2 * columns :]))
+    own = s_own[:, :columns].astype(F32) + s_own[:, columns : 2 * columns].astype(F32)
+    a2[...] = own + (s_got[:, :columns].astype(F32) + s_got[:, columns : 2 * columns].astype(F32))
 
 
 def node_sum_kernel(s_own, s_got, sent, got, sums, scal):
@@ -260,7 +268,7 @@
     sums[:, columns:] = packed(unpacked(s_own[:, columns:]) + unpacked(s_got[:, columns:]))
 
 
-def third_avg_kernel(total, got1, got2, scal, avg, send):
+def third_avg_kernel(total, got1, got2, scal, avg):
     quarter = quarter_of()
     cut = total.shape[0] - got2.shape[0]
     for k in range(HALF):
@@ -268,7 +276,6 @@
         got = got1[k] if k < cut else got2[k - cut]
         value = (total[k] + got.astype(F32)) / node_mass(scal, node)
         avg[k] = value
-        send[k] = value.astype(BF16)
 
 
 def write_duals(sols, y_v, avg_of, out, buf, sems, section):
@@ -302,7 +309,7 @@
     quarter = quarter_of()
     share = columns // 4
     whole = jnp.sum(scal[2:3, :], axis=1, keepdims=True)
-    full[...] = (a_own[...].astype(F32) + a_got[...].astype(F32)) / whole
+    full[...] = (a_own[...] + a_got[...]) / whole
     own = pl.ds(pl.multiple_of(quarter * share, share), share)
     copies = [
         pltpu.make_async_copy(full.at[:, own], second_avg.at[0], sems.at[0]),
@@ -312,7 +319,7 @@
         copy.start()
     copies += write_duals((left, right), y2, lambda s: full[...], out, buf2, sems2, 1)
     table[:HALF] = avg[...]
-    table[HALF:] = got[...].astype(F32)
+    table[HALF:] = got[...]
     copies += write_duals(
         (sol3,), y3, lambda s: table[place_of(sec[s] % BRANCH, quarter)], out, buf3, sems3, 2
     )
@@ -461,7 +468,7 @@
         out_shape=[
             pltpu.VMEM(half_block, F32),
             pltpu.VMEM((1, scenarios), F32),
-            pltpu.VMEM((length, columns + 3 * LANES), BF16),
+            pltpu.VMEM((length, 2 * columns + 3 * LANES), BF16),
         ],
         scratch_shapes=[pltpu.VMEM((scenarios, length, LANES), F32)],
     )(w, w_row, level_row, target2, c2, inv_v, cost, a2, mass)
@@ -472,7 +479,7 @@
         8,
         in_specs=[VMEM] * 2,
         out_specs=[VMEM] * 2,
-        out_shape=[pltpu.VMEM((length, 3 * LANES), BF16), pltpu.VMEM((length, columns), BF16)],
+        out_shape=[pltpu.VMEM((length, 3 * LANES), BF16), pltpu.VMEM((length, columns), F32)],
     )(sums, core_sums)
     y_scal = partner(scal_chip, 2)
     node_got2 = partner(chip_send2, 2)
@@ -494,17 +501,10 @@
 
     buf = pltpu.VMEM(block, BF16)
     duals_shape = shape(hour_duals.shape, BF16)
-    avg, avg_send = call(
-        third_avg_kernel,
-        8,
-        in_specs=[VMEM] * 4,
-        out_specs=[VMEM] * 2,
-        out_shape=[
-            pltpu.VMEM((HALF, length, columns), F32),
-            pltpu.VMEM((HALF, length, columns), BF16),
-        ],
+    avg = call(
+        third_avg_kernel, 8, in_specs=[VMEM] * 4, out_specs=VMEM, out_shape=pltpu.VMEM((HALF, length, columns), F32)
     )(chip_total, node_got1, node_got2, scal)
-    avg_got = partner(avg_send, 1)
+    avg_got = partner(avg, 1)
     out, second_avg, third_avg = call(
         later_duals_kernel,
         12,

time: 44.2 us -> 40 us (0.905)
  waiting for transfers between devices: 13.1 us -> 8.98 us
    ppermute x12, waiting for transfers between devices: 13.1 us -> 8.98 us  [partner(): return lax.ppermute(value, 'node', pairs)]
  transfers between devices with their start and end apart: 12 -> 12, of which waited for: 6 -> 6; matrix products, arithmetic and copies ran while one was open for 0% -> 0% of each run, Pallas kernels for 23% -> 26%
where the time goes in v8:
time: 40 us; the launch traced here: 39.8 us
  Pallas kernels  14.5 us (36%)
  starting transfers between devices  13.9 us (35%)
  waiting for transfers between devices  8.98 us (22%)
  between operations  1.39 us (3%)
  other arithmetic  1.01 us (3%)
    ppermute x12, starting transfers between devices, partner(): return lax.ppermute(value, 'node', pairs)  13.9 us
    ppermute x12, waiting for transfers between devices, partner(): return lax.ppermute(value, 'node', pairs)  8.98 us
    pallas_call x1, Pallas kernels, step(): call(first_kernel, 32, in_specs=[HBM] * 8, out_specs=[SMEM, SMEM] + [VMEM...  5.53 us
    pallas_call x1, Pallas kernels, step(): call(third_kernel, 30, in_specs=[SMEM] + [VMEM] * 10, out_specs=[VMEM] *...  2.92 us
    pallas_call x1, Pallas kernels, step(): call(later_duals_kernel, 12, in_specs=[SMEM] + [VMEM] * 10, out_specs=[HB...  1.67 us
    pallas_call x1, Pallas kernels, step(): call(right_kernel, 30, in_specs=[SMEM] + [VMEM] * 8, out_specs=[VMEM] * 3...  1.6 us
    pallas_call x1, Pallas kernels, step(): call(left_kernel, 30, in_specs=[SMEM] + [VMEM] * 8, out_specs=[VMEM] * 4,...  1.37 us
    pallas_call x1, Pallas kernels, step(): call(last_kernel, 8, in_specs=[VMEM] * 6 + [HBM], out_specs=[HBM] * 4, ou...  1.14 us
  transfers between devices with their start and end apart: 12, of which 6 were waited for; matrix products, arithmetic and copies ran while one was open for 0% of the time, Pallas kernels for 26%

profile of v8, /device:TPU:0, one launch (start us, length us, event | category | flops | bytes accessed | tf_op | source)
XLA Modules:
  0.0 39.8 jit_solution(18417330292577620679)
XLA Ops:
  0.6 0.9 %fusion.1.p0 = bf16[5,8,2048]{2,1,0:T(8,128)(2,1)S(1)} fusion(bf16[1,8,512]{2,1,0:T(8,128)(2,1)} %param.16, bf16[4,8,2048]{2,1,0:T(8,128)(2,1)} %param.17), kind=kLoop, calls=%fused_computation.2 | loop fusion | flops 491520 | bytes 303104 | tf_op jit(solution)/shard_map/concatenate | solution.py:377
  1.6 3.1 %collective-permute-start = (bf16[5,8,2048]{2,1,0:T(8,128)(2,1)S(1)}, bf16[5,8,2048]{2,1,0:T(8,128)(2,1)S(1)}, u32[]{:S(2)}, u32[]{:S(2)}) collective-permute-start(bf16[5,8,2048]{2,1,0:T(8,128)(2,1)S(1)} %fusion.1.p0), channel_id=1, source_target_pairs={{0,2},{1,3},{2,0},{3,1},{4,6},{5,7},{6,4},{7,5},{8,10},{9,11},{10,... | collective-permute-start | bytes 491528 | tf_op jit(solution)/shard_map/ppermute | solution.py:27
  4.6 0.0 collective-permute-start.1
  4.6 4.2 %collective-permute-done.p2 = bf16[5,8,2048]{2,1,0:T(8,128)(2,1)S(1)} collective-permute-done((bf16[5,8,2048]{2,1,0:T(8,128)(2,1)S(1)}, bf16[5,8,2048]{2,1,0:T(8,128)(2,1)S(1)}, u32[]{:S(2)}, u32[]{:S(2)}) %collective-permute-start) | collective-permute-done | bytes 163872 | tf_op jit(solution)/shard_map/ppermute | solution.py:27
  8.8 0.0 collective-permute-start.2
  8.8 5.5 %shard_map.145 = (s32[32]{0:T(128)S(4)}, s32[32]{0:T(128)S(4)}, bf16[32,8,2048]{2,1,0:T(8,128)(2,1)S(1)}, bf16[32,8,2048]{2,1,0:T(8,128)(2,1)S(1)}, bf16[32,8,20...) custom-call(s32[32]{0:T(128)} %w_hbm.1, ...), custom_call_target="tpu_custom_call" | custom-call | tf_op jit(solution)/shard_map/pallas_call | solution.py:380
  14.4 0.0 collective-permute-done.1.p1
  14.4 0.0 collective-permute-done.2.p3
  14.4 0.0 copy-start.1
  14.4 2.9 %shard_map.146 = (f32[32,8,2048]{2,1,0:T(8,128)S(1)}, f32[32,8,128]{2,1,0:T(8,128)S(1)}, f32[8,8,2048]{2,1,0:T(8,128)S(1)}, bf16[9,8,2048]{2,1,0:T(8,128)(2,1)S(1)}) custom-call(s32[32]{0:T(128)S(4)} %get-tuple-element.56.sec, bf16[5,8,2048]{2,1,0:T(8,128)(2,1)S(1)} %fusion.1.p0, bf16[5,8,2048]{2,1,0:T(8,128)(2,1)S(1)} %collective-permute-done.1.p1, ...), custom_call_target="tpu_custom_call" | custom-call | tf_op jit(solution)/shard_map/pallas_call | solution.py:420
  17.3 0.6 %collective-permute-start.5 = (bf16[9,8,2048]{2,1,0:T(8,128)(2,1)S(1)}, bf16[9,8,2048]{2,1,0:T(8,128)(2,1)S(1)}, u32[]{:S(2)}, u32[]{:S(2)}) collective-permute-start(bf16[9,8,2048]{2,1,0:T(8,128)(2,1)S(1)} %get-tuple-element.70.sent), channel_id=1, source_target_pairs={{0,1},{1,0},{2,3},{3,2},{4,5},{5,4},{6,7},{7,6},{8,9},{9,8},{10,11... | collective-permute-start | bytes 884744 | tf_op jit(solution)/shard_map/ppermute | solution.py:27
  18.6 0.6 %collective-permute-done.5.got = bf16[9,8,2048]{2,1,0:T(8,128)(2,1)S(1)} collective-permute-done((bf16[9,8,2048]{2,1,0:T(8,128)(2,1)S(1)}, bf16[9,8,2048]{2,1,0:T(8,128)(2,1)S(1)}, u32[]{:S(2)}, u32[]{:S(2)}) %collective-permute-start.5) | collective-permute-done | bytes 294944 | tf_op jit(solution)/shard_map/ppermute | solution.py:27
  19.1 0.1 shard_map.150
  19.2 1.8 %collective-permute-start.6 = (bf16[5,8,2048]{2,1,0:T(8,128)(2,1)S(1)}, bf16[5,8,2048]{2,1,0:T(8,128)(2,1)S(1)}, u32[]{:S(2)}, u32[]{:S(2)}) collective-permute-start(bf16[5,8,2048]{2,1,0:T(8,128)(2,1)S(1)} %get-tuple-element.71.sent), channel_id=1, source_target_pairs={{0,2},{1,3},{2,0},{3,1},{4,6},{5,7},{6,4},{7,5},{8,10},{9,11},{10,... | collective-permute-start | bytes 491528 | tf_op jit(solution)/shard_map/ppermute | solution.py:27
  21.0 0.3 collective-permute-start.10
  21.3 0.0 copy-done.1
  21.3 0.1 maximum_bitcast_fusion.level_row
  21.4 0.0 copy-start
  21.4 1.4 %shard_map.147 = (bf16[256,2048]{1,0:T(8,128)(2,1)S(1)}, f32[32,8,1024]{2,1,0:T(8,128)S(1)}, f32[8,1024]{1,0:T(8,128)S(1)}, f32[32,8,128]{2,1,0:T(8,128)S(1)}) custom-call(s32[32]{0:T(128)S(4)} %get-tuple-element.49.w, bf16[5,8,2048]{2,1,0:T(8,128)(2,1)S(1)} %fusion.1.p0, bf16[5,8,2048]{2,1,0:T(8,128)(2,1)S(1)} %collective-permute-done.1.p1, ...), custom_call_target="tpu_custom_call" | custom-call | tf_op jit(solution)/shard_map/pallas_call | solution.py:436
  22.7 0.0 copy-done
  22.8 1.6 %shard_map.148 = (f32[32,8,1024]{2,1,0:T(8,128)S(1)}, f32[1,32]{1,0:T(1,128)S(1)}, bf16[8,4480]{1,0:T(8,128)(2,1)S(1)}) custom-call(s32[32]{0:T(128)S(4)} %get-tuple-element.49.w, s32[1,32]{1,0:T(1,128)S(1)} %bitcast.7, f32[1,33]{1,0:T(1,128)S(1)} %maximum_bitcast_fusion.level_row, bf16[256,2048]{1,0:T(8,128)(2,1)S(1)} %get-tuple-element.63.target, ...), custom_call_target="tpu_custom_call" | custom-call | tf_op jit(solution)/shard_map/pallas_call | solution.py:463
  24.4 0.0 collective-permute-start.3
  24.4 1.3 %collective-permute-done.3.s_got = bf16[8,4480]{1,0:T(8,128)(2,1)S(1)} collective-permute-done((bf16[8,4480]{1,0:T(8,128)(2,1)S(1)}, bf16[8,4480]{1,0:T(8,128)(2,1)S(1)}, u32[]{:S(2)}, u32[]{:S(2)}) %collective-permute-start.3) | collective-permute-done | bytes 71712 | tf_op jit(solution)/shard_map/ppermute | solution.py:27
  25.6 1.8 %collective-permute-start.4 = (bf16[8,384]{1,0:T(8,128)(2,1)S(1)}, bf16[8,384]{1,0:T(8,128)(2,1)S(1)}, u32[]{:S(2)}, u32[]{:S(2)}) collective-permute-start(bf16[8,384]{1,0:T(8,128)(2,1)S(1)} %get-tuple-element.68.s_own), channel_id=1, source_target_pairs={{0,2},{1,3},{2,0},{3,1},{4,6},{5,7},{6,4},{7,5},{8,10},{9,11},{10,... | collective-permute-start | bytes 18440 | tf_op jit(solution)/shard_map/ppermute | solution.py:27
  27.5 1.9 %collective-permute-done.4.s_got = bf16[8,384]{1,0:T(8,128)(2,1)S(1)} collective-permute-done((bf16[8,384]{1,0:T(8,128)(2,1)S(1)}, bf16[8,384]{1,0:T(8,128)(2,1)S(1)}, u32[]{:S(2)}, u32[]{:S(2)}) %collective-permute-start.4) | collective-permute-done | bytes 6176 | tf_op jit(solution)/shard_map/ppermute | solution.py:27
  29.3 0.0 collective-permute-done.6.got.got1
  29.4 0.0 collective-permute-done.10.got2
  29.4 0.1 shard_map.153.avg
  29.5 0.1 collective-permute-start.11
  29.6 1.9 %collective-permute-start.7 = (bf16[8,2432]{1,0:T(8,128)(2,1)S(1)}, bf16[8,2432]{1,0:T(8,128)(2,1)S(1)}, u32[]{:S(2)}, u32[]{:S(2)}) collective-permute-start(bf16[8,2432]{1,0:T(8,128)(2,1)S(1)} %get-tuple-element.72.s_own), channel_id=1, source_target_pairs={{0,4},{1,5},{2,6},{3,7},{4,0},{5,1},{6,2},{7,3},{8,12},{9,13},{10,... | collective-permute-start | bytes 116744 | tf_op jit(solution)/shard_map/ppermute | solution.py:27
  31.5 1.5 %collective-permute-start.9 = (f32[8,2048]{1,0:T(8,128)S(1)}, f32[8,2048]{1,0:T(8,128)S(1)}, u32[]{:S(2)}, u32[]{:S(2)}) collective-permute-start(f32[8,2048]{1,0:T(8,128)S(1)} %get-tuple-element.76.a_own), channel_id=1, source_target_pairs={{0,2},{1,3},{2,0},{3,1},{4,6},{5,7},{6,4},{7,5},{8,10},{9,11},{10,... | collective-permute-start | bytes 196616 | tf_op jit(solution)/shard_map/ppermute | solution.py:27
  33.0 0.7 %collective-permute-done.7.s_got = bf16[8,2432]{1,0:T(8,128)(2,1)S(1)} collective-permute-done((bf16[8,2432]{1,0:T(8,128)(2,1)S(1)}, bf16[8,2432]{1,0:T(8,128)(2,1)S(1)}, u32[]{:S(2)}, u32[]{:S(2)}) %collective-permute-start.7) | collective-permute-done | bytes 38944 | tf_op jit(solution)/shard_map/ppermute | solution.py:27
  33.7 2.9 %collective-permute-start.8 = (bf16[8,2432]{1,0:T(8,128)(2,1)S(1)}, bf16[8,2432]{1,0:T(8,128)(2,1)S(1)}, u32[]{:S(2)}, u32[]{:S(2)}) collective-permute-start(bf16[8,2432]{1,0:T(8,128)(2,1)S(1)} %shard_map.152.s_own), channel_id=1, source_target_pairs={{0,8},{1,9},{2,10},{3,11},{4,12},{5,13},{6,14},{7,15},{8,0},{9,1},... | collective-permute-start | bytes 116744 | tf_op jit(solution)/shard_map/ppermute | solution.py:27
  36.5 0.0 collective-permute-done.9.a_got
  36.5 0.0 collective-permute-done.11.got
  36.5 1.7 %shard_map.154 = (bf16[32,24,2048]{2,1,0:T(8,128)(2,1)}, f32[1,8,512]{2,1,0:T(8,128)}, f32[4,8,2048]{2,1,0:T(8,128)}) custom-call(s32[32]{0:T(128)S(4)} %get-tuple-element.56.sec, f32[32,8,1024]{2,1,0:T(8,128)S(1)} %get-tuple-element.74.left, f32[32,8,1024]{2,1,0:T(8,128)S(1)} %get-tuple-element.75.right, bf16[32,8,2048]{2,1,0:T(8,128)(2,1)S(1)} %get-tuple-element.54.y_v.y2, ...), custom_call_target="tpu_custom_call" | custom-call | tf_op jit(solution)/shard_map/pallas_call | solution.py:508
  38.2 0.4 collective-permute-done.8.s_got
  38.6 1.1 %shard_map.155 = (bf16[32,24,2048]{2,1,0:T(8,128)(2,1)}, f32[8,2048]{1,0:T(8,128)}, f32[1]{0:T(128)}, f32[1,32]{1,0:T(1,128)}) custom-call(f32[32,8,2048]{2,1,0:T(8,128)S(1)} %get-tuple-element.47.sol, bf16[32,8,2048]{2,1,0:T(8,128)(2,1)S(1)} %get-tuple-element.48.y_v, bf16[8,2432]{1,0:T(8,128)(2,1)S(1)} %shard_map.152.s_own, ...), custom_call_target="tpu_custom_call", output_to_operand_aliasing={{0}: (6, {})} | custom-call | tf_op jit(solution)/shard_map/pallas_call | solution.py:528
  (3 shorter events, 0.1 us)
Async XLA Ops:
  1.6 7.3 %collective-permute-start = (bf16[5,8,2048]{2,1,0:T(8,128)(2,1)S(1)}, bf16[5,8,2048]{2,1,0:T(8,128)(2,1)S(1)}, u32[]{:S(2)}, u32[]{:S(2)}) collective-permute-start(bf16[5,8,2048]{2,1,0:T(8,128)(2,1)S(1)} %fusion.1.p0), channel_id=1, source_target_pairs={{0,2},{1,3},{2,0},{3,1},{4,6},{5,7},{6,4},{7,5},{8,10},{9,11},{10,... | collective-permute-start | bytes 491528 | tf_op jit(solution)/shard_map/ppermute | solution.py:27
  4.6 9.7 %collective-permute-start.1 = (bf16[5,8,2048]{2,1,0:T(8,128)(2,1)S(1)}, bf16[5,8,2048]{2,1,0:T(8,128)(2,1)S(1)}, u32[]{:S(2)}, u32[]{:S(2)}) collective-permute-start(bf16[5,8,2048]{2,1,0:T(8,128)(2,1)S(1)} %fusion.1.p0), channel_id=1, source_target_pairs={{0,1},{1,0},{2,3},{3,2},{4,5},{5,4},{6,7},{7,6},{8,9},{9,8},{10,11... | collective-permute-start | bytes 491528 | tf_op jit(solution)/shard_map/ppermute | solution.py:27
  8.8 5.6 %collective-permute-start.2 = (bf16[5,8,2048]{2,1,0:T(8,128)(2,1)S(1)}, bf16[5,8,2048]{2,1,0:T(8,128)(2,1)S(1)}, u32[]{:S(2)}, u32[]{:S(2)}) collective-permute-start(bf16[5,8,2048]{2,1,0:T(8,128)(2,1)S(1)} %collective-permute-done.p2), channel_id=1, source_target_pairs={{0,1},{1,0},{2,3},{3,2},{4,5},{5,4},{6,7},{7,6},{8,9},{9,8},{10,11... | collective-permute-start | bytes 491528 | tf_op jit(solution)/shard_map/ppermute | solution.py:27
  14.4 6.9 %copy-start.1 = (f32[32]{0:T(128)S(1)}, f32[32]{0:T(128)}, u32[]{:S(2)}) copy-start(f32[32]{0:T(128)} %param.19) | copy-start | bytes 388
  17.3 1.8 %collective-permute-start.5 = (bf16[9,8,2048]{2,1,0:T(8,128)(2,1)S(1)}, bf16[9,8,2048]{2,1,0:T(8,128)(2,1)S(1)}, u32[]{:S(2)}, u32[]{:S(2)}) collective-permute-start(bf16[9,8,2048]{2,1,0:T(8,128)(2,1)S(1)} %get-tuple-element.70.sent), channel_id=1, source_target_pairs={{0,1},{1,0},{2,3},{3,2},{4,5},{5,4},{6,7},{7,6},{8,9},{9,8},{10,11... | collective-permute-start | bytes 884744 | tf_op jit(solution)/shard_map/ppermute | solution.py:27
  19.2 10.2 %collective-permute-start.6 = (bf16[5,8,2048]{2,1,0:T(8,128)(2,1)S(1)}, bf16[5,8,2048]{2,1,0:T(8,128)(2,1)S(1)}, u32[]{:S(2)}, u32[]{:S(2)}) collective-permute-start(bf16[5,8,2048]{2,1,0:T(8,128)(2,1)S(1)} %get-tuple-element.71.sent), channel_id=1, source_target_pairs={{0,2},{1,3},{2,0},{3,1},{4,6},{5,7},{6,4},{7,5},{8,10},{9,11},{10,... | collective-permute-start | bytes 491528 | tf_op jit(solution)/shard_map/ppermute | solution.py:27
  21.0 8.4 %collective-permute-start.10 = (bf16[4,8,2048]{2,1,0:T(8,128)(2,1)S(1)}, bf16[4,8,2048]{2,1,0:T(8,128)(2,1)S(1)}, u32[]{:S(2)}, u32[]{:S(2)}) collective-permute-start(bf16[4,8,2048]{2,1,0:T(8,128)(2,1)S(1)} %get-tuple-element.80), channel_id=1, source_target_pairs={{0,2},{1,3},{2,0},{3,1},{4,6},{5,7},{6,4},{7,5},{8,10},{9,11},{10,... | collective-permute-start | bytes 393224 | tf_op jit(solution)/shard_map/ppermute | solution.py:27
  21.4 1.4 %copy-start = (s32[32]{0:T(128)S(1)}, s32[32]{0:T(128)}, u32[]{:S(2)}) copy-start(s32[32]{0:T(128)} %w_hbm.1) | copy-start | bytes 388
  24.4 1.3 %collective-permute-start.3 = (bf16[8,4480]{1,0:T(8,128)(2,1)S(1)}, bf16[8,4480]{1,0:T(8,128)(2,1)S(1)}, u32[]{:S(2)}, u32[]{:S(2)}) collective-permute-start(bf16[8,4480]{1,0:T(8,128)(2,1)S(1)} %get-tuple-element.67.s_own), channel_id=1, source_target_pairs={{0,1},{1,0},{2,3},{3,2},{4,5},{5,4},{6,7},{7,6},{8,9},{9,8},{10,11... | collective-permute-start | bytes 215048 | tf_op jit(solution)/shard_map/ppermute | solution.py:27
  25.6 3.7 %collective-permute-start.4 = (bf16[8,384]{1,0:T(8,128)(2,1)S(1)}, bf16[8,384]{1,0:T(8,128)(2,1)S(1)}, u32[]{:S(2)}, u32[]{:S(2)}) collective-permute-start(bf16[8,384]{1,0:T(8,128)(2,1)S(1)} %get-tuple-element.68.s_own), channel_id=1, source_target_pairs={{0,2},{1,3},{2,0},{3,1},{4,6},{5,7},{6,4},{7,5},{8,10},{9,11},{10,... | collective-permute-start | bytes 18440 | tf_op jit(solution)/shard_map/ppermute | solution.py:27
  29.5 7.0 %collective-permute-start.11 = (f32[8,8,2048]{2,1,0:T(8,128)S(1)}, f32[8,8,2048]{2,1,0:T(8,128)S(1)}, u32[]{:S(2)}, u32[]{:S(2)}) collective-permute-start(f32[8,8,2048]{2,1,0:T(8,128)S(1)} %shard_map.153.avg), channel_id=1, source_target_pairs={{0,1},{1,0},{2,3},{3,2},{4,5},{5,4},{6,7},{7,6},{8,9},{9,8},{10,11... | collective-permute-start | bytes 1572872 | tf_op jit(solution)/shard_map/ppermute | solution.py:27
  29.6 4.0 %collective-permute-start.7 = (bf16[8,2432]{1,0:T(8,128)(2,1)S(1)}, bf16[8,2432]{1,0:T(8,128)(2,1)S(1)}, u32[]{:S(2)}, u32[]{:S(2)}) collective-permute-start(bf16[8,2432]{1,0:T(8,128)(2,1)S(1)} %get-tuple-element.72.s_own), channel_id=1, source_target_pairs={{0,4},{1,5},{2,6},{3,7},{4,0},{5,1},{6,2},{7,3},{8,12},{9,13},{10,... | collective-permute-start | bytes 116744 | tf_op jit(solution)/shard_map/ppermute | solution.py:27
  31.5 5.1 %collective-permute-start.9 = (f32[8,2048]{1,0:T(8,128)S(1)}, f32[8,2048]{1,0:T(8,128)S(1)}, u32[]{:S(2)}, u32[]{:S(2)}) collective-permute-start(f32[8,2048]{1,0:T(8,128)S(1)} %get-tuple-element.76.a_own), channel_id=1, source_target_pairs={{0,2},{1,3},{2,0},{3,1},{4,6},{5,7},{6,4},{7,5},{8,10},{9,11},{10,... | collective-permute-start | bytes 196616 | tf_op jit(solution)/shard_map/ppermute | solution.py:27
  33.7 4.9 %collective-permute-start.8 = (bf16[8,2432]{1,0:T(8,128)(2,1)S(1)}, bf16[8,2432]{1,0:T(8,128)(2,1)S(1)}, u32[]{:S(2)}, u32[]{:S(2)}) collective-permute-start(bf16[8,2432]{1,0:T(8,128)(2,1)S(1)} %shard_map.152.s_own), channel_id=1, source_target_pairs={{0,8},{1,9},{2,10},{3,11},{4,12},{5,13},{6,14},{7,15},{8,0},{9,1},... | collective-permute-start | bytes 116744 | tf_op jit(solution)/shard_map/ppermute | solution.py:27

commit v9 on v8

--- a/solution.py
+++ b/solution.py
@@ -279,7 +279,7 @@
 
 
 def write_duals(sols, y_v, avg_of, out, buf, sems, section):
-    scenarios, length, _ = y_v.shape
+    scenarios, length, _ = buf.shape
     group = scenarios // 4
 
     def copy(g):
@@ -294,7 +294,10 @@
             start = 0
             for sol in sols:
                 cols = slice(start, start + sol.shape[2])
-                fresh = y_v[s, :, cols].astype(F32) + PENALTY * (sol[s] - avg[:, cols])
+                if y_v is None:
+                    fresh = sol[s] - PENALTY * avg[:, cols]
+                else:
+                    fresh = y_v[s, :, cols].astype(F32) + PENALTY * (sol[s] - avg[:, cols])
                 buf[s, :, cols] = fresh.astype(BF16)
                 start = cols.stop
         copy(g).start()
@@ -302,8 +305,8 @@
 
 
 def later_duals_kernel(
-    sec, left, right, y2, a_own, a_got, scal, sol3, y3, avg, got,
-    out, second_avg, third_avg, buf2, buf3, full, table, sems2, sems3, sems,
+    sec, left, right, y2, a_own, a_got, scal, sol3, y3, avg, got, sol1, y1,
+    base, out, second_avg, third_avg, buf2, buf3, full, table, sems2, sems3, sems,
 ):
     _, columns = full.shape
     quarter = quarter_of()
@@ -323,12 +326,14 @@
     copies += write_duals(
         (sol3,), y3, lambda s: table[place_of(sec[s] % BRANCH, quarter)], out, buf3, sems3, 2
     )
+    for k in range(sol1.shape[0]):
+        base[k] = y1[k].astype(F32) + PENALTY * sol1[k]
     for copy in copies:
         copy.wait()
 
 
 def last_kernel(
-    sol, y_v, s_own, s_got, eta, duals_row, prior,
+    base, s_own, s_got, eta, duals_row, prior,
     out, first_avg, eta_avg, eta_duals, buf, full, row, one, sems, sems2,
 ):
     columns = full.shape[1]
@@ -345,7 +350,7 @@
     ]
     for copy in copies:
         copy.start()
-    copies += write_duals((sol,), y_v, lambda s: full[...], out, buf, sems, 0)
+    copies += write_duals((base,), None, lambda s: full[...], out, buf, sems, 0)
     for copy in copies:
         copy.wait()
 
@@ -505,12 +510,13 @@
         third_avg_kernel, 8, in_specs=[VMEM] * 4, out_specs=VMEM, out_shape=pltpu.VMEM((HALF, length, columns), F32)
     )(chip_total, node_got1, node_got2, scal)
     avg_got = partner(avg, 1)
-    out, second_avg, third_avg = call(
+    base1, out, second_avg, third_avg = call(
         later_duals_kernel,
         12,
-        in_specs=[SMEM] + [VMEM] * 10,
-        out_specs=[HBM] * 3,
-        out_shape=[
+        in_specs=[SMEM] + [VMEM] * 12,
+        out_specs=[VMEM] + [HBM] * 3,
+        out_shape=[
+            pltpu.VMEM(block, F32),
             duals_shape,
             shape((1, length, columns // 4), F32),
             shape((SHARES, length, columns), F32),
@@ -524,11 +530,11 @@
             dma((4,)),
             dma((2,)),
         ],
-    )(sec, left, right, y2, a2, a2_got, scal, sol3, y3, avg, avg_got)
+    )(sec, left, right, y2, a2, a2_got, scal, sol3, y3, avg, avg_got, sol1, y1)
     out, first_avg, eta_avg, eta_duals_new = call(
         last_kernel,
         8,
-        in_specs=[VMEM] * 6 + [HBM],
+        in_specs=[VMEM] * 5 + [HBM],
         out_specs=[HBM] * 4,
         out_shape=[
             duals_shape,
@@ -544,8 +550,8 @@
             dma((4,)),
             dma((3,)),
         ],
-        input_output_aliases={6: 0},
-    )(sol1, y1, far, far_got, eta, duals_row, out)
+        input_output_aliases={5: 0},
+    )(base1, far, far_got, eta, duals_row, out)
     return out, first_avg, second_avg, third_avg, eta_avg, eta_duals_new.reshape(scenarios)
 
 

time: 40 us -> 40 us (level)
  no operation moved by 1% of the time
where the time goes in v9:
time: 40 us; the launch traced here: 39.7 us
  Pallas kernels  14.5 us (36%)
  starting transfers between devices  13.9 us (35%)
  waiting for transfers between devices  8.96 us (22%)
  between operations  1.39 us (3%)
  other arithmetic  1.01 us (3%)
    ppermute x12, starting transfers between devices, partner(): return lax.ppermute(value, 'node', pairs)  13.9 us
    ppermute x12, waiting for transfers between devices, partner(): return lax.ppermute(value, 'node', pairs)  8.96 us
    pallas_call x1, Pallas kernels, step(): call(first_kernel, 32, in_specs=[HBM] * 8, out_specs=[SMEM, SMEM] + [VMEM...  5.53 us
    pallas_call x1, Pallas kernels, step(): call(third_kernel, 30, in_specs=[SMEM] + [VMEM] * 10, out_specs=[VMEM] *...  2.93 us
    pallas_call x1, Pallas kernels, step(): call(later_duals_kernel, 12, in_specs=[SMEM] + [VMEM] * 12, out_specs=[VM...  1.67 us
    pallas_call x1, Pallas kernels, step(): call(right_kernel, 30, in_specs=[SMEM] + [VMEM] * 8, out_specs=[VMEM] * 3...  1.59 us
    pallas_call x1, Pallas kernels, step(): call(left_kernel, 30, in_specs=[SMEM] + [VMEM] * 8, out_specs=[VMEM] * 4,...  1.38 us
    pallas_call x1, Pallas kernels, step(): call(last_kernel, 8, in_specs=[VMEM] * 5 + [HBM], out_specs=[HBM] * 4, ou...  1.11 us
  transfers between devices with their start and end apart: 12, of which 6 were waited for; matrix products, arithmetic and copies ran while one was open for 0% of the time, Pallas kernels for 26%

profile of v9, /device:TPU:0, one launch (start us, length us, event | category | flops | bytes accessed | tf_op | source)
XLA Modules:
  0.0 39.7 jit_solution(18161171337905667299)
XLA Ops:
  0.6 0.9 %fusion.1.p0 = bf16[5,8,2048]{2,1,0:T(8,128)(2,1)S(1)} fusion(bf16[1,8,512]{2,1,0:T(8,128)(2,1)} %param.16, bf16[4,8,2048]{2,1,0:T(8,128)(2,1)} %param.17), kind=kLoop, calls=%fused_computation.2 | loop fusion | flops 491520 | bytes 303104 | tf_op jit(solution)/shard_map/concatenate | solution.py:382
  1.6 3.1 %collective-permute-start.1 = (bf16[5,8,2048]{2,1,0:T(8,128)(2,1)S(1)}, bf16[5,8,2048]{2,1,0:T(8,128)(2,1)S(1)}, u32[]{:S(2)}, u32[]{:S(2)}) collective-permute-start(bf16[5,8,2048]{2,1,0:T(8,128)(2,1)S(1)} %fusion.1.p0), channel_id=1, source_target_pairs={{0,2},{1,3},{2,0},{3,1},{4,6},{5,7},{6,4},{7,5},{8,10},{9,11},{10,... | collective-permute-start | bytes 491528 | tf_op jit(solution)/shard_map/ppermute | solution.py:27
  4.6 0.0 collective-permute-start
  4.6 4.2 %collective-permute-done.1.p2 = bf16[5,8,2048]{2,1,0:T(8,128)(2,1)S(1)} collective-permute-done((bf16[5,8,2048]{2,1,0:T(8,128)(2,1)S(1)}, bf16[5,8,2048]{2,1,0:T(8,128)(2,1)S(1)}, u32[]{:S(2)}, u32[]{:S(2)}) %collective-permute-start.1) | collective-permute-done | bytes 163872 | tf_op jit(solution)/shard_map/ppermute | solution.py:27
  8.8 0.0 collective-permute-start.2
  8.8 5.5 %shard_map.145 = (s32[32]{0:T(128)S(4)}, s32[32]{0:T(128)S(4)}, bf16[32,8,2048]{2,1,0:T(8,128)(2,1)S(1)}, bf16[32,8,2048]{2,1,0:T(8,128)(2,1)S(1)}, bf16[32,8,20...) custom-call(s32[32]{0:T(128)} %w_hbm.1, ...), custom_call_target="tpu_custom_call" | custom-call | tf_op jit(solution)/shard_map/pallas_call | solution.py:385
  14.4 0.0 collective-permute-done.p1
  14.4 0.0 collective-permute-done.2.p3
  14.4 0.0 copy-start.1
  14.4 2.9 %shard_map.146 = (f32[32,8,2048]{2,1,0:T(8,128)S(1)}, f32[32,8,128]{2,1,0:T(8,128)S(1)}, f32[8,8,2048]{2,1,0:T(8,128)S(1)}, bf16[9,8,2048]{2,1,0:T(8,128)(2,1)S(1)}) custom-call(s32[32]{0:T(128)S(4)} %get-tuple-element.48.sec, bf16[5,8,2048]{2,1,0:T(8,128)(2,1)S(1)} %fusion.1.p0, bf16[5,8,2048]{2,1,0:T(8,128)(2,1)S(1)} %collective-permute-done.p1, ...), custom_call_target="tpu_custom_call" | custom-call | tf_op jit(solution)/shard_map/pallas_call | solution.py:425
  17.3 0.6 %collective-permute-start.6 = (bf16[9,8,2048]{2,1,0:T(8,128)(2,1)S(1)}, bf16[9,8,2048]{2,1,0:T(8,128)(2,1)S(1)}, u32[]{:S(2)}, u32[]{:S(2)}) collective-permute-start(bf16[9,8,2048]{2,1,0:T(8,128)(2,1)S(1)} %get-tuple-element.72.sent), channel_id=1, source_target_pairs={{0,1},{1,0},{2,3},{3,2},{4,5},{5,4},{6,7},{7,6},{8,9},{9,8},{10,11... | collective-permute-start | bytes 884744 | tf_op jit(solution)/shard_map/ppermute | solution.py:27
  18.6 0.6 %collective-permute-done.6.got = bf16[9,8,2048]{2,1,0:T(8,128)(2,1)S(1)} collective-permute-done((bf16[9,8,2048]{2,1,0:T(8,128)(2,1)S(1)}, bf16[9,8,2048]{2,1,0:T(8,128)(2,1)S(1)}, u32[]{:S(2)}, u32[]{:S(2)}) %collective-permute-start.6) | collective-permute-done | bytes 294944 | tf_op jit(solution)/shard_map/ppermute | solution.py:27
  19.1 0.1 shard_map.150
  19.2 1.8 %collective-permute-start.7 = (bf16[5,8,2048]{2,1,0:T(8,128)(2,1)S(1)}, bf16[5,8,2048]{2,1,0:T(8,128)(2,1)S(1)}, u32[]{:S(2)}, u32[]{:S(2)}) collective-permute-start(bf16[5,8,2048]{2,1,0:T(8,128)(2,1)S(1)} %get-tuple-element.73.sent), channel_id=1, source_target_pairs={{0,2},{1,3},{2,0},{3,1},{4,6},{5,7},{6,4},{7,5},{8,10},{9,11},{10,... | collective-permute-start | bytes 491528 | tf_op jit(solution)/shard_map/ppermute | solution.py:27
  21.0 0.3 collective-permute-start.8
  21.3 0.0 copy-done.1
  21.3 0.1 maximum_bitcast_fusion.level_row
  21.4 0.0 copy-start
  21.4 1.4 %shard_map.147 = (bf16[256,2048]{1,0:T(8,128)(2,1)S(1)}, f32[32,8,1024]{2,1,0:T(8,128)S(1)}, f32[8,1024]{1,0:T(8,128)S(1)}, f32[32,8,128]{2,1,0:T(8,128)S(1)}) custom-call(s32[32]{0:T(128)S(4)} %get-tuple-element.49.w, bf16[5,8,2048]{2,1,0:T(8,128)(2,1)S(1)} %fusion.1.p0, bf16[5,8,2048]{2,1,0:T(8,128)(2,1)S(1)} %collective-permute-done.p1, ...), custom_call_target="tpu_custom_call" | custom-call | tf_op jit(solution)/shard_map/pallas_call | solution.py:441
  22.8 0.0 copy-done
  22.8 1.6 %shard_map.148 = (f32[32,8,1024]{2,1,0:T(8,128)S(1)}, f32[1,32]{1,0:T(1,128)S(1)}, bf16[8,4480]{1,0:T(8,128)(2,1)S(1)}) custom-call(s32[32]{0:T(128)S(4)} %get-tuple-element.49.w, s32[1,32]{1,0:T(1,128)S(1)} %bitcast.7, f32[1,33]{1,0:T(1,128)S(1)} %maximum_bitcast_fusion.level_row, bf16[256,2048]{1,0:T(8,128)(2,1)S(1)} %get-tuple-element.63.target, ...), custom_call_target="tpu_custom_call" | custom-call | tf_op jit(solution)/shard_map/pallas_call | solution.py:468
  24.4 0.0 collective-permute-start.3
  24.4 1.3 %collective-permute-done.3.s_got = bf16[8,4480]{1,0:T(8,128)(2,1)S(1)} collective-permute-done((bf16[8,4480]{1,0:T(8,128)(2,1)S(1)}, bf16[8,4480]{1,0:T(8,128)(2,1)S(1)}, u32[]{:S(2)}, u32[]{:S(2)}) %collective-permute-start.3) | collective-permute-done | bytes 71712 | tf_op jit(solution)/shard_map/ppermute | solution.py:27
  25.7 1.8 %collective-permute-start.5 = (bf16[8,384]{1,0:T(8,128)(2,1)S(1)}, bf16[8,384]{1,0:T(8,128)(2,1)S(1)}, u32[]{:S(2)}, u32[]{:S(2)}) collective-permute-start(bf16[8,384]{1,0:T(8,128)(2,1)S(1)} %get-tuple-element.70.s_own), channel_id=1, source_target_pairs={{0,2},{1,3},{2,0},{3,1},{4,6},{5,7},{6,4},{7,5},{8,10},{9,11},{10,... | collective-permute-start | bytes 18440 | tf_op jit(solution)/shard_map/ppermute | solution.py:27
  27.5 1.9 %collective-permute-done.5.s_got = bf16[8,384]{1,0:T(8,128)(2,1)S(1)} collective-permute-done((bf16[8,384]{1,0:T(8,128)(2,1)S(1)}, bf16[8,384]{1,0:T(8,128)(2,1)S(1)}, u32[]{:S(2)}, u32[]{:S(2)}) %collective-permute-start.5) | collective-permute-done | bytes 6176 | tf_op jit(solution)/shard_map/ppermute | solution.py:27
  29.4 0.0 collective-permute-done.7.got.got1
  29.4 0.0 collective-permute-done.8.got2
  29.4 0.1 shard_map.152.avg
  29.5 0.1 collective-permute-start.9
  29.6 1.9 %collective-permute-start.10 = (bf16[8,2432]{1,0:T(8,128)(2,1)S(1)}, bf16[8,2432]{1,0:T(8,128)(2,1)S(1)}, u32[]{:S(2)}, u32[]{:S(2)}) collective-permute-start(bf16[8,2432]{1,0:T(8,128)(2,1)S(1)} %get-tuple-element.81.s_own), channel_id=1, source_target_pairs={{0,4},{1,5},{2,6},{3,7},{4,0},{5,1},{6,2},{7,3},{8,12},{9,13},{10,... | collective-permute-start | bytes 116744 | tf_op jit(solution)/shard_map/ppermute | solution.py:27
  31.5 1.5 %collective-permute-start.4 = (f32[8,2048]{1,0:T(8,128)S(1)}, f32[8,2048]{1,0:T(8,128)S(1)}, u32[]{:S(2)}, u32[]{:S(2)}) collective-permute-start(f32[8,2048]{1,0:T(8,128)S(1)} %get-tuple-element.69.a_own), channel_id=1, source_target_pairs={{0,2},{1,3},{2,0},{3,1},{4,6},{5,7},{6,4},{7,5},{8,10},{9,11},{10,... | collective-permute-start | bytes 196616 | tf_op jit(solution)/shard_map/ppermute | solution.py:27
  33.0 0.7 %collective-permute-done.10.s_got = bf16[8,2432]{1,0:T(8,128)(2,1)S(1)} collective-permute-done((bf16[8,2432]{1,0:T(8,128)(2,1)S(1)}, bf16[8,2432]{1,0:T(8,128)(2,1)S(1)}, u32[]{:S(2)}, u32[]{:S(2)}) %collective-permute-start.10) | collective-permute-done | bytes 38944 | tf_op jit(solution)/shard_map/ppermute | solution.py:27
  33.7 2.9 %collective-permute-start.11 = (bf16[8,2432]{1,0:T(8,128)(2,1)S(1)}, bf16[8,2432]{1,0:T(8,128)(2,1)S(1)}, u32[]{:S(2)}, u32[]{:S(2)}) collective-permute-start(bf16[8,2432]{1,0:T(8,128)(2,1)S(1)} %shard_map.154.s_own), channel_id=1, source_target_pairs={{0,8},{1,9},{2,10},{3,11},{4,12},{5,13},{6,14},{7,15},{8,0},{9,1},... | collective-permute-start | bytes 116744 | tf_op jit(solution)/shard_map/ppermute | solution.py:27
  36.6 0.0 collective-permute-done.4.a_got
  36.6 0.0 collective-permute-done.9.got
  36.6 1.7 %shard_map.153 = (f32[32,8,2048]{2,1,0:T(8,128)S(1)}, bf16[32,24,2048]{2,1,0:T(8,128)(2,1)}, f32[1,8,512]{2,1,0:T(8,128)}, f32[4,8,2048]{2,1,0:T(8,128)}) custom-call(s32[32]{0:T(128)S(4)} %get-tuple-element.48.sec, f32[32,8,1024]{2,1,0:T(8,128)S(1)} %get-tuple-element.60.left, f32[32,8,1024]{2,1,0:T(8,128)S(1)} %get-tuple-element.67.right, ...), custom_call_target="tpu_custom_call" | custom-call | tf_op jit(solution)/shard_map/pallas_call | solution.py:513
  38.2 0.4 collective-permute-done.11.s_got
  38.6 1.1 %shard_map.155 = (bf16[32,24,2048]{2,1,0:T(8,128)(2,1)}, f32[8,2048]{1,0:T(8,128)}, f32[1]{0:T(128)}, f32[1,32]{1,0:T(1,128)}) custom-call(f32[32,8,2048]{2,1,0:T(8,128)S(1)} %get-tuple-element.80.base, bf16[8,2432]{1,0:T(8,128)(2,1)S(1)} %shard_map.154.s_own, bf16[8,2432]{1,0:T(8,128)(2,1)S(1)} %collective-permute-done.11.s_got, ...), custom_call_target="tpu_custom_call", output_to_operand_aliasing={{0}: (5, {})} | custom-call | tf_op jit(solution)/shard_map/pallas_call | solution.py:534
  (3 shorter events, 0.1 us)
Async XLA Ops:
  1.6 7.3 %collective-permute-start.1 = (bf16[5,8,2048]{2,1,0:T(8,128)(2,1)S(1)}, bf16[5,8,2048]{2,1,0:T(8,128)(2,1)S(1)}, u32[]{:S(2)}, u32[]{:S(2)}) collective-permute-start(bf16[5,8,2048]{2,1,0:T(8,128)(2,1)S(1)} %fusion.1.p0), channel_id=1, source_target_pairs={{0,2},{1,3},{2,0},{3,1},{4,6},{5,7},{6,4},{7,5},{8,10},{9,11},{10,... | collective-permute-start | bytes 491528 | tf_op jit(solution)/shard_map/ppermute | solution.py:27
  4.6 9.7 %collective-permute-start = (bf16[5,8,2048]{2,1,0:T(8,128)(2,1)S(1)}, bf16[5,8,2048]{2,1,0:T(8,128)(2,1)S(1)}, u32[]{:S(2)}, u32[]{:S(2)}) collective-permute-start(bf16[5,8,2048]{2,1,0:T(8,128)(2,1)S(1)} %fusion.1.p0), channel_id=1, source_target_pairs={{0,1},{1,0},{2,3},{3,2},{4,5},{5,4},{6,7},{7,6},{8,9},{9,8},{10,11... | collective-permute-start | bytes 491528 | tf_op jit(solution)/shard_map/ppermute | solution.py:27
  8.8 5.6 %collective-permute-start.2 = (bf16[5,8,2048]{2,1,0:T(8,128)(2,1)S(1)}, bf16[5,8,2048]{2,1,0:T(8,128)(2,1)S(1)}, u32[]{:S(2)}, u32[]{:S(2)}) collective-permute-start(bf16[5,8,2048]{2,1,0:T(8,128)(2,1)S(1)} %collective-permute-done.1.p2), channel_id=1, source_target_pairs={{0,1},{1,0},{2,3},{3,2},{4,5},{5,4},{6,7},{7,6},{8,9},{9,8},{10,11... | collective-permute-start | bytes 491528 | tf_op jit(solution)/shard_map/ppermute | solution.py:27
  14.4 6.9 %copy-start.1 = (f32[32]{0:T(128)S(1)}, f32[32]{0:T(128)}, u32[]{:S(2)}) copy-start(f32[32]{0:T(128)} %param.19) | copy-start | bytes 388
  17.3 1.8 %collective-permute-start.6 = (bf16[9,8,2048]{2,1,0:T(8,128)(2,1)S(1)}, bf16[9,8,2048]{2,1,0:T(8,128)(2,1)S(1)}, u32[]{:S(2)}, u32[]{:S(2)}) collective-permute-start(bf16[9,8,2048]{2,1,0:T(8,128)(2,1)S(1)} %get-tuple-element.72.sent), channel_id=1, source_target_pairs={{0,1},{1,0},{2,3},{3,2},{4,5},{5,4},{6,7},{7,6},{8,9},{9,8},{10,11... | collective-permute-start | bytes 884744 | tf_op jit(solution)/shard_map/ppermute | solution.py:27
  19.2 10.2 %collective-permute-start.7 = (bf16[5,8,2048]{2,1,0:T(8,128)(2,1)S(1)}, bf16[5,8,2048]{2,1,0:T(8,128)(2,1)S(1)}, u32[]{:S(2)}, u32[]{:S(2)}) collective-permute-start(bf16[5,8,2048]{2,1,0:T(8,128)(2,1)S(1)} %get-tuple-element.73.sent), channel_id=1, source_target_pairs={{0,2},{1,3},{2,0},{3,1},{4,6},{5,7},{6,4},{7,5},{8,10},{9,11},{10,... | collective-permute-start | bytes 491528 | tf_op jit(solution)/shard_map/ppermute | solution.py:27
  21.0 8.4 %collective-permute-start.8 = (bf16[4,8,2048]{2,1,0:T(8,128)(2,1)S(1)}, bf16[4,8,2048]{2,1,0:T(8,128)(2,1)S(1)}, u32[]{:S(2)}, u32[]{:S(2)}) collective-permute-start(bf16[4,8,2048]{2,1,0:T(8,128)(2,1)S(1)} %get-tuple-element.77), channel_id=1, source_target_pairs={{0,2},{1,3},{2,0},{3,1},{4,6},{5,7},{6,4},{7,5},{8,10},{9,11},{10,... | collective-permute-start | bytes 393224 | tf_op jit(solution)/shard_map/ppermute | solution.py:27
  21.4 1.4 %copy-start = (s32[32]{0:T(128)S(1)}, s32[32]{0:T(128)}, u32[]{:S(2)}) copy-start(s32[32]{0:T(128)} %w_hbm.1) | copy-start | bytes 388
  24.4 1.3 %collective-permute-start.3 = (bf16[8,4480]{1,0:T(8,128)(2,1)S(1)}, bf16[8,4480]{1,0:T(8,128)(2,1)S(1)}, u32[]{:S(2)}, u32[]{:S(2)}) collective-permute-start(bf16[8,4480]{1,0:T(8,128)(2,1)S(1)} %get-tuple-element.68.s_own), channel_id=1, source_target_pairs={{0,1},{1,0},{2,3},{3,2},{4,5},{5,4},{6,7},{7,6},{8,9},{9,8},{10,11... | collective-permute-start | bytes 215048 | tf_op jit(solution)/shard_map/ppermute | solution.py:27
  25.7 3.7 %collective-permute-start.5 = (bf16[8,384]{1,0:T(8,128)(2,1)S(1)}, bf16[8,384]{1,0:T(8,128)(2,1)S(1)}, u32[]{:S(2)}, u32[]{:S(2)}) collective-permute-start(bf16[8,384]{1,0:T(8,128)(2,1)S(1)} %get-tuple-element.70.s_own), channel_id=1, source_target_pairs={{0,2},{1,3},{2,0},{3,1},{4,6},{5,7},{6,4},{7,5},{8,10},{9,11},{10,... | collective-permute-start | bytes 18440 | tf_op jit(solution)/shard_map/ppermute | solution.py:27
  29.5 7.0 %collective-permute-start.9 = (f32[8,8,2048]{2,1,0:T(8,128)S(1)}, f32[8,8,2048]{2,1,0:T(8,128)S(1)}, u32[]{:S(2)}, u32[]{:S(2)}) collective-permute-start(f32[8,8,2048]{2,1,0:T(8,128)S(1)} %shard_map.152.avg), channel_id=1, source_target_pairs={{0,1},{1,0},{2,3},{3,2},{4,5},{5,4},{6,7},{7,6},{8,9},{9,8},{10,11... | collective-permute-start | bytes 1572872 | tf_op jit(solution)/shard_map/ppermute | solution.py:27
  29.6 4.0 %collective-permute-start.10 = (bf16[8,2432]{1,0:T(8,128)(2,1)S(1)}, bf16[8,2432]{1,0:T(8,128)(2,1)S(1)}, u32[]{:S(2)}, u32[]{:S(2)}) collective-permute-start(bf16[8,2432]{1,0:T(8,128)(2,1)S(1)} %get-tuple-element.81.s_own), channel_id=1, source_target_pairs={{0,4},{1,5},{2,6},{3,7},{4,0},{5,1},{6,2},{7,3},{8,12},{9,13},{10,... | collective-permute-start | bytes 116744 | tf_op jit(solution)/shard_map/ppermute | solution.py:27
  31.5 5.1 %collective-permute-start.4 = (f32[8,2048]{1,0:T(8,128)S(1)}, f32[8,2048]{1,0:T(8,128)S(1)}, u32[]{:S(2)}, u32[]{:S(2)}) collective-permute-start(f32[8,2048]{1,0:T(8,128)S(1)} %get-tuple-element.69.a_own), channel_id=1, source_target_pairs={{0,2},{1,3},{2,0},{3,1},{4,6},{5,7},{6,4},{7,5},{8,10},{9,11},{10,... | collective-permute-start | bytes 196616 | tf_op jit(solution)/shard_map/ppermute | solution.py:27
  33.7 4.9 %collective-permute-start.11 = (bf16[8,2432]{1,0:T(8,128)(2,1)S(1)}, bf16[8,2432]{1,0:T(8,128)(2,1)S(1)}, u32[]{:S(2)}, u32[]{:S(2)}) collective-permute-start(bf16[8,2432]{1,0:T(8,128)(2,1)S(1)} %shard_map.154.s_own), channel_id=1, source_target_pairs={{0,8},{1,9},{2,10},{3,11},{4,12},{5,13},{6,14},{7,15},{8,0},{9,1},... | collective-permute-start | bytes 116744 | tf_op jit(solution)/shard_map/ppermute | solution.py:27

commit v10 on v9

--- a/solution.py
+++ b/solution.py
@@ -44,9 +44,9 @@
     return ((half ^ (quarter % 2)) * 2 + node // (2 * SHARES)) * SHARES + node % SHARES
 
 
-def build_target(target, anchor_of, c_v, y_v):
+def build_target(target, anchor_of, c_v, y_v, span=None):
     scenarios, length, _ = c_v.shape
-    for i in range(scenarios // 2):
+    for i in span or range(scenarios // 2):
         rows = [
             PENALTY * anchor_of(s).astype(F32) - c_v[s].astype(F32) - y_v[s].astype(F32)
             for s in (2 * i, 2 * i + 1)
@@ -104,13 +104,21 @@
             pltpu.make_async_copy(y_hbm.at[:, own, :], y_v, sems.at[6 + 2 * k]),
         ]
 
+    def part_rows(g):
+        own = pl.ds(0, length)
+        some = pl.ds(g * scenarios // 2, scenarios // 2)
+        return [
+            pltpu.make_async_copy(c_hbm.at[some, own, :], c1.at[some], sems.at[5 if g else 11 + CHUNKS]),
+            pltpu.make_async_copy(y_hbm.at[some, own, :], y1.at[some], sems.at[6 if g else 12 + CHUNKS]),
+        ]
+
     small = [
         pltpu.make_async_copy(source, into, sems.at[k])
         for k, (source, into) in enumerate(
             ((w_row_hbm, w_row), (sec_row_hbm, sec_row), (w_hbm, w), (sec_hbm, sec), (pf_hbm, pf))
         )
     ]
-    first = rows(0, c1, y1)
+    first = part_rows(0) + part_rows(1)
     later = rows(2, c3, y3) + rows(1, c2, y2)
     for copy in small + first + [chunk(j) for j in range(CHUNKS)] + later:
         copy.start()
@@ -135,9 +143,12 @@
     column = lax.broadcasted_iota(jnp.int32, pick.shape, 1)
     pick[...] = jnp.where(row % length == column % length, weight, 0.0).astype(BF16)
 
-    for copy in first:
+    for copy in first[:2]:
         copy.wait()
-    build_target(target, lambda s: pf[...], c1, y1)
+    build_target(target, lambda s: pf[...], c1, y1, range(scenarios // 4))
+    for copy in first[2:]:
+        copy.wait()
+    build_target(target, lambda s: pf[...], c1, y1, range(scenarios // 4, scenarios // 2))
 
     def after(cols, total):
         a1[:, cols] = total
@@ -404,7 +415,7 @@
             pltpu.VMEM((1, scenarios), jnp.int32),
             pltpu.VMEM((1, scenarios), jnp.int32),
             pltpu.VMEM((rows, columns), BF16),
-            dma((11 + CHUNKS,)),
+            dma((13 + CHUNKS,)),
         ],
     )(
         in_hbm(weights),

time: 40 us -> 40 us (level)
  no operation moved by 1% of the time
where the time goes in v10:
time: 40 us; the launch traced here: 39.7 us
  Pallas kernels  14.5 us (36%)
  starting transfers between devices  13.9 us (35%)
  waiting for transfers between devices  8.96 us (22%)
  between operations  1.39 us (3%)
  other arithmetic  1.01 us (3%)
    ppermute x12, starting transfers between devices, partner(): return lax.ppermute(value, 'node', pairs)  13.9 us
    ppermute x12, waiting for transfers between devices, partner(): return lax.ppermute(value, 'node', pairs)  8.96 us
    pallas_call x1, Pallas kernels, step(): call(first_kernel, 32, in_specs=[HBM] * 8, out_specs=[SMEM, SMEM] + [VMEM...  5.54 us
    pallas_call x1, Pallas kernels, step(): call(third_kernel, 30, in_specs=[SMEM] + [VMEM] * 10, out_specs=[VMEM] *...  2.93 us
    pallas_call x1, Pallas kernels, step(): call(later_duals_kernel, 12, in_specs=[SMEM] + [VMEM] * 12, out_specs=[VM...  1.67 us
    pallas_call x1, Pallas kernels, step(): call(right_kernel, 30, in_specs=[SMEM] + [VMEM] * 8, out_specs=[VMEM] * 3...  1.59 us
    pallas_call x1, Pallas kernels, step(): call(left_kernel, 30, in_specs=[SMEM] + [VMEM] * 8, out_specs=[VMEM] * 4,...  1.38 us
    pallas_call x1, Pallas kernels, step(): call(last_kernel, 8, in_specs=[VMEM] * 5 + [HBM], out_specs=[HBM] * 4, ou...  1.11 us
  transfers between devices with their start and end apart: 12, of which 6 were waited for; matrix products, arithmetic and copies ran while one was open for 0% of the time, Pallas kernels for 26%

profile of v10, /device:TPU:0, one launch (start us, length us, event | category | flops | bytes accessed | tf_op | source)
XLA Modules:
  0.0 39.7 jit_solution(8280781436028053146)
XLA Ops:
  0.6 0.9 %fusion.1.p0 = bf16[5,8,2048]{2,1,0:T(8,128)(2,1)S(1)} fusion(bf16[1,8,512]{2,1,0:T(8,128)(2,1)} %param.16, bf16[4,8,2048]{2,1,0:T(8,128)(2,1)} %param.17), kind=kLoop, calls=%fused_computation.2 | loop fusion | flops 491520 | bytes 303104 | tf_op jit(solution)/shard_map/concatenate | solution.py:393
  1.6 3.1 %collective-permute-start.1 = (bf16[5,8,2048]{2,1,0:T(8,128)(2,1)S(1)}, bf16[5,8,2048]{2,1,0:T(8,128)(2,1)S(1)}, u32[]{:S(2)}, u32[]{:S(2)}) collective-permute-start(bf16[5,8,2048]{2,1,0:T(8,128)(2,1)S(1)} %fusion.1.p0), channel_id=1, source_target_pairs={{0,2},{1,3},{2,0},{3,1},{4,6},{5,7},{6,4},{7,5},{8,10},{9,11},{10,... | collective-permute-start | bytes 491528 | tf_op jit(solution)/shard_map/ppermute | solution.py:27
  4.6 0.0 collective-permute-start
  4.6 4.2 %collective-permute-done.1.p2 = bf16[5,8,2048]{2,1,0:T(8,128)(2,1)S(1)} collective-permute-done((bf16[5,8,2048]{2,1,0:T(8,128)(2,1)S(1)}, bf16[5,8,2048]{2,1,0:T(8,128)(2,1)S(1)}, u32[]{:S(2)}, u32[]{:S(2)}) %collective-permute-start.1) | collective-permute-done | bytes 163872 | tf_op jit(solution)/shard_map/ppermute | solution.py:27
  8.8 0.0 collective-permute-start.2
  8.8 5.5 %shard_map.145 = (s32[32]{0:T(128)S(4)}, s32[32]{0:T(128)S(4)}, bf16[32,8,2048]{2,1,0:T(8,128)(2,1)S(1)}, bf16[32,8,2048]{2,1,0:T(8,128)(2,1)S(1)}, bf16[32,8,20...) custom-call(s32[32]{0:T(128)} %w_hbm.1, ...), custom_call_target="tpu_custom_call" | custom-call | tf_op jit(solution)/shard_map/pallas_call | solution.py:396
  14.4 0.0 collective-permute-done.p1
  14.4 0.0 collective-permute-done.2.p3
  14.4 0.0 copy-start.1
  14.4 2.9 %shard_map.146 = (f32[32,8,2048]{2,1,0:T(8,128)S(1)}, f32[32,8,128]{2,1,0:T(8,128)S(1)}, f32[8,8,2048]{2,1,0:T(8,128)S(1)}, bf16[9,8,2048]{2,1,0:T(8,128)(2,1)S(1)}) custom-call(s32[32]{0:T(128)S(4)} %get-tuple-element.48.sec, bf16[5,8,2048]{2,1,0:T(8,128)(2,1)S(1)} %fusion.1.p0, bf16[5,8,2048]{2,1,0:T(8,128)(2,1)S(1)} %collective-permute-done.p1, ...), custom_call_target="tpu_custom_call" | custom-call | tf_op jit(solution)/shard_map/pallas_call | solution.py:436
  17.4 0.6 %collective-permute-start.6 = (bf16[9,8,2048]{2,1,0:T(8,128)(2,1)S(1)}, bf16[9,8,2048]{2,1,0:T(8,128)(2,1)S(1)}, u32[]{:S(2)}, u32[]{:S(2)}) collective-permute-start(bf16[9,8,2048]{2,1,0:T(8,128)(2,1)S(1)} %get-tuple-element.72.sent), channel_id=1, source_target_pairs={{0,1},{1,0},{2,3},{3,2},{4,5},{5,4},{6,7},{7,6},{8,9},{9,8},{10,11... | collective-permute-start | bytes 884744 | tf_op jit(solution)/shard_map/ppermute | solution.py:27
  18.6 0.6 %collective-permute-done.6.got = bf16[9,8,2048]{2,1,0:T(8,128)(2,1)S(1)} collective-permute-done((bf16[9,8,2048]{2,1,0:T(8,128)(2,1)S(1)}, bf16[9,8,2048]{2,1,0:T(8,128)(2,1)S(1)}, u32[]{:S(2)}, u32[]{:S(2)}) %collective-permute-start.6) | collective-permute-done | bytes 294944 | tf_op jit(solution)/shard_map/ppermute | solution.py:27
  19.1 0.1 shard_map.150
  19.2 1.8 %collective-permute-start.7 = (bf16[5,8,2048]{2,1,0:T(8,128)(2,1)S(1)}, bf16[5,8,2048]{2,1,0:T(8,128)(2,1)S(1)}, u32[]{:S(2)}, u32[]{:S(2)}) collective-permute-start(bf16[5,8,2048]{2,1,0:T(8,128)(2,1)S(1)} %get-tuple-element.73.sent), channel_id=1, source_target_pairs={{0,2},{1,3},{2,0},{3,1},{4,6},{5,7},{6,4},{7,5},{8,10},{9,11},{10,... | collective-permute-start | bytes 491528 | tf_op jit(solution)/shard_map/ppermute | solution.py:27
  21.0 0.3 collective-permute-start.8
  21.3 0.0 copy-done.1
  21.3 0.1 maximum_bitcast_fusion.level_row
  21.4 0.0 copy-start
  21.4 1.4 %shard_map.147 = (bf16[256,2048]{1,0:T(8,128)(2,1)S(1)}, f32[32,8,1024]{2,1,0:T(8,128)S(1)}, f32[8,1024]{1,0:T(8,128)S(1)}, f32[32,8,128]{2,1,0:T(8,128)S(1)}) custom-call(s32[32]{0:T(128)S(4)} %get-tuple-element.49.w, bf16[5,8,2048]{2,1,0:T(8,128)(2,1)S(1)} %fusion.1.p0, bf16[5,8,2048]{2,1,0:T(8,128)(2,1)S(1)} %collective-permute-done.p1, ...), custom_call_target="tpu_custom_call" | custom-call | tf_op jit(solution)/shard_map/pallas_call | solution.py:452
  22.8 0.0 copy-done
  22.8 1.6 %shard_map.148 = (f32[32,8,1024]{2,1,0:T(8,128)S(1)}, f32[1,32]{1,0:T(1,128)S(1)}, bf16[8,4480]{1,0:T(8,128)(2,1)S(1)}) custom-call(s32[32]{0:T(128)S(4)} %get-tuple-element.49.w, s32[1,32]{1,0:T(1,128)S(1)} %bitcast.7, f32[1,33]{1,0:T(1,128)S(1)} %maximum_bitcast_fusion.level_row, bf16[256,2048]{1,0:T(8,128)(2,1)S(1)} %get-tuple-element.63.target, ...), custom_call_target="tpu_custom_call" | custom-call | tf_op jit(solution)/shard_map/pallas_call | solution.py:479
  24.4 0.0 collective-permute-start.3
  24.4 1.3 %collective-permute-done.3.s_got = bf16[8,4480]{1,0:T(8,128)(2,1)S(1)} collective-permute-done((bf16[8,4480]{1,0:T(8,128)(2,1)S(1)}, bf16[8,4480]{1,0:T(8,128)(2,1)S(1)}, u32[]{:S(2)}, u32[]{:S(2)}) %collective-permute-start.3) | collective-permute-done | bytes 71712 | tf_op jit(solution)/shard_map/ppermute | solution.py:27
  25.7 1.8 %collective-permute-start.5 = (bf16[8,384]{1,0:T(8,128)(2,1)S(1)}, bf16[8,384]{1,0:T(8,128)(2,1)S(1)}, u32[]{:S(2)}, u32[]{:S(2)}) collective-permute-start(bf16[8,384]{1,0:T(8,128)(2,1)S(1)} %get-tuple-element.70.s_own), channel_id=1, source_target_pairs={{0,2},{1,3},{2,0},{3,1},{4,6},{5,7},{6,4},{7,5},{8,10},{9,11},{10,... | collective-permute-start | bytes 18440 | tf_op jit(solution)/shard_map/ppermute | solution.py:27
  27.5 1.9 %collective-permute-done.5.s_got = bf16[8,384]{1,0:T(8,128)(2,1)S(1)} collective-permute-done((bf16[8,384]{1,0:T(8,128)(2,1)S(1)}, bf16[8,384]{1,0:T(8,128)(2,1)S(1)}, u32[]{:S(2)}, u32[]{:S(2)}) %collective-permute-start.5) | collective-permute-done | bytes 6176 | tf_op jit(solution)/shard_map/ppermute | solution.py:27
  29.4 0.0 collective-permute-done.7.got.got1
  29.4 0.0 collective-permute-done.8.got2
  29.4 0.1 shard_map.152.avg
  29.6 0.1 collective-permute-start.9
  29.6 1.9 %collective-permute-start.10 = (bf16[8,2432]{1,0:T(8,128)(2,1)S(1)}, bf16[8,2432]{1,0:T(8,128)(2,1)S(1)}, u32[]{:S(2)}, u32[]{:S(2)}) collective-permute-start(bf16[8,2432]{1,0:T(8,128)(2,1)S(1)} %get-tuple-element.81.s_own), channel_id=1, source_target_pairs={{0,4},{1,5},{2,6},{3,7},{4,0},{5,1},{6,2},{7,3},{8,12},{9,13},{10,... | collective-permute-start | bytes 116744 | tf_op jit(solution)/shard_map/ppermute | solution.py:27
  31.5 1.5 %collective-permute-start.4 = (f32[8,2048]{1,0:T(8,128)S(1)}, f32[8,2048]{1,0:T(8,128)S(1)}, u32[]{:S(2)}, u32[]{:S(2)}) collective-permute-start(f32[8,2048]{1,0:T(8,128)S(1)} %get-tuple-element.69.a_own), channel_id=1, source_target_pairs={{0,2},{1,3},{2,0},{3,1},{4,6},{5,7},{6,4},{7,5},{8,10},{9,11},{10,... | collective-permute-start | bytes 196616 | tf_op jit(solution)/shard_map/ppermute | solution.py:27
  33.0 0.7 %collective-permute-done.10.s_got = bf16[8,2432]{1,0:T(8,128)(2,1)S(1)} collective-permute-done((bf16[8,2432]{1,0:T(8,128)(2,1)S(1)}, bf16[8,2432]{1,0:T(8,128)(2,1)S(1)}, u32[]{:S(2)}, u32[]{:S(2)}) %collective-permute-start.10) | collective-permute-done | bytes 38944 | tf_op jit(solution)/shard_map/ppermute | solution.py:27
  33.7 2.9 %collective-permute-start.11 = (bf16[8,2432]{1,0:T(8,128)(2,1)S(1)}, bf16[8,2432]{1,0:T(8,128)(2,1)S(1)}, u32[]{:S(2)}, u32[]{:S(2)}) collective-permute-start(bf16[8,2432]{1,0:T(8,128)(2,1)S(1)} %shard_map.154.s_own), channel_id=1, source_target_pairs={{0,8},{1,9},{2,10},{3,11},{4,12},{5,13},{6,14},{7,15},{8,0},{9,1},... | collective-permute-start | bytes 116744 | tf_op jit(solution)/shard_map/ppermute | solution.py:27
  36.6 0.0 collective-permute-done.4.a_got
  36.6 0.0 collective-permute-done.9.got
  36.6 1.7 %shard_map.153 = (f32[32,8,2048]{2,1,0:T(8,128)S(1)}, bf16[32,24,2048]{2,1,0:T(8,128)(2,1)}, f32[1,8,512]{2,1,0:T(8,128)}, f32[4,8,2048]{2,1,0:T(8,128)}) custom-call(s32[32]{0:T(128)S(4)} %get-tuple-element.48.sec, f32[32,8,1024]{2,1,0:T(8,128)S(1)} %get-tuple-element.60.left, f32[32,8,1024]{2,1,0:T(8,128)S(1)} %get-tuple-element.67.right, ...), custom_call_target="tpu_custom_call" | custom-call | tf_op jit(solution)/shard_map/pallas_call | solution.py:524
  38.3 0.4 collective-permute-done.11.s_got
  38.6 1.1 %shard_map.155 = (bf16[32,24,2048]{2,1,0:T(8,128)(2,1)}, f32[8,2048]{1,0:T(8,128)}, f32[1]{0:T(128)}, f32[1,32]{1,0:T(1,128)}) custom-call(f32[32,8,2048]{2,1,0:T(8,128)S(1)} %get-tuple-element.80.base, bf16[8,2432]{1,0:T(8,128)(2,1)S(1)} %shard_map.154.s_own, bf16[8,2432]{1,0:T(8,128)(2,1)S(1)} %collective-permute-done.11.s_got, ...), custom_call_target="tpu_custom_call", output_to_operand_aliasing={{0}: (5, {})} | custom-call | tf_op jit(solution)/shard_map/pallas_call | solution.py:545
  (3 shorter events, 0.1 us)
Async XLA Ops:
  1.6 7.3 %collective-permute-start.1 = (bf16[5,8,2048]{2,1,0:T(8,128)(2,1)S(1)}, bf16[5,8,2048]{2,1,0:T(8,128)(2,1)S(1)}, u32[]{:S(2)}, u32[]{:S(2)}) collective-permute-start(bf16[5,8,2048]{2,1,0:T(8,128)(2,1)S(1)} %fusion.1.p0), channel_id=1, source_target_pairs={{0,2},{1,3},{2,0},{3,1},{4,6},{5,7},{6,4},{7,5},{8,10},{9,11},{10,... | collective-permute-start | bytes 491528 | tf_op jit(solution)/shard_map/ppermute | solution.py:27
  4.6 9.8 %collective-permute-start = (bf16[5,8,2048]{2,1,0:T(8,128)(2,1)S(1)}, bf16[5,8,2048]{2,1,0:T(8,128)(2,1)S(1)}, u32[]{:S(2)}, u32[]{:S(2)}) collective-permute-start(bf16[5,8,2048]{2,1,0:T(8,128)(2,1)S(1)} %fusion.1.p0), channel_id=1, source_target_pairs={{0,1},{1,0},{2,3},{3,2},{4,5},{5,4},{6,7},{7,6},{8,9},{9,8},{10,11... | collective-permute-start | bytes 491528 | tf_op jit(solution)/shard_map/ppermute | solution.py:27
  8.8 5.6 %collective-permute-start.2 = (bf16[5,8,2048]{2,1,0:T(8,128)(2,1)S(1)}, bf16[5,8,2048]{2,1,0:T(8,128)(2,1)S(1)}, u32[]{:S(2)}, u32[]{:S(2)}) collective-permute-start(bf16[5,8,2048]{2,1,0:T(8,128)(2,1)S(1)} %collective-permute-done.1.p2), channel_id=1, source_target_pairs={{0,1},{1,0},{2,3},{3,2},{4,5},{5,4},{6,7},{7,6},{8,9},{9,8},{10,11... | collective-permute-start | bytes 491528 | tf_op jit(solution)/shard_map/ppermute | solution.py:27
  14.4 6.9 %copy-start.1 = (f32[32]{0:T(128)S(1)}, f32[32]{0:T(128)}, u32[]{:S(2)}) copy-start(f32[32]{0:T(128)} %param.19) | copy-start | bytes 388
  17.4 1.8 %collective-permute-start.6 = (bf16[9,8,2048]{2,1,0:T(8,128)(2,1)S(1)}, bf16[9,8,2048]{2,1,0:T(8,128)(2,1)S(1)}, u32[]{:S(2)}, u32[]{:S(2)}) collective-permute-start(bf16[9,8,2048]{2,1,0:T(8,128)(2,1)S(1)} %get-tuple-element.72.sent), channel_id=1, source_target_pairs={{0,1},{1,0},{2,3},{3,2},{4,5},{5,4},{6,7},{7,6},{8,9},{9,8},{10,11... | collective-permute-start | bytes 884744 | tf_op jit(solution)/shard_map/ppermute | solution.py:27
  19.2 10.2 %collective-permute-start.7 = (bf16[5,8,2048]{2,1,0:T(8,128)(2,1)S(1)}, bf16[5,8,2048]{2,1,0:T(8,128)(2,1)S(1)}, u32[]{:S(2)}, u32[]{:S(2)}) collective-permute-start(bf16[5,8,2048]{2,1,0:T(8,128)(2,1)S(1)} %get-tuple-element.73.sent), channel_id=1, source_target_pairs={{0,2},{1,3},{2,0},{3,1},{4,6},{5,7},{6,4},{7,5},{8,10},{9,11},{10,... | collective-permute-start | bytes 491528 | tf_op jit(solution)/shard_map/ppermute | solution.py:27
  21.0 8.4 %collective-permute-start.8 = (bf16[4,8,2048]{2,1,0:T(8,128)(2,1)S(1)}, bf16[4,8,2048]{2,1,0:T(8,128)(2,1)S(1)}, u32[]{:S(2)}, u32[]{:S(2)}) collective-permute-start(bf16[4,8,2048]{2,1,0:T(8,128)(2,1)S(1)} %get-tuple-element.77), channel_id=1, source_target_pairs={{0,2},{1,3},{2,0},{3,1},{4,6},{5,7},{6,4},{7,5},{8,10},{9,11},{10,... | collective-permute-start | bytes 393224 | tf_op jit(solution)/shard_map/ppermute | solution.py:27
  21.4 1.4 %copy-start = (s32[32]{0:T(128)S(1)}, s32[32]{0:T(128)}, u32[]{:S(2)}) copy-start(s32[32]{0:T(128)} %w_hbm.1) | copy-start | bytes 388
  24.4 1.3 %collective-permute-start.3 = (bf16[8,4480]{1,0:T(8,128)(2,1)S(1)}, bf16[8,4480]{1,0:T(8,128)(2,1)S(1)}, u32[]{:S(2)}, u32[]{:S(2)}) collective-permute-start(bf16[8,4480]{1,0:T(8,128)(2,1)S(1)} %get-tuple-element.68.s_own), channel_id=1, source_target_pairs={{0,1},{1,0},{2,3},{3,2},{4,5},{5,4},{6,7},{7,6},{8,9},{9,8},{10,11... | collective-permute-start | bytes 215048 | tf_op jit(solution)/shard_map/ppermute | solution.py:27
  25.7 3.7 %collective-permute-start.5 = (bf16[8,384]{1,0:T(8,128)(2,1)S(1)}, bf16[8,384]{1,0:T(8,128)(2,1)S(1)}, u32[]{:S(2)}, u32[]{:S(2)}) collective-permute-start(bf16[8,384]{1,0:T(8,128)(2,1)S(1)} %get-tuple-element.70.s_own), channel_id=1, source_target_pairs={{0,2},{1,3},{2,0},{3,1},{4,6},{5,7},{6,4},{7,5},{8,10},{9,11},{10,... | collective-permute-start | bytes 18440 | tf_op jit(solution)/shard_map/ppermute | solution.py:27
  29.6 7.0 %collective-permute-start.9 = (f32[8,8,2048]{2,1,0:T(8,128)S(1)}, f32[8,8,2048]{2,1,0:T(8,128)S(1)}, u32[]{:S(2)}, u32[]{:S(2)}) collective-permute-start(f32[8,8,2048]{2,1,0:T(8,128)S(1)} %shard_map.152.avg), channel_id=1, source_target_pairs={{0,1},{1,0},{2,3},{3,2},{4,5},{5,4},{6,7},{7,6},{8,9},{9,8},{10,11... | collective-permute-start | bytes 1572872 | tf_op jit(solution)/shard_map/ppermute | solution.py:27
  29.6 4.0 %collective-permute-start.10 = (bf16[8,2432]{1,0:T(8,128)(2,1)S(1)}, bf16[8,2432]{1,0:T(8,128)(2,1)S(1)}, u32[]{:S(2)}, u32[]{:S(2)}) collective-permute-start(bf16[8,2432]{1,0:T(8,128)(2,1)S(1)} %get-tuple-element.81.s_own), channel_id=1, source_target_pairs={{0,4},{1,5},{2,6},{3,7},{4,0},{5,1},{6,2},{7,3},{8,12},{9,13},{10,... | collective-permute-start | bytes 116744 | tf_op jit(solution)/shard_map/ppermute | solution.py:27
  31.5 5.1 %collective-permute-start.4 = (f32[8,2048]{1,0:T(8,128)S(1)}, f32[8,2048]{1,0:T(8,128)S(1)}, u32[]{:S(2)}, u32[]{:S(2)}) collective-permute-start(f32[8,2048]{1,0:T(8,128)S(1)} %get-tuple-element.69.a_own), channel_id=1, source_target_pairs={{0,2},{1,3},{2,0},{3,1},{4,6},{5,7},{6,4},{7,5},{8,10},{9,11},{10,... | collective-permute-start | bytes 196616 | tf_op jit(solution)/shard_map/ppermute | solution.py:27
  33.7 4.9 %collective-permute-start.11 = (bf16[8,2432]{1,0:T(8,128)(2,1)S(1)}, bf16[8,2432]{1,0:T(8,128)(2,1)S(1)}, u32[]{:S(2)}, u32[]{:S(2)}) collective-permute-start(bf16[8,2432]{1,0:T(8,128)(2,1)S(1)} %shard_map.154.s_own), channel_id=1, source_target_pairs={{0,8},{1,9},{2,10},{3,11},{4,12},{5,13},{6,14},{7,15},{8,0},{9,1},... | collective-permute-start | bytes 116744 | tf_op jit(solution)/shard_map/ppermute | solution.py:27
